TPU v7x, 256 devices: a whole 4x4x8 slice. The times are simulated.
256 devices in a mesh: span: 32 (over z, x), cross: 8 (over y, core).
Axes of the slice: x: 4, y: 4, z: 8, core: 2. Of those that a mesh axis runs over, the one named last changes fastest.
Arguments:
- velocity: float32 [3, 2048, 32, 128], P(None, 'span', 'cross'), may hold values from -6 to 6
- viscosity: float32 [2048, 32, 128], P('span', 'cross'), may hold values from 0.02 to 0.4
Outputs:
- advanced: float32 [3, 2048, 32, 128], P(None, 'span', 'cross')
All inputs are finite; a program needn't handle non-finite values.
Results may differ from a plain program's by a relative error of at most 0.0001.
Values sent between devices are 32-bit elements; how exact they have to be, the bound alone decides.
No kernel may reach another device: no remote copies, remote signals or barrier semaphores. Data moves between devices by JAX's collectives and lax.ppermute only.
A program may use at most 64 MiB of HBM per device.

v0:
```python
import functools

import jax
import jax.numpy as jnp
import numpy as np
from jax import lax
from jax.experimental import pallas as pl
from jax.experimental.pallas import tpu as pltpu
from jax.sharding import PartitionSpec as P

SWEEPS = 4
ROWS = 4
LANES = 128
REACH = SWEEPS + 1
time_step = 0.1
highest = lax.Precision.HIGHEST
PAD_V = 16
PAD_S = 16
PAD_M = 8


def symbols(length):
    w = 2.0 * np.pi * np.arange(length) / length
    first = (14.0 / 9.0 * np.sin(w) + np.sin(2.0 * w) / 18.0) / (1.0 + 2.0 / 3.0 * np.cos(w))
    second = (24.0 / 11.0 * (1.0 - np.cos(w)) + 3.0 / 22.0 * (1.0 - np.cos(2.0 * w))) / (
        1.0 + 4.0 / 11.0 * np.cos(w)
    )
    return 1j * first, -second, 1.0 / (4.0 + second)


def block_of(symbol, cells, offset):
    kernel = np.fft.ifft(symbol).real
    at = np.arange(cells)
    return kernel[(at[:, None] - (at[None, :] + offset * cells)) % len(kernel)]


def low_rank(stack, rank):
    left, scale, right = np.linalg.svd(stack, full_matrices=False)
    return left[:, :rank] * scale[:rank], right[:rank]


@functools.lru_cache(None)
def tables(length, cells):
    first, second, inverse = symbols(length)
    at = lambda symbol, offset: block_of(symbol, cells, offset)
    slope_rank = 3
    from_left, take_left = low_rank(np.concatenate([at(first, -1), at(second, -1)]), slope_rank)
    from_right, take_right = low_rank(np.concatenate([at(first, 1), at(second, 1)]), slope_rank)
    own = np.concatenate([at(first, 0), at(second, 0)])
    slopes = np.zeros((3, 2 * cells, cells + 2 * PAD_V))
    moments = np.zeros((2 * PAD_V, 3 * cells))
    for c in range(3):
        rows = slice(slope_rank * c, slope_rank * (c + 1))
        slopes[c, :, :cells] = own
        slopes[c, :, cells:][:, rows] = from_left
        slopes[c, :, cells + PAD_V :][:, rows] = from_right
        moments[rows, cells * c : cells * (c + 1)] = take_left
        moments[PAD_V:][rows, cells * c : cells * (c + 1)] = take_right
    rank_m = 2
    m_left, t_left = low_rank(at(first, -1), rank_m)
    m_right, t_right = low_rank(at(first, 1), rank_m)
    lateral = np.zeros((cells + PAD_M, cells))
    lateral[:cells] = at(first, 0)
    lateral[cells : cells + rank_m] = t_left
    lateral[cells + rank_m : cells + 2 * rank_m] = t_right
    powers = [inverse ** (j + 1) for j in range(SWEEPS)]
    stacked = [p for p in powers] + [first * p for p in powers]
    rank_s = 2 * SWEEPS + 1
    s_left, q_left = low_rank(np.concatenate([at(p, -1) for p in stacked]), rank_s)
    s_right, q_right = low_rank(np.concatenate([at(p, 1) for p in stacked]), rank_s)
    source = np.zeros((2 * PAD_S, cells + PAD_M))
    source[:rank_s, :cells] = q_left
    source[rank_s : rank_s + rank_m, cells : cells + rank_m] = np.eye(rank_m)
    source[PAD_S : PAD_S + rank_s, :cells] = q_right
    source[PAD_S + rank_s : PAD_S + rank_s + rank_m, cells + rank_m : cells + 2 * rank_m] = np.eye(rank_m)
    depth = cells + 2 * PAD_S + PAD_M
    solve = np.zeros((2 * cells, SWEEPS * depth))
    for j in range(SWEEPS):
        for half in range(2):
            index = half * SWEEPS + j
            rows = slice(cells * index, cells * (index + 1))
            part = np.zeros((cells, depth))
            center = at(stacked[index], 0)
            part[:, :cells] = center
            low, high, mine = cells, cells + PAD_S, cells + 2 * PAD_S
            part[:, low : low + rank_s] = s_left[rows]
            part[:, low + rank_s : low + rank_s + rank_m] = center @ m_left
            part[:, high : high + rank_s] = s_right[rows]
            part[:, high + rank_s : high + rank_s + rank_m] = center @ m_right
            part[:, mine : mine + rank_m] = s_right[rows] @ (q_right @ m_left)
            part[:, mine + rank_m : mine + 2 * rank_m] = s_left[rows] @ (q_left @ m_right)
            solve[cells * half : cells * (half + 1), depth * j : depth * (j + 1)] = -part
    return tuple(x.astype(np.float32) for x in (slopes, moments, lateral, source, solve))


def dot(a, b):
    return jnp.dot(a, b, precision=highest, preferred_element_type=jnp.float32)


def lane(r, count=1):
    return slice(r * LANES, (r + count) * LANES)


def turned(tile, step):
    return pltpu.roll(tile, (-step) % LANES, 1)


def edge_masks():
    at = lax.axis_index("cross")
    last = lax.axis_size("cross") - 1
    flag = lambda test: jnp.where(test, 1.0, 0.0).astype(jnp.float32)
    return (flag(at >= 1), flag(at >= 2), flag(at <= last - 1), flag(at <= last - 2))


def masked(tile, e, masks):
    if e < -ROWS:
        return tile * masks[1]
    if e < 0:
        return tile * masks[0]
    if e >= 2 * ROWS:
        return tile * masks[3]
    if e >= ROWS:
        return tile * masks[2]
    return tile


def first_diff(up_one, down_one, up_two, down_two):
    return (8.0 * (up_one - down_one) - (up_two - down_two)) * (1.0 / 12.0)


def second_diff(middle, up_one, down_one, up_two, down_two):
    return (16.0 * (up_one + down_one) - (up_two + down_two) - 30.0 * middle) * (1.0 / 12.0)


def stream_slope(tile):
    return first_diff(turned(tile, 1), turned(tile, -1), turned(tile, 2), turned(tile, -2))


def open_kernel(cells, velocity, viscosity, moments, flat, thick, to_right, to_left, upward, downward):
    for r in range(ROWS):
        thick[:, lane(r)] = viscosity[:, r, :]
        for c in range(3):
            flat[cells * c : cells * (c + 1), lane(r)] = velocity[c, :, r, :]
    edges_kernel(flat, moments, to_right, to_left, upward, downward)


def edges_kernel(flat, moments, to_right, to_left, upward, downward):
    upward[...] = flat[:, lane(ROWS - 2, 2)]
    downward[...] = flat[:, lane(0, 2)]
    both = dot(moments[...], flat[...])
    to_right[...] = both[:PAD_V]
    to_left[...] = both[PAD_V:]


def tendency_kernel(cells, second, *refs):
    if second:
        base, *refs = refs
    flat, thick, left, right, low, high, slopes, lateral, section, near, up_far, down_far = refs
    masks = edge_masks()

    def tile(c, r):
        rows = slice(cells * c, cells * (c + 1))
        if r < 0:
            return masked(low[rows, lane(r + 2)], r, masks)
        if r >= ROWS:
            return masked(high[rows, lane(r - ROWS)], r, masks)
        return flat[rows, lane(r)]

    sides = jnp.concatenate([left[...], right[...]], axis=0)
    for c in range(3):
        rows = slice(cells * c, cells * (c + 1))
        spanned = dot(slopes[c], jnp.concatenate([flat[rows, :], sides], axis=0))
        for r in range(ROWS):
            here = tile(c, r)
            up_one, down_one = turned(here, 1), turned(here, -1)
            up_two, down_two = turned(here, 2), turned(here, -2)
            above_one, below_one = tile(c, r + 1), tile(c, r - 1)
            above_two, below_two = tile(c, r + 2), tile(c, r - 2)
            carried = (
                tile(0, r) * first_diff(up_one, down_one, up_two, down_two)
                + tile(1, r) * first_diff(above_one, below_one, above_two, below_two)
                + tile(2, r) * spanned[:cells, lane(r)]
            )
            spread = (
                second_diff(here, up_one, down_one, up_two, down_two)
                + second_diff(here, above_one, below_one, above_two, below_two)
                + spanned[cells:, lane(r)]
            )
            moved = here + time_step * (thick[:, lane(r)] * spread - carried)
            if second:
                moved = 0.5 * base[rows, lane(r)] + 0.5 * moved
            section[rows, lane(r)] = moved
            if c == 0:
                near[:cells, lane(r)] = stream_slope(moved)
            if c == 1:
                near[:cells, lane(ROWS + r)] = moved
    side = dot(lateral[...], section[2 * cells :, :])
    near[:cells, : ROWS * LANES] += side[:cells]
    near[cells:, : ROWS * LANES] = side[cells:]
    near[cells:, ROWS * LANES :] = jnp.zeros_like(near[cells:, ROWS * LANES :])
    up_far[:, lane(0)] = near[:, lane(ROWS - 1)]
    up_far[:, lane(1, 3)] = near[:, lane(ROWS + 1, 3)]
    down_far[:, lane(0)] = near[:, lane(0)]
    down_far[:, lane(1, 3)] = near[:, lane(ROWS, 3)]


def source_kernel(cells, near, low_one, high_one, low_two, high_two, source, ext, to_right, to_left):
    masks = edge_masks()

    def joined(e, rows):
        if e < -ROWS:
            return low_two[rows, lane(e + REACH)]
        if e < 0:
            return low_one[rows, lane(e + ROWS)]
        if e >= 2 * ROWS:
            return high_two[rows, lane(e - 2 * ROWS)]
        if e >= ROWS:
            return high_one[rows, lane(e - ROWS)]
        return near[rows, lane(e)]

    def across(e):
        rows = slice(0, cells)
        if e < -ROWS:
            return masked(low_two[rows, lane(e + 2 * ROWS)], e, masks)
        if e < 0:
            return masked(low_one[rows, lane(e + 2 * ROWS)], e, masks)
        if e >= 2 * ROWS:
            return masked(high_two[rows, lane(1 + e - 2 * ROWS)], e, masks)
        if e >= ROWS:
            return masked(high_one[rows, lane(e)], e, masks)
        return near[rows, lane(ROWS + e)]

    for e in range(-REACH, ROWS + REACH):
        total = joined(e, slice(0, cells)) + first_diff(
            across(e + 1), across(e - 1), across(e + 2), across(e - 2)
        )
        ext[:cells, lane(e + REACH)] = masked(total, e, masks)
        ext[cells:, lane(e + REACH)] = masked(joined(e, slice(cells, cells + PAD_M)), e, masks)
    both = dot(source[...], ext[...])
    to_right[...] = both[:PAD_S]
    to_left[...] = both[PAD_S:]


def solve_kernel(cells, last, ext, left, right, section, solve, *refs):
    if last:
        out, levels = refs
    else:
        moments, flat, to_right, to_left, upward, downward, levels = refs
    masks = edge_masks()
    depth = cells + 2 * PAD_S + PAD_M
    levels[:cells, :] = ext[:cells, :]
    levels[cells : cells + PAD_S, :] = left[...]
    levels[cells + PAD_S : cells + 2 * PAD_S, :] = right[...]
    levels[cells + 2 * PAD_S : depth, :] = ext[cells:, :]
    for j in range(1, SWEEPS):
        before = slice(depth * (j - 1), depth * j)
        after = slice(depth * j, depth * (j + 1))
        for e in range(-REACH + j, ROWS + REACH - j):
            here = levels[before, lane(e + REACH)]
            beside = (
                turned(here, 1)
                + turned(here, -1)
                + levels[before, lane(e + REACH + 1)]
                + levels[before, lane(e + REACH - 1)]
            )
            levels[after, lane(e + REACH)] = masked(beside, e, masks)
    found = dot(solve[...], levels[:, lane(REACH - 2, ROWS + 4)])
    phi = lambda r: masked(found[:cells, lane(r + 2)], r, masks)
    for r in range(ROWS):
        gradient = (
            stream_slope(phi(r)),
            first_diff(phi(r + 1), phi(r - 1), phi(r + 2), phi(r - 2)),
            found[cells:, lane(r + 2)],
        )
        for c in range(3):
            rows = slice(cells * c, cells * (c + 1))
            value = section[rows, lane(r)] - gradient[c]
            if last:
                out[c, :, r, :] = value
            else:
                flat[rows, lane(r)] = value
    if not last:
        edges_kernel(flat, moments, to_right, to_left, upward, downward)


def call(body, shapes, *args, scratch=()):
    return pl.pallas_call(
        body,
        out_shape=[jax.ShapeDtypeStruct(s, jnp.float32) for s in shapes],
        scratch_shapes=scratch,
        compiler_params=pltpu.CompilerParams(vmem_limit_bytes=40 * 1024 * 1024),
    )(*args)


def shifted(block, axis, step):
    count = lax.axis_size(axis)
    return lax.ppermute(block, axis, [(i, (i + step) % count) for i in range(count)])


def per_device(velocity, viscosity):
    components, cells, row_cells, columns = velocity.shape
    slopes, moments, lateral, source, solve = (
        jnp.asarray(t) for t in tables(cells * lax.axis_size("span"), cells)
    )
    width = row_cells * columns
    wide = (row_cells + 2 * REACH) * columns
    depth = cells + 2 * PAD_S + PAD_M
    edges = [(PAD_V, width), (PAD_V, width), (3 * cells, 2 * columns), (3 * cells, 2 * columns)]
    start, thick, to_right, to_left, upward, downward = call(
        functools.partial(open_kernel, cells),
        [(3 * cells, width), (cells, width)] + edges,
        velocity, viscosity, moments,
    )
    flat = start
    for second in (False, True):
        left = shifted(to_right, "span", 1)
        right = shifted(to_left, "span", -1)
        low = shifted(upward, "cross", 1)
        high = shifted(downward, "cross", -1)
        base = (start,) if second else ()
        section, near, up_far, down_far = call(
            functools.partial(tendency_kernel, cells, second),
            [(3 * cells, width), (cells + PAD_M, 2 * width), (cells + PAD_M, width), (cells + PAD_M, width)],
            *base, flat, thick, left, right, low, high, slopes, lateral,
        )
        low_one = shifted(near, "cross", 1)
        high_one = shifted(near, "cross", -1)
        low_two = shifted(up_far, "cross", 2)
        high_two = shifted(down_far, "cross", -2)
        ext, to_right, to_left = call(
            functools.partial(source_kernel, cells),
            [(cells + PAD_M, wide), (PAD_S, wide), (PAD_S, wide)],
            near, low_one, high_one, low_two, high_two, source,
        )
        left = shifted(to_right, "span", 1)
        right = shifted(to_left, "span", -1)
        scratch = [pltpu.VMEM((SWEEPS * depth, wide), jnp.float32)]
        if second:
            (out,) = call(
                functools.partial(solve_kernel, cells, True),
                [velocity.shape],
                ext, left, right, section, solve,
                scratch=scratch,
            )
        else:
            flat, to_right, to_left, upward, downward = call(
                functools.partial(solve_kernel, cells, False),
                [(3 * cells, width)] + edges,
                ext, left, right, section, solve, moments,
                scratch=scratch,
            )
    return out


def solution(mesh):
    in_specs = (P(None, "span", "cross", None), P("span", "cross", None))
    out_specs = P(None, "span", "cross", None)
    return jax.shard_map(
        per_device, mesh=mesh, in_specs=in_specs, out_specs=out_specs, check_vma=False
    )
```

profile of v0, /device:TPU:1, one launch (start us, length us, event | category | flops | bytes accessed | tf_op | source)
XLA Modules:
  0.0 71.4 jit_solution(2815940395611841632)
XLA Ops:
  0.0 0.0 copy-start.1
  0.0 0.0 copy-start.2
  0.0 1.0 %copy-done.2 = f32[3,64,4,128]{3,2,1,0:T(4,128)S(1)} copy-done((f32[3,64,4,128]{3,2,1,0:T(4,128)S(1)}, f32[3,64,4,128]{3,2,1,0:T(4,128)}, u32[]{:S(2)}) %copy-start.2) | copy-done | bytes 393240
  1.0 0.0 copy-start.4
  1.0 0.9 %copy-done.4 = f32[64,4,128]{2,1,0:T(4,128)S(1)} copy-done((f32[64,4,128]{2,1,0:T(4,128)S(1)}, f32[64,4,128]{2,1,0:T(4,128)}, u32[]{:S(2)}) %copy-start.4) | copy-done | bytes 131096
  1.9 0.0 copy-start.5
  1.9 0.8 %copy-done.5 = f32[32,192]{1,0:T(8,128)S(1)} copy-done((f32[32,192]{1,0:T(8,128)S(1)}, f32[32,192]{1,0:T(8,128)}, u32[]{:S(2)}) %copy-start.5) | copy-done | bytes 24600
  2.7 0.0 copy-start.3
  2.7 0.6 shard_map.73
  3.3 2.7 %collective-permute-start.2 = (f32[192,256]{1,0:T(8,128)S(1)}, f32[192,256]{1,0:T(8,128)S(1)}, u32[]{:S(2)}, u32[]{:S(2)}) collective-permute-start(f32[192,256]{1,0:T(8,128)S(1)} %get-tuple-element.34), channel_id=1, source_target_pairs={{0,1},{1,2},{2,3},{3,4},{4,5},{5,6},{6,7},{7,0},{8,9},{9,10},{10,1... | collective-permute-start | bytes 589832 | tf_op jit(solution)/shard_map/ppermute | solution.py:297
  6.0 0.6 collective-permute-start.3
  6.6 0.6 collective-permute-start
  7.2 6.6 %collective-permute-start.1 = (f32[16,512]{1,0:T(8,128)S(1)}, f32[16,512]{1,0:T(8,128)S(1)}, u32[]{:S(2)}, u32[]{:S(2)}) collective-permute-start(f32[16,512]{1,0:T(8,128)S(1)} %get-tuple-element.33), channel_id=1, source_target_pairs={{0,248},{8,0},{16,8},{24,16},{32,24},{40,32},{48,40},{56,48},{64,5... | collective-permute-start | bytes 98312 | tf_op jit(solution)/shard_map/ppermute | solution.py:297
  13.8 1.3 %collective-permute-done.refs_2_ = f32[16,512]{1,0:T(8,128)S(1)} collective-permute-done((f32[16,512]{1,0:T(8,128)S(1)}, f32[16,512]{1,0:T(8,128)S(1)}, u32[]{:S(2)}, u32[]{:S(2)}) %collective-permute-start) | collective-permute-done | bytes 32800 | tf_op jit(solution)/shard_map/ppermute | solution.py:297
  15.1 0.0 collective-permute-done.1.refs_3_
  15.1 0.0 collective-permute-done.2.refs_4_
  15.1 0.0 collective-permute-done.3.refs_5_
  15.1 0.0 copy-done.1
  15.1 0.0 copy-done.3
  15.1 0.0 copy-start.7
  15.1 1.3 %shard_map.74 = (f32[192,512]{1,0:T(8,128)S(1)}, f32[72,1024]{1,0:T(8,128)S(1)}, f32[72,512]{1,0:T(8,128)S(1)}, f32[72,512]{1,0:T(8,128)S(1)}) custom-call(f32[192,512]{1,0:T(8,128)S(1)} %get-tuple-element.30.refs_0_, f32[64,512]{1,0:T(8,128)S(1)} %get-tuple-element.31.refs_1_.refs_2_, f32[16,512]{1,0:T(8,128)S(1)} %collective-permute-done.refs_2_, ...), custom_call_target="tpu_custom_call" | custom-call | tf_op jit(solution)/shard_map/pallas_call | solution.py:287
  16.4 2.7 %collective-permute-start.5 = (f32[72,1024]{1,0:T(8,128)S(1)}, f32[72,1024]{1,0:T(8,128)S(1)}, u32[]{:S(2)}, u32[]{:S(2)}) collective-permute-start(f32[72,1024]{1,0:T(8,128)S(1)} %get-tuple-element.36.near), channel_id=1, source_target_pairs={{0,7},{1,0},{2,1},{3,2},{4,3},{5,4},{6,5},{7,6},{8,15},{9,8},{10,9... | collective-permute-start | bytes 884744 | tf_op jit(solution)/shard_map/ppermute | solution.py:297
  19.1 0.0 collective-permute-start.4
  19.1 1.3 %collective-permute-start.6 = (f32[72,512]{1,0:T(8,128)S(1)}, f32[72,512]{1,0:T(8,128)S(1)}, u32[]{:S(2)}, u32[]{:S(2)}) collective-permute-start(f32[72,512]{1,0:T(8,128)S(1)} %get-tuple-element.37), channel_id=1, source_target_pairs={{0,2},{1,3},{2,4},{3,5},{4,6},{5,7},{6,0},{7,1},{8,10},{9,11},{10,... | collective-permute-start | bytes 442376 | tf_op jit(solution)/shard_map/ppermute | solution.py:297
  20.4 0.0 copy-start
  20.4 0.0 copy-start.6
  20.4 1.4 %collective-permute-start.7 = (f32[72,512]{1,0:T(8,128)S(1)}, f32[72,512]{1,0:T(8,128)S(1)}, u32[]{:S(2)}, u32[]{:S(2)}) collective-permute-start(f32[72,512]{1,0:T(8,128)S(1)} %get-tuple-element.38), channel_id=1, source_target_pairs={{0,6},{1,7},{2,0},{3,1},{4,2},{5,3},{6,4},{7,5},{8,14},{9,15},{10,... | collective-permute-start | bytes 442376 | tf_op jit(solution)/shard_map/ppermute | solution.py:297
  21.8 7.2 %collective-permute-done.6.low_two = f32[72,512]{1,0:T(8,128)S(1)} collective-permute-done((f32[72,512]{1,0:T(8,128)S(1)}, f32[72,512]{1,0:T(8,128)S(1)}, u32[]{:S(2)}, u32[]{:S(2)}) %collective-permute-start.6) | collective-permute-done | bytes 147488 | tf_op jit(solution)/shard_map/ppermute | solution.py:297
  28.9 0.0 collective-permute-done.7.high_two
  28.9 0.0 collective-permute-done.5.high_one
  28.9 0.0 collective-permute-done.4.low_one
  29.0 0.0 copy-done.7
  29.0 0.5 shard_map.75
  29.4 0.1 collective-permute-start.8
  29.5 5.1 %collective-permute-start.9 = (f32[16,1792]{1,0:T(8,128)S(1)}, f32[16,1792]{1,0:T(8,128)S(1)}, u32[]{:S(2)}, u32[]{:S(2)}) collective-permute-start(f32[16,1792]{1,0:T(8,128)S(1)} %get-tuple-element.41), channel_id=1, source_target_pairs={{0,248},{8,0},{16,8},{24,16},{32,24},{40,32},{48,40},{56,48},{64,5... | collective-permute-start | bytes 344072 | tf_op jit(solution)/shard_map/ppermute | solution.py:297
  34.6 2.6 %collective-permute-done.8.left = f32[16,1792]{1,0:T(8,128)S(1)} collective-permute-done((f32[16,1792]{1,0:T(8,128)S(1)}, f32[16,1792]{1,0:T(8,128)S(1)}, u32[]{:S(2)}, u32[]{:S(2)}) %collective-permute-start.8) | collective-permute-done | bytes 114720 | tf_op jit(solution)/shard_map/ppermute | solution.py:297
  37.2 0.0 collective-permute-done.9.right
  37.2 0.0 copy-done
  37.2 0.0 copy-done.6
  37.2 1.8 %shard_map.76 = (f32[192,512]{1,0:T(8,128)S(1)}, f32[16,512]{1,0:T(8,128)S(1)}, f32[16,512]{1,0:T(8,128)S(1)}, f32[192,256]{1,0:T(8,128)S(1)}, f32[192,256]{1,0:T(8,128)S(1)}) custom-call(f32[72,1792]{1,0:T(8,128)S(1)} %get-tuple-element.39.ext, f32[16,1792]{1,0:T(8,128)S(1)} %collective-permute-done.8.left, f32[16,1792]{1,0:T(8,128)S(1)} %collective-permute-done.9.right, ...), custom_call_target="tpu_custom_call" | custom-call | tf_op jit(solution)/shard_map/pallas_call | solution.py:287
  39.0 0.5 collective-permute-start.12
  39.5 0.0 collective-permute-start.13
  39.6 0.0 collective-permute-start.10
  39.6 5.1 %collective-permute-start.11 = (f32[16,512]{1,0:T(8,128)S(1)}, f32[16,512]{1,0:T(8,128)S(1)}, u32[]{:S(2)}, u32[]{:S(2)}) collective-permute-start(f32[16,512]{1,0:T(8,128)S(1)} %get-tuple-element.45), channel_id=1, source_target_pairs={{0,248},{8,0},{16,8},{24,16},{32,24},{40,32},{48,40},{56,48},{64,5... | collective-permute-start | bytes 98312 | tf_op jit(solution)/shard_map/ppermute | solution.py:297
  44.7 1.3 %collective-permute-done.10.refs_3_ = f32[16,512]{1,0:T(8,128)S(1)} collective-permute-done((f32[16,512]{1,0:T(8,128)S(1)}, f32[16,512]{1,0:T(8,128)S(1)}, u32[]{:S(2)}, u32[]{:S(2)}) %collective-permute-start.10) | collective-permute-done | bytes 32800 | tf_op jit(solution)/shard_map/ppermute | solution.py:297
  46.0 0.0 collective-permute-done.11.refs_4_
  46.0 0.0 collective-permute-done.12.refs_5_
  46.0 0.0 collective-permute-done.13.refs_6_
  46.0 1.3 %shard_map.77 = (f32[192,512]{1,0:T(8,128)S(1)}, f32[72,1024]{1,0:T(8,128)S(1)}, f32[72,512]{1,0:T(8,128)S(1)}, f32[72,512]{1,0:T(8,128)S(1)}) custom-call(f32[192,512]{1,0:T(8,128)S(1)} %get-tuple-element.30.refs_0_, f32[192,512]{1,0:T(8,128)S(1)} %get-tuple-element.43.refs_1_, f32[64,512]{1,0:T(8,128)S(1)} %get-tuple-element.31.refs_1_.refs_2_, ...), custom_call_target="tpu_custom_call" | custom-call | tf_op jit(solution)/shard_map/pallas_call | solution.py:287
  47.3 3.6 %collective-permute-start.15 = (f32[72,1024]{1,0:T(8,128)S(1)}, f32[72,1024]{1,0:T(8,128)S(1)}, u32[]{:S(2)}, u32[]{:S(2)}) collective-permute-start(f32[72,1024]{1,0:T(8,128)S(1)} %get-tuple-element.48.near), channel_id=1, source_target_pairs={{0,7},{1,0},{2,1},{3,2},{4,3},{5,4},{6,5},{7,6},{8,15},{9,8},{10,9... | collective-permute-start | bytes 884744 | tf_op jit(solution)/shard_map/ppermute | solution.py:297
  50.9 0.0 collective-permute-start.14
  50.9 0.0 collective-permute-start.16
  50.9 2.7 %collective-permute-start.17 = (f32[72,512]{1,0:T(8,128)S(1)}, f32[72,512]{1,0:T(8,128)S(1)}, u32[]{:S(2)}, u32[]{:S(2)}) collective-permute-start(f32[72,512]{1,0:T(8,128)S(1)} %get-tuple-element.50), channel_id=1, source_target_pairs={{0,6},{1,7},{2,0},{3,1},{4,2},{5,3},{6,4},{7,5},{8,14},{9,15},{10,... | collective-permute-start | bytes 442376 | tf_op jit(solution)/shard_map/ppermute | solution.py:297
  53.6 7.2 %collective-permute-done.16.low_two = f32[72,512]{1,0:T(8,128)S(1)} collective-permute-done((f32[72,512]{1,0:T(8,128)S(1)}, f32[72,512]{1,0:T(8,128)S(1)}, u32[]{:S(2)}, u32[]{:S(2)}) %collective-permute-start.16) | collective-permute-done | bytes 147488 | tf_op jit(solution)/shard_map/ppermute | solution.py:297
  60.8 0.0 collective-permute-done.17.high_two
  60.8 0.0 collective-permute-done.15.high_one
  60.8 0.0 collective-permute-done.14.low_one
  60.8 0.5 shard_map.78
  61.3 0.1 collective-permute-start.18
  61.3 5.1 %collective-permute-start.19 = (f32[16,1792]{1,0:T(8,128)S(1)}, f32[16,1792]{1,0:T(8,128)S(1)}, u32[]{:S(2)}, u32[]{:S(2)}) collective-permute-start(f32[16,1792]{1,0:T(8,128)S(1)} %get-tuple-element.53), channel_id=1, source_target_pairs={{0,248},{8,0},{16,8},{24,16},{32,24},{40,32},{48,40},{56,48},{64,5... | collective-permute-start | bytes 344072 | tf_op jit(solution)/shard_map/ppermute | solution.py:297
  66.5 2.6 %collective-permute-done.18.left = f32[16,1792]{1,0:T(8,128)S(1)} collective-permute-done((f32[16,1792]{1,0:T(8,128)S(1)}, f32[16,1792]{1,0:T(8,128)S(1)}, u32[]{:S(2)}, u32[]{:S(2)}) %collective-permute-start.18) | collective-permute-done | bytes 114720 | tf_op jit(solution)/shard_map/ppermute | solution.py:297
  69.1 0.0 collective-permute-done.19.right
  69.1 2.4 %shard_map.79 = f32[3,64,4,128]{3,2,1,0:T(4,128)} custom-call(f32[72,1792]{1,0:T(8,128)S(1)} %get-tuple-element.51.ext, f32[16,1792]{1,0:T(8,128)S(1)} %collective-permute-done.18.left, f32[16,1792]{1,0:T(8,128)S(1)} %collective-permute-done.19.right, f32[192,512]{1,0:T(8,128)S(1)} %get-tuple-element.54.section, f32[128,416]{1,0:T(8,128)S(1)} %copy-done), custom_call_target="tpu_custom_call" | custom-call | tf_op jit(solution)/shard_map/pallas_call | solution.py:287
Async XLA Ops:
  0.0 15.1 %copy-start.1 = (f32[3,128,96]{2,1,0:T(8,128)S(1)}, f32[3,128,96]{2,1,0:T(8,128)}, u32[]{:S(2)}) copy-start(f32[3,128,96]{2,1,0:T(8,128)} %constant.10.clone.refs_6_.refs_7_) | copy-start | bytes 442372
  0.0 1.0 %copy-start.2 = (f32[3,64,4,128]{3,2,1,0:T(4,128)S(1)}, f32[3,64,4,128]{3,2,1,0:T(4,128)}, u32[]{:S(2)}) copy-start(f32[3,64,4,128]{3,2,1,0:T(4,128)} %velocity.1) | copy-start | bytes 1179652
  1.0 0.9 %copy-start.4 = (f32[64,4,128]{2,1,0:T(4,128)S(1)}, f32[64,4,128]{2,1,0:T(4,128)}, u32[]{:S(2)}) copy-start(f32[64,4,128]{2,1,0:T(4,128)} %viscosity.1) | copy-start | bytes 393220
  1.9 0.8 %copy-start.5 = (f32[32,192]{1,0:T(8,128)S(1)}, f32[32,192]{1,0:T(8,128)}, u32[]{:S(2)}) copy-start(f32[32,192]{1,0:T(8,128)} %constant.11.clone.moments.refs_0_) | copy-start | bytes 73732
  2.7 12.4 %copy-start.3 = (f32[72,64]{1,0:T(8,128)S(1)}, f32[72,64]{1,0:T(8,128)}, u32[]{:S(2)}) copy-start(f32[72,64]{1,0:T(8,128)} %constant.12.clone.refs_7_.refs_8_) | copy-start | bytes 55300
  3.3 11.8 %collective-permute-start.2 = (f32[192,256]{1,0:T(8,128)S(1)}, f32[192,256]{1,0:T(8,128)S(1)}, u32[]{:S(2)}, u32[]{:S(2)}) collective-permute-start(f32[192,256]{1,0:T(8,128)S(1)} %get-tuple-element.34), channel_id=1, source_target_pairs={{0,1},{1,2},{2,3},{3,4},{4,5},{5,6},{6,7},{7,0},{8,9},{9,10},{10,1... | collective-permute-start | bytes 589832 | tf_op jit(solution)/shard_map/ppermute | solution.py:297
  6.0 9.1 %collective-permute-start.3 = (f32[192,256]{1,0:T(8,128)S(1)}, f32[192,256]{1,0:T(8,128)S(1)}, u32[]{:S(2)}, u32[]{:S(2)}) collective-permute-start(f32[192,256]{1,0:T(8,128)S(1)} %get-tuple-element.35), channel_id=1, source_target_pairs={{0,7},{1,0},{2,1},{3,2},{4,3},{5,4},{6,5},{7,6},{8,15},{9,8},{10,9... | collective-permute-start | bytes 589832 | tf_op jit(solution)/shard_map/ppermute | solution.py:297
  6.6 8.5 %collective-permute-start = (f32[16,512]{1,0:T(8,128)S(1)}, f32[16,512]{1,0:T(8,128)S(1)}, u32[]{:S(2)}, u32[]{:S(2)}) collective-permute-start(f32[16,512]{1,0:T(8,128)S(1)} %get-tuple-element.32), channel_id=1, source_target_pairs={{0,8},{8,16},{16,24},{24,32},{32,40},{40,48},{48,56},{56,64},{64,7... | collective-permute-start | bytes 98312 | tf_op jit(solution)/shard_map/ppermute | solution.py:297
  7.2 7.9 %collective-permute-start.1 = (f32[16,512]{1,0:T(8,128)S(1)}, f32[16,512]{1,0:T(8,128)S(1)}, u32[]{:S(2)}, u32[]{:S(2)}) collective-permute-start(f32[16,512]{1,0:T(8,128)S(1)} %get-tuple-element.33), channel_id=1, source_target_pairs={{0,248},{8,0},{16,8},{24,16},{32,24},{40,32},{48,40},{56,48},{64,5... | collective-permute-start | bytes 98312 | tf_op jit(solution)/shard_map/ppermute | solution.py:297
  15.1 13.8 %copy-start.7 = (f32[32,72]{1,0:T(8,128)S(1)}, f32[32,72]{1,0:T(8,128)}, u32[]{:S(2)}) copy-start(f32[32,72]{1,0:T(8,128)} %constant.13.clone.source) | copy-start | bytes 27652
  16.4 12.5 %collective-permute-start.5 = (f32[72,1024]{1,0:T(8,128)S(1)}, f32[72,1024]{1,0:T(8,128)S(1)}, u32[]{:S(2)}, u32[]{:S(2)}) collective-permute-start(f32[72,1024]{1,0:T(8,128)S(1)} %get-tuple-element.36.near), channel_id=1, source_target_pairs={{0,7},{1,0},{2,1},{3,2},{4,3},{5,4},{6,5},{7,6},{8,15},{9,8},{10,9... | collective-permute-start | bytes 884744 | tf_op jit(solution)/shard_map/ppermute | solution.py:297
  19.1 9.9 %collective-permute-start.4 = (f32[72,1024]{1,0:T(8,128)S(1)}, f32[72,1024]{1,0:T(8,128)S(1)}, u32[]{:S(2)}, u32[]{:S(2)}) collective-permute-start(f32[72,1024]{1,0:T(8,128)S(1)} %get-tuple-element.36.near), channel_id=1, source_target_pairs={{0,1},{1,2},{2,3},{3,4},{4,5},{5,6},{6,7},{7,0},{8,9},{9,10},{10,1... | collective-permute-start | bytes 884744 | tf_op jit(solution)/shard_map/ppermute | solution.py:297
  19.1 9.9 %collective-permute-start.6 = (f32[72,512]{1,0:T(8,128)S(1)}, f32[72,512]{1,0:T(8,128)S(1)}, u32[]{:S(2)}, u32[]{:S(2)}) collective-permute-start(f32[72,512]{1,0:T(8,128)S(1)} %get-tuple-element.37), channel_id=1, source_target_pairs={{0,2},{1,3},{2,4},{3,5},{4,6},{5,7},{6,0},{7,1},{8,10},{9,11},{10,... | collective-permute-start | bytes 442376 | tf_op jit(solution)/shard_map/ppermute | solution.py:297
  20.4 16.9 %copy-start = (f32[128,416]{1,0:T(8,128)S(1)}, f32[128,416]{1,0:T(8,128)}, u32[]{:S(2)}) copy-start(f32[128,416]{1,0:T(8,128)} %constant.14.clone.solve) | copy-start | bytes 638980
  20.4 16.9 %copy-start.6 = (f32[32,192]{1,0:T(8,128)S(1)}, f32[32,192]{1,0:T(8,128)}, u32[]{:S(2)}) copy-start(f32[32,192]{1,0:T(8,128)} %constant.11.clone.moments.refs_0_) | copy-start | bytes 73732
  20.4 8.6 %collective-permute-start.7 = (f32[72,512]{1,0:T(8,128)S(1)}, f32[72,512]{1,0:T(8,128)S(1)}, u32[]{:S(2)}, u32[]{:S(2)}) collective-permute-start(f32[72,512]{1,0:T(8,128)S(1)} %get-tuple-element.38), channel_id=1, source_target_pairs={{0,6},{1,7},{2,0},{3,1},{4,2},{5,3},{6,4},{7,5},{8,14},{9,15},{10,... | collective-permute-start | bytes 442376 | tf_op jit(solution)/shard_map/ppermute | solution.py:297
  29.4 7.8 %collective-permute-start.8 = (f32[16,1792]{1,0:T(8,128)S(1)}, f32[16,1792]{1,0:T(8,128)S(1)}, u32[]{:S(2)}, u32[]{:S(2)}) collective-permute-start(f32[16,1792]{1,0:T(8,128)S(1)} %get-tuple-element.40), channel_id=1, source_target_pairs={{0,8},{8,16},{16,24},{24,32},{32,40},{40,48},{48,56},{56,64},{64,7... | collective-permute-start | bytes 344072 | tf_op jit(solution)/shard_map/ppermute | solution.py:297
  29.5 7.7 %collective-permute-start.9 = (f32[16,1792]{1,0:T(8,128)S(1)}, f32[16,1792]{1,0:T(8,128)S(1)}, u32[]{:S(2)}, u32[]{:S(2)}) collective-permute-start(f32[16,1792]{1,0:T(8,128)S(1)} %get-tuple-element.41), channel_id=1, source_target_pairs={{0,248},{8,0},{16,8},{24,16},{32,24},{40,32},{48,40},{56,48},{64,5... | collective-permute-start | bytes 344072 | tf_op jit(solution)/shard_map/ppermute | solution.py:297
  39.0 7.0 %collective-permute-start.12 = (f32[192,256]{1,0:T(8,128)S(1)}, f32[192,256]{1,0:T(8,128)S(1)}, u32[]{:S(2)}, u32[]{:S(2)}) collective-permute-start(f32[192,256]{1,0:T(8,128)S(1)} %get-tuple-element.46), channel_id=1, source_target_pairs={{0,1},{1,2},{2,3},{3,4},{4,5},{5,6},{6,7},{7,0},{8,9},{9,10},{10,1... | collective-permute-start | bytes 589832 | tf_op jit(solution)/shard_map/ppermute | solution.py:297
  39.5 6.5 %collective-permute-start.13 = (f32[192,256]{1,0:T(8,128)S(1)}, f32[192,256]{1,0:T(8,128)S(1)}, u32[]{:S(2)}, u32[]{:S(2)}) collective-permute-start(f32[192,256]{1,0:T(8,128)S(1)} %get-tuple-element.47), channel_id=1, source_target_pairs={{0,7},{1,0},{2,1},{3,2},{4,3},{5,4},{6,5},{7,6},{8,15},{9,8},{10,9... | collective-permute-start | bytes 589832 | tf_op jit(solution)/shard_map/ppermute | solution.py:297
  39.6 6.4 %collective-permute-start.10 = (f32[16,512]{1,0:T(8,128)S(1)}, f32[16,512]{1,0:T(8,128)S(1)}, u32[]{:S(2)}, u32[]{:S(2)}) collective-permute-start(f32[16,512]{1,0:T(8,128)S(1)} %get-tuple-element.44), channel_id=1, source_target_pairs={{0,8},{8,16},{16,24},{24,32},{32,40},{40,48},{48,56},{56,64},{64,7... | collective-permute-start | bytes 98312 | tf_op jit(solution)/shard_map/ppermute | solution.py:297
  39.6 6.4 %collective-permute-start.11 = (f32[16,512]{1,0:T(8,128)S(1)}, f32[16,512]{1,0:T(8,128)S(1)}, u32[]{:S(2)}, u32[]{:S(2)}) collective-permute-start(f32[16,512]{1,0:T(8,128)S(1)} %get-tuple-element.45), channel_id=1, source_target_pairs={{0,248},{8,0},{16,8},{24,16},{32,24},{40,32},{48,40},{56,48},{64,5... | collective-permute-start | bytes 98312 | tf_op jit(solution)/shard_map/ppermute | solution.py:297
  47.3 13.5 %collective-permute-start.15 = (f32[72,1024]{1,0:T(8,128)S(1)}, f32[72,1024]{1,0:T(8,128)S(1)}, u32[]{:S(2)}, u32[]{:S(2)}) collective-permute-start(f32[72,1024]{1,0:T(8,128)S(1)} %get-tuple-element.48.near), channel_id=1, source_target_pairs={{0,7},{1,0},{2,1},{3,2},{4,3},{5,4},{6,5},{7,6},{8,15},{9,8},{10,9... | collective-permute-start | bytes 884744 | tf_op jit(solution)/shard_map/ppermute | solution.py:297
  50.9 9.9 %collective-permute-start.14 = (f32[72,1024]{1,0:T(8,128)S(1)}, f32[72,1024]{1,0:T(8,128)S(1)}, u32[]{:S(2)}, u32[]{:S(2)}) collective-permute-start(f32[72,1024]{1,0:T(8,128)S(1)} %get-tuple-element.48.near), channel_id=1, source_target_pairs={{0,1},{1,2},{2,3},{3,4},{4,5},{5,6},{6,7},{7,0},{8,9},{9,10},{10,1... | collective-permute-start | bytes 884744 | tf_op jit(solution)/shard_map/ppermute | solution.py:297
  50.9 9.9 %collective-permute-start.16 = (f32[72,512]{1,0:T(8,128)S(1)}, f32[72,512]{1,0:T(8,128)S(1)}, u32[]{:S(2)}, u32[]{:S(2)}) collective-permute-start(f32[72,512]{1,0:T(8,128)S(1)} %get-tuple-element.49), channel_id=1, source_target_pairs={{0,2},{1,3},{2,4},{3,5},{4,6},{5,7},{6,0},{7,1},{8,10},{9,11},{10,... | collective-permute-start | bytes 442376 | tf_op jit(solution)/shard_map/ppermute | solution.py:297
  50.9 9.8 %collective-permute-start.17 = (f32[72,512]{1,0:T(8,128)S(1)}, f32[72,512]{1,0:T(8,128)S(1)}, u32[]{:S(2)}, u32[]{:S(2)}) collective-permute-start(f32[72,512]{1,0:T(8,128)S(1)} %get-tuple-element.50), channel_id=1, source_target_pairs={{0,6},{1,7},{2,0},{3,1},{4,2},{5,3},{6,4},{7,5},{8,14},{9,15},{10,... | collective-permute-start | bytes 442376 | tf_op jit(solution)/shard_map/ppermute | solution.py:297
  61.3 7.8 %collective-permute-start.18 = (f32[16,1792]{1,0:T(8,128)S(1)}, f32[16,1792]{1,0:T(8,128)S(1)}, u32[]{:S(2)}, u32[]{:S(2)}) collective-permute-start(f32[16,1792]{1,0:T(8,128)S(1)} %get-tuple-element.52), channel_id=1, source_target_pairs={{0,8},{8,16},{16,24},{24,32},{32,40},{40,48},{48,56},{56,64},{64,7... | collective-permute-start | bytes 344072 | tf_op jit(solution)/shard_map/ppermute | solution.py:297
  61.3 7.7 %collective-permute-start.19 = (f32[16,1792]{1,0:T(8,128)S(1)}, f32[16,1792]{1,0:T(8,128)S(1)}, u32[]{:S(2)}, u32[]{:S(2)}) collective-permute-start(f32[16,1792]{1,0:T(8,128)S(1)} %get-tuple-element.53), channel_id=1, source_target_pairs={{0,248},{8,0},{16,8},{24,16},{32,24},{40,32},{48,40},{56,48},{64,5... | collective-permute-start | bytes 344072 | tf_op jit(solution)/shard_map/ppermute | solution.py:297
where the time goes:
time: 71.6 us; the launch traced here: 71.4 us
  starting transfers between devices  38.2 us (53%)
  waiting for transfers between devices  22.2 us (31%)
  Pallas kernels  8.27 us (12%)
  local copies, waits for them, and re-layouts  2.72 us (4%)
    ppermute x20, starting transfers between devices, shifted(): lax.ppermute(block, axis, [(i, (i + step) % count) for i in range(count)])  38.2 us
    ppermute x20, waiting for transfers between devices, shifted(): lax.ppermute(block, axis, [(i, (i + step) % count) for i in range(count)])  22.2 us
    pallas_call x7, Pallas kernels, call(): pl.pallas_call(body, out_shape=[jax.ShapeDtypeStruct(s, jnp.float32) for...  8.27 us
    unnamed x16, local copies, waits for them, and re-layouts  2.72 us
  transfers between devices with their start and end apart: 20, of which 6 were waited for; matrix products, arithmetic and copies ran while one was open for 0% of the time, Pallas kernels for 0%

commit v1 on v0

v1 whole, which is shorter than its diff:
```python
import functools

import jax
import jax.numpy as jnp
import numpy as np
from jax import lax
from jax.experimental import pallas as pl
from jax.experimental.pallas import tpu as pltpu
from jax.sharding import PartitionSpec as P

SWEEPS = 4
ROWS = 4
LANES = 128
REACH = SWEEPS + 1
time_step = 0.1
highest = lax.Precision.HIGHEST
PAD_V = 16
PAD_S = 16
PAD_M = 8
GROUP = 8
RANK_V = 3
RANK_M = 2
RANK_S = 2 * SWEEPS + 3


def symbols(length):
    w = 2.0 * np.pi * np.arange(length) / length
    first = (14.0 / 9.0 * np.sin(w) + np.sin(2.0 * w) / 18.0) / (1.0 + 2.0 / 3.0 * np.cos(w))
    second = (24.0 / 11.0 * (1.0 - np.cos(w)) + 3.0 / 22.0 * (1.0 - np.cos(2.0 * w))) / (
        1.0 + 4.0 / 11.0 * np.cos(w)
    )
    return 1j * first, -second, 1.0 / (4.0 + second)


def block_of(symbol, cells, offset):
    kernel = np.fft.ifft(symbol).real
    at = np.arange(cells)
    return kernel[(at[:, None] - (at[None, :] + offset * cells)) % len(kernel)]


def low_rank(stack, rank):
    left, scale, right = np.linalg.svd(stack, full_matrices=False)
    return left[:, :rank] * scale[:rank], right[:rank]


@functools.lru_cache(None)
def tables(length, cells):
    first, second, inverse = symbols(length)
    at = lambda symbol, offset: block_of(symbol, cells, offset)
    from_left, take_left = low_rank(np.concatenate([at(first, -1), at(second, -1)]), RANK_V)
    from_right, take_right = low_rank(np.concatenate([at(first, 1), at(second, 1)]), RANK_V)
    own = np.concatenate([at(first, 0), at(second, 0)])
    slopes = np.zeros((3, 2 * cells, cells + 2 * PAD_V))
    moments = np.zeros((2 * PAD_V, 3 * cells))
    for c in range(3):
        rows = slice(RANK_V * c, RANK_V * (c + 1))
        slopes[c, :, :cells] = own
        slopes[c, :, cells:][:, rows] = from_left
        slopes[c, :, cells + PAD_V :][:, rows] = from_right
        moments[rows, cells * c : cells * (c + 1)] = take_left
        moments[PAD_V:][rows, cells * c : cells * (c + 1)] = take_right
    m_left, t_left = low_rank(at(first, -1), RANK_M)
    m_right, t_right = low_rank(at(first, 1), RANK_M)
    lateral = np.zeros((cells + PAD_M, cells))
    lateral[:cells] = at(first, 0)
    lateral[cells : cells + RANK_M] = t_left
    lateral[cells + RANK_M : cells + 2 * RANK_M] = t_right
    powers = [inverse ** (j + 1) for j in range(SWEEPS)]
    stacked = [p for p in powers] + [first * p for p in powers]
    count = len(stacked)
    s_left, q_left = low_rank(
        np.concatenate([at(p, -1) for p in stacked] + [take_left @ at(p, 0) for p in stacked]), RANK_S
    )
    s_right, q_right = low_rank(
        np.concatenate([at(p, 1) for p in stacked] + [take_right @ at(p, 0) for p in stacked]), RANK_S
    )
    e_left, e_right = s_left[count * cells :], s_right[count * cells :]
    source = np.zeros((2 * PAD_S, cells + PAD_M))
    source[:RANK_S, :cells] = q_left
    source[RANK_S : RANK_S + RANK_M, cells : cells + RANK_M] = np.eye(RANK_M)
    source[PAD_S : PAD_S + RANK_S, :cells] = q_right
    source[PAD_S + RANK_S : PAD_S + RANK_S + RANK_M, cells + RANK_M : cells + 2 * RANK_M] = np.eye(RANK_M)
    near, wide = cells + PAD_M, 2 * PAD_S
    height = 2 * cells + 4 * GROUP
    solve_own = np.zeros((height, SWEEPS * near))
    solve_sides = np.zeros((height, SWEEPS * wide))
    for j in range(SWEEPS):
        for half in range(2):
            index = half * SWEEPS + j
            rows = slice(cells * index, cells * (index + 1))
            edge = slice(RANK_V * index, RANK_V * (index + 1))
            center = at(stacked[index], 0)
            by_left, by_right = s_left[rows], s_right[rows]
            mine, sides = np.zeros((cells, near)), np.zeros((cells, wide))
            mine[:, :cells] = center
            mine[:, cells : cells + RANK_M] = by_right @ (q_right @ m_left)
            mine[:, cells + RANK_M : cells + 2 * RANK_M] = by_left @ (q_left @ m_right)
            sides[:, :RANK_S] = by_left
            sides[:, RANK_S : RANK_S + RANK_M] = center @ m_left
            sides[:, PAD_S : PAD_S + RANK_S] = by_right
            sides[:, PAD_S + RANK_S : PAD_S + RANK_S + RANK_M] = center @ m_right
            solve_own[cells * half : cells * (half + 1), near * j : near * (j + 1)] = -mine
            solve_sides[cells * half : cells * (half + 1), wide * j : wide * (j + 1)] = -sides
            for side in range(2):
                mine, sides = np.zeros((RANK_V, near)), np.zeros((RANK_V, wide))
                if side == 0:
                    back = take_left @ by_right @ q_right
                    mine[:, cells + RANK_M : cells + 2 * RANK_M] = take_left @ center @ m_right
                    sides[:, :RANK_S] = e_left[edge]
                else:
                    back = take_right @ by_left @ q_left
                    mine[:, cells : cells + RANK_M] = take_right @ center @ m_left
                    sides[:, PAD_S : PAD_S + RANK_S] = e_right[edge]
                mine[:, :cells] = back
                sides[:, RANK_S : RANK_S + RANK_M] = back @ m_left
                sides[:, PAD_S + RANK_S : PAD_S + RANK_S + RANK_M] = back @ m_right
                top = 2 * cells + GROUP * (2 * side + half)
                solve_own[top : top + RANK_V, near * j : near * (j + 1)] = -mine
                solve_sides[top : top + RANK_V, wide * j : wide * (j + 1)] = -sides
    return tuple(
        x.astype(np.float32) for x in (slopes, moments, lateral, source, solve_own, solve_sides)
    )


def dot(a, b):
    return jnp.dot(a, b, precision=highest, preferred_element_type=jnp.float32)


DIFFERENCE = ((1, 2.0 / 3.0), (-1, -2.0 / 3.0), (2, -1.0 / 12.0), (-2, 1.0 / 12.0))


def lane(r, count=1):
    return slice(r * LANES, (r + count) * LANES)


def turned(tile, step):
    return pltpu.roll(tile, (-step) % LANES, 1)


def edge_masks():
    at = lax.axis_index("cross")
    last = lax.axis_size("cross") - 1
    flag = lambda test: jnp.where(test, 1.0, 0.0).astype(jnp.float32)
    return (flag(at >= 1), flag(at >= 2), flag(at <= last - 1), flag(at <= last - 2))


def masked(tile, e, masks):
    if e < -ROWS:
        return tile * masks[1]
    if e < 0:
        return tile * masks[0]
    if e >= 2 * ROWS:
        return tile * masks[3]
    if e >= ROWS:
        return tile * masks[2]
    return tile


def first_diff(up_one, down_one, up_two, down_two):
    return (8.0 * (up_one - down_one) - (up_two - down_two)) * (1.0 / 12.0)


def second_diff(middle, up_one, down_one, up_two, down_two):
    return (16.0 * (up_one + down_one) - (up_two + down_two) - 30.0 * middle) * (1.0 / 12.0)


def stream_slope(tile):
    return first_diff(turned(tile, 1), turned(tile, -1), turned(tile, 2), turned(tile, -2))


def open_kernel(cells, velocity, moments, flat, to_right, to_left, upward, downward, landed, weights, sems):
    copies = (
        pltpu.make_async_copy(velocity, landed, sems.at[0]),
        pltpu.make_async_copy(moments, weights, sems.at[1]),
    )
    for copy in copies:
        copy.start()
    for copy in copies:
        copy.wait()
    for r in range(ROWS):
        for c in range(3):
            flat[cells * c : cells * (c + 1), lane(r)] = landed[c, :, r, :]
    upward[...] = flat[:, lane(ROWS - 2, 2)]
    downward[...] = flat[:, lane(0, 2)]
    both = dot(weights[...], flat[...])
    to_right[...] = both[:PAD_V]
    to_left[...] = both[PAD_V:]


def tendency_kernel(cells, second, *refs):
    if second:
        base, *refs = refs
    flat, thick, left, right, low, high, slopes, lateral, section, parts, up_near, down_near, up_far, down_far = refs
    masks = edge_masks()

    def tile(c, r):
        rows = slice(cells * c, cells * (c + 1))
        if r < 0:
            return masked(low[rows, lane(r + 2)], r, masks)
        if r >= ROWS:
            return masked(high[rows, lane(r - ROWS)], r, masks)
        return flat[rows, lane(r)]

    sides = jnp.concatenate([left[...], right[...]], axis=0)
    for c in range(3):
        rows = slice(cells * c, cells * (c + 1))
        spanned = dot(slopes[c], jnp.concatenate([flat[rows, :], sides], axis=0))
        for r in range(ROWS):
            here = tile(c, r)
            up_one, down_one = turned(here, 1), turned(here, -1)
            up_two, down_two = turned(here, 2), turned(here, -2)
            above_one, below_one = tile(c, r + 1), tile(c, r - 1)
            above_two, below_two = tile(c, r + 2), tile(c, r - 2)
            carried = (
                tile(0, r) * first_diff(up_one, down_one, up_two, down_two)
                + tile(1, r) * first_diff(above_one, below_one, above_two, below_two)
                + tile(2, r) * spanned[:cells, lane(r)]
            )
            spread = (
                second_diff(here, up_one, down_one, up_two, down_two)
                + second_diff(here, above_one, below_one, above_two, below_two)
                + spanned[cells:, lane(r)]
            )
            moved = here + time_step * (thick[:, r, :] * spread - carried)
            if second:
                moved = 0.5 * base[rows, lane(r)] + 0.5 * moved
            section[rows, lane(r)] = moved
    side = dot(lateral[...], section[2 * cells :, :])
    span = slice(0, cells)
    at = lambda r: section[cells : 2 * cells, lane(r)]
    for r in range(ROWS):
        total = stream_slope(section[:cells, lane(r)]) + side[:cells, lane(r)]
        for reach, factor in DIFFERENCE:
            if 0 <= r + reach < ROWS:
                total = total + factor * at(r + reach)
        parts[span, lane(r)] = total
        up_near[span, lane(r)] = total
        down_near[span, lane(r)] = total
    tail = slice(cells, cells + PAD_M)
    parts[tail, :] = side[cells:]
    for near in (up_near, down_near):
        near[tail, lane(0, ROWS)] = side[cells:]
        near[tail, lane(ROWS, 3)] = jnp.zeros((PAD_M, 3 * LANES), jnp.float32)
    for far, r in ((up_far, ROWS - 1), (down_far, 0)):
        far[:, lane(0)] = parts[:, lane(r)]
        far[tail, lane(1, 2)] = jnp.zeros((PAD_M, 2 * LANES), jnp.float32)
    for k in range(2):
        up_near[span, lane(ROWS + k)] = at(ROWS - 2 + k)
        up_far[span, lane(1 + k)] = at(ROWS - 2 + k)
        down_near[span, lane(ROWS + k)] = at(k)
        down_far[span, lane(1 + k)] = at(k)
    up_near[span, lane(ROWS + 2)] = (2.0 / 3.0) * at(0) - (1.0 / 12.0) * at(1)
    down_near[span, lane(ROWS + 2)] = (1.0 / 12.0) * at(ROWS - 2) - (2.0 / 3.0) * at(ROWS - 1)


def source_kernel(cells, keep, parts, section, low_one, high_one, low_two, high_two, source, *refs):
    if keep:
        moments, ext, to_right, to_left = refs
    else:
        ext, to_right, to_left = refs
    masks = edge_masks()
    span, tail = slice(0, cells), slice(cells, cells + PAD_M)

    def joined(e):
        if e < -ROWS:
            return low_two[:, lane(e + REACH)]
        if e < 0:
            return low_one[:, lane(e + ROWS)]
        if e >= 2 * ROWS:
            return high_two[:, lane(e - 2 * ROWS)]
        if e >= ROWS:
            return high_one[:, lane(e - ROWS)]
        return parts[:, lane(e)]

    def across(e, home):
        owner = lambda x: x // ROWS
        if owner(e) == owner(home):
            return None
        if owner(home) == -2 or owner(home) == 2:
            return None
        if -ROWS - 2 <= e < -ROWS:
            return masked(low_two[span, lane(1 + e + ROWS + 2)], e, masks)
        if -2 <= e < 0:
            return masked(low_one[span, lane(ROWS + e + 2)], e, masks)
        if 0 <= e < ROWS:
            return section[cells : 2 * cells, lane(e)]
        if ROWS <= e < ROWS + 2:
            return masked(high_one[span, lane(e)], e, masks)
        return masked(high_two[span, lane(1 + e - 2 * ROWS)], e, masks)

    for e in range(-REACH, ROWS + REACH):
        both = joined(e)
        total = both[:cells]
        if e == -REACH:
            total = total + low_one[span, lane(ROWS + 2)]
        if e == ROWS + REACH - 1:
            total = total + high_one[span, lane(ROWS + 2)]
        for reach, factor in DIFFERENCE:
            other = across(e + reach, e)
            if other is not None:
                total = total + factor * other
        ext[span, lane(e + REACH)] = masked(total, e, masks)
        ext[tail, lane(e + REACH)] = masked(both[cells:], e, masks)
    wide = ext.shape[1]
    both = dot(source[...], ext[...])
    to_right[:, :wide] = both[:PAD_S]
    to_left[:, :wide] = both[PAD_S:]
    if keep:
        both = dot(moments[...], section[...])
        to_right[:, wide:] = both[:PAD_V]
        to_left[:, wide:] = both[PAD_V:]


def climb(levels, depth, masks):
    for j in range(1, SWEEPS):
        before = slice(depth * (j - 1), depth * j)
        after = slice(depth * j, depth * (j + 1))
        for e in range(-REACH + j, ROWS + REACH - j):
            here = levels[before, lane(e + REACH)]
            beside = (
                turned(here, 1)
                + turned(here, -1)
                + levels[before, lane(e + REACH + 1)]
                + levels[before, lane(e + REACH - 1)]
            )
            levels[after, lane(e + REACH)] = masked(beside, e, masks)
    return levels[:, lane(REACH - 2, ROWS + 4)]


def home_kernel(ext, solve, partial, levels):
    depth = ext.shape[0]
    levels[:depth, :] = ext[...]
    partial[...] = dot(solve[...], climb(levels, depth, edge_masks()))


def solve_kernel(cells, last, partial, left, right, section, solve, *refs):
    if last:
        out, levels = refs
    else:
        flat, next_left, next_right, upward, downward, levels = refs
    masks = edge_masks()
    wide = levels.shape[1]
    levels[:PAD_S, :] = left[:, :wide]
    levels[PAD_S : 2 * PAD_S, :] = right[:, :wide]
    found = partial[...] + dot(solve[...], climb(levels, 2 * PAD_S, masks))

    def gradient(rows, slope_rows, r):
        phi = lambda r: masked(found[rows, lane(r + 2)], r, masks)
        return (
            stream_slope(phi(r)),
            first_diff(phi(r + 1), phi(r - 1), phi(r + 2), phi(r - 2)),
            found[slope_rows, lane(r + 2)],
        )

    for r in range(ROWS):
        slopes = gradient(slice(0, cells), slice(cells, 2 * cells), r)
        for c in range(3):
            rows = slice(cells * c, cells * (c + 1))
            value = section[rows, lane(r)] - slopes[c]
            if last:
                out[c, :, r, :] = value
            else:
                flat[rows, lane(r)] = value
                if r < 2:
                    downward[rows, lane(r)] = value
                if r >= ROWS - 2:
                    upward[rows, lane(r - ROWS + 2)] = value
    if not last:
        for side, (given, target) in enumerate(((left, next_left), (right, next_right))):
            top = 2 * cells + 2 * GROUP * side
            target[...] = given[:, wide:]
            for r in range(ROWS):
                slopes = gradient(slice(top, top + GROUP), slice(top + GROUP, top + 2 * GROUP), r)
                for c in range(3):
                    rows = slice(RANK_V * c, RANK_V * (c + 1))
                    target[rows, lane(r)] = given[rows, wide + r * LANES : wide + (r + 1) * LANES] - slopes[c][:RANK_V]


def call(body, shapes, *args, scratch=(), **options):
    return pl.pallas_call(
        body,
        out_shape=[jax.ShapeDtypeStruct(s, jnp.float32) for s in shapes],
        scratch_shapes=scratch,
        compiler_params=pltpu.CompilerParams(vmem_limit_bytes=40 * 1024 * 1024),
        **options,
    )(*args)


def shifted(block, axis, step):
    count = lax.axis_size(axis)
    return lax.ppermute(block, axis, [(i, (i + step) % count) for i in range(count)])


def per_device(velocity, viscosity):
    components, cells, row_cells, columns = velocity.shape
    slopes, moments, lateral, source, solve_own, solve_sides = (
        jnp.asarray(t) for t in tables(cells * lax.axis_size("span"), cells)
    )
    width = row_cells * columns
    wide = (row_cells + 2 * REACH) * columns
    near = cells + PAD_M
    edge, rim = (PAD_V, width), (components * cells, 2 * columns)
    start, to_right, to_left, upward, downward = call(
        functools.partial(open_kernel, cells),
        [(components * cells, width), edge, edge, rim, rim],
        velocity, moments,
        in_specs=[pl.BlockSpec(memory_space=pltpu.HBM)] * 2,
        scratch=[
            pltpu.VMEM(velocity.shape, jnp.float32),
            pltpu.VMEM(moments.shape, jnp.float32),
            pltpu.SemaphoreType.DMA((2,)),
        ],
    )
    left = shifted(to_right, "span", 1)
    right = shifted(to_left, "span", -1)
    flat = start
    for second in (False, True):
        low = shifted(upward, "cross", 1)
        high = shifted(downward, "cross", -1)
        base = (start,) if second else ()
        section, parts, up_near, down_near, up_far, down_far = call(
            functools.partial(tendency_kernel, cells, second),
            [(components * cells, width), (near, width)] + [(near, 7 * columns)] * 2 + [(near, 3 * columns)] * 2,
            *base, flat, viscosity, left, right, low, high, slopes, lateral,
        )
        low_one = shifted(up_near, "cross", 1)
        high_one = shifted(down_near, "cross", -1)
        low_two = shifted(up_far, "cross", 2)
        high_two = shifted(down_far, "cross", -2)
        sent = (PAD_S, wide if second else wide + width)
        extra = () if second else (moments,)
        ext, to_right, to_left = call(
            functools.partial(source_kernel, cells, not second),
            [(near, wide), sent, sent],
            parts, section, low_one, high_one, low_two, high_two, source, *extra,
        )
        left = shifted(to_right, "span", 1)
        right = shifted(to_left, "span", -1)
        height = 2 * cells if second else solve_own.shape[0]
        (partial,) = call(
            home_kernel,
            [(height, (row_cells + 4) * columns)],
            ext, solve_own[:height],
            scratch=[pltpu.VMEM((SWEEPS * near, wide), jnp.float32)],
        )
        scratch = [pltpu.VMEM((SWEEPS * 2 * PAD_S, wide), jnp.float32)]
        given = (partial, left, right, section, solve_sides[:height])
        body = functools.partial(solve_kernel, cells, second)
        if second:
            (out,) = call(body, [velocity.shape], *given, scratch=scratch)
        else:
            flat, left, right, upward, downward = call(
                body, [(components * cells, width), edge, edge, rim, rim], *given, scratch=scratch
            )
    return out


def solution(mesh):
    in_specs = (P(None, "span", "cross", None), P("span", "cross", None))
    out_specs = P(None, "span", "cross", None)
    return jax.shard_map(
        per_device, mesh=mesh, in_specs=in_specs, out_specs=out_specs, check_vma=False
    )
```

time: 71.6 us -> 65 us (0.908)
  the two profiles are of different devices: /device:TPU:1 before, /device:TPU:126 now
where the time goes in v1:
time: 65 us; the launch traced here: 64.8 us
  waiting for transfers between devices  33.2 us (51%)
  starting transfers between devices  19.5 us (30%)
  Pallas kernels  10.2 us (16%)
  local copies, waits for them, and re-layouts  1.84 us (3%)
    ppermute x18, waiting for transfers between devices, shifted(): lax.ppermute(block, axis, [(i, (i + step) % count) for i in range(count)])  33.2 us
    ppermute x18, starting transfers between devices, shifted(): lax.ppermute(block, axis, [(i, (i + step) % count) for i in range(count)])  19.5 us
    pallas_call x9, Pallas kernels, call(): pl.pallas_call(body, out_shape=[jax.ShapeDtypeStruct(s, jnp.float32) for...  10.2 us
    unnamed x22, local copies, waits for them, and re-layouts  1.84 us
  transfers between devices with their start and end apart: 18, of which 11 were waited for; matrix products, arithmetic and copies ran while one was open for 0% of the time, Pallas kernels for 5%

profile of v1, /device:TPU:126, one launch (start us, length us, event | category | flops | bytes accessed | tf_op | source)
XLA Modules:
  0.0 64.8 jit_solution(156965116687419851)
XLA Ops:
  0.0 0.0 copy-start
  0.0 0.0 copy-start.2
  0.0 1.0 %copy-done.2 = f32[3,64,4,128]{3,2,1,0:T(4,128)S(1)} copy-done((f32[3,64,4,128]{3,2,1,0:T(4,128)S(1)}, f32[3,64,4,128]{3,2,1,0:T(4,128)}, u32[]{:S(2)}) %copy-start.2) | copy-done | bytes 393240
  1.0 0.0 copy-start.6
  1.0 0.8 %copy-done.6 = f32[32,192]{1,0:T(8,128)S(1)} copy-done((f32[32,192]{1,0:T(8,128)S(1)}, f32[32,192]{1,0:T(8,128)}, u32[]{:S(2)}) %copy-start.6) | copy-done | bytes 24600
  1.8 0.0 copy-start.1
  1.8 0.0 copy-start.5
  1.8 0.8 %shard_map.82 = (f32[192,512]{1,0:T(8,128)S(1)}, f32[16,512]{1,0:T(8,128)S(1)}, f32[16,512]{1,0:T(8,128)S(1)}, f32[192,256]{1,0:T(8,128)S(1)}, f32[192,256]{1,0:T(8,128)S(1)}) custom-call(f32[3,64,4,128]{3,2,1,0:T(4,128)S(1)} %copy-done.2, f32[32,192]{1,0:T(8,128)S(1)} %copy-done.6), custom_call_target="tpu_custom_call" | custom-call | tf_op jit(solution)/shard_map/pallas_call | solution.py:380
  2.6 0.0 collective-permute-start.2
  2.6 1.7 %collective-permute-start.3 = (f32[192,256]{1,0:T(8,128)S(1)}, f32[192,256]{1,0:T(8,128)S(1)}, u32[]{:S(2)}, u32[]{:S(2)}) collective-permute-start(f32[192,256]{1,0:T(8,128)S(1)} %get-tuple-element.37), channel_id=1, source_target_pairs={{0,7},{1,0},{2,1},{3,2},{4,3},{5,4},{6,5},{7,6},{8,15},{9,8},{10,9... | collective-permute-start | bytes 589832 | tf_op jit(solution)/shard_map/ppermute | solution.py:391
  4.4 3.0 %collective-permute-start = (f32[16,512]{1,0:T(8,128)S(1)}, f32[16,512]{1,0:T(8,128)S(1)}, u32[]{:S(2)}, u32[]{:S(2)}) collective-permute-start(f32[16,512]{1,0:T(8,128)S(1)} %get-tuple-element.34), channel_id=1, source_target_pairs={{0,8},{8,16},{16,24},{24,32},{32,40},{40,48},{48,56},{56,64},{64,7... | collective-permute-start | bytes 98312 | tf_op jit(solution)/shard_map/ppermute | solution.py:391
  7.4 0.0 collective-permute-start.1
  7.4 1.6 %collective-permute-done.refs_2_ = f32[16,512]{1,0:T(8,128)S(1)} collective-permute-done((f32[16,512]{1,0:T(8,128)S(1)}, f32[16,512]{1,0:T(8,128)S(1)}, u32[]{:S(2)}, u32[]{:S(2)}) %collective-permute-start) | collective-permute-done | bytes 32800 | tf_op jit(solution)/shard_map/ppermute | solution.py:391
  9.0 5.6 %collective-permute-done.1.refs_3_ = f32[16,512]{1,0:T(8,128)S(1)} collective-permute-done((f32[16,512]{1,0:T(8,128)S(1)}, f32[16,512]{1,0:T(8,128)S(1)}, u32[]{:S(2)}, u32[]{:S(2)}) %collective-permute-start.1) | collective-permute-done | bytes 32800 | tf_op jit(solution)/shard_map/ppermute | solution.py:391
  14.6 0.0 collective-permute-done.2.refs_4_
  14.6 0.0 collective-permute-done.3.refs_5_
  14.7 0.0 copy-done
  14.7 0.0 copy-done.1
  14.7 0.0 copy-done.5
  14.7 0.0 copy-start.7
  14.7 0.0 copy-start.10
  14.7 1.4 %shard_map.83 = (f32[192,512]{1,0:T(8,128)S(1)}, f32[72,512]{1,0:T(8,128)S(1)}, f32[72,896]{1,0:T(8,128)S(1)}, f32[72,896]{1,0:T(8,128)S(1)}, f32[72,384]{1,0:T(8,128)S(1)}, /*index=5*/f32[72,384]{1,0:T(8,128)S(1)}) custom-call(f32[192,512]{1,0:T(8,128)S(1)} %get-tuple-element.33.refs_0_, f32[64,4,128]{2,1,0:T(4,128)S(1)} %copy-done.1, ...), custom_call_target="tpu_custom_call" | custom-call | tf_op jit(solution)/shard_map/pallas_call | solution.py:380
  16.1 0.0 collective-permute-start.4
  16.1 1.7 %collective-permute-start.5 = (f32[72,896]{1,0:T(8,128)S(1)}, f32[72,896]{1,0:T(8,128)S(1)}, u32[]{:S(2)}, u32[]{:S(2)}) collective-permute-start(f32[72,896]{1,0:T(8,128)S(1)} %get-tuple-element.41), channel_id=1, source_target_pairs={{0,7},{1,0},{2,1},{3,2},{4,3},{5,4},{6,5},{7,6},{8,15},{9,8},{10,9... | collective-permute-start | bytes 774152 | tf_op jit(solution)/shard_map/ppermute | solution.py:391
  17.8 2.6 %collective-permute-start.6 = (f32[72,384]{1,0:T(8,128)S(1)}, f32[72,384]{1,0:T(8,128)S(1)}, u32[]{:S(2)}, u32[]{:S(2)}) collective-permute-start(f32[72,384]{1,0:T(8,128)S(1)} %get-tuple-element.42), channel_id=1, source_target_pairs={{0,2},{1,3},{2,4},{3,5},{4,6},{5,7},{6,0},{7,1},{8,10},{9,11},{10,... | collective-permute-start | bytes 331784 | tf_op jit(solution)/shard_map/ppermute | solution.py:391
  20.5 0.0 collective-permute-start.7
  20.5 3.4 %collective-permute-done.6.low_two = f32[72,384]{1,0:T(8,128)S(1)} collective-permute-done((f32[72,384]{1,0:T(8,128)S(1)}, f32[72,384]{1,0:T(8,128)S(1)}, u32[]{:S(2)}, u32[]{:S(2)}) %collective-permute-start.6) | collective-permute-done | bytes 110624 | tf_op jit(solution)/shard_map/ppermute | solution.py:391
  23.8 2.9 %collective-permute-done.7.high_two = f32[72,384]{1,0:T(8,128)S(1)} collective-permute-done((f32[72,384]{1,0:T(8,128)S(1)}, f32[72,384]{1,0:T(8,128)S(1)}, u32[]{:S(2)}, u32[]{:S(2)}) %collective-permute-start.7) | collective-permute-done | bytes 110624 | tf_op jit(solution)/shard_map/ppermute | solution.py:391
  26.7 0.0 collective-permute-done.4.low_one
  26.7 0.0 collective-permute-done.5.high_one
  26.7 0.0 copy-done.7
  26.7 0.0 copy-done.10
  26.8 0.0 copy-start.3
  26.8 0.6 shard_map.84
  27.3 0.1 collective-permute-start.8
  27.4 2.0 %collective-permute-start.9 = (f32[16,2304]{1,0:T(8,128)S(1)}, f32[16,2304]{1,0:T(8,128)S(1)}, u32[]{:S(2)}, u32[]{:S(2)}) collective-permute-start(f32[16,2304]{1,0:T(8,128)S(1)} %get-tuple-element.46), channel_id=1, source_target_pairs={{0,248},{8,0},{16,8},{24,16},{32,24},{40,32},{48,40},{56,48},{64,5... | collective-permute-start | bytes 442376 | tf_op jit(solution)/shard_map/ppermute | solution.py:391
  29.4 0.0 copy-done.3
  29.4 1.5 %shard_map.85.partial = f32[160,1024]{1,0:T(8,128)S(1)} custom-call(f32[72,1792]{1,0:T(8,128)S(1)} %get-tuple-element.44.ext, f32[160,288]{1,0:T(8,128)S(1)} %copy-done.3), custom_call_target="tpu_custom_call" | custom-call | tf_op jit(solution)/shard_map/pallas_call | solution.py:380
  31.0 1.6 %collective-permute-done.8.left = f32[16,2304]{1,0:T(8,128)S(1)} collective-permute-done((f32[16,2304]{1,0:T(8,128)S(1)}, f32[16,2304]{1,0:T(8,128)S(1)}, u32[]{:S(2)}, u32[]{:S(2)}) %collective-permute-start.8) | collective-permute-done | bytes 147488 | tf_op jit(solution)/shard_map/ppermute | solution.py:391
  32.6 3.4 %collective-permute-done.9.right = f32[16,2304]{1,0:T(8,128)S(1)} collective-permute-done((f32[16,2304]{1,0:T(8,128)S(1)}, f32[16,2304]{1,0:T(8,128)S(1)}, u32[]{:S(2)}, u32[]{:S(2)}) %collective-permute-start.9) | collective-permute-done | bytes 147488 | tf_op jit(solution)/shard_map/ppermute | solution.py:391
  36.0 0.0 copy-done.8
  36.0 1.0 %shard_map.86 = (f32[192,512]{1,0:T(8,128)S(1)}, f32[16,512]{1,0:T(8,128)S(1)}, f32[16,512]{1,0:T(8,128)S(1)}, f32[192,256]{1,0:T(8,128)S(1)}, f32[192,256]{1,0:T(8,128)S(1)}) custom-call(f32[160,1024]{1,0:T(8,128)S(1)} %shard_map.85.partial, f32[16,2304]{1,0:T(8,128)S(1)} %collective-permute-done.8.left, f32[16,2304]{1,0:T(8,128)S(1)} %collective-permute-done.9.right, ...), custom_call_target="tpu_custom_call" | custom-call | tf_op jit(solution)/shard_map/pallas_call | solution.py:380
  37.0 0.0 collective-permute-start.10
  37.0 1.7 %collective-permute-start.11 = (f32[192,256]{1,0:T(8,128)S(1)}, f32[192,256]{1,0:T(8,128)S(1)}, u32[]{:S(2)}, u32[]{:S(2)}) collective-permute-start(f32[192,256]{1,0:T(8,128)S(1)} %get-tuple-element.51), channel_id=1, source_target_pairs={{0,7},{1,0},{2,1},{3,2},{4,3},{5,4},{6,5},{7,6},{8,15},{9,8},{10,9... | collective-permute-start | bytes 589832 | tf_op jit(solution)/shard_map/ppermute | solution.py:391
  38.7 3.3 %collective-permute-done.10.refs_5_ = f32[192,256]{1,0:T(8,128)S(1)} collective-permute-done((f32[192,256]{1,0:T(8,128)S(1)}, f32[192,256]{1,0:T(8,128)S(1)}, u32[]{:S(2)}, u32[]{:S(2)}) %collective-permute-start.10) | collective-permute-done | bytes 196640 | tf_op jit(solution)/shard_map/ppermute | solution.py:391
  42.1 0.0 collective-permute-done.11.refs_6_
  42.1 1.4 %shard_map.87 = (f32[192,512]{1,0:T(8,128)S(1)}, f32[72,512]{1,0:T(8,128)S(1)}, f32[72,896]{1,0:T(8,128)S(1)}, f32[72,896]{1,0:T(8,128)S(1)}, f32[72,384]{1,0:T(8,128)S(1)}, /*index=5*/f32[72,384]{1,0:T(8,128)S(1)}) custom-call(f32[192,512]{1,0:T(8,128)S(1)} %get-tuple-element.33.refs_0_, f32[192,512]{1,0:T(8,128)S(1)} %get-tuple-element.47.refs_1_, ...), custom_call_target="tpu_custom_call" | custom-call | tf_op jit(solution)/shard_map/pallas_call | solution.py:380
  43.5 1.5 %collective-permute-start.12 = (f32[72,896]{1,0:T(8,128)S(1)}, f32[72,896]{1,0:T(8,128)S(1)}, u32[]{:S(2)}, u32[]{:S(2)}) collective-permute-start(f32[72,896]{1,0:T(8,128)S(1)} %get-tuple-element.54), channel_id=1, source_target_pairs={{0,1},{1,2},{2,3},{3,4},{4,5},{5,6},{6,7},{7,0},{8,9},{9,10},{10,1... | collective-permute-start | bytes 774152 | tf_op jit(solution)/shard_map/ppermute | solution.py:391
  45.0 0.3 collective-permute-start.13
  45.3 2.6 %collective-permute-start.14 = (f32[72,384]{1,0:T(8,128)S(1)}, f32[72,384]{1,0:T(8,128)S(1)}, u32[]{:S(2)}, u32[]{:S(2)}) collective-permute-start(f32[72,384]{1,0:T(8,128)S(1)} %get-tuple-element.56), channel_id=1, source_target_pairs={{0,2},{1,3},{2,4},{3,5},{4,6},{5,7},{6,0},{7,1},{8,10},{9,11},{10,... | collective-permute-start | bytes 331784 | tf_op jit(solution)/shard_map/ppermute | solution.py:391
  47.9 0.0 collective-permute-start.15
  47.9 3.4 %collective-permute-done.14.low_two = f32[72,384]{1,0:T(8,128)S(1)} collective-permute-done((f32[72,384]{1,0:T(8,128)S(1)}, f32[72,384]{1,0:T(8,128)S(1)}, u32[]{:S(2)}, u32[]{:S(2)}) %collective-permute-start.14) | collective-permute-done | bytes 110624 | tf_op jit(solution)/shard_map/ppermute | solution.py:391
  51.3 3.2 %collective-permute-done.15.high_two = f32[72,384]{1,0:T(8,128)S(1)} collective-permute-done((f32[72,384]{1,0:T(8,128)S(1)}, f32[72,384]{1,0:T(8,128)S(1)}, u32[]{:S(2)}, u32[]{:S(2)}) %collective-permute-start.15) | collective-permute-done | bytes 110624 | tf_op jit(solution)/shard_map/ppermute | solution.py:391
  54.4 0.0 collective-permute-done.12.low_one
  54.4 0.0 collective-permute-done.13.high_one
  54.5 0.4 shard_map.88
  54.9 0.1 collective-permute-start.16
  55.0 1.9 %collective-permute-start.17 = (f32[16,1792]{1,0:T(8,128)S(1)}, f32[16,1792]{1,0:T(8,128)S(1)}, u32[]{:S(2)}, u32[]{:S(2)}) collective-permute-start(f32[16,1792]{1,0:T(8,128)S(1)} %get-tuple-element.60), channel_id=1, source_target_pairs={{0,248},{8,0},{16,8},{24,16},{32,24},{40,32},{48,40},{56,48},{64,5... | collective-permute-start | bytes 344072 | tf_op jit(solution)/shard_map/ppermute | solution.py:391
  56.9 0.0 copy-done.4
  56.9 1.4 %shard_map.89.partial = f32[128,1024]{1,0:T(8,128)S(1)} custom-call(f32[72,1792]{1,0:T(8,128)S(1)} %get-tuple-element.58.ext, f32[128,288]{1,0:T(8,128)S(1)} %copy-done.4), custom_call_target="tpu_custom_call" | custom-call | tf_op jit(solution)/shard_map/pallas_call | solution.py:380
  58.3 1.4 %collective-permute-done.16.left = f32[16,1792]{1,0:T(8,128)S(1)} collective-permute-done((f32[16,1792]{1,0:T(8,128)S(1)}, f32[16,1792]{1,0:T(8,128)S(1)}, u32[]{:S(2)}, u32[]{:S(2)}) %collective-permute-start.16) | collective-permute-done | bytes 114720 | tf_op jit(solution)/shard_map/ppermute | solution.py:391
  59.7 3.4 %collective-permute-done.17.right = f32[16,1792]{1,0:T(8,128)S(1)} collective-permute-done((f32[16,1792]{1,0:T(8,128)S(1)}, f32[16,1792]{1,0:T(8,128)S(1)}, u32[]{:S(2)}, u32[]{:S(2)}) %collective-permute-start.17) | collective-permute-done | bytes 114720 | tf_op jit(solution)/shard_map/ppermute | solution.py:391
  63.1 0.0 copy-done.9
  63.1 1.7 %shard_map.90 = f32[3,64,4,128]{3,2,1,0:T(4,128)} custom-call(f32[128,1024]{1,0:T(8,128)S(1)} %shard_map.89.partial, f32[16,1792]{1,0:T(8,128)S(1)} %collective-permute-done.16.left, f32[16,1792]{1,0:T(8,128)S(1)} %collective-permute-done.17.right, f32[192,512]{1,0:T(8,128)S(1)} %get-tuple-element.53.section, f32[128,128]{1,0:T(8,128)S(1)} %copy-done.9), custom_call_target="tpu_custom_call" | custom-call | tf_op jit(solution)/shard_map/pallas_call | solution.py:380
  (3 shorter events, 0.0 us)
Async XLA Ops:
  0.0 14.7 %copy-start = (f32[3,128,96]{2,1,0:T(8,128)S(1)}, f32[3,128,96]{2,1,0:T(8,128)}, u32[]{:S(2)}) copy-start(f32[3,128,96]{2,1,0:T(8,128)} %constant.12.clone.refs_6_.refs_7_) | copy-start | bytes 442372
  0.0 1.0 %copy-start.2 = (f32[3,64,4,128]{3,2,1,0:T(4,128)S(1)}, f32[3,64,4,128]{3,2,1,0:T(4,128)}, u32[]{:S(2)}) copy-start(f32[3,64,4,128]{3,2,1,0:T(4,128)} %velocity.1) | copy-start | bytes 1179652
  1.0 0.8 %copy-start.6 = (f32[32,192]{1,0:T(8,128)S(1)}, f32[32,192]{1,0:T(8,128)}, u32[]{:S(2)}) copy-start(f32[32,192]{1,0:T(8,128)} %constant.13.clone.moments.refs_0_) | copy-start | bytes 73732
  1.8 12.9 %copy-start.1 = (f32[64,4,128]{2,1,0:T(4,128)S(1)}, f32[64,4,128]{2,1,0:T(4,128)}, u32[]{:S(2)}) copy-start(f32[64,4,128]{2,1,0:T(4,128)} %refs_2_.1) | copy-start | bytes 393220
  1.8 12.9 %copy-start.5 = (f32[72,64]{1,0:T(8,128)S(1)}, f32[72,64]{1,0:T(8,128)}, u32[]{:S(2)}) copy-start(f32[72,64]{1,0:T(8,128)} %constant.14.clone.refs_7_.refs_8_) | copy-start | bytes 55300
  2.6 12.0 %collective-permute-start.2 = (f32[192,256]{1,0:T(8,128)S(1)}, f32[192,256]{1,0:T(8,128)S(1)}, u32[]{:S(2)}, u32[]{:S(2)}) collective-permute-start(f32[192,256]{1,0:T(8,128)S(1)} %get-tuple-element.36), channel_id=1, source_target_pairs={{0,1},{1,2},{2,3},{3,4},{4,5},{5,6},{6,7},{7,0},{8,9},{9,10},{10,1... | collective-permute-start | bytes 589832 | tf_op jit(solution)/shard_map/ppermute | solution.py:391
  2.6 12.0 %collective-permute-start.3 = (f32[192,256]{1,0:T(8,128)S(1)}, f32[192,256]{1,0:T(8,128)S(1)}, u32[]{:S(2)}, u32[]{:S(2)}) collective-permute-start(f32[192,256]{1,0:T(8,128)S(1)} %get-tuple-element.37), channel_id=1, source_target_pairs={{0,7},{1,0},{2,1},{3,2},{4,3},{5,4},{6,5},{7,6},{8,15},{9,8},{10,9... | collective-permute-start | bytes 589832 | tf_op jit(solution)/shard_map/ppermute | solution.py:391
  4.4 4.6 %collective-permute-start = (f32[16,512]{1,0:T(8,128)S(1)}, f32[16,512]{1,0:T(8,128)S(1)}, u32[]{:S(2)}, u32[]{:S(2)}) collective-permute-start(f32[16,512]{1,0:T(8,128)S(1)} %get-tuple-element.34), channel_id=1, source_target_pairs={{0,8},{8,16},{16,24},{24,32},{32,40},{40,48},{48,56},{56,64},{64,7... | collective-permute-start | bytes 98312 | tf_op jit(solution)/shard_map/ppermute | solution.py:391
  7.4 7.2 %collective-permute-start.1 = (f32[16,512]{1,0:T(8,128)S(1)}, f32[16,512]{1,0:T(8,128)S(1)}, u32[]{:S(2)}, u32[]{:S(2)}) collective-permute-start(f32[16,512]{1,0:T(8,128)S(1)} %get-tuple-element.35), channel_id=1, source_target_pairs={{0,248},{8,0},{16,8},{24,16},{32,24},{40,32},{48,40},{56,48},{64,5... | collective-permute-start | bytes 98312 | tf_op jit(solution)/shard_map/ppermute | solution.py:391
  14.7 12.1 %copy-start.7 = (f32[32,192]{1,0:T(8,128)S(1)}, f32[32,192]{1,0:T(8,128)}, u32[]{:S(2)}) copy-start(f32[32,192]{1,0:T(8,128)} %constant.13.clone.moments.refs_0_) | copy-start | bytes 73732
  14.7 12.1 %copy-start.10 = (f32[32,72]{1,0:T(8,128)S(1)}, f32[32,72]{1,0:T(8,128)}, u32[]{:S(2)}) copy-start(f32[32,72]{1,0:T(8,128)} %constant.15.clone.source) | copy-start | bytes 27652
  16.1 10.6 %collective-permute-start.4 = (f32[72,896]{1,0:T(8,128)S(1)}, f32[72,896]{1,0:T(8,128)S(1)}, u32[]{:S(2)}, u32[]{:S(2)}) collective-permute-start(f32[72,896]{1,0:T(8,128)S(1)} %get-tuple-element.40), channel_id=1, source_target_pairs={{0,1},{1,2},{2,3},{3,4},{4,5},{5,6},{6,7},{7,0},{8,9},{9,10},{10,1... | collective-permute-start | bytes 774152 | tf_op jit(solution)/shard_map/ppermute | solution.py:391
  16.1 10.6 %collective-permute-start.5 = (f32[72,896]{1,0:T(8,128)S(1)}, f32[72,896]{1,0:T(8,128)S(1)}, u32[]{:S(2)}, u32[]{:S(2)}) collective-permute-start(f32[72,896]{1,0:T(8,128)S(1)} %get-tuple-element.41), channel_id=1, source_target_pairs={{0,7},{1,0},{2,1},{3,2},{4,3},{5,4},{6,5},{7,6},{8,15},{9,8},{10,9... | collective-permute-start | bytes 774152 | tf_op jit(solution)/shard_map/ppermute | solution.py:391
  17.8 6.0 %collective-permute-start.6 = (f32[72,384]{1,0:T(8,128)S(1)}, f32[72,384]{1,0:T(8,128)S(1)}, u32[]{:S(2)}, u32[]{:S(2)}) collective-permute-start(f32[72,384]{1,0:T(8,128)S(1)} %get-tuple-element.42), channel_id=1, source_target_pairs={{0,2},{1,3},{2,4},{3,5},{4,6},{5,7},{6,0},{7,1},{8,10},{9,11},{10,... | collective-permute-start | bytes 331784 | tf_op jit(solution)/shard_map/ppermute | solution.py:391
  20.5 6.2 %collective-permute-start.7 = (f32[72,384]{1,0:T(8,128)S(1)}, f32[72,384]{1,0:T(8,128)S(1)}, u32[]{:S(2)}, u32[]{:S(2)}) collective-permute-start(f32[72,384]{1,0:T(8,128)S(1)} %get-tuple-element.43), channel_id=1, source_target_pairs={{0,6},{1,7},{2,0},{3,1},{4,2},{5,3},{6,4},{7,5},{8,14},{9,15},{10,... | collective-permute-start | bytes 331784 | tf_op jit(solution)/shard_map/ppermute | solution.py:391
  26.8 2.7 %copy-start.3 = (f32[160,288]{1,0:T(8,128)S(1)}, f32[160,288]{1,0:T(8,128)}, u32[]{:S(2)}) copy-start(f32[160,288]{1,0:T(8,128)} %constant.16.clone.solve) | copy-start | bytes 552964
  27.3 5.2 %collective-permute-start.8 = (f32[16,2304]{1,0:T(8,128)S(1)}, f32[16,2304]{1,0:T(8,128)S(1)}, u32[]{:S(2)}, u32[]{:S(2)}) collective-permute-start(f32[16,2304]{1,0:T(8,128)S(1)} %get-tuple-element.45), channel_id=1, source_target_pairs={{0,8},{8,16},{16,24},{24,32},{32,40},{40,48},{48,56},{56,64},{64,7... | collective-permute-start | bytes 442376 | tf_op jit(solution)/shard_map/ppermute | solution.py:391
  27.4 8.5 %collective-permute-start.9 = (f32[16,2304]{1,0:T(8,128)S(1)}, f32[16,2304]{1,0:T(8,128)S(1)}, u32[]{:S(2)}, u32[]{:S(2)}) collective-permute-start(f32[16,2304]{1,0:T(8,128)S(1)} %get-tuple-element.46), channel_id=1, source_target_pairs={{0,248},{8,0},{16,8},{24,16},{32,24},{40,32},{48,40},{56,48},{64,5... | collective-permute-start | bytes 442376 | tf_op jit(solution)/shard_map/ppermute | solution.py:391
  29.4 6.5 %copy-start.8 = (f32[160,128]{1,0:T(8,128)S(1)}, f32[160,128]{1,0:T(8,128)}, u32[]{:S(2)}) copy-start(f32[160,128]{1,0:T(8,128)} %constant.17.clone.solve) | copy-start | bytes 245764
  37.0 5.1 %collective-permute-start.10 = (f32[192,256]{1,0:T(8,128)S(1)}, f32[192,256]{1,0:T(8,128)S(1)}, u32[]{:S(2)}, u32[]{:S(2)}) collective-permute-start(f32[192,256]{1,0:T(8,128)S(1)} %get-tuple-element.50), channel_id=1, source_target_pairs={{0,1},{1,2},{2,3},{3,4},{4,5},{5,6},{6,7},{7,0},{8,9},{9,10},{10,1... | collective-permute-start | bytes 589832 | tf_op jit(solution)/shard_map/ppermute | solution.py:391
  37.0 5.1 %collective-permute-start.11 = (f32[192,256]{1,0:T(8,128)S(1)}, f32[192,256]{1,0:T(8,128)S(1)}, u32[]{:S(2)}, u32[]{:S(2)}) collective-permute-start(f32[192,256]{1,0:T(8,128)S(1)} %get-tuple-element.51), channel_id=1, source_target_pairs={{0,7},{1,0},{2,1},{3,2},{4,3},{5,4},{6,5},{7,6},{8,15},{9,8},{10,9... | collective-permute-start | bytes 589832 | tf_op jit(solution)/shard_map/ppermute | solution.py:391
  43.5 10.9 %collective-permute-start.12 = (f32[72,896]{1,0:T(8,128)S(1)}, f32[72,896]{1,0:T(8,128)S(1)}, u32[]{:S(2)}, u32[]{:S(2)}) collective-permute-start(f32[72,896]{1,0:T(8,128)S(1)} %get-tuple-element.54), channel_id=1, source_target_pairs={{0,1},{1,2},{2,3},{3,4},{4,5},{5,6},{6,7},{7,0},{8,9},{9,10},{10,1... | collective-permute-start | bytes 774152 | tf_op jit(solution)/shard_map/ppermute | solution.py:391
  45.0 9.5 %collective-permute-start.13 = (f32[72,896]{1,0:T(8,128)S(1)}, f32[72,896]{1,0:T(8,128)S(1)}, u32[]{:S(2)}, u32[]{:S(2)}) collective-permute-start(f32[72,896]{1,0:T(8,128)S(1)} %get-tuple-element.55), channel_id=1, source_target_pairs={{0,7},{1,0},{2,1},{3,2},{4,3},{5,4},{6,5},{7,6},{8,15},{9,8},{10,9... | collective-permute-start | bytes 774152 | tf_op jit(solution)/shard_map/ppermute | solution.py:391
  45.3 6.0 %collective-permute-start.14 = (f32[72,384]{1,0:T(8,128)S(1)}, f32[72,384]{1,0:T(8,128)S(1)}, u32[]{:S(2)}, u32[]{:S(2)}) collective-permute-start(f32[72,384]{1,0:T(8,128)S(1)} %get-tuple-element.56), channel_id=1, source_target_pairs={{0,2},{1,3},{2,4},{3,5},{4,6},{5,7},{6,0},{7,1},{8,10},{9,11},{10,... | collective-permute-start | bytes 331784 | tf_op jit(solution)/shard_map/ppermute | solution.py:391
  47.9 6.6 %collective-permute-start.15 = (f32[72,384]{1,0:T(8,128)S(1)}, f32[72,384]{1,0:T(8,128)S(1)}, u32[]{:S(2)}, u32[]{:S(2)}) collective-permute-start(f32[72,384]{1,0:T(8,128)S(1)} %get-tuple-element.57), channel_id=1, source_target_pairs={{0,6},{1,7},{2,0},{3,1},{4,2},{5,3},{6,4},{7,5},{8,14},{9,15},{10,... | collective-permute-start | bytes 331784 | tf_op jit(solution)/shard_map/ppermute | solution.py:391
  54.5 2.5 %copy-start.4 = (f32[128,288]{1,0:T(8,128)S(1)}, f32[128,288]{1,0:T(8,128)}, u32[]{:S(2)}) copy-start(f32[128,288]{1,0:T(8,128)} %constant.20.solve) | copy-start | bytes 442372
  54.9 4.8 %collective-permute-start.16 = (f32[16,1792]{1,0:T(8,128)S(1)}, f32[16,1792]{1,0:T(8,128)S(1)}, u32[]{:S(2)}, u32[]{:S(2)}) collective-permute-start(f32[16,1792]{1,0:T(8,128)S(1)} %get-tuple-element.59), channel_id=1, source_target_pairs={{0,8},{8,16},{16,24},{24,32},{32,40},{40,48},{48,56},{56,64},{64,7... | collective-permute-start | bytes 344072 | tf_op jit(solution)/shard_map/ppermute | solution.py:391
  55.0 8.1 %collective-permute-start.17 = (f32[16,1792]{1,0:T(8,128)S(1)}, f32[16,1792]{1,0:T(8,128)S(1)}, u32[]{:S(2)}, u32[]{:S(2)}) collective-permute-start(f32[16,1792]{1,0:T(8,128)S(1)} %get-tuple-element.60), channel_id=1, source_target_pairs={{0,248},{8,0},{16,8},{24,16},{32,24},{40,32},{48,40},{56,48},{64,5... | collective-permute-start | bytes 344072 | tf_op jit(solution)/shard_map/ppermute | solution.py:391
  56.9 6.2 %copy-start.9 = (f32[128,128]{1,0:T(8,128)S(1)}, f32[128,128]{1,0:T(8,128)}, u32[]{:S(2)}) copy-start(f32[128,128]{1,0:T(8,128)} %constant.21.solve) | copy-start | bytes 196612

commit v2 on v1

--- a/solution.py
+++ b/solution.py
@@ -20,7 +20,6 @@
 GROUP = 8
 RANK_V = 3
 RANK_M = 2
-RANK_S = 2 * SWEEPS + 3
 
 
 def symbols(length):
@@ -44,7 +43,7 @@
 
 
 @functools.lru_cache(None)
-def tables(length, cells):
+def tables(length, cells, last):
     first, second, inverse = symbols(length)
     at = lambda symbol, offset: block_of(symbol, cells, offset)
     from_left, take_left = low_rank(np.concatenate([at(first, -1), at(second, -1)]), RANK_V)
@@ -68,20 +67,28 @@
     powers = [inverse ** (j + 1) for j in range(SWEEPS)]
     stacked = [p for p in powers] + [first * p for p in powers]
     count = len(stacked)
+    RANK_S = 2 * SWEEPS + (1 if last else 3)
+    kept = [] if last else stacked
     s_left, q_left = low_rank(
-        np.concatenate([at(p, -1) for p in stacked] + [take_left @ at(p, 0) for p in stacked]), RANK_S
+        np.concatenate([at(p, -1) for p in stacked] + [take_left @ at(p, 0) for p in kept]), RANK_S
     )
     s_right, q_right = low_rank(
-        np.concatenate([at(p, 1) for p in stacked] + [take_right @ at(p, 0) for p in stacked]), RANK_S
+        np.concatenate([at(p, 1) for p in stacked] + [take_right @ at(p, 0) for p in kept]), RANK_S
     )
     e_left, e_right = s_left[count * cells :], s_right[count * cells :]
-    source = np.zeros((2 * PAD_S, cells + PAD_M))
-    source[:RANK_S, :cells] = q_left
-    source[RANK_S : RANK_S + RANK_M, cells : cells + RANK_M] = np.eye(RANK_M)
-    source[PAD_S : PAD_S + RANK_S, :cells] = q_right
-    source[PAD_S + RANK_S : PAD_S + RANK_S + RANK_M, cells + RANK_M : cells + 2 * RANK_M] = np.eye(RANK_M)
+    source = np.zeros((8 * GROUP, cells + PAD_M))
+    for side, q in enumerate((q_left, q_right)):
+        rows = np.zeros((PAD_S, cells + PAD_M))
+        rows[:RANK_S, :cells] = q
+        at_m = cells + RANK_M * side
+        rows[RANK_S : RANK_S + RANK_M, at_m : at_m + RANK_M] = np.eye(RANK_M)
+        top = 4 * GROUP * side
+        source[top : top + 8] = rows[:8]
+        source[top + 8 : top + 12] = rows[8:12]
+        source[top + 20 : top + 24] = rows[8:12]
+        source[top + 24] = rows[12]
     near, wide = cells + PAD_M, 2 * PAD_S
-    height = 2 * cells + 4 * GROUP
+    height = 2 * cells + (0 if last else 4 * GROUP)
     solve_own = np.zeros((height, SWEEPS * near))
     solve_sides = np.zeros((height, SWEEPS * wide))
     for j in range(SWEEPS):
@@ -101,7 +108,7 @@
             sides[:, PAD_S + RANK_S : PAD_S + RANK_S + RANK_M] = center @ m_right
             solve_own[cells * half : cells * (half + 1), near * j : near * (j + 1)] = -mine
             solve_sides[cells * half : cells * (half + 1), wide * j : wide * (j + 1)] = -sides
-            for side in range(2):
+            for side in range(0 if last else 2):
                 mine, sides = np.zeros((RANK_V, near)), np.zeros((RANK_V, wide))
                 if side == 0:
                     back = take_left @ by_right @ q_right
@@ -126,6 +133,9 @@
     return jnp.dot(a, b, precision=highest, preferred_element_type=jnp.float32)
 
 
+BREADTH = ROWS + 2 * REACH
+PACKED = BREADTH + BREADTH // 2
+
 DIFFERENCE = ((1, 2.0 / 3.0), (-1, -2.0 / 3.0), (2, -1.0 / 12.0), (-2, 1.0 / 12.0))
 
 
@@ -169,19 +179,18 @@
 
 
 def open_kernel(cells, velocity, moments, flat, to_right, to_left, upward, downward, landed, weights, sems):
-    copies = (
-        pltpu.make_async_copy(velocity, landed, sems.at[0]),
-        pltpu.make_async_copy(moments, weights, sems.at[1]),
-    )
+    copies = [pltpu.make_async_copy(velocity.at[c], landed.at[c], sems.at[c]) for c in range(3)]
+    copies.append(pltpu.make_async_copy(moments, weights, sems.at[3]))
     for copy in copies:
         copy.start()
-    for copy in copies:
-        copy.wait()
-    for r in range(ROWS):
-        for c in range(3):
-            flat[cells * c : cells * (c + 1), lane(r)] = landed[c, :, r, :]
-    upward[...] = flat[:, lane(ROWS - 2, 2)]
-    downward[...] = flat[:, lane(0, 2)]
+    for c in range(3):
+        copies[c].wait()
+        rows = slice(cells * c, cells * (c + 1))
+        for r in range(ROWS):
+            flat[rows, lane(r)] = landed[c, :, r, :]
+        upward[rows, :] = flat[rows, lane(ROWS - 2, 2)]
+        downward[rows, :] = flat[rows, lane(0, 2)]
+    copies[3].wait()
     both = dot(weights[...], flat[...])
     to_right[...] = both[:PAD_V]
     to_left[...] = both[PAD_V:]
@@ -234,23 +243,24 @@
             if 0 <= r + reach < ROWS:
                 total = total + factor * at(r + reach)
         parts[span, lane(r)] = total
-        up_near[span, lane(r)] = total
-        down_near[span, lane(r)] = total
+        for block in (up_near, down_near):
+            block[cells * r : cells * (r + 1), :] = total
+            block[7 * cells + PAD_M * r : 7 * cells + PAD_M * (r + 1), :] = side[cells:, lane(r)]
     tail = slice(cells, cells + PAD_M)
     parts[tail, :] = side[cells:]
-    for near in (up_near, down_near):
-        near[tail, lane(0, ROWS)] = side[cells:]
-        near[tail, lane(ROWS, 3)] = jnp.zeros((PAD_M, 3 * LANES), jnp.float32)
     for far, r in ((up_far, ROWS - 1), (down_far, 0)):
-        far[:, lane(0)] = parts[:, lane(r)]
-        far[tail, lane(1, 2)] = jnp.zeros((PAD_M, 2 * LANES), jnp.float32)
+        far[:cells, :] = parts[span, lane(r)]
+        far[3 * cells :, :] = parts[tail, lane(r)]
     for k in range(2):
-        up_near[span, lane(ROWS + k)] = at(ROWS - 2 + k)
-        up_far[span, lane(1 + k)] = at(ROWS - 2 + k)
-        down_near[span, lane(ROWS + k)] = at(k)
-        down_far[span, lane(1 + k)] = at(k)
-    up_near[span, lane(ROWS + 2)] = (2.0 / 3.0) * at(0) - (1.0 / 12.0) * at(1)
-    down_near[span, lane(ROWS + 2)] = (1.0 / 12.0) * at(ROWS - 2) - (2.0 / 3.0) * at(ROWS - 1)
+        near_rows = slice(cells * (ROWS + k), cells * (ROWS + k + 1))
+        far_rows = slice(cells * (1 + k), cells * (2 + k))
+        up_near[near_rows, :] = at(ROWS - 2 + k)
+        up_far[far_rows, :] = at(ROWS - 2 + k)
+        down_near[near_rows, :] = at(k)
+        down_far[far_rows, :] = at(k)
+    rest = slice(6 * cells, 7 * cells)
+    up_near[rest, :] = (2.0 / 3.0) * at(0) - (1.0 / 12.0) * at(1)
+    down_near[rest, :] = (1.0 / 12.0) * at(ROWS - 2) - (2.0 / 3.0) * at(ROWS - 1)
 
 
 def source_kernel(cells, keep, parts, section, low_one, high_one, low_two, high_two, source, *refs):
@@ -260,55 +270,66 @@
         ext, to_right, to_left = refs
     masks = edge_masks()
     span, tail = slice(0, cells), slice(cells, cells + PAD_M)
+    pick = lambda ref, k: ref[cells * k : cells * (k + 1), :]
 
     def joined(e):
         if e < -ROWS:
-            return low_two[:, lane(e + REACH)]
+            return low_two[:cells, :], low_two[3 * cells :, :]
+        if e >= 2 * ROWS:
+            return high_two[:cells, :], high_two[3 * cells :, :]
+        if 0 <= e < ROWS:
+            return parts[span, lane(e)], parts[tail, lane(e)]
+        near, r = (low_one, e + ROWS) if e < 0 else (high_one, e - ROWS)
+        top = 7 * cells + PAD_M * r
+        return pick(near, r), near[top : top + PAD_M, :]
+
+    def across(e, home):
+        if e // ROWS == home // ROWS or home // ROWS in (-2, 2):
+            return None
+        if e < -ROWS:
+            return masked(pick(low_two, 1 + e + ROWS + 2), e, masks)
         if e < 0:
-            return low_one[:, lane(e + ROWS)]
-        if e >= 2 * ROWS:
-            return high_two[:, lane(e - 2 * ROWS)]
-        if e >= ROWS:
-            return high_one[:, lane(e - ROWS)]
-        return parts[:, lane(e)]
-
-    def across(e, home):
-        owner = lambda x: x // ROWS
-        if owner(e) == owner(home):
-            return None
-        if owner(home) == -2 or owner(home) == 2:
-            return None
-        if -ROWS - 2 <= e < -ROWS:
-            return masked(low_two[span, lane(1 + e + ROWS + 2)], e, masks)
-        if -2 <= e < 0:
-            return masked(low_one[span, lane(ROWS + e + 2)], e, masks)
-        if 0 <= e < ROWS:
+            return masked(pick(low_one, ROWS + e + 2), e, masks)
+        if e < ROWS:
             return section[cells : 2 * cells, lane(e)]
-        if ROWS <= e < ROWS + 2:
-            return masked(high_one[span, lane(e)], e, masks)
-        return masked(high_two[span, lane(1 + e - 2 * ROWS)], e, masks)
+        if e < 2 * ROWS:
+            return masked(pick(high_one, e), e, masks)
+        return masked(pick(high_two, 1 + e - 2 * ROWS), e, masks)
 
     for e in range(-REACH, ROWS + REACH):
-        both = joined(e)
-        total = both[:cells]
+        total, side = joined(e)
         if e == -REACH:
-            total = total + low_one[span, lane(ROWS + 2)]
+            total = total + pick(low_one, 6)
         if e == ROWS + REACH - 1:
-            total = total + high_one[span, lane(ROWS + 2)]
+            total = total + pick(high_one, 6)
         for reach, factor in DIFFERENCE:
             other = across(e + reach, e)
             if other is not None:
                 total = total + factor * other
         ext[span, lane(e + REACH)] = masked(total, e, masks)
-        ext[tail, lane(e + REACH)] = masked(both[cells:], e, masks)
-    wide = ext.shape[1]
+        ext[tail, lane(e + REACH)] = masked(side, e, masks)
     both = dot(source[...], ext[...])
-    to_right[:, :wide] = both[:PAD_S]
-    to_left[:, :wide] = both[PAD_S:]
     if keep:
-        both = dot(moments[...], section[...])
-        to_right[:, wide:] = both[:PAD_V]
-        to_left[:, wide:] = both[PAD_V:]
+        held = dot(moments[...], section[...])
+    for side, out in enumerate((to_right, to_left)):
+        top = 4 * GROUP * side
+        out[:, lane(0, BREADTH)] = both[top : top + 8]
+        for k in range(BREADTH // 2):
+            out[:, lane(BREADTH + k)] = (
+                both[top + 8 : top + 16, lane(2 * k)] + both[top + 16 : top + 24, lane(2 * k + 1)]
+            )
+        if keep:
+            base = PAD_V * side
+            out[:, lane(PACKED, ROWS)] = held[base : base + 8]
+            out[:, lane(PACKED + ROWS, 3)] = jnp.zeros((GROUP, 3 * LANES), jnp.float32)
+            for e in range(BREADTH + ROWS):
+                value = (
+                    both[top + 24 : top + 25, lane(e)]
+                    if e < BREADTH
+                    else held[base + 8 : base + 9, lane(e - BREADTH)]
+                )
+                row, tile = e % GROUP, PACKED + ROWS + e // GROUP
+                out[row : row + 1, lane(tile)] = value
 
 
 def climb(levels, depth, masks):
@@ -335,45 +356,62 @@
 
 def solve_kernel(cells, last, partial, left, right, section, solve, *refs):
     if last:
-        out, levels = refs
+        out, levels, staged, sems = refs
     else:
         flat, next_left, next_right, upward, downward, levels = refs
     masks = edge_masks()
-    wide = levels.shape[1]
-    levels[:PAD_S, :] = left[:, :wide]
-    levels[PAD_S : 2 * PAD_S, :] = right[:, :wide]
+
+    def spare(given, e):
+        row, tile = e % GROUP, PACKED + ROWS + e // GROUP
+        return given[row : row + 1, lane(tile)]
+
+    for side, given in enumerate((left, right)):
+        top = PAD_S * side
+        levels[top : top + 8, :] = given[:, lane(0, BREADTH)]
+        for e in range(BREADTH):
+            tile = given[:, lane(BREADTH + e // 2)]
+            levels[top + 8 : top + 16, lane(e)] = pltpu.roll(tile, 4, 0) if e % 2 else tile
+            if not last:
+                levels[top + 12 : top + 13, lane(e)] = spare(given, e)
     found = partial[...] + dot(solve[...], climb(levels, 2 * PAD_S, masks))
 
-    def gradient(rows, slope_rows, r):
+    def slope(c, rows, slope_rows, r):
         phi = lambda r: masked(found[rows, lane(r + 2)], r, masks)
-        return (
-            stream_slope(phi(r)),
-            first_diff(phi(r + 1), phi(r - 1), phi(r + 2), phi(r - 2)),
-            found[slope_rows, lane(r + 2)],
-        )
-
-    for r in range(ROWS):
-        slopes = gradient(slice(0, cells), slice(cells, 2 * cells), r)
-        for c in range(3):
-            rows = slice(cells * c, cells * (c + 1))
-            value = section[rows, lane(r)] - slopes[c]
+        if c == 0:
+            return stream_slope(phi(r))
+        if c == 1:
+            return first_diff(phi(r + 1), phi(r - 1), phi(r + 2), phi(r - 2))
+        return found[slope_rows, lane(r + 2)]
+
+    copies = []
+    for c in range(3):
+        rows = slice(cells * c, cells * (c + 1))
+        for r in range(ROWS):
+            value = section[rows, lane(r)] - slope(c, slice(0, cells), slice(cells, 2 * cells), r)
             if last:
-                out[c, :, r, :] = value
-            else:
-                flat[rows, lane(r)] = value
-                if r < 2:
-                    downward[rows, lane(r)] = value
-                if r >= ROWS - 2:
-                    upward[rows, lane(r - ROWS + 2)] = value
+                staged[c, :, r, :] = value
+                continue
+            flat[rows, lane(r)] = value
+            if r < 2:
+                downward[rows, lane(r)] = value
+            if r >= ROWS - 2:
+                upward[rows, lane(r - ROWS + 2)] = value
+        if last:
+            copies.append(pltpu.make_async_copy(staged.at[c], out.at[c], sems.at[c]))
+            copies[c].start()
+    for copy in copies:
+        copy.wait()
     if not last:
         for side, (given, target) in enumerate(((left, next_left), (right, next_right))):
             top = 2 * cells + 2 * GROUP * side
-            target[...] = given[:, wide:]
+            phi_rows, slope_rows = slice(top, top + GROUP), slice(top + GROUP, top + 2 * GROUP)
+            target[:GROUP, :] = given[:, lane(PACKED, ROWS)]
+            target[GROUP:, :] = jnp.zeros((PAD_V - GROUP, ROWS * LANES), jnp.float32)
             for r in range(ROWS):
-                slopes = gradient(slice(top, top + GROUP), slice(top + GROUP, top + 2 * GROUP), r)
+                target[GROUP : GROUP + 1, lane(r)] = spare(given, BREADTH + r)
                 for c in range(3):
                     rows = slice(RANK_V * c, RANK_V * (c + 1))
-                    target[rows, lane(r)] = given[rows, wide + r * LANES : wide + (r + 1) * LANES] - slopes[c][:RANK_V]
+                    target[rows, lane(r)] = target[rows, lane(r)] - slope(c, phi_rows, slope_rows, r)[:RANK_V]
 
 
 def call(body, shapes, *args, scratch=(), **options):
@@ -393,9 +431,9 @@
 
 def per_device(velocity, viscosity):
     components, cells, row_cells, columns = velocity.shape
-    slopes, moments, lateral, source, solve_own, solve_sides = (
-        jnp.asarray(t) for t in tables(cells * lax.axis_size("span"), cells)
-    )
+    length = cells * lax.axis_size("span")
+    slopes, moments, lateral, *first_tables = (jnp.asarray(t) for t in tables(length, cells, False))
+    last_tables = [jnp.asarray(t) for t in tables(length, cells, True)[3:]]
     width = row_cells * columns
     wide = (row_cells + 2 * REACH) * columns
     near = cells + PAD_M
@@ -403,12 +441,13 @@
     start, to_right, to_left, upward, downward = call(
         functools.partial(open_kernel, cells),
         [(components * cells, width), edge, edge, rim, rim],
-        velocity, moments,
+        pltpu.with_memory_space_constraint(velocity, pltpu.HBM),
+        pltpu.with_memory_space_constraint(moments, pltpu.HBM),
         in_specs=[pl.BlockSpec(memory_space=pltpu.HBM)] * 2,
         scratch=[
             pltpu.VMEM(velocity.shape, jnp.float32),
             pltpu.VMEM(moments.shape, jnp.float32),
-            pltpu.SemaphoreType.DMA((2,)),
+            pltpu.SemaphoreType.DMA((4,)),
         ],
     )
     left = shifted(to_right, "span", 1)
@@ -418,16 +457,17 @@
         low = shifted(upward, "cross", 1)
         high = shifted(downward, "cross", -1)
         base = (start,) if second else ()
+        source, solve_own, solve_sides = last_tables if second else first_tables
         section, parts, up_near, down_near, up_far, down_far = call(
             functools.partial(tendency_kernel, cells, second),
-            [(components * cells, width), (near, width)] + [(near, 7 * columns)] * 2 + [(near, 3 * columns)] * 2,
+            [(components * cells, width), (near, width)] + [(7 * cells + 4 * PAD_M, columns)] * 2 + [(3 * cells + PAD_M, columns)] * 2,
             *base, flat, viscosity, left, right, low, high, slopes, lateral,
         )
         low_one = shifted(up_near, "cross", 1)
         high_one = shifted(down_near, "cross", -1)
         low_two = shifted(up_far, "cross", 2)
         high_two = shifted(down_far, "cross", -2)
-        sent = (PAD_S, wide if second else wide + width)
+        sent = (GROUP, (PACKED if second else PACKED + ROWS + 3) * columns)
         extra = () if second else (moments,)
         ext, to_right, to_left = call(
             functools.partial(source_kernel, cells, not second),
@@ -436,18 +476,21 @@
         )
         left = shifted(to_right, "span", 1)
         right = shifted(to_left, "span", -1)
-        height = 2 * cells if second else solve_own.shape[0]
         (partial,) = call(
             home_kernel,
-            [(height, (row_cells + 4) * columns)],
-            ext, solve_own[:height],
+            [(solve_own.shape[0], (row_cells + 4) * columns)],
+            ext, solve_own,
             scratch=[pltpu.VMEM((SWEEPS * near, wide), jnp.float32)],
         )
         scratch = [pltpu.VMEM((SWEEPS * 2 * PAD_S, wide), jnp.float32)]
-        given = (partial, left, right, section, solve_sides[:height])
+        given = (partial, left, right, section, solve_sides)
         body = functools.partial(solve_kernel, cells, second)
         if second:
-            (out,) = call(body, [velocity.shape], *given, scratch=scratch)
+            (out,) = call(
+                body, [velocity.shape], *given,
+                scratch=scratch + [pltpu.VMEM(velocity.shape, jnp.float32), pltpu.SemaphoreType.DMA((3,))],
+                out_specs=[pl.BlockSpec(memory_space=pltpu.HBM)],
+            )
         else:
             flat, left, right, upward, downward = call(
                 body, [(components * cells, width), edge, edge, rim, rim], *given, scratch=scratch

time: 65 us -> 63.4 us (0.975)
  local copies, waits for them, and re-layouts: 1.84 us -> 0.05 us
  Pallas kernels: 10.2 us -> 11.6 us
  waiting for transfers between devices: 33.2 us -> 31.9 us
    unnamed x22 -> x20, local copies, waits for them, and re-layouts: 1.84 us -> 0.05 us
    pallas_call x9, Pallas kernels: 10.2 us -> 11.6 us  [call(): pl.pallas_call(body, out_shape=[jax.ShapeDtypeStruct(s, jnp.float32) for...]
    ppermute x18, waiting for transfers between devices: 33.2 us -> 31.9 us  [shifted(): lax.ppermute(block, axis, [(i, (i + step) % count) for i in range(count)])]
where the time goes in v2:
time: 63.4 us; the launch traced here: 63.3 us
  waiting for transfers between devices  31.9 us (50%)
  starting transfers between devices  19.5 us (31%)
  Pallas kernels  11.6 us (18%)
    ppermute x18, waiting for transfers between devices, shifted(): lax.ppermute(block, axis, [(i, (i + step) % count) for i in range(count)])  31.9 us
    ppermute x18, starting transfers between devices, shifted(): lax.ppermute(block, axis, [(i, (i + step) % count) for i in range(count)])  19.5 us
    pallas_call x9, Pallas kernels, call(): pl.pallas_call(body, out_shape=[jax.ShapeDtypeStruct(s, jnp.float32) for...  11.6 us
  transfers between devices with their start and end apart: 18, of which 11 were waited for; matrix products, arithmetic and copies ran while one was open for 0% of the time, Pallas kernels for 5%

profile of v2, /device:TPU:126, one launch (start us, length us, event | category | flops | bytes accessed | tf_op | source)
XLA Modules:
  0.0 63.3 jit_solution(17322102665426718836)
XLA Ops:
  0.0 0.0 copy-start
  0.0 0.0 copy-start.4
  0.0 0.0 copy-start.1
  0.0 1.6 %shard_map.109 = (f32[192,512]{1,0:T(8,128)S(1)}, f32[16,512]{1,0:T(8,128)S(1)}, f32[16,512]{1,0:T(8,128)S(1)}, f32[192,256]{1,0:T(8,128)S(1)}, f32[192,256]{1,0:T(8,128)S(1)}) custom-call(f32[3,64,4,128]{3,2,1,0:T(4,128)} %velocity.1, f32[32,192]{1,0:T(8,128)} %constant.19.clone.moments.refs_0_), custom_call_target="tpu_custom_call" | custom-call | tf_op jit(solution)/shard_map/pallas_call | solution.py:418
  1.6 0.0 collective-permute-start.2
  1.6 1.7 %collective-permute-start.3 = (f32[192,256]{1,0:T(8,128)S(1)}, f32[192,256]{1,0:T(8,128)S(1)}, u32[]{:S(2)}, u32[]{:S(2)}) collective-permute-start(f32[192,256]{1,0:T(8,128)S(1)} %get-tuple-element.37), channel_id=1, source_target_pairs={{0,7},{1,0},{2,1},{3,2},{4,3},{5,4},{6,5},{7,6},{8,15},{9,8},{10,9... | collective-permute-start | bytes 589832 | tf_op jit(solution)/shard_map/ppermute | solution.py:429
  3.4 3.0 %collective-permute-start = (f32[16,512]{1,0:T(8,128)S(1)}, f32[16,512]{1,0:T(8,128)S(1)}, u32[]{:S(2)}, u32[]{:S(2)}) collective-permute-start(f32[16,512]{1,0:T(8,128)S(1)} %get-tuple-element.34), channel_id=1, source_target_pairs={{0,8},{8,16},{16,24},{24,32},{32,40},{40,48},{48,56},{56,64},{64,7... | collective-permute-start | bytes 98312 | tf_op jit(solution)/shard_map/ppermute | solution.py:429
  6.4 0.0 collective-permute-start.1
  6.4 1.6 %collective-permute-done.refs_2_ = f32[16,512]{1,0:T(8,128)S(1)} collective-permute-done((f32[16,512]{1,0:T(8,128)S(1)}, f32[16,512]{1,0:T(8,128)S(1)}, u32[]{:S(2)}, u32[]{:S(2)}) %collective-permute-start) | collective-permute-done | bytes 32800 | tf_op jit(solution)/shard_map/ppermute | solution.py:429
  8.0 5.6 %collective-permute-done.1.refs_3_ = f32[16,512]{1,0:T(8,128)S(1)} collective-permute-done((f32[16,512]{1,0:T(8,128)S(1)}, f32[16,512]{1,0:T(8,128)S(1)}, u32[]{:S(2)}, u32[]{:S(2)}) %collective-permute-start.1) | collective-permute-done | bytes 32800 | tf_op jit(solution)/shard_map/ppermute | solution.py:429
  13.6 0.0 collective-permute-done.2.refs_4_
  13.6 0.0 collective-permute-done.3.refs_5_
  13.6 0.0 copy-done
  13.6 0.0 copy-done.4
  13.7 0.0 copy-done.1
  13.7 0.0 copy-start.5
  13.7 0.0 copy-start.9
  13.7 1.5 %shard_map.110 = (f32[192,512]{1,0:T(8,128)S(1)}, f32[72,512]{1,0:T(8,128)S(1)}, f32[480,128]{1,0:T(8,128)S(1)}, f32[480,128]{1,0:T(8,128)S(1)}, f32[200,128]{1,0:T(8,128)S(1)}, /*index=5*/f32[200,128]{1,0:T(8,128)S(1)}) custom-call(f32[192,512]{1,0:T(8,128)S(1)} %get-tuple-element.33.refs_0_, f32[64,4,128]{2,1,0:T(4,128)S(1)} %copy-done.1, ...), custom_call_target="tpu_custom_call" | custom-call | tf_op jit(solution)/shard_map/pallas_call | solution.py:418
  15.2 0.0 collective-permute-start.4
  15.2 1.7 %collective-permute-start.5 = (f32[480,128]{1,0:T(8,128)S(1)}, f32[480,128]{1,0:T(8,128)S(1)}, u32[]{:S(2)}, u32[]{:S(2)}) collective-permute-start(f32[480,128]{1,0:T(8,128)S(1)} %get-tuple-element.41), channel_id=1, source_target_pairs={{0,7},{1,0},{2,1},{3,2},{4,3},{5,4},{6,5},{7,6},{8,15},{9,8},{10,9... | collective-permute-start | bytes 737288 | tf_op jit(solution)/shard_map/ppermute | solution.py:429
  17.0 2.6 %collective-permute-start.6 = (f32[200,128]{1,0:T(8,128)S(1)}, f32[200,128]{1,0:T(8,128)S(1)}, u32[]{:S(2)}, u32[]{:S(2)}) collective-permute-start(f32[200,128]{1,0:T(8,128)S(1)} %get-tuple-element.42), channel_id=1, source_target_pairs={{0,2},{1,3},{2,4},{3,5},{4,6},{5,7},{6,0},{7,1},{8,10},{9,11},{10,... | collective-permute-start | bytes 307208 | tf_op jit(solution)/shard_map/ppermute | solution.py:429
  19.6 0.0 collective-permute-start.7
  19.6 3.2 %collective-permute-done.6.low_two = f32[200,128]{1,0:T(8,128)S(1)} collective-permute-done((f32[200,128]{1,0:T(8,128)S(1)}, f32[200,128]{1,0:T(8,128)S(1)}, u32[]{:S(2)}, u32[]{:S(2)}) %collective-permute-start.6) | collective-permute-done | bytes 102432 | tf_op jit(solution)/shard_map/ppermute | solution.py:429
  22.8 2.8 %collective-permute-done.7.high_two = f32[200,128]{1,0:T(8,128)S(1)} collective-permute-done((f32[200,128]{1,0:T(8,128)S(1)}, f32[200,128]{1,0:T(8,128)S(1)}, u32[]{:S(2)}, u32[]{:S(2)}) %collective-permute-start.7) | collective-permute-done | bytes 102432 | tf_op jit(solution)/shard_map/ppermute | solution.py:429
  25.5 0.0 collective-permute-done.4.low_one
  25.5 0.0 collective-permute-done.5.high_one
  25.5 0.0 copy-done.5
  25.5 0.0 copy-done.9
  25.5 0.0 copy-start.2
  25.6 0.7 %shard_map.111 = (f32[72,1792]{1,0:T(8,128)S(1)}, f32[8,3584]{1,0:T(8,128)S(1)}, f32[8,3584]{1,0:T(8,128)S(1)}) custom-call(f32[72,512]{1,0:T(8,128)S(1)} %get-tuple-element.38.parts, f32[192,512]{1,0:T(8,128)S(1)} %get-tuple-element.39.section, f32[480,128]{1,0:T(8,128)S(1)} %collective-permute-done.4.low_one, ...), custom_call_target="tpu_custom_call" | custom-call | tf_op jit(solution)/shard_map/pallas_call | solution.py:418
  26.3 0.1 collective-permute-start.8
  26.4 2.0 %collective-permute-start.9 = (f32[8,3584]{1,0:T(8,128)S(1)}, f32[8,3584]{1,0:T(8,128)S(1)}, u32[]{:S(2)}, u32[]{:S(2)}) collective-permute-start(f32[8,3584]{1,0:T(8,128)S(1)} %get-tuple-element.46), channel_id=1, source_target_pairs={{0,248},{8,0},{16,8},{24,16},{32,24},{40,32},{48,40},{56,48},{64,5... | collective-permute-start | bytes 344072 | tf_op jit(solution)/shard_map/ppermute | solution.py:429
  28.4 0.0 copy-done.2
  28.4 0.0 copy-start.6
  28.4 1.6 %shard_map.112.partial = f32[160,1024]{1,0:T(8,128)S(1)} custom-call(f32[72,1792]{1,0:T(8,128)S(1)} %get-tuple-element.44.ext, f32[160,288]{1,0:T(8,128)S(1)} %copy-done.2), custom_call_target="tpu_custom_call" | custom-call | tf_op jit(solution)/shard_map/pallas_call | solution.py:418
  29.9 1.2 %collective-permute-done.8.left = f32[8,3584]{1,0:T(8,128)S(1)} collective-permute-done((f32[8,3584]{1,0:T(8,128)S(1)}, f32[8,3584]{1,0:T(8,128)S(1)}, u32[]{:S(2)}, u32[]{:S(2)}) %collective-permute-start.8) | collective-permute-done | bytes 114720 | tf_op jit(solution)/shard_map/ppermute | solution.py:429
  31.1 3.4 %collective-permute-done.9.right = f32[8,3584]{1,0:T(8,128)S(1)} collective-permute-done((f32[8,3584]{1,0:T(8,128)S(1)}, f32[8,3584]{1,0:T(8,128)S(1)}, u32[]{:S(2)}, u32[]{:S(2)}) %collective-permute-start.9) | collective-permute-done | bytes 114720 | tf_op jit(solution)/shard_map/ppermute | solution.py:429
  34.5 0.0 copy-done.6
  34.5 1.0 %shard_map.113 = (f32[192,512]{1,0:T(8,128)S(1)}, f32[16,512]{1,0:T(8,128)S(1)}, f32[16,512]{1,0:T(8,128)S(1)}, f32[192,256]{1,0:T(8,128)S(1)}, f32[192,256]{1,0:T(8,128)S(1)}) custom-call(f32[160,1024]{1,0:T(8,128)S(1)} %shard_map.112.partial, f32[8,3584]{1,0:T(8,128)S(1)} %collective-permute-done.8.left, f32[8,3584]{1,0:T(8,128)S(1)} %collective-permute-done.9.right, ...), custom_call_target="tpu_custom_call" | custom-call | tf_op jit(solution)/shard_map/pallas_call | solution.py:418
  35.6 0.0 collective-permute-start.10
  35.6 1.7 %collective-permute-start.11 = (f32[192,256]{1,0:T(8,128)S(1)}, f32[192,256]{1,0:T(8,128)S(1)}, u32[]{:S(2)}, u32[]{:S(2)}) collective-permute-start(f32[192,256]{1,0:T(8,128)S(1)} %get-tuple-element.51), channel_id=1, source_target_pairs={{0,7},{1,0},{2,1},{3,2},{4,3},{5,4},{6,5},{7,6},{8,15},{9,8},{10,9... | collective-permute-start | bytes 589832 | tf_op jit(solution)/shard_map/ppermute | solution.py:429
  37.3 3.3 %collective-permute-done.10.refs_5_ = f32[192,256]{1,0:T(8,128)S(1)} collective-permute-done((f32[192,256]{1,0:T(8,128)S(1)}, f32[192,256]{1,0:T(8,128)S(1)}, u32[]{:S(2)}, u32[]{:S(2)}) %collective-permute-start.10) | collective-permute-done | bytes 196640 | tf_op jit(solution)/shard_map/ppermute | solution.py:429
  40.7 0.0 collective-permute-done.11.refs_6_
  40.7 0.0 copy-start.8
  40.7 1.5 %shard_map.114 = (f32[192,512]{1,0:T(8,128)S(1)}, f32[72,512]{1,0:T(8,128)S(1)}, f32[480,128]{1,0:T(8,128)S(1)}, f32[480,128]{1,0:T(8,128)S(1)}, f32[200,128]{1,0:T(8,128)S(1)}, /*index=5*/f32[200,128]{1,0:T(8,128)S(1)}) custom-call(f32[192,512]{1,0:T(8,128)S(1)} %get-tuple-element.33.refs_0_, f32[192,512]{1,0:T(8,128)S(1)} %get-tuple-element.47.refs_1_, ...), custom_call_target="tpu_custom_call" | custom-call | tf_op jit(solution)/shard_map/pallas_call | solution.py:418
  42.2 1.5 %collective-permute-start.12 = (f32[480,128]{1,0:T(8,128)S(1)}, f32[480,128]{1,0:T(8,128)S(1)}, u32[]{:S(2)}, u32[]{:S(2)}) collective-permute-start(f32[480,128]{1,0:T(8,128)S(1)} %get-tuple-element.54), channel_id=1, source_target_pairs={{0,1},{1,2},{2,3},{3,4},{4,5},{5,6},{6,7},{7,0},{8,9},{9,10},{10,1... | collective-permute-start | bytes 737288 | tf_op jit(solution)/shard_map/ppermute | solution.py:429
  43.7 0.3 collective-permute-start.13
  44.0 2.6 %collective-permute-start.14 = (f32[200,128]{1,0:T(8,128)S(1)}, f32[200,128]{1,0:T(8,128)S(1)}, u32[]{:S(2)}, u32[]{:S(2)}) collective-permute-start(f32[200,128]{1,0:T(8,128)S(1)} %get-tuple-element.56), channel_id=1, source_target_pairs={{0,2},{1,3},{2,4},{3,5},{4,6},{5,7},{6,0},{7,1},{8,10},{9,11},{10,... | collective-permute-start | bytes 307208 | tf_op jit(solution)/shard_map/ppermute | solution.py:429
  46.6 0.0 collective-permute-start.15
  46.6 3.2 %collective-permute-done.14.low_two = f32[200,128]{1,0:T(8,128)S(1)} collective-permute-done((f32[200,128]{1,0:T(8,128)S(1)}, f32[200,128]{1,0:T(8,128)S(1)}, u32[]{:S(2)}, u32[]{:S(2)}) %collective-permute-start.14) | collective-permute-done | bytes 102432 | tf_op jit(solution)/shard_map/ppermute | solution.py:429
  49.8 3.0 %collective-permute-done.15.high_two = f32[200,128]{1,0:T(8,128)S(1)} collective-permute-done((f32[200,128]{1,0:T(8,128)S(1)}, f32[200,128]{1,0:T(8,128)S(1)}, u32[]{:S(2)}, u32[]{:S(2)}) %collective-permute-start.15) | collective-permute-done | bytes 102432 | tf_op jit(solution)/shard_map/ppermute | solution.py:429
  52.8 0.0 collective-permute-done.12.low_one
  52.8 0.0 collective-permute-done.13.high_one
  52.8 0.0 copy-done.8
  52.9 0.0 copy-start.3
  52.9 0.5 shard_map.115
  53.4 0.1 collective-permute-start.16
  53.5 2.0 %collective-permute-start.17 = (f32[8,2688]{1,0:T(8,128)S(1)}, f32[8,2688]{1,0:T(8,128)S(1)}, u32[]{:S(2)}, u32[]{:S(2)}) collective-permute-start(f32[8,2688]{1,0:T(8,128)S(1)} %get-tuple-element.60), channel_id=1, source_target_pairs={{0,248},{8,0},{16,8},{24,16},{32,24},{40,32},{48,40},{56,48},{64,5... | collective-permute-start | bytes 258056 | tf_op jit(solution)/shard_map/ppermute | solution.py:429
  55.5 0.0 copy-done.3
  55.5 1.4 %shard_map.116.partial = f32[128,1024]{1,0:T(8,128)S(1)} custom-call(f32[72,1792]{1,0:T(8,128)S(1)} %get-tuple-element.58.ext, f32[128,288]{1,0:T(8,128)S(1)} %copy-done.3), custom_call_target="tpu_custom_call" | custom-call | tf_op jit(solution)/shard_map/pallas_call | solution.py:418
  56.9 1.1 %collective-permute-done.16.left = f32[8,2688]{1,0:T(8,128)S(1)} collective-permute-done((f32[8,2688]{1,0:T(8,128)S(1)}, f32[8,2688]{1,0:T(8,128)S(1)}, u32[]{:S(2)}, u32[]{:S(2)}) %collective-permute-start.16) | collective-permute-done | bytes 86048 | tf_op jit(solution)/shard_map/ppermute | solution.py:429
  58.0 3.4 %collective-permute-done.17.right = f32[8,2688]{1,0:T(8,128)S(1)} collective-permute-done((f32[8,2688]{1,0:T(8,128)S(1)}, f32[8,2688]{1,0:T(8,128)S(1)}, u32[]{:S(2)}, u32[]{:S(2)}) %collective-permute-start.17) | collective-permute-done | bytes 86048 | tf_op jit(solution)/shard_map/ppermute | solution.py:429
  61.4 0.0 copy-done.7
  61.4 1.8 %shard_map.117 = f32[3,64,4,128]{3,2,1,0:T(4,128)} custom-call(f32[128,1024]{1,0:T(8,128)S(1)} %shard_map.116.partial, f32[8,2688]{1,0:T(8,128)S(1)} %collective-permute-done.16.left, f32[8,2688]{1,0:T(8,128)S(1)} %collective-permute-done.17.right, f32[192,512]{1,0:T(8,128)S(1)} %get-tuple-element.53.section, f32[128,128]{1,0:T(8,128)S(1)} %copy-done.7), custom_call_target="tpu_custom_call" | custom-call | tf_op jit(solution)/shard_map/pallas_call | solution.py:418
  (1 shorter events, 0.0 us)
Async XLA Ops:
  0.0 13.6 %copy-start = (f32[3,128,96]{2,1,0:T(8,128)S(1)}, f32[3,128,96]{2,1,0:T(8,128)}, u32[]{:S(2)}) copy-start(f32[3,128,96]{2,1,0:T(8,128)} %constant.18.clone.refs_6_.refs_7_) | copy-start | bytes 442372
  0.0 13.6 %copy-start.4 = (f32[72,64]{1,0:T(8,128)S(1)}, f32[72,64]{1,0:T(8,128)}, u32[]{:S(2)}) copy-start(f32[72,64]{1,0:T(8,128)} %constant.20.clone.refs_7_.refs_8_) | copy-start | bytes 55300
  0.0 13.7 %copy-start.1 = (f32[64,4,128]{2,1,0:T(4,128)S(1)}, f32[64,4,128]{2,1,0:T(4,128)}, u32[]{:S(2)}) copy-start(f32[64,4,128]{2,1,0:T(4,128)} %refs_2_.1) | copy-start | bytes 393220
  1.6 12.0 %collective-permute-start.2 = (f32[192,256]{1,0:T(8,128)S(1)}, f32[192,256]{1,0:T(8,128)S(1)}, u32[]{:S(2)}, u32[]{:S(2)}) collective-permute-start(f32[192,256]{1,0:T(8,128)S(1)} %get-tuple-element.36), channel_id=1, source_target_pairs={{0,1},{1,2},{2,3},{3,4},{4,5},{5,6},{6,7},{7,0},{8,9},{9,10},{10,1... | collective-permute-start | bytes 589832 | tf_op jit(solution)/shard_map/ppermute | solution.py:429
  1.6 12.0 %collective-permute-start.3 = (f32[192,256]{1,0:T(8,128)S(1)}, f32[192,256]{1,0:T(8,128)S(1)}, u32[]{:S(2)}, u32[]{:S(2)}) collective-permute-start(f32[192,256]{1,0:T(8,128)S(1)} %get-tuple-element.37), channel_id=1, source_target_pairs={{0,7},{1,0},{2,1},{3,2},{4,3},{5,4},{6,5},{7,6},{8,15},{9,8},{10,9... | collective-permute-start | bytes 589832 | tf_op jit(solution)/shard_map/ppermute | solution.py:429
  3.4 4.6 %collective-permute-start = (f32[16,512]{1,0:T(8,128)S(1)}, f32[16,512]{1,0:T(8,128)S(1)}, u32[]{:S(2)}, u32[]{:S(2)}) collective-permute-start(f32[16,512]{1,0:T(8,128)S(1)} %get-tuple-element.34), channel_id=1, source_target_pairs={{0,8},{8,16},{16,24},{24,32},{32,40},{40,48},{48,56},{56,64},{64,7... | collective-permute-start | bytes 98312 | tf_op jit(solution)/shard_map/ppermute | solution.py:429
  6.4 7.2 %collective-permute-start.1 = (f32[16,512]{1,0:T(8,128)S(1)}, f32[16,512]{1,0:T(8,128)S(1)}, u32[]{:S(2)}, u32[]{:S(2)}) collective-permute-start(f32[16,512]{1,0:T(8,128)S(1)} %get-tuple-element.35), channel_id=1, source_target_pairs={{0,248},{8,0},{16,8},{24,16},{32,24},{40,32},{48,40},{56,48},{64,5... | collective-permute-start | bytes 98312 | tf_op jit(solution)/shard_map/ppermute | solution.py:429
  13.7 11.9 %copy-start.5 = (f32[32,192]{1,0:T(8,128)S(1)}, f32[32,192]{1,0:T(8,128)}, u32[]{:S(2)}) copy-start(f32[32,192]{1,0:T(8,128)} %constant.19.clone.moments.refs_0_) | copy-start | bytes 73732
  13.7 11.9 %copy-start.9 = (f32[64,72]{1,0:T(8,128)S(1)}, f32[64,72]{1,0:T(8,128)}, u32[]{:S(2)}) copy-start(f32[64,72]{1,0:T(8,128)} %constant.21.clone.source) | copy-start | bytes 55300
  15.2 10.3 %collective-permute-start.4 = (f32[480,128]{1,0:T(8,128)S(1)}, f32[480,128]{1,0:T(8,128)S(1)}, u32[]{:S(2)}, u32[]{:S(2)}) collective-permute-start(f32[480,128]{1,0:T(8,128)S(1)} %get-tuple-element.40), channel_id=1, source_target_pairs={{0,1},{1,2},{2,3},{3,4},{4,5},{5,6},{6,7},{7,0},{8,9},{9,10},{10,1... | collective-permute-start | bytes 737288 | tf_op jit(solution)/shard_map/ppermute | solution.py:429
  15.2 10.3 %collective-permute-start.5 = (f32[480,128]{1,0:T(8,128)S(1)}, f32[480,128]{1,0:T(8,128)S(1)}, u32[]{:S(2)}, u32[]{:S(2)}) collective-permute-start(f32[480,128]{1,0:T(8,128)S(1)} %get-tuple-element.41), channel_id=1, source_target_pairs={{0,7},{1,0},{2,1},{3,2},{4,3},{5,4},{6,5},{7,6},{8,15},{9,8},{10,9... | collective-permute-start | bytes 737288 | tf_op jit(solution)/shard_map/ppermute | solution.py:429
  17.0 5.8 %collective-permute-start.6 = (f32[200,128]{1,0:T(8,128)S(1)}, f32[200,128]{1,0:T(8,128)S(1)}, u32[]{:S(2)}, u32[]{:S(2)}) collective-permute-start(f32[200,128]{1,0:T(8,128)S(1)} %get-tuple-element.42), channel_id=1, source_target_pairs={{0,2},{1,3},{2,4},{3,5},{4,6},{5,7},{6,0},{7,1},{8,10},{9,11},{10,... | collective-permute-start | bytes 307208 | tf_op jit(solution)/shard_map/ppermute | solution.py:429
  19.6 5.9 %collective-permute-start.7 = (f32[200,128]{1,0:T(8,128)S(1)}, f32[200,128]{1,0:T(8,128)S(1)}, u32[]{:S(2)}, u32[]{:S(2)}) collective-permute-start(f32[200,128]{1,0:T(8,128)S(1)} %get-tuple-element.43), channel_id=1, source_target_pairs={{0,6},{1,7},{2,0},{3,1},{4,2},{5,3},{6,4},{7,5},{8,14},{9,15},{10,... | collective-permute-start | bytes 307208 | tf_op jit(solution)/shard_map/ppermute | solution.py:429
  25.5 2.8 %copy-start.2 = (f32[160,288]{1,0:T(8,128)S(1)}, f32[160,288]{1,0:T(8,128)}, u32[]{:S(2)}) copy-start(f32[160,288]{1,0:T(8,128)} %constant.22.clone.solve) | copy-start | bytes 552964
  26.3 4.9 %collective-permute-start.8 = (f32[8,3584]{1,0:T(8,128)S(1)}, f32[8,3584]{1,0:T(8,128)S(1)}, u32[]{:S(2)}, u32[]{:S(2)}) collective-permute-start(f32[8,3584]{1,0:T(8,128)S(1)} %get-tuple-element.45), channel_id=1, source_target_pairs={{0,8},{8,16},{16,24},{24,32},{32,40},{40,48},{48,56},{56,64},{64,7... | collective-permute-start | bytes 344072 | tf_op jit(solution)/shard_map/ppermute | solution.py:429
  26.4 8.2 %collective-permute-start.9 = (f32[8,3584]{1,0:T(8,128)S(1)}, f32[8,3584]{1,0:T(8,128)S(1)}, u32[]{:S(2)}, u32[]{:S(2)}) collective-permute-start(f32[8,3584]{1,0:T(8,128)S(1)} %get-tuple-element.46), channel_id=1, source_target_pairs={{0,248},{8,0},{16,8},{24,16},{32,24},{40,32},{48,40},{56,48},{64,5... | collective-permute-start | bytes 344072 | tf_op jit(solution)/shard_map/ppermute | solution.py:429
  28.4 6.2 %copy-start.6 = (f32[160,128]{1,0:T(8,128)S(1)}, f32[160,128]{1,0:T(8,128)}, u32[]{:S(2)}) copy-start(f32[160,128]{1,0:T(8,128)} %constant.23.clone.solve) | copy-start | bytes 245764
  35.6 5.1 %collective-permute-start.10 = (f32[192,256]{1,0:T(8,128)S(1)}, f32[192,256]{1,0:T(8,128)S(1)}, u32[]{:S(2)}, u32[]{:S(2)}) collective-permute-start(f32[192,256]{1,0:T(8,128)S(1)} %get-tuple-element.50), channel_id=1, source_target_pairs={{0,1},{1,2},{2,3},{3,4},{4,5},{5,6},{6,7},{7,0},{8,9},{9,10},{10,1... | collective-permute-start | bytes 589832 | tf_op jit(solution)/shard_map/ppermute | solution.py:429
  35.6 5.1 %collective-permute-start.11 = (f32[192,256]{1,0:T(8,128)S(1)}, f32[192,256]{1,0:T(8,128)S(1)}, u32[]{:S(2)}, u32[]{:S(2)}) collective-permute-start(f32[192,256]{1,0:T(8,128)S(1)} %get-tuple-element.51), channel_id=1, source_target_pairs={{0,7},{1,0},{2,1},{3,2},{4,3},{5,4},{6,5},{7,6},{8,15},{9,8},{10,9... | collective-permute-start | bytes 589832 | tf_op jit(solution)/shard_map/ppermute | solution.py:429
  40.7 12.2 %copy-start.8 = (f32[64,72]{1,0:T(8,128)S(1)}, f32[64,72]{1,0:T(8,128)}, u32[]{:S(2)}) copy-start(f32[64,72]{1,0:T(8,128)} %constant.24.clone.source) | copy-start | bytes 55300
  42.2 10.6 %collective-permute-start.12 = (f32[480,128]{1,0:T(8,128)S(1)}, f32[480,128]{1,0:T(8,128)S(1)}, u32[]{:S(2)}, u32[]{:S(2)}) collective-permute-start(f32[480,128]{1,0:T(8,128)S(1)} %get-tuple-element.54), channel_id=1, source_target_pairs={{0,1},{1,2},{2,3},{3,4},{4,5},{5,6},{6,7},{7,0},{8,9},{9,10},{10,1... | collective-permute-start | bytes 737288 | tf_op jit(solution)/shard_map/ppermute | solution.py:429
  43.7 9.2 %collective-permute-start.13 = (f32[480,128]{1,0:T(8,128)S(1)}, f32[480,128]{1,0:T(8,128)S(1)}, u32[]{:S(2)}, u32[]{:S(2)}) collective-permute-start(f32[480,128]{1,0:T(8,128)S(1)} %get-tuple-element.55), channel_id=1, source_target_pairs={{0,7},{1,0},{2,1},{3,2},{4,3},{5,4},{6,5},{7,6},{8,15},{9,8},{10,9... | collective-permute-start | bytes 737288 | tf_op jit(solution)/shard_map/ppermute | solution.py:429
  44.0 5.8 %collective-permute-start.14 = (f32[200,128]{1,0:T(8,128)S(1)}, f32[200,128]{1,0:T(8,128)S(1)}, u32[]{:S(2)}, u32[]{:S(2)}) collective-permute-start(f32[200,128]{1,0:T(8,128)S(1)} %get-tuple-element.56), channel_id=1, source_target_pairs={{0,2},{1,3},{2,4},{3,5},{4,6},{5,7},{6,0},{7,1},{8,10},{9,11},{10,... | collective-permute-start | bytes 307208 | tf_op jit(solution)/shard_map/ppermute | solution.py:429
  46.6 6.3 %collective-permute-start.15 = (f32[200,128]{1,0:T(8,128)S(1)}, f32[200,128]{1,0:T(8,128)S(1)}, u32[]{:S(2)}, u32[]{:S(2)}) collective-permute-start(f32[200,128]{1,0:T(8,128)S(1)} %get-tuple-element.57), channel_id=1, source_target_pairs={{0,6},{1,7},{2,0},{3,1},{4,2},{5,3},{6,4},{7,5},{8,14},{9,15},{10,... | collective-permute-start | bytes 307208 | tf_op jit(solution)/shard_map/ppermute | solution.py:429
  52.9 2.7 %copy-start.3 = (f32[128,288]{1,0:T(8,128)S(1)}, f32[128,288]{1,0:T(8,128)}, u32[]{:S(2)}) copy-start(f32[128,288]{1,0:T(8,128)} %constant.25.clone.solve) | copy-start | bytes 442372
  53.4 4.6 %collective-permute-start.16 = (f32[8,2688]{1,0:T(8,128)S(1)}, f32[8,2688]{1,0:T(8,128)S(1)}, u32[]{:S(2)}, u32[]{:S(2)}) collective-permute-start(f32[8,2688]{1,0:T(8,128)S(1)} %get-tuple-element.59), channel_id=1, source_target_pairs={{0,8},{8,16},{16,24},{24,32},{32,40},{40,48},{48,56},{56,64},{64,7... | collective-permute-start | bytes 258056 | tf_op jit(solution)/shard_map/ppermute | solution.py:429
  53.5 7.9 %collective-permute-start.17 = (f32[8,2688]{1,0:T(8,128)S(1)}, f32[8,2688]{1,0:T(8,128)S(1)}, u32[]{:S(2)}, u32[]{:S(2)}) collective-permute-start(f32[8,2688]{1,0:T(8,128)S(1)} %get-tuple-element.60), channel_id=1, source_target_pairs={{0,248},{8,0},{16,8},{24,16},{32,24},{40,32},{48,40},{56,48},{64,5... | collective-permute-start | bytes 258056 | tf_op jit(solution)/shard_map/ppermute | solution.py:429
  55.5 5.9 %copy-start.7 = (f32[128,128]{1,0:T(8,128)S(1)}, f32[128,128]{1,0:T(8,128)}, u32[]{:S(2)}) copy-start(f32[128,128]{1,0:T(8,128)} %constant.26.clone.solve) | copy-start | bytes 196612

commit v3 on v2

--- a/solution.py
+++ b/solution.py
@@ -49,13 +49,12 @@
     from_left, take_left = low_rank(np.concatenate([at(first, -1), at(second, -1)]), RANK_V)
     from_right, take_right = low_rank(np.concatenate([at(first, 1), at(second, 1)]), RANK_V)
     own = np.concatenate([at(first, 0), at(second, 0)])
-    slopes = np.zeros((3, 2 * cells, cells + 2 * PAD_V))
+    slopes = np.zeros((3, 2 * cells, 2 * PAD_V))
     moments = np.zeros((2 * PAD_V, 3 * cells))
     for c in range(3):
         rows = slice(RANK_V * c, RANK_V * (c + 1))
-        slopes[c, :, :cells] = own
-        slopes[c, :, cells:][:, rows] = from_left
-        slopes[c, :, cells + PAD_V :][:, rows] = from_right
+        slopes[c, :, :PAD_V][:, rows] = from_left
+        slopes[c, :, PAD_V:][:, rows] = from_right
         moments[rows, cells * c : cells * (c + 1)] = take_left
         moments[PAD_V:][rows, cells * c : cells * (c + 1)] = take_right
     m_left, t_left = low_rank(at(first, -1), RANK_M)
@@ -125,7 +124,7 @@
                 solve_own[top : top + RANK_V, near * j : near * (j + 1)] = -mine
                 solve_sides[top : top + RANK_V, wide * j : wide * (j + 1)] = -sides
     return tuple(
-        x.astype(np.float32) for x in (slopes, moments, lateral, source, solve_own, solve_sides)
+        x.astype(np.float32) for x in (own, slopes, moments, lateral, source, solve_own, solve_sides)
     )
 
 
@@ -137,6 +136,7 @@
 PACKED = BREADTH + BREADTH // 2
 
 DIFFERENCE = ((1, 2.0 / 3.0), (-1, -2.0 / 3.0), (2, -1.0 / 12.0), (-2, 1.0 / 12.0))
+CURVE = ((1, 4.0 / 3.0), (-1, 4.0 / 3.0), (2, -1.0 / 12.0), (-2, -1.0 / 12.0))
 
 
 def lane(r, count=1):
@@ -178,62 +178,91 @@
     return first_diff(turned(tile, 1), turned(tile, -1), turned(tile, 2), turned(tile, -2))
 
 
-def open_kernel(cells, velocity, moments, flat, to_right, to_left, upward, downward, landed, weights, sems):
-    copies = [pltpu.make_async_copy(velocity.at[c], landed.at[c], sems.at[c]) for c in range(3)]
-    copies.append(pltpu.make_async_copy(moments, weights, sems.at[3]))
+def open_kernel(
+    cells, velocity, viscosity, moments, flat, thick, to_right, to_left, upward, downward, weights, sems
+):
+    copies = [pltpu.make_async_copy(moments, weights, sems.at[0])]
+    for c in range(3):
+        rows = slice(cells * c, cells * (c + 1))
+        for r in range(ROWS):
+            copies.append(
+                pltpu.make_async_copy(velocity.at[c, :, r, :], flat.at[rows, lane(r)], sems.at[len(copies)])
+            )
+    apart = len(copies)
+    for r in range(ROWS):
+        copies.append(pltpu.make_async_copy(viscosity.at[:, r, :], thick.at[:, lane(r)], sems.at[len(copies)]))
     for copy in copies:
         copy.start()
-    for c in range(3):
-        copies[c].wait()
-        rows = slice(cells * c, cells * (c + 1))
-        for r in range(ROWS):
-            flat[rows, lane(r)] = landed[c, :, r, :]
-        upward[rows, :] = flat[rows, lane(ROWS - 2, 2)]
-        downward[rows, :] = flat[rows, lane(0, 2)]
-    copies[3].wait()
+    for copy in copies[:apart]:
+        copy.wait()
+    upward[...] = flat[:, lane(ROWS - 2, 2)]
+    downward[...] = flat[:, lane(0, 2)]
     both = dot(weights[...], flat[...])
     to_right[...] = both[:PAD_V]
     to_left[...] = both[PAD_V:]
-
-
-def tendency_kernel(cells, second, *refs):
+    for copy in copies[apart:]:
+        copy.wait()
+
+
+def weighed(weights, value_at, r, home):
+    total = None
+    for reach, factor in weights:
+        if (0 <= r + reach < ROWS) == home:
+            part = factor * value_at(r + reach)
+            total = part if total is None else total + part
+    return total
+
+
+def rough_kernel(cells, second, *refs):
     if second:
         base, *refs = refs
-    flat, thick, left, right, low, high, slopes, lateral, section, parts, up_near, down_near, up_far, down_far = refs
+    flat, thick, own, rough = refs
+    for c in range(3):
+        rows = slice(cells * c, cells * (c + 1))
+        at = lambda r: flat[rows, lane(r)]
+        spanned = dot(own[...], flat[rows, :])
+        for r in range(ROWS):
+            here = at(r)
+            up_one, down_one = turned(here, 1), turned(here, -1)
+            up_two, down_two = turned(here, 2), turned(here, -2)
+            carried = (
+                flat[:cells, lane(r)] * first_diff(up_one, down_one, up_two, down_two)
+                + flat[cells : 2 * cells, lane(r)] * weighed(DIFFERENCE, at, r, True)
+                + flat[2 * cells :, lane(r)] * spanned[:cells, lane(r)]
+            )
+            spread = (
+                (4.0 / 3.0) * (up_one + down_one)
+                - (1.0 / 12.0) * (up_two + down_two)
+                - 5.0 * here
+                + weighed(CURVE, at, r, True)
+                + spanned[cells:, lane(r)]
+            )
+            moved = here + time_step * (thick[:, lane(r)] * spread - carried)
+            if second:
+                moved = 0.5 * base[rows, lane(r)] + 0.5 * moved
+            rough[rows, lane(r)] = moved
+
+
+def tendency_kernel(
+    cells, scale, rough, flat, thick, left, right, low, high, slopes, lateral,
+    section, parts, up_near, down_near, up_far, down_far,
+):
     masks = edge_masks()
-
-    def tile(c, r):
-        rows = slice(cells * c, cells * (c + 1))
-        if r < 0:
-            return masked(low[rows, lane(r + 2)], r, masks)
-        if r >= ROWS:
-            return masked(high[rows, lane(r - ROWS)], r, masks)
-        return flat[rows, lane(r)]
-
     sides = jnp.concatenate([left[...], right[...]], axis=0)
     for c in range(3):
         rows = slice(cells * c, cells * (c + 1))
-        spanned = dot(slopes[c], jnp.concatenate([flat[rows, :], sides], axis=0))
+        spanned = dot(slopes[c], sides)
+
+        def beyond(r):
+            if r < 0:
+                return masked(low[rows, lane(r + 2)], r, masks)
+            return masked(high[rows, lane(r - ROWS)], r, masks)
+
         for r in range(ROWS):
-            here = tile(c, r)
-            up_one, down_one = turned(here, 1), turned(here, -1)
-            up_two, down_two = turned(here, 2), turned(here, -2)
-            above_one, below_one = tile(c, r + 1), tile(c, r - 1)
-            above_two, below_two = tile(c, r + 2), tile(c, r - 2)
-            carried = (
-                tile(0, r) * first_diff(up_one, down_one, up_two, down_two)
-                + tile(1, r) * first_diff(above_one, below_one, above_two, below_two)
-                + tile(2, r) * spanned[:cells, lane(r)]
-            )
-            spread = (
-                second_diff(here, up_one, down_one, up_two, down_two)
-                + second_diff(here, above_one, below_one, above_two, below_two)
-                + spanned[cells:, lane(r)]
-            )
-            moved = here + time_step * (thick[:, r, :] * spread - carried)
-            if second:
-                moved = 0.5 * base[rows, lane(r)] + 0.5 * moved
-            section[rows, lane(r)] = moved
+            spread = spanned[cells:, lane(r)] + weighed(CURVE, beyond, r, False)
+            carried = flat[cells : 2 * cells, lane(r)] * weighed(DIFFERENCE, beyond, r, False)
+            carried = carried + flat[2 * cells :, lane(r)] * spanned[:cells, lane(r)]
+            section[rows, lane(r)] = rough[rows, lane(r)] + scale * (thick[:, lane(r)] * spread - carried)
     side = dot(lateral[...], section[2 * cells :, :])
     span = slice(0, cells)
     at = lambda r: section[cells : 2 * cells, lane(r)]
@@ -389,16 +418,17 @@
         for r in range(ROWS):
             value = section[rows, lane(r)] - slope(c, slice(0, cells), slice(cells, 2 * cells), r)
             if last:
-                staged[c, :, r, :] = value
+                staged[rows, lane(r)] = value
+                copies.append(
+                    pltpu.make_async_copy(staged.at[rows, lane(r)], out.at[c, :, r, :], sems.at[len(copies)])
+                )
+                copies[-1].start()
                 continue
             flat[rows, lane(r)] = value
             if r < 2:
                 downward[rows, lane(r)] = value
             if r >= ROWS - 2:
                 upward[rows, lane(r - ROWS + 2)] = value
-        if last:
-            copies.append(pltpu.make_async_copy(staged.at[c], out.at[c], sems.at[c]))
-            copies[c].start()
     for copy in copies:
         copy.wait()
     if not last:
@@ -432,22 +462,20 @@
 def per_device(velocity, viscosity):
     components, cells, row_cells, columns = velocity.shape
     length = cells * lax.axis_size("span")
-    slopes, moments, lateral, *first_tables = (jnp.asarray(t) for t in tables(length, cells, False))
-    last_tables = [jnp.asarray(t) for t in tables(length, cells, True)[3:]]
+    own, slopes, moments, lateral, *first_tables = (jnp.asarray(t) for t in tables(length, cells, False))
+    last_tables = [jnp.asarray(t) for t in tables(length, cells, True)[4:]]
     width = row_cells * columns
     wide = (row_cells + 2 * REACH) * columns
     near = cells + PAD_M
     edge, rim = (PAD_V, width), (components * cells, 2 * columns)
-    start, to_right, to_left, upward, downward = call(
+    start, thick, to_right, to_left, upward, downward = call(
         functools.partial(open_kernel, cells),
-        [(components * cells, width), edge, edge, rim, rim],
-        pltpu.with_memory_space_constraint(velocity, pltpu.HBM),
-        pltpu.with_memory_space_constraint(moments, pltpu.HBM),
-        in_specs=[pl.BlockSpec(memory_space=pltpu.HBM)] * 2,
+        [(components * cells, width), (cells, width), edge, edge, rim, rim],
+        *(pltpu.with_memory_space_constraint(x, pltpu.HBM) for x in (velocity, viscosity, moments)),
+        in_specs=[pl.BlockSpec(memory_space=pltpu.HBM)] * 3,
         scratch=[
-            pltpu.VMEM(velocity.shape, jnp.float32),
             pltpu.VMEM(moments.shape, jnp.float32),
-            pltpu.SemaphoreType.DMA((4,)),
+            pltpu.SemaphoreType.DMA((1 + 4 * ROWS,)),
         ],
     )
     left = shifted(to_right, "span", 1)
@@ -458,10 +486,13 @@
         high = shifted(downward, "cross", -1)
         base = (start,) if second else ()
         source, solve_own, solve_sides = last_tables if second else first_tables
+        (rough,) = call(
+            functools.partial(rough_kernel, cells, second), [(components * cells, width)], *base, flat, thick, own
+        )
         section, parts, up_near, down_near, up_far, down_far = call(
-            functools.partial(tendency_kernel, cells, second),
+            functools.partial(tendency_kernel, cells, 0.5 * time_step if second else time_step),
             [(components * cells, width), (near, width)] + [(7 * cells + 4 * PAD_M, columns)] * 2 + [(3 * cells + PAD_M, columns)] * 2,
-            *base, flat, viscosity, left, right, low, high, slopes, lateral,
+            rough, flat, thick, left, right, low, high, slopes, lateral,
         )
         low_one = shifted(up_near, "cross", 1)
         high_one = shifted(down_near, "cross", -1)
@@ -488,7 +519,7 @@
         if second:
             (out,) = call(
                 body, [velocity.shape], *given,
-                scratch=scratch + [pltpu.VMEM(velocity.shape, jnp.float32), pltpu.SemaphoreType.DMA((3,))],
+                scratch=scratch + [pltpu.VMEM((components * cells, width), jnp.float32), pltpu.SemaphoreType.DMA((3 * ROWS,))],
                 out_specs=[pl.BlockSpec(memory_space=pltpu.HBM)],
             )
         else:

time: 63.4 us -> 62.5 us (0.986)
  waiting for transfers between devices: 31.9 us -> 29.9 us
  Pallas kernels: 11.6 us -> 12.5 us
    ppermute x18, waiting for transfers between devices: 31.9 us -> 29.9 us  [shifted(): lax.ppermute(block, axis, [(i, (i + step) % count) for i in range(count)])]
    pallas_call x9 -> x11, Pallas kernels: 11.6 us -> 12.5 us  [call(): pl.pallas_call(body, out_shape=[jax.ShapeDtypeStruct(s, jnp.float32) for...]
  transfers between devices with their start and end apart: 18 -> 18, of which waited for: 11 -> 11; matrix products, arithmetic and copies ran while one was open for 0% -> 0% of each run, Pallas kernels for 5% -> 8%
where the time goes in v3:
time: 62.5 us; the launch traced here: 62.4 us
  waiting for transfers between devices  29.9 us (48%)
  starting transfers between devices  19.5 us (31%)
  Pallas kernels  12.5 us (20%)
    ppermute x18, waiting for transfers between devices, shifted(): lax.ppermute(block, axis, [(i, (i + step) % count) for i in range(count)])  29.9 us
    ppermute x18, starting transfers between devices, shifted(): lax.ppermute(block, axis, [(i, (i + step) % count) for i in range(count)])  19.5 us
    pallas_call x11, Pallas kernels, call(): pl.pallas_call(body, out_shape=[jax.ShapeDtypeStruct(s, jnp.float32) for...  12.5 us
  transfers between devices with their start and end apart: 18, of which 11 were waited for; matrix products, arithmetic and copies ran while one was open for 0% of the time, Pallas kernels for 8%

profile of v3, /device:TPU:126, one launch (start us, length us, event | category | flops | bytes accessed | tf_op | source)
XLA Modules:
  0.0 62.4 jit_solution(252131681356642032)
XLA Ops:
  0.0 0.0 copy-start.1
  0.0 1.5 %shard_map.118 = (f32[192,512]{1,0:T(8,128)S(1)}, f32[64,512]{1,0:T(8,128)S(1)}, f32[16,512]{1,0:T(8,128)S(1)}, f32[16,512]{1,0:T(8,128)S(1)}, f32[192,256]{1,0:T(8,128)S(1)}, /*index=5*/f32[192,256]{1,0:T(8,128)S(1)}) custom-call(f32[3,64,4,128]{3,2,1,0:T(4,128)} %velocity.1, f32[64,4,128]{2,1,0:T(4,128)} %viscosity.1, f32[32,192]{1,0:T(8,128)} %constant.22.clone.moments.refs_0_), custom_call_target="tpu_custom_call" | custom-call | tf_op jit(solution)/shard_map/pallas_call | solution.py:448
  1.5 0.0 collective-permute-start.2
  1.5 1.7 %collective-permute-start.3 = (f32[192,256]{1,0:T(8,128)S(1)}, f32[192,256]{1,0:T(8,128)S(1)}, u32[]{:S(2)}, u32[]{:S(2)}) collective-permute-start(f32[192,256]{1,0:T(8,128)S(1)} %get-tuple-element.39), channel_id=1, source_target_pairs={{0,7},{1,0},{2,1},{3,2},{4,3},{5,4},{6,5},{7,6},{8,15},{9,8},{10,9... | collective-permute-start | bytes 589832 | tf_op jit(solution)/shard_map/ppermute | solution.py:459
  3.3 3.0 %collective-permute-start = (f32[16,512]{1,0:T(8,128)S(1)}, f32[16,512]{1,0:T(8,128)S(1)}, u32[]{:S(2)}, u32[]{:S(2)}) collective-permute-start(f32[16,512]{1,0:T(8,128)S(1)} %get-tuple-element.36), channel_id=1, source_target_pairs={{0,8},{8,16},{16,24},{24,32},{32,40},{40,48},{48,56},{56,64},{64,7... | collective-permute-start | bytes 98312 | tf_op jit(solution)/shard_map/ppermute | solution.py:459
  6.3 0.0 collective-permute-start.1
  6.3 0.0 copy-done.1
  6.3 0.0 copy-start
  6.3 0.0 copy-start.4
  6.3 0.9 %shard_map.119.rough = f32[192,512]{1,0:T(8,128)S(1)} custom-call(f32[192,512]{1,0:T(8,128)S(1)} %get-tuple-element.34.refs_0_.flat, f32[64,512]{1,0:T(8,128)S(1)} %get-tuple-element.35.refs_1_.thick.refs_2_, f32[128,64]{1,0:T(8,128)S(1)} %copy-done.1), custom_call_target="tpu_custom_call" | custom-call | tf_op jit(solution)/shard_map/pallas_call | solution.py:448
  7.3 0.6 %collective-permute-done.left = f32[16,512]{1,0:T(8,128)S(1)} collective-permute-done((f32[16,512]{1,0:T(8,128)S(1)}, f32[16,512]{1,0:T(8,128)S(1)}, u32[]{:S(2)}, u32[]{:S(2)}) %collective-permute-start) | collective-permute-done | bytes 32800 | tf_op jit(solution)/shard_map/ppermute | solution.py:459
  7.9 5.6 %collective-permute-done.1.right = f32[16,512]{1,0:T(8,128)S(1)} collective-permute-done((f32[16,512]{1,0:T(8,128)S(1)}, f32[16,512]{1,0:T(8,128)S(1)}, u32[]{:S(2)}, u32[]{:S(2)}) %collective-permute-start.1) | collective-permute-done | bytes 32800 | tf_op jit(solution)/shard_map/ppermute | solution.py:459
  13.6 0.0 collective-permute-done.2.low
  13.6 0.0 collective-permute-done.3.high
  13.6 0.0 copy-done
  13.6 0.0 copy-done.4
  13.6 0.0 copy-start.5
  13.6 0.0 copy-start.9
  13.6 1.1 %shard_map.120 = (f32[192,512]{1,0:T(8,128)S(1)}, f32[72,512]{1,0:T(8,128)S(1)}, f32[480,128]{1,0:T(8,128)S(1)}, f32[480,128]{1,0:T(8,128)S(1)}, f32[200,128]{1,0:T(8,128)S(1)}, /*index=5*/f32[200,128]{1,0:T(8,128)S(1)}) custom-call(f32[192,512]{1,0:T(8,128)S(1)} %shard_map.119.rough, f32[192,512]{1,0:T(8,128)S(1)} %get-tuple-element.34.refs_0_.flat, ...), custom_call_target="tpu_custom_call" | custom-call | tf_op jit(solution)/shard_map/pallas_call | solution.py:448
  14.7 0.0 collective-permute-start.4
  14.8 1.7 %collective-permute-start.5 = (f32[480,128]{1,0:T(8,128)S(1)}, f32[480,128]{1,0:T(8,128)S(1)}, u32[]{:S(2)}, u32[]{:S(2)}) collective-permute-start(f32[480,128]{1,0:T(8,128)S(1)} %get-tuple-element.43), channel_id=1, source_target_pairs={{0,7},{1,0},{2,1},{3,2},{4,3},{5,4},{6,5},{7,6},{8,15},{9,8},{10,9... | collective-permute-start | bytes 737288 | tf_op jit(solution)/shard_map/ppermute | solution.py:459
  16.5 2.6 %collective-permute-start.6 = (f32[200,128]{1,0:T(8,128)S(1)}, f32[200,128]{1,0:T(8,128)S(1)}, u32[]{:S(2)}, u32[]{:S(2)}) collective-permute-start(f32[200,128]{1,0:T(8,128)S(1)} %get-tuple-element.44), channel_id=1, source_target_pairs={{0,2},{1,3},{2,4},{3,5},{4,6},{5,7},{6,0},{7,1},{8,10},{9,11},{10,... | collective-permute-start | bytes 307208 | tf_op jit(solution)/shard_map/ppermute | solution.py:459
  19.1 0.0 collective-permute-start.7
  19.1 3.2 %collective-permute-done.6.low_two = f32[200,128]{1,0:T(8,128)S(1)} collective-permute-done((f32[200,128]{1,0:T(8,128)S(1)}, f32[200,128]{1,0:T(8,128)S(1)}, u32[]{:S(2)}, u32[]{:S(2)}) %collective-permute-start.6) | collective-permute-done | bytes 102432 | tf_op jit(solution)/shard_map/ppermute | solution.py:459
  22.3 2.7 %collective-permute-done.7.high_two = f32[200,128]{1,0:T(8,128)S(1)} collective-permute-done((f32[200,128]{1,0:T(8,128)S(1)}, f32[200,128]{1,0:T(8,128)S(1)}, u32[]{:S(2)}, u32[]{:S(2)}) %collective-permute-start.7) | collective-permute-done | bytes 102432 | tf_op jit(solution)/shard_map/ppermute | solution.py:459
  25.1 0.0 collective-permute-done.4.low_one
  25.1 0.0 collective-permute-done.5.high_one
  25.1 0.0 copy-done.5
  25.1 0.0 copy-done.9
  25.1 0.0 copy-start.2
  25.1 0.7 %shard_map.121 = (f32[72,1792]{1,0:T(8,128)S(1)}, f32[8,3584]{1,0:T(8,128)S(1)}, f32[8,3584]{1,0:T(8,128)S(1)}) custom-call(f32[72,512]{1,0:T(8,128)S(1)} %get-tuple-element.40.parts, f32[192,512]{1,0:T(8,128)S(1)} %get-tuple-element.41.section, f32[480,128]{1,0:T(8,128)S(1)} %collective-permute-done.4.low_one, ...), custom_call_target="tpu_custom_call" | custom-call | tf_op jit(solution)/shard_map/pallas_call | solution.py:448
  25.8 0.1 collective-permute-start.8
  25.9 2.0 %collective-permute-start.9 = (f32[8,3584]{1,0:T(8,128)S(1)}, f32[8,3584]{1,0:T(8,128)S(1)}, u32[]{:S(2)}, u32[]{:S(2)}) collective-permute-start(f32[8,3584]{1,0:T(8,128)S(1)} %get-tuple-element.48), channel_id=1, source_target_pairs={{0,248},{8,0},{16,8},{24,16},{32,24},{40,32},{48,40},{56,48},{64,5... | collective-permute-start | bytes 344072 | tf_op jit(solution)/shard_map/ppermute | solution.py:459
  27.9 0.0 copy-done.2
  27.9 1.6 %shard_map.122.partial = f32[160,1024]{1,0:T(8,128)S(1)} custom-call(f32[72,1792]{1,0:T(8,128)S(1)} %get-tuple-element.46.ext, f32[160,288]{1,0:T(8,128)S(1)} %copy-done.2), custom_call_target="tpu_custom_call" | custom-call | tf_op jit(solution)/shard_map/pallas_call | solution.py:448
  29.5 1.2 %collective-permute-done.8.left = f32[8,3584]{1,0:T(8,128)S(1)} collective-permute-done((f32[8,3584]{1,0:T(8,128)S(1)}, f32[8,3584]{1,0:T(8,128)S(1)}, u32[]{:S(2)}, u32[]{:S(2)}) %collective-permute-start.8) | collective-permute-done | bytes 114720 | tf_op jit(solution)/shard_map/ppermute | solution.py:459
  30.7 3.4 %collective-permute-done.9.right = f32[8,3584]{1,0:T(8,128)S(1)} collective-permute-done((f32[8,3584]{1,0:T(8,128)S(1)}, f32[8,3584]{1,0:T(8,128)S(1)}, u32[]{:S(2)}, u32[]{:S(2)}) %collective-permute-start.9) | collective-permute-done | bytes 114720 | tf_op jit(solution)/shard_map/ppermute | solution.py:459
  34.1 0.0 copy-done.6
  34.1 1.0 %shard_map.123 = (f32[192,512]{1,0:T(8,128)S(1)}, f32[16,512]{1,0:T(8,128)S(1)}, f32[16,512]{1,0:T(8,128)S(1)}, f32[192,256]{1,0:T(8,128)S(1)}, f32[192,256]{1,0:T(8,128)S(1)}) custom-call(f32[160,1024]{1,0:T(8,128)S(1)} %shard_map.122.partial, f32[8,3584]{1,0:T(8,128)S(1)} %collective-permute-done.8.left, f32[8,3584]{1,0:T(8,128)S(1)} %collective-permute-done.9.right, ...), custom_call_target="tpu_custom_call" | custom-call | tf_op jit(solution)/shard_map/pallas_call | solution.py:448
  35.1 0.0 collective-permute-start.10
  35.1 1.7 %collective-permute-start.11 = (f32[192,256]{1,0:T(8,128)S(1)}, f32[192,256]{1,0:T(8,128)S(1)}, u32[]{:S(2)}, u32[]{:S(2)}) collective-permute-start(f32[192,256]{1,0:T(8,128)S(1)} %get-tuple-element.53), channel_id=1, source_target_pairs={{0,7},{1,0},{2,1},{3,2},{4,3},{5,4},{6,5},{7,6},{8,15},{9,8},{10,9... | collective-permute-start | bytes 589832 | tf_op jit(solution)/shard_map/ppermute | solution.py:459
  36.9 1.0 %shard_map.124.rough = f32[192,512]{1,0:T(8,128)S(1)} custom-call(f32[192,512]{1,0:T(8,128)S(1)} %get-tuple-element.34.refs_0_.flat, f32[192,512]{1,0:T(8,128)S(1)} %get-tuple-element.49.refs_1_.flat, f32[64,512]{1,0:T(8,128)S(1)} %get-tuple-element.35.refs_1_.thick.refs_2_, f32[128,64]{1,0:T(8,128)S(1)} %copy-done.1), custom_call_target="tpu_custom_call" | custom-call | tf_op jit(solution)/shard_map/pallas_call | solution.py:448
  37.9 2.4 %collective-permute-done.10.low = f32[192,256]{1,0:T(8,128)S(1)} collective-permute-done((f32[192,256]{1,0:T(8,128)S(1)}, f32[192,256]{1,0:T(8,128)S(1)}, u32[]{:S(2)}, u32[]{:S(2)}) %collective-permute-start.10) | collective-permute-done | bytes 196640 | tf_op jit(solution)/shard_map/ppermute | solution.py:459
  40.2 0.0 collective-permute-done.11.high
  40.2 1.1 %shard_map.125 = (f32[192,512]{1,0:T(8,128)S(1)}, f32[72,512]{1,0:T(8,128)S(1)}, f32[480,128]{1,0:T(8,128)S(1)}, f32[480,128]{1,0:T(8,128)S(1)}, f32[200,128]{1,0:T(8,128)S(1)}, /*index=5*/f32[200,128]{1,0:T(8,128)S(1)}) custom-call(f32[192,512]{1,0:T(8,128)S(1)} %shard_map.124.rough, f32[192,512]{1,0:T(8,128)S(1)} %get-tuple-element.49.refs_1_.flat, ...), custom_call_target="tpu_custom_call" | custom-call | tf_op jit(solution)/shard_map/pallas_call | solution.py:448
  41.4 1.5 %collective-permute-start.12 = (f32[480,128]{1,0:T(8,128)S(1)}, f32[480,128]{1,0:T(8,128)S(1)}, u32[]{:S(2)}, u32[]{:S(2)}) collective-permute-start(f32[480,128]{1,0:T(8,128)S(1)} %get-tuple-element.56), channel_id=1, source_target_pairs={{0,1},{1,2},{2,3},{3,4},{4,5},{5,6},{6,7},{7,0},{8,9},{9,10},{10,1... | collective-permute-start | bytes 737288 | tf_op jit(solution)/shard_map/ppermute | solution.py:459
  42.8 0.3 collective-permute-start.13
  43.1 2.6 %collective-permute-start.14 = (f32[200,128]{1,0:T(8,128)S(1)}, f32[200,128]{1,0:T(8,128)S(1)}, u32[]{:S(2)}, u32[]{:S(2)}) collective-permute-start(f32[200,128]{1,0:T(8,128)S(1)} %get-tuple-element.58), channel_id=1, source_target_pairs={{0,2},{1,3},{2,4},{3,5},{4,6},{5,7},{6,0},{7,1},{8,10},{9,11},{10,... | collective-permute-start | bytes 307208 | tf_op jit(solution)/shard_map/ppermute | solution.py:459
  45.7 0.0 collective-permute-start.15
  45.7 3.2 %collective-permute-done.14.low_two = f32[200,128]{1,0:T(8,128)S(1)} collective-permute-done((f32[200,128]{1,0:T(8,128)S(1)}, f32[200,128]{1,0:T(8,128)S(1)}, u32[]{:S(2)}, u32[]{:S(2)}) %collective-permute-start.14) | collective-permute-done | bytes 102432 | tf_op jit(solution)/shard_map/ppermute | solution.py:459
  49.0 3.0 %collective-permute-done.15.high_two = f32[200,128]{1,0:T(8,128)S(1)} collective-permute-done((f32[200,128]{1,0:T(8,128)S(1)}, f32[200,128]{1,0:T(8,128)S(1)}, u32[]{:S(2)}, u32[]{:S(2)}) %collective-permute-start.15) | collective-permute-done | bytes 102432 | tf_op jit(solution)/shard_map/ppermute | solution.py:459
  52.0 0.0 collective-permute-done.12.low_one
  52.0 0.0 collective-permute-done.13.high_one
  52.0 0.0 copy-done.8
  52.0 0.0 copy-start.3
  52.0 0.5 shard_map.126
  52.6 0.1 collective-permute-start.16
  52.6 2.0 %collective-permute-start.17 = (f32[8,2688]{1,0:T(8,128)S(1)}, f32[8,2688]{1,0:T(8,128)S(1)}, u32[]{:S(2)}, u32[]{:S(2)}) collective-permute-start(f32[8,2688]{1,0:T(8,128)S(1)} %get-tuple-element.62), channel_id=1, source_target_pairs={{0,248},{8,0},{16,8},{24,16},{32,24},{40,32},{48,40},{56,48},{64,5... | collective-permute-start | bytes 258056 | tf_op jit(solution)/shard_map/ppermute | solution.py:459
  54.7 0.0 copy-done.3
  54.7 1.4 %shard_map.127.partial = f32[128,1024]{1,0:T(8,128)S(1)} custom-call(f32[72,1792]{1,0:T(8,128)S(1)} %get-tuple-element.60.ext, f32[128,288]{1,0:T(8,128)S(1)} %copy-done.3), custom_call_target="tpu_custom_call" | custom-call | tf_op jit(solution)/shard_map/pallas_call | solution.py:448
  56.0 1.1 %collective-permute-done.16.left = f32[8,2688]{1,0:T(8,128)S(1)} collective-permute-done((f32[8,2688]{1,0:T(8,128)S(1)}, f32[8,2688]{1,0:T(8,128)S(1)}, u32[]{:S(2)}, u32[]{:S(2)}) %collective-permute-start.16) | collective-permute-done | bytes 86048 | tf_op jit(solution)/shard_map/ppermute | solution.py:459
  57.1 3.4 %collective-permute-done.17.right = f32[8,2688]{1,0:T(8,128)S(1)} collective-permute-done((f32[8,2688]{1,0:T(8,128)S(1)}, f32[8,2688]{1,0:T(8,128)S(1)}, u32[]{:S(2)}, u32[]{:S(2)}) %collective-permute-start.17) | collective-permute-done | bytes 86048 | tf_op jit(solution)/shard_map/ppermute | solution.py:459
  60.5 0.0 copy-done.7
  60.5 1.7 %shard_map.128 = f32[3,64,4,128]{3,2,1,0:T(4,128)} custom-call(f32[128,1024]{1,0:T(8,128)S(1)} %shard_map.127.partial, f32[8,2688]{1,0:T(8,128)S(1)} %collective-permute-done.16.left, f32[8,2688]{1,0:T(8,128)S(1)} %collective-permute-done.17.right, f32[192,512]{1,0:T(8,128)S(1)} %get-tuple-element.55.section, f32[128,128]{1,0:T(8,128)S(1)} %copy-done.7), custom_call_target="tpu_custom_call" | custom-call | tf_op jit(solution)/shard_map/pallas_call | solution.py:448
  (3 shorter events, 0.0 us)
Async XLA Ops:
  0.0 6.3 %copy-start.1 = (f32[128,64]{1,0:T(8,128)S(1)}, f32[128,64]{1,0:T(8,128)}, u32[]{:S(2)}) copy-start(f32[128,64]{1,0:T(8,128)} %constant.20.clone.refs_2_.refs_3_) | copy-start | bytes 98308
  1.5 12.0 %collective-permute-start.2 = (f32[192,256]{1,0:T(8,128)S(1)}, f32[192,256]{1,0:T(8,128)S(1)}, u32[]{:S(2)}, u32[]{:S(2)}) collective-permute-start(f32[192,256]{1,0:T(8,128)S(1)} %get-tuple-element.38), channel_id=1, source_target_pairs={{0,1},{1,2},{2,3},{3,4},{4,5},{5,6},{6,7},{7,0},{8,9},{9,10},{10,1... | collective-permute-start | bytes 589832 | tf_op jit(solution)/shard_map/ppermute | solution.py:459
  1.5 12.0 %collective-permute-start.3 = (f32[192,256]{1,0:T(8,128)S(1)}, f32[192,256]{1,0:T(8,128)S(1)}, u32[]{:S(2)}, u32[]{:S(2)}) collective-permute-start(f32[192,256]{1,0:T(8,128)S(1)} %get-tuple-element.39), channel_id=1, source_target_pairs={{0,7},{1,0},{2,1},{3,2},{4,3},{5,4},{6,5},{7,6},{8,15},{9,8},{10,9... | collective-permute-start | bytes 589832 | tf_op jit(solution)/shard_map/ppermute | solution.py:459
  3.3 4.6 %collective-permute-start = (f32[16,512]{1,0:T(8,128)S(1)}, f32[16,512]{1,0:T(8,128)S(1)}, u32[]{:S(2)}, u32[]{:S(2)}) collective-permute-start(f32[16,512]{1,0:T(8,128)S(1)} %get-tuple-element.36), channel_id=1, source_target_pairs={{0,8},{8,16},{16,24},{24,32},{32,40},{40,48},{48,56},{56,64},{64,7... | collective-permute-start | bytes 98312 | tf_op jit(solution)/shard_map/ppermute | solution.py:459
  6.3 7.2 %collective-permute-start.1 = (f32[16,512]{1,0:T(8,128)S(1)}, f32[16,512]{1,0:T(8,128)S(1)}, u32[]{:S(2)}, u32[]{:S(2)}) collective-permute-start(f32[16,512]{1,0:T(8,128)S(1)} %get-tuple-element.37), channel_id=1, source_target_pairs={{0,248},{8,0},{16,8},{24,16},{32,24},{40,32},{48,40},{56,48},{64,5... | collective-permute-start | bytes 98312 | tf_op jit(solution)/shard_map/ppermute | solution.py:459
  6.3 7.2 %copy-start = (f32[3,128,32]{2,1,0:T(8,128)S(1)}, f32[3,128,32]{2,1,0:T(8,128)}, u32[]{:S(2)}) copy-start(f32[3,128,32]{2,1,0:T(8,128)} %constant.21.clone.slopes) | copy-start | bytes 147460
  6.3 7.2 %copy-start.4 = (f32[72,64]{1,0:T(8,128)S(1)}, f32[72,64]{1,0:T(8,128)}, u32[]{:S(2)}) copy-start(f32[72,64]{1,0:T(8,128)} %constant.23.clone.lateral) | copy-start | bytes 55300
  13.6 11.5 %copy-start.5 = (f32[32,192]{1,0:T(8,128)S(1)}, f32[32,192]{1,0:T(8,128)}, u32[]{:S(2)}) copy-start(f32[32,192]{1,0:T(8,128)} %constant.22.clone.moments.refs_0_) | copy-start | bytes 73732
  13.6 11.5 %copy-start.9 = (f32[64,72]{1,0:T(8,128)S(1)}, f32[64,72]{1,0:T(8,128)}, u32[]{:S(2)}) copy-start(f32[64,72]{1,0:T(8,128)} %constant.24.clone.source) | copy-start | bytes 55300
  14.7 10.3 %collective-permute-start.4 = (f32[480,128]{1,0:T(8,128)S(1)}, f32[480,128]{1,0:T(8,128)S(1)}, u32[]{:S(2)}, u32[]{:S(2)}) collective-permute-start(f32[480,128]{1,0:T(8,128)S(1)} %get-tuple-element.42), channel_id=1, source_target_pairs={{0,1},{1,2},{2,3},{3,4},{4,5},{5,6},{6,7},{7,0},{8,9},{9,10},{10,1... | collective-permute-start | bytes 737288 | tf_op jit(solution)/shard_map/ppermute | solution.py:459
  14.8 10.3 %collective-permute-start.5 = (f32[480,128]{1,0:T(8,128)S(1)}, f32[480,128]{1,0:T(8,128)S(1)}, u32[]{:S(2)}, u32[]{:S(2)}) collective-permute-start(f32[480,128]{1,0:T(8,128)S(1)} %get-tuple-element.43), channel_id=1, source_target_pairs={{0,7},{1,0},{2,1},{3,2},{4,3},{5,4},{6,5},{7,6},{8,15},{9,8},{10,9... | collective-permute-start | bytes 737288 | tf_op jit(solution)/shard_map/ppermute | solution.py:459
  16.5 5.8 %collective-permute-start.6 = (f32[200,128]{1,0:T(8,128)S(1)}, f32[200,128]{1,0:T(8,128)S(1)}, u32[]{:S(2)}, u32[]{:S(2)}) collective-permute-start(f32[200,128]{1,0:T(8,128)S(1)} %get-tuple-element.44), channel_id=1, source_target_pairs={{0,2},{1,3},{2,4},{3,5},{4,6},{5,7},{6,0},{7,1},{8,10},{9,11},{10,... | collective-permute-start | bytes 307208 | tf_op jit(solution)/shard_map/ppermute | solution.py:459
  19.1 5.9 %collective-permute-start.7 = (f32[200,128]{1,0:T(8,128)S(1)}, f32[200,128]{1,0:T(8,128)S(1)}, u32[]{:S(2)}, u32[]{:S(2)}) collective-permute-start(f32[200,128]{1,0:T(8,128)S(1)} %get-tuple-element.45), channel_id=1, source_target_pairs={{0,6},{1,7},{2,0},{3,1},{4,2},{5,3},{6,4},{7,5},{8,14},{9,15},{10,... | collective-permute-start | bytes 307208 | tf_op jit(solution)/shard_map/ppermute | solution.py:459
  25.1 2.8 %copy-start.2 = (f32[160,288]{1,0:T(8,128)S(1)}, f32[160,288]{1,0:T(8,128)}, u32[]{:S(2)}) copy-start(f32[160,288]{1,0:T(8,128)} %constant.25.clone.solve) | copy-start | bytes 552964
  25.8 4.9 %collective-permute-start.8 = (f32[8,3584]{1,0:T(8,128)S(1)}, f32[8,3584]{1,0:T(8,128)S(1)}, u32[]{:S(2)}, u32[]{:S(2)}) collective-permute-start(f32[8,3584]{1,0:T(8,128)S(1)} %get-tuple-element.47), channel_id=1, source_target_pairs={{0,8},{8,16},{16,24},{24,32},{32,40},{40,48},{48,56},{56,64},{64,7... | collective-permute-start | bytes 344072 | tf_op jit(solution)/shard_map/ppermute | solution.py:459
  25.9 8.2 %collective-permute-start.9 = (f32[8,3584]{1,0:T(8,128)S(1)}, f32[8,3584]{1,0:T(8,128)S(1)}, u32[]{:S(2)}, u32[]{:S(2)}) collective-permute-start(f32[8,3584]{1,0:T(8,128)S(1)} %get-tuple-element.48), channel_id=1, source_target_pairs={{0,248},{8,0},{16,8},{24,16},{32,24},{40,32},{48,40},{56,48},{64,5... | collective-permute-start | bytes 344072 | tf_op jit(solution)/shard_map/ppermute | solution.py:459
  27.9 6.2 %copy-start.6 = (f32[160,128]{1,0:T(8,128)S(1)}, f32[160,128]{1,0:T(8,128)}, u32[]{:S(2)}) copy-start(f32[160,128]{1,0:T(8,128)} %constant.26.clone.solve) | copy-start | bytes 245764
  35.1 5.1 %collective-permute-start.10 = (f32[192,256]{1,0:T(8,128)S(1)}, f32[192,256]{1,0:T(8,128)S(1)}, u32[]{:S(2)}, u32[]{:S(2)}) collective-permute-start(f32[192,256]{1,0:T(8,128)S(1)} %get-tuple-element.52), channel_id=1, source_target_pairs={{0,1},{1,2},{2,3},{3,4},{4,5},{5,6},{6,7},{7,0},{8,9},{9,10},{10,1... | collective-permute-start | bytes 589832 | tf_op jit(solution)/shard_map/ppermute | solution.py:459
  35.1 5.1 %collective-permute-start.11 = (f32[192,256]{1,0:T(8,128)S(1)}, f32[192,256]{1,0:T(8,128)S(1)}, u32[]{:S(2)}, u32[]{:S(2)}) collective-permute-start(f32[192,256]{1,0:T(8,128)S(1)} %get-tuple-element.53), channel_id=1, source_target_pairs={{0,7},{1,0},{2,1},{3,2},{4,3},{5,4},{6,5},{7,6},{8,15},{9,8},{10,9... | collective-permute-start | bytes 589832 | tf_op jit(solution)/shard_map/ppermute | solution.py:459
  40.2 11.8 %copy-start.8 = (f32[64,72]{1,0:T(8,128)S(1)}, f32[64,72]{1,0:T(8,128)}, u32[]{:S(2)}) copy-start(f32[64,72]{1,0:T(8,128)} %constant.27.clone.source) | copy-start | bytes 55300
  41.4 10.6 %collective-permute-start.12 = (f32[480,128]{1,0:T(8,128)S(1)}, f32[480,128]{1,0:T(8,128)S(1)}, u32[]{:S(2)}, u32[]{:S(2)}) collective-permute-start(f32[480,128]{1,0:T(8,128)S(1)} %get-tuple-element.56), channel_id=1, source_target_pairs={{0,1},{1,2},{2,3},{3,4},{4,5},{5,6},{6,7},{7,0},{8,9},{9,10},{10,1... | collective-permute-start | bytes 737288 | tf_op jit(solution)/shard_map/ppermute | solution.py:459
  42.8 9.2 %collective-permute-start.13 = (f32[480,128]{1,0:T(8,128)S(1)}, f32[480,128]{1,0:T(8,128)S(1)}, u32[]{:S(2)}, u32[]{:S(2)}) collective-permute-start(f32[480,128]{1,0:T(8,128)S(1)} %get-tuple-element.57), channel_id=1, source_target_pairs={{0,7},{1,0},{2,1},{3,2},{4,3},{5,4},{6,5},{7,6},{8,15},{9,8},{10,9... | collective-permute-start | bytes 737288 | tf_op jit(solution)/shard_map/ppermute | solution.py:459
  43.1 5.8 %collective-permute-start.14 = (f32[200,128]{1,0:T(8,128)S(1)}, f32[200,128]{1,0:T(8,128)S(1)}, u32[]{:S(2)}, u32[]{:S(2)}) collective-permute-start(f32[200,128]{1,0:T(8,128)S(1)} %get-tuple-element.58), channel_id=1, source_target_pairs={{0,2},{1,3},{2,4},{3,5},{4,6},{5,7},{6,0},{7,1},{8,10},{9,11},{10,... | collective-permute-start | bytes 307208 | tf_op jit(solution)/shard_map/ppermute | solution.py:459
  45.7 6.3 %collective-permute-start.15 = (f32[200,128]{1,0:T(8,128)S(1)}, f32[200,128]{1,0:T(8,128)S(1)}, u32[]{:S(2)}, u32[]{:S(2)}) collective-permute-start(f32[200,128]{1,0:T(8,128)S(1)} %get-tuple-element.59), channel_id=1, source_target_pairs={{0,6},{1,7},{2,0},{3,1},{4,2},{5,3},{6,4},{7,5},{8,14},{9,15},{10,... | collective-permute-start | bytes 307208 | tf_op jit(solution)/shard_map/ppermute | solution.py:459
  52.0 2.7 %copy-start.3 = (f32[128,288]{1,0:T(8,128)S(1)}, f32[128,288]{1,0:T(8,128)}, u32[]{:S(2)}) copy-start(f32[128,288]{1,0:T(8,128)} %constant.28.clone.solve) | copy-start | bytes 442372
  52.6 4.6 %collective-permute-start.16 = (f32[8,2688]{1,0:T(8,128)S(1)}, f32[8,2688]{1,0:T(8,128)S(1)}, u32[]{:S(2)}, u32[]{:S(2)}) collective-permute-start(f32[8,2688]{1,0:T(8,128)S(1)} %get-tuple-element.61), channel_id=1, source_target_pairs={{0,8},{8,16},{16,24},{24,32},{32,40},{40,48},{48,56},{56,64},{64,7... | collective-permute-start | bytes 258056 | tf_op jit(solution)/shard_map/ppermute | solution.py:459
  52.6 7.9 %collective-permute-start.17 = (f32[8,2688]{1,0:T(8,128)S(1)}, f32[8,2688]{1,0:T(8,128)S(1)}, u32[]{:S(2)}, u32[]{:S(2)}) collective-permute-start(f32[8,2688]{1,0:T(8,128)S(1)} %get-tuple-element.62), channel_id=1, source_target_pairs={{0,248},{8,0},{16,8},{24,16},{32,24},{40,32},{48,40},{56,48},{64,5... | collective-permute-start | bytes 258056 | tf_op jit(solution)/shard_map/ppermute | solution.py:459
  54.7 5.9 %copy-start.7 = (f32[128,128]{1,0:T(8,128)S(1)}, f32[128,128]{1,0:T(8,128)}, u32[]{:S(2)}) copy-start(f32[128,128]{1,0:T(8,128)} %constant.29.clone.solve) | copy-start | bytes 196612

commit v4 on v3

--- a/solution.py
+++ b/solution.py
@@ -2,6 +2,7 @@
 
 import jax
 import jax.numpy as jnp
+import ml_dtypes
 import numpy as np
 from jax import lax
 from jax.experimental import pallas as pl
@@ -18,6 +19,7 @@
 PAD_S = 16
 PAD_M = 8
 GROUP = 8
+PACK = 16
 RANK_V = 3
 RANK_M = 2
 
@@ -123,13 +125,33 @@
                 top = 2 * cells + GROUP * (2 * side + half)
                 solve_own[top : top + RANK_V, near * j : near * (j + 1)] = -mine
                 solve_sides[top : top + RANK_V, wide * j : wide * (j + 1)] = -sides
-    return tuple(
-        x.astype(np.float32) for x in (own, slopes, moments, lateral, source, solve_own, solve_sides)
-    )
+    plain, split = (own, solve_own), (slopes, moments, lateral, source, solve_sides)
+    return [x.astype(np.float32) for x in plain] + [split_table(x.astype(np.float32)) for x in split]
 
 
 def dot(a, b):
     return jnp.dot(a, b, precision=highest, preferred_element_type=jnp.float32)
+
+
+def halves(x):
+    high = x.astype(jnp.bfloat16)
+    return high, (x - high.astype(jnp.float32)).astype(jnp.bfloat16)
+
+
+def split_table(table):
+    gap = -table.shape[-1] % PACK
+    table = np.pad(table, [(0, 0)] * (table.ndim - 1) + [(0, gap)])
+    high = table.astype(ml_dtypes.bfloat16)
+    low = (table - high.astype(np.float32)).astype(ml_dtypes.bfloat16)
+    return np.concatenate([high, high, low], axis=-1)
+
+
+def split_dot(table, x):
+    gap = -x.shape[0] % PACK
+    if gap:
+        x = jnp.concatenate([x, jnp.zeros((gap, x.shape[1]), x.dtype)], axis=0)
+    high, low = halves(x)
+    return jnp.dot(table, jnp.concatenate([high, low, high], axis=0), preferred_element_type=jnp.float32)
 
 
 BREADTH = ROWS + 2 * REACH
@@ -197,7 +219,7 @@
         copy.wait()
     upward[...] = flat[:, lane(ROWS - 2, 2)]
     downward[...] = flat[:, lane(0, 2)]
-    both = dot(weights[...], flat[...])
+    both = split_dot(weights[...], flat[...])
     to_right[...] = both[:PAD_V]
     to_left[...] = both[PAD_V:]
     for copy in copies[apart:]:
@@ -251,7 +273,7 @@
     sides = jnp.concatenate([left[...], right[...]], axis=0)
     for c in range(3):
         rows = slice(cells * c, cells * (c + 1))
-        spanned = dot(slopes[c], sides)
+        spanned = split_dot(slopes[c], sides)
 
         def beyond(r):
             if r < 0:
@@ -263,7 +285,7 @@
             carried = flat[cells : 2 * cells, lane(r)] * weighed(DIFFERENCE, beyond, r, False)
             carried = carried + flat[2 * cells :, lane(r)] * spanned[:cells, lane(r)]
             section[rows, lane(r)] = rough[rows, lane(r)] + scale * (thick[:, lane(r)] * spread - carried)
-    side = dot(lateral[...], section[2 * cells :, :])
+    side = split_dot(lateral[...], section[2 * cells :, :])
     span = slice(0, cells)
     at = lambda r: section[cells : 2 * cells, lane(r)]
     for r in range(ROWS):
@@ -337,9 +359,9 @@
                 total = total + factor * other
         ext[span, lane(e + REACH)] = masked(total, e, masks)
         ext[tail, lane(e + REACH)] = masked(side, e, masks)
-    both = dot(source[...], ext[...])
+    both = split_dot(source[...], ext[...])
     if keep:
-        held = dot(moments[...], section[...])
+        held = split_dot(moments[...], section[...])
     for side, out in enumerate((to_right, to_left)):
         top = 4 * GROUP * side
         out[:, lane(0, BREADTH)] = both[top : top + 8]
@@ -402,7 +424,7 @@
             levels[top + 8 : top + 16, lane(e)] = pltpu.roll(tile, 4, 0) if e % 2 else tile
             if not last:
                 levels[top + 12 : top + 13, lane(e)] = spare(given, e)
-    found = partial[...] + dot(solve[...], climb(levels, 2 * PAD_S, masks))
+    found = partial[...] + split_dot(solve[...], climb(levels, 2 * PAD_S, masks))
 
     def slope(c, rows, slope_rows, r):
         phi = lambda r: masked(found[rows, lane(r + 2)], r, masks)
@@ -462,8 +484,8 @@
 def per_device(velocity, viscosity):
     components, cells, row_cells, columns = velocity.shape
     length = cells * lax.axis_size("span")
-    own, slopes, moments, lateral, *first_tables = (jnp.asarray(t) for t in tables(length, cells, False))
-    last_tables = [jnp.asarray(t) for t in tables(length, cells, True)[4:]]
+    own, first_own, slopes, moments, lateral, *first = (jnp.asarray(t) for t in tables(length, cells, False))
+    _, last_own, _, _, _, *last = (jnp.asarray(t) for t in tables(length, cells, True))
     width = row_cells * columns
     wide = (row_cells + 2 * REACH) * columns
     near = cells + PAD_M
@@ -474,7 +496,7 @@
         *(pltpu.with_memory_space_constraint(x, pltpu.HBM) for x in (velocity, viscosity, moments)),
         in_specs=[pl.BlockSpec(memory_space=pltpu.HBM)] * 3,
         scratch=[
-            pltpu.VMEM(moments.shape, jnp.float32),
+            pltpu.VMEM(moments.shape, moments.dtype),
             pltpu.SemaphoreType.DMA((1 + 4 * ROWS,)),
         ],
     )
@@ -485,7 +507,8 @@
         low = shifted(upward, "cross", 1)
         high = shifted(downward, "cross", -1)
         base = (start,) if second else ()
-        source, solve_own, solve_sides = last_tables if second else first_tables
+        source, solve_sides = last if second else first
+        solve_own = last_own if second else first_own
         (rough,) = call(
             functools.partial(rough_kernel, cells, second), [(components * cells, width)], *base, flat, thick, own
         )

time: 62.5 us -> 60.4 us (0.966)
  Pallas kernels: 12.5 us -> 10.2 us
    pallas_call x11, Pallas kernels: 12.5 us -> 10.2 us  [call(): pl.pallas_call(body, out_shape=[jax.ShapeDtypeStruct(s, jnp.float32) for...]
where the time goes in v4:
time: 60.4 us; the launch traced here: 60.2 us
  waiting for transfers between devices  30 us (50%)
  starting transfers between devices  19.7 us (33%)
  Pallas kernels  10.2 us (17%)
    ppermute x18, waiting for transfers between devices, shifted(): lax.ppermute(block, axis, [(i, (i + step) % count) for i in range(count)])  30 us
    ppermute x18, starting transfers between devices, shifted(): lax.ppermute(block, axis, [(i, (i + step) % count) for i in range(count)])  19.7 us
    pallas_call x11, Pallas kernels, call(): pl.pallas_call(body, out_shape=[jax.ShapeDtypeStruct(s, jnp.float32) for...  10.2 us
  transfers between devices with their start and end apart: 18, of which 11 were waited for; matrix products, arithmetic and copies ran while one was open for 0% of the time, Pallas kernels for 8%

profile of v4, /device:TPU:126, one launch (start us, length us, event | category | flops | bytes accessed | tf_op | source)
XLA Modules:
  0.0 60.2 jit_solution(15678692247160801744)
XLA Ops:
  0.0 0.0 copy-start.1
  0.0 1.4 %shard_map.118 = (f32[192,512]{1,0:T(8,128)S(1)}, f32[64,512]{1,0:T(8,128)S(1)}, f32[16,512]{1,0:T(8,128)S(1)}, f32[16,512]{1,0:T(8,128)S(1)}, f32[192,256]{1,0:T(8,128)S(1)}, /*index=5*/f32[192,256]{1,0:T(8,128)S(1)}) custom-call(f32[3,64,4,128]{3,2,1,0:T(4,128)} %velocity.1, f32[64,4,128]{2,1,0:T(4,128)} %viscosity.1, ...), custom_call_target="tpu_custom_call" | custom-call | tf_op jit(solution)/shard_map/pallas_call | solution.py:470
  1.4 0.0 collective-permute-start.2
  1.4 1.7 %collective-permute-start.3 = (f32[192,256]{1,0:T(8,128)S(1)}, f32[192,256]{1,0:T(8,128)S(1)}, u32[]{:S(2)}, u32[]{:S(2)}) collective-permute-start(f32[192,256]{1,0:T(8,128)S(1)} %get-tuple-element.39), channel_id=1, source_target_pairs={{0,7},{1,0},{2,1},{3,2},{4,3},{5,4},{6,5},{7,6},{8,15},{9,8},{10,9... | collective-permute-start | bytes 589832 | tf_op jit(solution)/shard_map/ppermute | solution.py:481
  3.2 3.0 %collective-permute-start = (f32[16,512]{1,0:T(8,128)S(1)}, f32[16,512]{1,0:T(8,128)S(1)}, u32[]{:S(2)}, u32[]{:S(2)}) collective-permute-start(f32[16,512]{1,0:T(8,128)S(1)} %get-tuple-element.36), channel_id=1, source_target_pairs={{0,8},{8,16},{16,24},{24,32},{32,40},{40,48},{48,56},{56,64},{64,7... | collective-permute-start | bytes 98312 | tf_op jit(solution)/shard_map/ppermute | solution.py:481
  6.2 0.0 collective-permute-start.1
  6.2 0.0 copy-done.1
  6.2 0.0 copy-start
  6.2 0.0 copy-start.5
  6.2 0.9 %shard_map.119.rough = f32[192,512]{1,0:T(8,128)S(1)} custom-call(f32[192,512]{1,0:T(8,128)S(1)} %get-tuple-element.34.refs_0_.flat, f32[64,512]{1,0:T(8,128)S(1)} %get-tuple-element.35.refs_1_.thick.refs_2_, f32[128,64]{1,0:T(8,128)S(1)} %copy-done.1), custom_call_target="tpu_custom_call" | custom-call | tf_op jit(solution)/shard_map/pallas_call | solution.py:470
  7.2 0.0 copy-start.4
  7.2 0.6 %collective-permute-done.left = f32[16,512]{1,0:T(8,128)S(1)} collective-permute-done((f32[16,512]{1,0:T(8,128)S(1)}, f32[16,512]{1,0:T(8,128)S(1)}, u32[]{:S(2)}, u32[]{:S(2)}) %collective-permute-start) | collective-permute-done | bytes 32800 | tf_op jit(solution)/shard_map/ppermute | solution.py:481
  7.8 5.6 %collective-permute-done.1.right = f32[16,512]{1,0:T(8,128)S(1)} collective-permute-done((f32[16,512]{1,0:T(8,128)S(1)}, f32[16,512]{1,0:T(8,128)S(1)}, u32[]{:S(2)}, u32[]{:S(2)}) %collective-permute-start.1) | collective-permute-done | bytes 32800 | tf_op jit(solution)/shard_map/ppermute | solution.py:481
  13.4 0.0 collective-permute-done.2.low
  13.4 0.0 collective-permute-done.3.high
  13.4 0.0 copy-done
  13.4 0.0 copy-done.5
  13.5 0.0 copy-start.9
  13.5 0.5 shard_map.120
  14.0 0.0 collective-permute-start.4
  14.0 1.7 %collective-permute-start.5 = (f32[480,128]{1,0:T(8,128)S(1)}, f32[480,128]{1,0:T(8,128)S(1)}, u32[]{:S(2)}, u32[]{:S(2)}) collective-permute-start(f32[480,128]{1,0:T(8,128)S(1)} %get-tuple-element.43), channel_id=1, source_target_pairs={{0,7},{1,0},{2,1},{3,2},{4,3},{5,4},{6,5},{7,6},{8,15},{9,8},{10,9... | collective-permute-start | bytes 737288 | tf_op jit(solution)/shard_map/ppermute | solution.py:481
  15.8 2.6 %collective-permute-start.6 = (f32[200,128]{1,0:T(8,128)S(1)}, f32[200,128]{1,0:T(8,128)S(1)}, u32[]{:S(2)}, u32[]{:S(2)}) collective-permute-start(f32[200,128]{1,0:T(8,128)S(1)} %get-tuple-element.44), channel_id=1, source_target_pairs={{0,2},{1,3},{2,4},{3,5},{4,6},{5,7},{6,0},{7,1},{8,10},{9,11},{10,... | collective-permute-start | bytes 307208 | tf_op jit(solution)/shard_map/ppermute | solution.py:481
  18.4 0.0 collective-permute-start.7
  18.4 3.2 %collective-permute-done.6.low_two = f32[200,128]{1,0:T(8,128)S(1)} collective-permute-done((f32[200,128]{1,0:T(8,128)S(1)}, f32[200,128]{1,0:T(8,128)S(1)}, u32[]{:S(2)}, u32[]{:S(2)}) %collective-permute-start.6) | collective-permute-done | bytes 102432 | tf_op jit(solution)/shard_map/ppermute | solution.py:481
  21.6 2.8 %collective-permute-done.7.high_two = f32[200,128]{1,0:T(8,128)S(1)} collective-permute-done((f32[200,128]{1,0:T(8,128)S(1)}, f32[200,128]{1,0:T(8,128)S(1)}, u32[]{:S(2)}, u32[]{:S(2)}) %collective-permute-start.7) | collective-permute-done | bytes 102432 | tf_op jit(solution)/shard_map/ppermute | solution.py:481
  24.3 0.0 collective-permute-done.4.low_one
  24.3 0.0 collective-permute-done.5.high_one
  24.3 0.0 copy-done.4
  24.4 0.0 copy-done.9
  24.4 0.0 copy-start.2
  24.4 0.4 shard_map.121
  24.8 0.1 collective-permute-start.8
  24.9 2.0 %collective-permute-start.9 = (f32[8,3584]{1,0:T(8,128)S(1)}, f32[8,3584]{1,0:T(8,128)S(1)}, u32[]{:S(2)}, u32[]{:S(2)}) collective-permute-start(f32[8,3584]{1,0:T(8,128)S(1)} %get-tuple-element.48), channel_id=1, source_target_pairs={{0,248},{8,0},{16,8},{24,16},{32,24},{40,32},{48,40},{56,48},{64,5... | collective-permute-start | bytes 344072 | tf_op jit(solution)/shard_map/ppermute | solution.py:481
  26.9 0.0 copy-done.2
  26.9 1.5 %shard_map.122.partial = f32[160,1024]{1,0:T(8,128)S(1)} custom-call(f32[72,1792]{1,0:T(8,128)S(1)} %get-tuple-element.46.ext, f32[160,288]{1,0:T(8,128)S(1)} %copy-done.2), custom_call_target="tpu_custom_call" | custom-call | tf_op jit(solution)/shard_map/pallas_call | solution.py:470
  28.4 1.2 %collective-permute-done.8.left = f32[8,3584]{1,0:T(8,128)S(1)} collective-permute-done((f32[8,3584]{1,0:T(8,128)S(1)}, f32[8,3584]{1,0:T(8,128)S(1)}, u32[]{:S(2)}, u32[]{:S(2)}) %collective-permute-start.8) | collective-permute-done | bytes 114720 | tf_op jit(solution)/shard_map/ppermute | solution.py:481
  29.7 3.4 %collective-permute-done.9.right = f32[8,3584]{1,0:T(8,128)S(1)} collective-permute-done((f32[8,3584]{1,0:T(8,128)S(1)}, f32[8,3584]{1,0:T(8,128)S(1)}, u32[]{:S(2)}, u32[]{:S(2)}) %collective-permute-start.9) | collective-permute-done | bytes 114720 | tf_op jit(solution)/shard_map/ppermute | solution.py:481
  33.1 0.0 copy-done.6
  33.1 0.7 %shard_map.123 = (f32[192,512]{1,0:T(8,128)S(1)}, f32[16,512]{1,0:T(8,128)S(1)}, f32[16,512]{1,0:T(8,128)S(1)}, f32[192,256]{1,0:T(8,128)S(1)}, f32[192,256]{1,0:T(8,128)S(1)}) custom-call(f32[160,1024]{1,0:T(8,128)S(1)} %shard_map.122.partial, f32[8,3584]{1,0:T(8,128)S(1)} %collective-permute-done.8.left, f32[8,3584]{1,0:T(8,128)S(1)} %collective-permute-done.9.right, ...), custom_call_target="tpu_custom_call" | custom-call | tf_op jit(solution)/shard_map/pallas_call | solution.py:470
  33.8 0.0 collective-permute-start.10
  33.8 1.7 %collective-permute-start.11 = (f32[192,256]{1,0:T(8,128)S(1)}, f32[192,256]{1,0:T(8,128)S(1)}, u32[]{:S(2)}, u32[]{:S(2)}) collective-permute-start(f32[192,256]{1,0:T(8,128)S(1)} %get-tuple-element.53), channel_id=1, source_target_pairs={{0,7},{1,0},{2,1},{3,2},{4,3},{5,4},{6,5},{7,6},{8,15},{9,8},{10,9... | collective-permute-start | bytes 589832 | tf_op jit(solution)/shard_map/ppermute | solution.py:481
  35.6 1.0 %shard_map.124.rough = f32[192,512]{1,0:T(8,128)S(1)} custom-call(f32[192,512]{1,0:T(8,128)S(1)} %get-tuple-element.34.refs_0_.flat, f32[192,512]{1,0:T(8,128)S(1)} %get-tuple-element.49.refs_1_.flat, f32[64,512]{1,0:T(8,128)S(1)} %get-tuple-element.35.refs_1_.thick.refs_2_, f32[128,64]{1,0:T(8,128)S(1)} %copy-done.1), custom_call_target="tpu_custom_call" | custom-call | tf_op jit(solution)/shard_map/pallas_call | solution.py:470
  36.5 2.4 %collective-permute-done.10.low = f32[192,256]{1,0:T(8,128)S(1)} collective-permute-done((f32[192,256]{1,0:T(8,128)S(1)}, f32[192,256]{1,0:T(8,128)S(1)}, u32[]{:S(2)}, u32[]{:S(2)}) %collective-permute-start.10) | collective-permute-done | bytes 196640 | tf_op jit(solution)/shard_map/ppermute | solution.py:481
  38.9 0.0 collective-permute-done.11.high
  38.9 0.5 shard_map.125
  39.5 1.5 %collective-permute-start.12 = (f32[480,128]{1,0:T(8,128)S(1)}, f32[480,128]{1,0:T(8,128)S(1)}, u32[]{:S(2)}, u32[]{:S(2)}) collective-permute-start(f32[480,128]{1,0:T(8,128)S(1)} %get-tuple-element.56), channel_id=1, source_target_pairs={{0,1},{1,2},{2,3},{3,4},{4,5},{5,6},{6,7},{7,0},{8,9},{9,10},{10,1... | collective-permute-start | bytes 737288 | tf_op jit(solution)/shard_map/ppermute | solution.py:481
  40.9 0.3 collective-permute-start.13
  41.2 2.6 %collective-permute-start.14 = (f32[200,128]{1,0:T(8,128)S(1)}, f32[200,128]{1,0:T(8,128)S(1)}, u32[]{:S(2)}, u32[]{:S(2)}) collective-permute-start(f32[200,128]{1,0:T(8,128)S(1)} %get-tuple-element.58), channel_id=1, source_target_pairs={{0,2},{1,3},{2,4},{3,5},{4,6},{5,7},{6,0},{7,1},{8,10},{9,11},{10,... | collective-permute-start | bytes 307208 | tf_op jit(solution)/shard_map/ppermute | solution.py:481
  43.8 0.0 collective-permute-start.15
  43.8 3.2 %collective-permute-done.14.low_two = f32[200,128]{1,0:T(8,128)S(1)} collective-permute-done((f32[200,128]{1,0:T(8,128)S(1)}, f32[200,128]{1,0:T(8,128)S(1)}, u32[]{:S(2)}, u32[]{:S(2)}) %collective-permute-start.14) | collective-permute-done | bytes 102432 | tf_op jit(solution)/shard_map/ppermute | solution.py:481
  47.1 3.0 %collective-permute-done.15.high_two = f32[200,128]{1,0:T(8,128)S(1)} collective-permute-done((f32[200,128]{1,0:T(8,128)S(1)}, f32[200,128]{1,0:T(8,128)S(1)}, u32[]{:S(2)}, u32[]{:S(2)}) %collective-permute-start.15) | collective-permute-done | bytes 102432 | tf_op jit(solution)/shard_map/ppermute | solution.py:481
  50.1 0.0 collective-permute-done.12.low_one
  50.1 0.0 collective-permute-done.13.high_one
  50.1 0.0 copy-done.8
  50.1 0.0 copy-start.3
  50.1 0.3 shard_map.126
  50.4 0.3 collective-permute-start.16
  50.7 2.0 %collective-permute-start.17 = (f32[8,2688]{1,0:T(8,128)S(1)}, f32[8,2688]{1,0:T(8,128)S(1)}, u32[]{:S(2)}, u32[]{:S(2)}) collective-permute-start(f32[8,2688]{1,0:T(8,128)S(1)} %get-tuple-element.62), channel_id=1, source_target_pairs={{0,248},{8,0},{16,8},{24,16},{32,24},{40,32},{48,40},{56,48},{64,5... | collective-permute-start | bytes 258056 | tf_op jit(solution)/shard_map/ppermute | solution.py:481
  52.7 0.0 copy-done.3
  52.7 1.4 %shard_map.127.partial = f32[128,1024]{1,0:T(8,128)S(1)} custom-call(f32[72,1792]{1,0:T(8,128)S(1)} %get-tuple-element.60.ext, f32[128,288]{1,0:T(8,128)S(1)} %copy-done.3), custom_call_target="tpu_custom_call" | custom-call | tf_op jit(solution)/shard_map/pallas_call | solution.py:470
  54.1 1.1 %collective-permute-done.16.left = f32[8,2688]{1,0:T(8,128)S(1)} collective-permute-done((f32[8,2688]{1,0:T(8,128)S(1)}, f32[8,2688]{1,0:T(8,128)S(1)}, u32[]{:S(2)}, u32[]{:S(2)}) %collective-permute-start.16) | collective-permute-done | bytes 86048 | tf_op jit(solution)/shard_map/ppermute | solution.py:481
  55.2 3.4 %collective-permute-done.17.right = f32[8,2688]{1,0:T(8,128)S(1)} collective-permute-done((f32[8,2688]{1,0:T(8,128)S(1)}, f32[8,2688]{1,0:T(8,128)S(1)}, u32[]{:S(2)}, u32[]{:S(2)}) %collective-permute-start.17) | collective-permute-done | bytes 86048 | tf_op jit(solution)/shard_map/ppermute | solution.py:481
  58.6 0.0 copy-done.7
  58.6 1.5 %shard_map.128 = f32[3,64,4,128]{3,2,1,0:T(4,128)} custom-call(f32[128,1024]{1,0:T(8,128)S(1)} %shard_map.127.partial, f32[8,2688]{1,0:T(8,128)S(1)} %collective-permute-done.16.left, f32[8,2688]{1,0:T(8,128)S(1)} %collective-permute-done.17.right, f32[192,512]{1,0:T(8,128)S(1)} %get-tuple-element.55.section, bf16[128,384]{1,0:T(8,128)(2,1)S(1)} %copy-done.7), custom_call_target="tpu_custom_call" | custom-call | tf_op jit(solution)/shard_map/pallas_call | solution.py:470
  (3 shorter events, 0.0 us)
Async XLA Ops:
  0.0 6.2 %copy-start.1 = (f32[128,64]{1,0:T(8,128)S(1)}, f32[128,64]{1,0:T(8,128)}, u32[]{:S(2)}) copy-start(f32[128,64]{1,0:T(8,128)} %constant.20.clone.refs_2_.refs_3_) | copy-start | bytes 98308
  1.4 12.0 %collective-permute-start.2 = (f32[192,256]{1,0:T(8,128)S(1)}, f32[192,256]{1,0:T(8,128)S(1)}, u32[]{:S(2)}, u32[]{:S(2)}) collective-permute-start(f32[192,256]{1,0:T(8,128)S(1)} %get-tuple-element.38), channel_id=1, source_target_pairs={{0,1},{1,2},{2,3},{3,4},{4,5},{5,6},{6,7},{7,0},{8,9},{9,10},{10,1... | collective-permute-start | bytes 589832 | tf_op jit(solution)/shard_map/ppermute | solution.py:481
  1.4 12.0 %collective-permute-start.3 = (f32[192,256]{1,0:T(8,128)S(1)}, f32[192,256]{1,0:T(8,128)S(1)}, u32[]{:S(2)}, u32[]{:S(2)}) collective-permute-start(f32[192,256]{1,0:T(8,128)S(1)} %get-tuple-element.39), channel_id=1, source_target_pairs={{0,7},{1,0},{2,1},{3,2},{4,3},{5,4},{6,5},{7,6},{8,15},{9,8},{10,9... | collective-permute-start | bytes 589832 | tf_op jit(solution)/shard_map/ppermute | solution.py:481
  3.2 4.6 %collective-permute-start = (f32[16,512]{1,0:T(8,128)S(1)}, f32[16,512]{1,0:T(8,128)S(1)}, u32[]{:S(2)}, u32[]{:S(2)}) collective-permute-start(f32[16,512]{1,0:T(8,128)S(1)} %get-tuple-element.36), channel_id=1, source_target_pairs={{0,8},{8,16},{16,24},{24,32},{32,40},{40,48},{48,56},{56,64},{64,7... | collective-permute-start | bytes 98312 | tf_op jit(solution)/shard_map/ppermute | solution.py:481
  6.2 7.2 %collective-permute-start.1 = (f32[16,512]{1,0:T(8,128)S(1)}, f32[16,512]{1,0:T(8,128)S(1)}, u32[]{:S(2)}, u32[]{:S(2)}) collective-permute-start(f32[16,512]{1,0:T(8,128)S(1)} %get-tuple-element.37), channel_id=1, source_target_pairs={{0,248},{8,0},{16,8},{24,16},{32,24},{40,32},{48,40},{56,48},{64,5... | collective-permute-start | bytes 98312 | tf_op jit(solution)/shard_map/ppermute | solution.py:481
  6.2 7.2 %copy-start = (bf16[3,128,96]{2,1,0:T(8,128)(2,1)S(1)}, bf16[3,128,96]{2,1,0:T(8,128)(2,1)}, u32[]{:S(2)}) copy-start(bf16[3,128,96]{2,1,0:T(8,128)(2,1)} %constant.22.clone.slopes) | copy-start | bytes 221188
  6.2 7.2 %copy-start.5 = (bf16[72,192]{1,0:T(8,128)(2,1)S(1)}, bf16[72,192]{1,0:T(8,128)(2,1)}, u32[]{:S(2)}) copy-start(bf16[72,192]{1,0:T(8,128)(2,1)} %constant.24.clone.lateral) | copy-start | bytes 82948
  7.2 17.2 %copy-start.4 = (bf16[32,576]{1,0:T(8,128)(2,1)S(1)}, bf16[32,576]{1,0:T(8,128)(2,1)}, u32[]{:S(2)}) copy-start(bf16[32,576]{1,0:T(8,128)(2,1)} %constant.23.clone.moments.refs_0_) | copy-start | bytes 110596
  13.5 10.9 %copy-start.9 = (bf16[64,240]{1,0:T(8,128)(2,1)S(1)}, bf16[64,240]{1,0:T(8,128)(2,1)}, u32[]{:S(2)}) copy-start(bf16[64,240]{1,0:T(8,128)(2,1)} %constant.25.clone.source) | copy-start | bytes 92164
  14.0 10.3 %collective-permute-start.4 = (f32[480,128]{1,0:T(8,128)S(1)}, f32[480,128]{1,0:T(8,128)S(1)}, u32[]{:S(2)}, u32[]{:S(2)}) collective-permute-start(f32[480,128]{1,0:T(8,128)S(1)} %get-tuple-element.42), channel_id=1, source_target_pairs={{0,1},{1,2},{2,3},{3,4},{4,5},{5,6},{6,7},{7,0},{8,9},{9,10},{10,1... | collective-permute-start | bytes 737288 | tf_op jit(solution)/shard_map/ppermute | solution.py:481
  14.0 10.3 %collective-permute-start.5 = (f32[480,128]{1,0:T(8,128)S(1)}, f32[480,128]{1,0:T(8,128)S(1)}, u32[]{:S(2)}, u32[]{:S(2)}) collective-permute-start(f32[480,128]{1,0:T(8,128)S(1)} %get-tuple-element.43), channel_id=1, source_target_pairs={{0,7},{1,0},{2,1},{3,2},{4,3},{5,4},{6,5},{7,6},{8,15},{9,8},{10,9... | collective-permute-start | bytes 737288 | tf_op jit(solution)/shard_map/ppermute | solution.py:481
  15.8 5.8 %collective-permute-start.6 = (f32[200,128]{1,0:T(8,128)S(1)}, f32[200,128]{1,0:T(8,128)S(1)}, u32[]{:S(2)}, u32[]{:S(2)}) collective-permute-start(f32[200,128]{1,0:T(8,128)S(1)} %get-tuple-element.44), channel_id=1, source_target_pairs={{0,2},{1,3},{2,4},{3,5},{4,6},{5,7},{6,0},{7,1},{8,10},{9,11},{10,... | collective-permute-start | bytes 307208 | tf_op jit(solution)/shard_map/ppermute | solution.py:481
  18.4 5.9 %collective-permute-start.7 = (f32[200,128]{1,0:T(8,128)S(1)}, f32[200,128]{1,0:T(8,128)S(1)}, u32[]{:S(2)}, u32[]{:S(2)}) collective-permute-start(f32[200,128]{1,0:T(8,128)S(1)} %get-tuple-element.45), channel_id=1, source_target_pairs={{0,6},{1,7},{2,0},{3,1},{4,2},{5,3},{6,4},{7,5},{8,14},{9,15},{10,... | collective-permute-start | bytes 307208 | tf_op jit(solution)/shard_map/ppermute | solution.py:481
  24.4 2.5 %copy-start.2 = (f32[160,288]{1,0:T(8,128)S(1)}, f32[160,288]{1,0:T(8,128)}, u32[]{:S(2)}) copy-start(f32[160,288]{1,0:T(8,128)} %constant.21.clone.solve) | copy-start | bytes 552964
  24.8 4.9 %collective-permute-start.8 = (f32[8,3584]{1,0:T(8,128)S(1)}, f32[8,3584]{1,0:T(8,128)S(1)}, u32[]{:S(2)}, u32[]{:S(2)}) collective-permute-start(f32[8,3584]{1,0:T(8,128)S(1)} %get-tuple-element.47), channel_id=1, source_target_pairs={{0,8},{8,16},{16,24},{24,32},{32,40},{40,48},{48,56},{56,64},{64,7... | collective-permute-start | bytes 344072 | tf_op jit(solution)/shard_map/ppermute | solution.py:481
  24.9 8.2 %collective-permute-start.9 = (f32[8,3584]{1,0:T(8,128)S(1)}, f32[8,3584]{1,0:T(8,128)S(1)}, u32[]{:S(2)}, u32[]{:S(2)}) collective-permute-start(f32[8,3584]{1,0:T(8,128)S(1)} %get-tuple-element.48), channel_id=1, source_target_pairs={{0,248},{8,0},{16,8},{24,16},{32,24},{40,32},{48,40},{56,48},{64,5... | collective-permute-start | bytes 344072 | tf_op jit(solution)/shard_map/ppermute | solution.py:481
  26.9 6.2 %copy-start.6 = (bf16[160,384]{1,0:T(8,128)(2,1)S(1)}, bf16[160,384]{1,0:T(8,128)(2,1)}, u32[]{:S(2)}) copy-start(bf16[160,384]{1,0:T(8,128)(2,1)} %constant.26.clone.solve) | copy-start | bytes 368644
  33.8 5.1 %collective-permute-start.10 = (f32[192,256]{1,0:T(8,128)S(1)}, f32[192,256]{1,0:T(8,128)S(1)}, u32[]{:S(2)}, u32[]{:S(2)}) collective-permute-start(f32[192,256]{1,0:T(8,128)S(1)} %get-tuple-element.52), channel_id=1, source_target_pairs={{0,1},{1,2},{2,3},{3,4},{4,5},{5,6},{6,7},{7,0},{8,9},{9,10},{10,1... | collective-permute-start | bytes 589832 | tf_op jit(solution)/shard_map/ppermute | solution.py:481
  33.8 5.1 %collective-permute-start.11 = (f32[192,256]{1,0:T(8,128)S(1)}, f32[192,256]{1,0:T(8,128)S(1)}, u32[]{:S(2)}, u32[]{:S(2)}) collective-permute-start(f32[192,256]{1,0:T(8,128)S(1)} %get-tuple-element.53), channel_id=1, source_target_pairs={{0,7},{1,0},{2,1},{3,2},{4,3},{5,4},{6,5},{7,6},{8,15},{9,8},{10,9... | collective-permute-start | bytes 589832 | tf_op jit(solution)/shard_map/ppermute | solution.py:481
  38.9 11.2 %copy-start.8 = (bf16[64,240]{1,0:T(8,128)(2,1)S(1)}, bf16[64,240]{1,0:T(8,128)(2,1)}, u32[]{:S(2)}) copy-start(bf16[64,240]{1,0:T(8,128)(2,1)} %constant.28.clone.source) | copy-start | bytes 92164
  39.5 10.6 %collective-permute-start.12 = (f32[480,128]{1,0:T(8,128)S(1)}, f32[480,128]{1,0:T(8,128)S(1)}, u32[]{:S(2)}, u32[]{:S(2)}) collective-permute-start(f32[480,128]{1,0:T(8,128)S(1)} %get-tuple-element.56), channel_id=1, source_target_pairs={{0,1},{1,2},{2,3},{3,4},{4,5},{5,6},{6,7},{7,0},{8,9},{9,10},{10,1... | collective-permute-start | bytes 737288 | tf_op jit(solution)/shard_map/ppermute | solution.py:481
  40.9 9.2 %collective-permute-start.13 = (f32[480,128]{1,0:T(8,128)S(1)}, f32[480,128]{1,0:T(8,128)S(1)}, u32[]{:S(2)}, u32[]{:S(2)}) collective-permute-start(f32[480,128]{1,0:T(8,128)S(1)} %get-tuple-element.57), channel_id=1, source_target_pairs={{0,7},{1,0},{2,1},{3,2},{4,3},{5,4},{6,5},{7,6},{8,15},{9,8},{10,9... | collective-permute-start | bytes 737288 | tf_op jit(solution)/shard_map/ppermute | solution.py:481
  41.2 5.8 %collective-permute-start.14 = (f32[200,128]{1,0:T(8,128)S(1)}, f32[200,128]{1,0:T(8,128)S(1)}, u32[]{:S(2)}, u32[]{:S(2)}) collective-permute-start(f32[200,128]{1,0:T(8,128)S(1)} %get-tuple-element.58), channel_id=1, source_target_pairs={{0,2},{1,3},{2,4},{3,5},{4,6},{5,7},{6,0},{7,1},{8,10},{9,11},{10,... | collective-permute-start | bytes 307208 | tf_op jit(solution)/shard_map/ppermute | solution.py:481
  43.8 6.3 %collective-permute-start.15 = (f32[200,128]{1,0:T(8,128)S(1)}, f32[200,128]{1,0:T(8,128)S(1)}, u32[]{:S(2)}, u32[]{:S(2)}) collective-permute-start(f32[200,128]{1,0:T(8,128)S(1)} %get-tuple-element.59), channel_id=1, source_target_pairs={{0,6},{1,7},{2,0},{3,1},{4,2},{5,3},{6,4},{7,5},{8,14},{9,15},{10,... | collective-permute-start | bytes 307208 | tf_op jit(solution)/shard_map/ppermute | solution.py:481
  50.1 2.6 %copy-start.3 = (f32[128,288]{1,0:T(8,128)S(1)}, f32[128,288]{1,0:T(8,128)}, u32[]{:S(2)}) copy-start(f32[128,288]{1,0:T(8,128)} %constant.27.clone.solve) | copy-start | bytes 442372
  50.4 4.7 %collective-permute-start.16 = (f32[8,2688]{1,0:T(8,128)S(1)}, f32[8,2688]{1,0:T(8,128)S(1)}, u32[]{:S(2)}, u32[]{:S(2)}) collective-permute-start(f32[8,2688]{1,0:T(8,128)S(1)} %get-tuple-element.61), channel_id=1, source_target_pairs={{0,8},{8,16},{16,24},{24,32},{32,40},{40,48},{48,56},{56,64},{64,7... | collective-permute-start | bytes 258056 | tf_op jit(solution)/shard_map/ppermute | solution.py:481
  50.7 7.9 %collective-permute-start.17 = (f32[8,2688]{1,0:T(8,128)S(1)}, f32[8,2688]{1,0:T(8,128)S(1)}, u32[]{:S(2)}, u32[]{:S(2)}) collective-permute-start(f32[8,2688]{1,0:T(8,128)S(1)} %get-tuple-element.62), channel_id=1, source_target_pairs={{0,248},{8,0},{16,8},{24,16},{32,24},{40,32},{48,40},{56,48},{64,5... | collective-permute-start | bytes 258056 | tf_op jit(solution)/shard_map/ppermute | solution.py:481
  52.7 5.9 %copy-start.7 = (bf16[128,384]{1,0:T(8,128)(2,1)S(1)}, bf16[128,384]{1,0:T(8,128)(2,1)}, u32[]{:S(2)}) copy-start(bf16[128,384]{1,0:T(8,128)(2,1)} %constant.29.clone.solve) | copy-start | bytes 294916

commit v5 on v4

--- a/solution.py
+++ b/solution.py
@@ -125,7 +125,8 @@
                 top = 2 * cells + GROUP * (2 * side + half)
                 solve_own[top : top + RANK_V, near * j : near * (j + 1)] = -mine
                 solve_sides[top : top + RANK_V, wide * j : wide * (j + 1)] = -sides
-    plain, split = (own, solve_own), (slopes, moments, lateral, source, solve_sides)
+    rim = np.concatenate([own, from_left, from_right], axis=1)
+    plain, split = (own, solve_own), (slopes, rim, moments, lateral, source, solve_sides)
     return [x.astype(np.float32) for x in plain] + [split_table(x.astype(np.float32)) for x in split]
 
 
@@ -210,20 +211,19 @@
             copies.append(
                 pltpu.make_async_copy(velocity.at[c, :, r, :], flat.at[rows, lane(r)], sems.at[len(copies)])
             )
-    apart = len(copies)
     for r in range(ROWS):
         copies.append(pltpu.make_async_copy(viscosity.at[:, r, :], thick.at[:, lane(r)], sems.at[len(copies)]))
     for copy in copies:
         copy.start()
-    for copy in copies[:apart]:
+    for copy in copies:
         copy.wait()
-    upward[...] = flat[:, lane(ROWS - 2, 2)]
-    downward[...] = flat[:, lane(0, 2)]
+    upward[: 3 * cells, :] = flat[:, lane(ROWS - 2, 2)]
+    downward[: 3 * cells, :] = flat[:, lane(0, 2)]
+    upward[3 * cells :, :] = thick[:, lane(ROWS - 2, 2)]
+    downward[3 * cells :, :] = thick[:, lane(0, 2)]
     both = split_dot(weights[...], flat[...])
     to_right[...] = both[:PAD_V]
     to_left[...] = both[PAD_V:]
-    for copy in copies[apart:]:
-        copy.wait()
 
 
 def weighed(weights, value_at, r, home):
@@ -265,26 +265,38 @@
             rough[rows, lane(r)] = moved
 
 
-def tendency_kernel(
-    cells, scale, rough, flat, thick, left, right, low, high, slopes, lateral,
-    section, parts, up_near, down_near, up_far, down_far,
-):
-    masks = edge_masks()
+def beyond_rows(cells, low, high, stacked, masks):
+    def value(c, r):
+        given, k = (low, r + ROWS) if r < 0 else (high, r - ROWS)
+        if not stacked:
+            tile = given[cells * c : cells * (c + 1), lane(k % 2)]
+        else:
+            slot = k if c == 1 else ROWS + c + k % 2
+            tile = given[cells * slot : cells * (slot + 1), :]
+        return masked(tile, r, masks)
+
+    return value
+
+
+def add_beyond(cells, scale, rough, flat, thick, left, right, slopes, beyond, section):
     sides = jnp.concatenate([left[...], right[...]], axis=0)
     for c in range(3):
         rows = slice(cells * c, cells * (c + 1))
         spanned = split_dot(slopes[c], sides)
-
-        def beyond(r):
-            if r < 0:
-                return masked(low[rows, lane(r + 2)], r, masks)
-            return masked(high[rows, lane(r - ROWS)], r, masks)
-
+        value = lambda r: beyond(c, r)
         for r in range(ROWS):
-            spread = spanned[cells:, lane(r)] + weighed(CURVE, beyond, r, False)
-            carried = flat[cells : 2 * cells, lane(r)] * weighed(DIFFERENCE, beyond, r, False)
+            spread = spanned[cells:, lane(r)] + weighed(CURVE, value, r, False)
+            carried = flat[cells : 2 * cells, lane(r)] * weighed(DIFFERENCE, value, r, False)
             carried = carried + flat[2 * cells :, lane(r)] * spanned[:cells, lane(r)]
             section[rows, lane(r)] = rough[rows, lane(r)] + scale * (thick[:, lane(r)] * spread - carried)
+
+
+def tendency_kernel(
+    cells, rough, flat, thick, left, right, low, high, slopes, lateral,
+    section, parts, up_near, down_near, up_far, down_far,
+):
+    beyond = beyond_rows(cells, low, high, False, edge_masks())
+    add_beyond(cells, time_step, rough, flat, thick, left, right, slopes, beyond, section)
     side = split_dot(lateral[...], section[2 * cells :, :])
     span = slice(0, cells)
     at = lambda r: section[cells : 2 * cells, lane(r)]
@@ -314,11 +326,89 @@
     down_near[rest, :] = (1.0 / 12.0) * at(ROWS - 2) - (2.0 / 3.0) * at(ROWS - 1)
 
 
-def source_kernel(cells, keep, parts, section, low_one, high_one, low_two, high_two, source, *refs):
-    if keep:
-        moments, ext, to_right, to_left = refs
-    else:
-        ext, to_right, to_left = refs
+def last_tendency_kernel(
+    cells, rough, flat, thick, left, right, low, high, first_low, first_high, slopes, rim, lateral,
+    section, near, up_far, down_far,
+):
+    masks = edge_masks()
+    beyond = beyond_rows(cells, low, high, True, masks)
+    base = beyond_rows(cells, first_low, first_high, False, masks)
+    add_beyond(cells, 0.5 * time_step, rough, flat, thick, left, right, slopes, beyond, section)
+    outer = (-2, -1, ROWS, ROWS + 1)
+    v1 = lambda r: flat[cells : 2 * cells, lane(r)] if 0 <= r < ROWS else beyond(1, r)
+
+    def rim_moments(r):
+        given, k = (low, r + 2) if r < 0 else (high, r - ROWS)
+        return given[8 * cells + GROUP * k : 8 * cells + GROUP * (k + 1), :]
+
+    columns = [jnp.concatenate([v1(r), rim_moments(r)], axis=0) for r in outer]
+    spanned = split_dot(rim[...], jnp.concatenate(columns, axis=1))
+    moved = {}
+    for k, r in enumerate(outer):
+        here = v1(r)
+        up_one, down_one = turned(here, 1), turned(here, -1)
+        up_two, down_two = turned(here, 2), turned(here, -2)
+        slope = sum(factor * v1(r + reach) for reach, factor in DIFFERENCE)
+        curve = sum(factor * v1(r + reach) for reach, factor in CURVE)
+        carried = (
+            beyond(0, r) * first_diff(up_one, down_one, up_two, down_two)
+            + here * slope
+            + beyond(2, r) * spanned[:cells, lane(k)]
+        )
+        spread = (
+            (4.0 / 3.0) * (up_one + down_one)
+            - (1.0 / 12.0) * (up_two + down_two)
+            - 5.0 * here
+            + curve
+            + spanned[cells:, lane(k)]
+        )
+        value = 0.5 * base(1, r) + 0.5 * (here + time_step * (base(3, r) * spread - carried))
+        moved[r] = masked(value, r, masks)
+    side = split_dot(lateral[...], section[2 * cells :, :])
+    at = lambda r: section[cells : 2 * cells, lane(r)] if 0 <= r < ROWS else moved[r]
+    for r in range(ROWS):
+        total = stream_slope(section[:cells, lane(r)]) + side[:cells, lane(r)]
+        for reach, factor in DIFFERENCE:
+            total = total + factor * at(r + reach)
+        tail = slice(ROWS * cells + PAD_M * r, ROWS * cells + PAD_M * (r + 1))
+        near[cells * r : cells * (r + 1), :] = total
+        near[tail, :] = side[cells:, lane(r)]
+        for far, row in ((up_far, ROWS - 1), (down_far, 0)):
+            if r == row:
+                far[:cells, :] = total
+                far[cells:, :] = side[cells:, lane(r)]
+
+
+def last_source_kernel(cells, near, low_one, high_one, low_two, high_two, source, ext, to_right, to_left):
+    masks = edge_masks()
+    span, tail = slice(0, cells), slice(cells, cells + PAD_M)
+    for e in range(-REACH, ROWS + REACH):
+        if e < -ROWS or e >= 2 * ROWS:
+            given = low_two if e < 0 else high_two
+            total, side = given[span, :], given[tail, :]
+        else:
+            given = low_one if e < 0 else near if e < ROWS else high_one
+            r = e % ROWS
+            total = given[cells * r : cells * (r + 1), :]
+            side = given[ROWS * cells + PAD_M * r : ROWS * cells + PAD_M * (r + 1), :]
+        ext[span, lane(e + REACH)] = masked(total, e, masks)
+        ext[tail, lane(e + REACH)] = masked(side, e, masks)
+    pack_moments(split_dot(source[...], ext[...]), to_right, to_left)
+
+
+def pack_moments(both, to_right, to_left):
+    for side, out in enumerate((to_right, to_left)):
+        top = 4 * GROUP * side
+        out[:, lane(0, BREADTH)] = both[top : top + 8]
+        for k in range(BREADTH // 2):
+            out[:, lane(BREADTH + k)] = (
+                both[top + 8 : top + 16, lane(2 * k)] + both[top + 16 : top + 24, lane(2 * k + 1)]
+            )
+
+
+def source_kernel(
+    cells, parts, section, low_one, high_one, low_two, high_two, source, moments, ext, to_right, to_left
+):
     masks = edge_masks()
     span, tail = slice(0, cells), slice(cells, cells + PAD_M)
     pick = lambda ref, k: ref[cells * k : cells * (k + 1), :]
@@ -360,27 +450,20 @@
         ext[span, lane(e + REACH)] = masked(total, e, masks)
         ext[tail, lane(e + REACH)] = masked(side, e, masks)
     both = split_dot(source[...], ext[...])
-    if keep:
-        held = split_dot(moments[...], section[...])
+    pack_moments(both, to_right, to_left)
+    held = split_dot(moments[...], section[...])
     for side, out in enumerate((to_right, to_left)):
-        top = 4 * GROUP * side
-        out[:, lane(0, BREADTH)] = both[top : top + 8]
-        for k in range(BREADTH // 2):
-            out[:, lane(BREADTH + k)] = (
-                both[top + 8 : top + 16, lane(2 * k)] + both[top + 16 : top + 24, lane(2 * k + 1)]
+        top, base = 4 * GROUP * side, PAD_V * side
+        out[:, lane(PACKED, ROWS)] = held[base : base + 8]
+        out[:, lane(PACKED + ROWS, 3)] = jnp.zeros((GROUP, 3 * LANES), jnp.float32)
+        for e in range(BREADTH + ROWS):
+            value = (
+                both[top + 24 : top + 25, lane(e)]
+                if e < BREADTH
+                else held[base + 8 : base + 9, lane(e - BREADTH)]
             )
-        if keep:
-            base = PAD_V * side
-            out[:, lane(PACKED, ROWS)] = held[base : base + 8]
-            out[:, lane(PACKED + ROWS, 3)] = jnp.zeros((GROUP, 3 * LANES), jnp.float32)
-            for e in range(BREADTH + ROWS):
-                value = (
-                    both[top + 24 : top + 25, lane(e)]
-                    if e < BREADTH
-                    else held[base + 8 : base + 9, lane(e - BREADTH)]
-                )
-                row, tile = e % GROUP, PACKED + ROWS + e // GROUP
-                out[row : row + 1, lane(tile)] = value
+            row, tile = e % GROUP, PACKED + ROWS + e // GROUP
+            out[row : row + 1, lane(tile)] = value
 
 
 def climb(levels, depth, masks):
@@ -447,10 +530,13 @@
                 copies[-1].start()
                 continue
             flat[rows, lane(r)] = value
-            if r < 2:
-                downward[rows, lane(r)] = value
-            if r >= ROWS - 2:
-                upward[rows, lane(r - ROWS + 2)] = value
+            if c == 1:
+                upward[cells * r : cells * (r + 1), :] = value
+                downward[cells * r : cells * (r + 1), :] = value
+            else:
+                slot = ROWS + c + r % 2
+                target = downward if r < 2 else upward
+                target[cells * slot : cells * (slot + 1), :] = value
     for copy in copies:
         copy.wait()
     if not last:
@@ -464,6 +550,12 @@
                 for c in range(3):
                     rows = slice(RANK_V * c, RANK_V * (c + 1))
                     target[rows, lane(r)] = target[rows, lane(r)] - slope(c, phi_rows, slope_rows, r)[:RANK_V]
+        for sent, first in ((downward, 0), (upward, ROWS - 2)):
+            sent[8 * cells :, :] = jnp.zeros((2 * GROUP, LANES), jnp.float32)
+            for k in range(2):
+                top = 8 * cells + GROUP * k
+                sent[top : top + RANK_V, :] = next_left[RANK_V : 2 * RANK_V, lane(first + k)]
+                sent[top + RANK_V : top + 2 * RANK_V, :] = next_right[RANK_V : 2 * RANK_V, lane(first + k)]
 
 
 def call(body, shapes, *args, scratch=(), **options):
@@ -484,71 +576,83 @@
 def per_device(velocity, viscosity):
     components, cells, row_cells, columns = velocity.shape
     length = cells * lax.axis_size("span")
-    own, first_own, slopes, moments, lateral, *first = (jnp.asarray(t) for t in tables(length, cells, False))
-    _, last_own, _, _, _, *last = (jnp.asarray(t) for t in tables(length, cells, True))
+    own, first_own, slopes, rim, moments, lateral, *first = (
+        jnp.asarray(t) for t in tables(length, cells, False)
+    )
+    _, last_own, _, _, _, _, *last = (jnp.asarray(t) for t in tables(length, cells, True))
     width = row_cells * columns
     wide = (row_cells + 2 * REACH) * columns
     near = cells + PAD_M
-    edge, rim = (PAD_V, width), (components * cells, 2 * columns)
+    whole, edge = (components * cells, width), (PAD_V, width)
     start, thick, to_right, to_left, upward, downward = call(
         functools.partial(open_kernel, cells),
-        [(components * cells, width), (cells, width), edge, edge, rim, rim],
+        [whole, (cells, width), edge, edge] + [((components + 1) * cells, 2 * columns)] * 2,
         *(pltpu.with_memory_space_constraint(x, pltpu.HBM) for x in (velocity, viscosity, moments)),
         in_specs=[pl.BlockSpec(memory_space=pltpu.HBM)] * 3,
-        scratch=[
-            pltpu.VMEM(moments.shape, moments.dtype),
-            pltpu.SemaphoreType.DMA((1 + 4 * ROWS,)),
-        ],
+        scratch=[pltpu.VMEM(moments.shape, moments.dtype), pltpu.SemaphoreType.DMA((1 + 4 * ROWS,))],
     )
     left = shifted(to_right, "span", 1)
     right = shifted(to_left, "span", -1)
-    flat = start
-    for second in (False, True):
-        low = shifted(upward, "cross", 1)
-        high = shifted(downward, "cross", -1)
-        base = (start,) if second else ()
-        source, solve_sides = last if second else first
-        solve_own = last_own if second else first_own
-        (rough,) = call(
-            functools.partial(rough_kernel, cells, second), [(components * cells, width)], *base, flat, thick, own
-        )
-        section, parts, up_near, down_near, up_far, down_far = call(
-            functools.partial(tendency_kernel, cells, 0.5 * time_step if second else time_step),
-            [(components * cells, width), (near, width)] + [(7 * cells + 4 * PAD_M, columns)] * 2 + [(3 * cells + PAD_M, columns)] * 2,
-            rough, flat, thick, left, right, low, high, slopes, lateral,
-        )
-        low_one = shifted(up_near, "cross", 1)
-        high_one = shifted(down_near, "cross", -1)
-        low_two = shifted(up_far, "cross", 2)
-        high_two = shifted(down_far, "cross", -2)
-        sent = (GROUP, (PACKED if second else PACKED + ROWS + 3) * columns)
-        extra = () if second else (moments,)
-        ext, to_right, to_left = call(
-            functools.partial(source_kernel, cells, not second),
-            [(near, wide), sent, sent],
-            parts, section, low_one, high_one, low_two, high_two, source, *extra,
-        )
-        left = shifted(to_right, "span", 1)
-        right = shifted(to_left, "span", -1)
-        (partial,) = call(
-            home_kernel,
-            [(solve_own.shape[0], (row_cells + 4) * columns)],
-            ext, solve_own,
-            scratch=[pltpu.VMEM((SWEEPS * near, wide), jnp.float32)],
-        )
-        scratch = [pltpu.VMEM((SWEEPS * 2 * PAD_S, wide), jnp.float32)]
-        given = (partial, left, right, section, solve_sides)
-        body = functools.partial(solve_kernel, cells, second)
-        if second:
-            (out,) = call(
-                body, [velocity.shape], *given,
-                scratch=scratch + [pltpu.VMEM((components * cells, width), jnp.float32), pltpu.SemaphoreType.DMA((3 * ROWS,))],
-                out_specs=[pl.BlockSpec(memory_space=pltpu.HBM)],
-            )
-        else:
-            flat, left, right, upward, downward = call(
-                body, [(components * cells, width), edge, edge, rim, rim], *given, scratch=scratch
-            )
+    first_low = shifted(upward, "cross", 1)
+    first_high = shifted(downward, "cross", -1)
+
+    (rough,) = call(functools.partial(rough_kernel, cells, False), [whole], start, thick, own)
+    section, parts, up_near, down_near, up_far, down_far = call(
+        functools.partial(tendency_kernel, cells),
+        [whole, (near, width)]
+        + [(7 * cells + 4 * PAD_M, columns)] * 2
+        + [(3 * cells + PAD_M, columns)] * 2,
+        rough, start, thick, left, right, first_low, first_high, slopes, lateral,
+    )
+    low_one = shifted(up_near, "cross", 1)
+    high_one = shifted(down_near, "cross", -1)
+    low_two = shifted(up_far, "cross", 2)
+    high_two = shifted(down_far, "cross", -2)
+    ext, to_right, to_left = call(
+        functools.partial(source_kernel, cells),
+        [(near, wide)] + [(GROUP, (PACKED + ROWS + 3) * columns)] * 2,
+        parts, section, low_one, high_one, low_two, high_two, first[0], moments,
+    )
+    levels = pltpu.VMEM((SWEEPS * near, wide), jnp.float32)
+    side_levels = pltpu.VMEM((SWEEPS * 2 * PAD_S, wide), jnp.float32)
+    found = (row_cells + 4) * columns
+    left = shifted(to_right, "span", 1)
+    right = shifted(to_left, "span", -1)
+    (partial,) = call(home_kernel, [(first_own.shape[0], found)], ext, first_own, scratch=[levels])
+    flat, left, right, upward, downward = call(
+        functools.partial(solve_kernel, cells, False),
+        [whole, edge, edge] + [(8 * cells + 2 * GROUP, columns)] * 2,
+        partial, left, right, section, first[1],
+        scratch=[side_levels],
+    )
+
+    low = shifted(upward, "cross", 1)
+    high = shifted(downward, "cross", -1)
+    (rough,) = call(functools.partial(rough_kernel, cells, True), [whole], start, flat, thick, own)
+    section, sent, up_far, down_far = call(
+        functools.partial(last_tendency_kernel, cells),
+        [whole, (row_cells * near, columns)] + [(near, columns)] * 2,
+        rough, flat, thick, left, right, low, high, first_low, first_high, slopes, rim, lateral,
+    )
+    low_one = shifted(sent, "cross", 1)
+    high_one = shifted(sent, "cross", -1)
+    low_two = shifted(up_far, "cross", 2)
+    high_two = shifted(down_far, "cross", -2)
+    ext, to_right, to_left = call(
+        functools.partial(last_source_kernel, cells),
+        [(near, wide)] + [(GROUP, PACKED * columns)] * 2,
+        sent, low_one, high_one, low_two, high_two, last[0],
+    )
+    left = shifted(to_right, "span", 1)
+    right = shifted(to_left, "span", -1)
+    (partial,) = call(home_kernel, [(last_own.shape[0], found)], ext, last_own, scratch=[levels])
+    (out,) = call(
+        functools.partial(solve_kernel, cells, True),
+        [velocity.shape],
+        partial, left, right, section, last[1],
+        scratch=[side_levels, pltpu.VMEM(whole, jnp.float32), pltpu.SemaphoreType.DMA((3 * ROWS,))],
+        out_specs=[pl.BlockSpec(memory_space=pltpu.HBM)],
+    )
     return out
 
 

time: 60.4 us -> 61.7 us (1.022)
  the two profiles are of different devices: /device:TPU:126 before, /device:TPU:1 now
where the time goes in v5:
time: 61.7 us; the launch traced here: 61.5 us
  starting transfers between devices  35.1 us (57%)
  waiting for transfers between devices  15.5 us (25%)
  Pallas kernels  10.5 us (17%)
    ppermute x18, starting transfers between devices, shifted(): lax.ppermute(block, axis, [(i, (i + step) % count) for i in range(count)])  35.1 us
    ppermute x18, waiting for transfers between devices, shifted(): lax.ppermute(block, axis, [(i, (i + step) % count) for i in range(count)])  15.5 us
    pallas_call x11, Pallas kernels, call(): pl.pallas_call(body, out_shape=[jax.ShapeDtypeStruct(s, jnp.float32) for...  10.5 us
  transfers between devices with their start and end apart: 18, of which 7 were waited for; matrix products, arithmetic and copies ran while one was open for 0% of the time, Pallas kernels for 8%

profile of v5, /device:TPU:1, one launch (start us, length us, event | category | flops | bytes accessed | tf_op | source)
XLA Modules:
  0.0 61.5 jit_solution(7994110091927764200)
XLA Ops:
  0.0 0.0 copy-start.1
  0.0 1.5 %shard_map.127 = (f32[192,512]{1,0:T(8,128)S(1)}, f32[64,512]{1,0:T(8,128)S(1)}, f32[16,512]{1,0:T(8,128)S(1)}, f32[16,512]{1,0:T(8,128)S(1)}, f32[256,256]{1,0:T(8,128)S(1)}, /*index=5*/f32[256,256]{1,0:T(8,128)S(1)}) custom-call(f32[3,64,4,128]{3,2,1,0:T(4,128)} %velocity.1, f32[64,4,128]{2,1,0:T(4,128)} %viscosity.1, bf16[32,576]{1,0:T(8,128)(2,1)} %constant.26.clone.moments), custom_call_target="tpu_custom_call" | custom-call | tf_op jit(solution)/shard_map/pallas_call | solution.py:562
  1.5 2.7 %collective-permute-start.2 = (f32[256,256]{1,0:T(8,128)S(1)}, f32[256,256]{1,0:T(8,128)S(1)}, u32[]{:S(2)}, u32[]{:S(2)}) collective-permute-start(f32[256,256]{1,0:T(8,128)S(1)} %get-tuple-element.36), channel_id=1, source_target_pairs={{0,1},{1,2},{2,3},{3,4},{4,5},{5,6},{6,7},{7,0},{8,9},{9,10},{10,1... | collective-permute-start | bytes 786440 | tf_op jit(solution)/shard_map/ppermute | solution.py:573
  4.2 0.6 collective-permute-start.3
  4.7 0.6 %collective-permute-start = (f32[16,512]{1,0:T(8,128)S(1)}, f32[16,512]{1,0:T(8,128)S(1)}, u32[]{:S(2)}, u32[]{:S(2)}) collective-permute-start(f32[16,512]{1,0:T(8,128)S(1)} %get-tuple-element.34), channel_id=1, source_target_pairs={{0,8},{8,16},{16,24},{24,32},{32,40},{40,48},{48,56},{56,64},{64,7... | collective-permute-start | bytes 98312 | tf_op jit(solution)/shard_map/ppermute | solution.py:573
  5.4 6.6 %collective-permute-start.1 = (f32[16,512]{1,0:T(8,128)S(1)}, f32[16,512]{1,0:T(8,128)S(1)}, u32[]{:S(2)}, u32[]{:S(2)}) collective-permute-start(f32[16,512]{1,0:T(8,128)S(1)} %get-tuple-element.35), channel_id=1, source_target_pairs={{0,248},{8,0},{16,8},{24,16},{32,24},{40,32},{48,40},{56,48},{64,5... | collective-permute-start | bytes 98312 | tf_op jit(solution)/shard_map/ppermute | solution.py:573
  11.9 0.0 copy-done.1
  11.9 0.0 copy-start
  11.9 0.0 copy-start.5
  11.9 0.9 %shard_map.128.rough = f32[192,512]{1,0:T(8,128)S(1)} custom-call(f32[192,512]{1,0:T(8,128)S(1)} %get-tuple-element.32.refs_0_.flat, f32[64,512]{1,0:T(8,128)S(1)} %get-tuple-element.33.refs_1_.thick.refs_2_, f32[128,64]{1,0:T(8,128)S(1)} %copy-done.1), custom_call_target="tpu_custom_call" | custom-call | tf_op jit(solution)/shard_map/pallas_call | solution.py:562
  12.9 0.0 copy-start.4
  12.9 0.3 collective-permute-done.left
  13.2 0.0 collective-permute-done.1.right
  13.2 0.0 collective-permute-done.2.low.first_low
  13.2 0.0 collective-permute-done.3.high.first_high
  13.3 0.0 copy-done
  13.3 0.0 copy-done.5
  13.3 0.0 copy-start.10
  13.3 0.5 shard_map.129
  13.8 2.6 %collective-permute-start.4 = (f32[480,128]{1,0:T(8,128)S(1)}, f32[480,128]{1,0:T(8,128)S(1)}, u32[]{:S(2)}, u32[]{:S(2)}) collective-permute-start(f32[480,128]{1,0:T(8,128)S(1)} %get-tuple-element.40), channel_id=1, source_target_pairs={{0,1},{1,2},{2,3},{3,4},{4,5},{5,6},{6,7},{7,0},{8,9},{9,10},{10,1... | collective-permute-start | bytes 737288 | tf_op jit(solution)/shard_map/ppermute | solution.py:573
  16.4 0.1 collective-permute-start.5
  16.5 1.2 %collective-permute-start.6 = (f32[200,128]{1,0:T(8,128)S(1)}, f32[200,128]{1,0:T(8,128)S(1)}, u32[]{:S(2)}, u32[]{:S(2)}) collective-permute-start(f32[200,128]{1,0:T(8,128)S(1)} %get-tuple-element.42), channel_id=1, source_target_pairs={{0,2},{1,3},{2,4},{3,5},{4,6},{5,7},{6,0},{7,1},{8,10},{9,11},{10,... | collective-permute-start | bytes 307208 | tf_op jit(solution)/shard_map/ppermute | solution.py:573
  17.7 1.4 %collective-permute-start.7 = (f32[200,128]{1,0:T(8,128)S(1)}, f32[200,128]{1,0:T(8,128)S(1)}, u32[]{:S(2)}, u32[]{:S(2)}) collective-permute-start(f32[200,128]{1,0:T(8,128)S(1)} %get-tuple-element.43), channel_id=1, source_target_pairs={{0,6},{1,7},{2,0},{3,1},{4,2},{5,3},{6,4},{7,5},{8,14},{9,15},{10,... | collective-permute-start | bytes 307208 | tf_op jit(solution)/shard_map/ppermute | solution.py:573
  19.2 5.0 %collective-permute-done.6.low_two = f32[200,128]{1,0:T(8,128)S(1)} collective-permute-done((f32[200,128]{1,0:T(8,128)S(1)}, f32[200,128]{1,0:T(8,128)S(1)}, u32[]{:S(2)}, u32[]{:S(2)}) %collective-permute-start.6) | collective-permute-done | bytes 102432 | tf_op jit(solution)/shard_map/ppermute | solution.py:573
  24.1 0.0 collective-permute-done.7.high_two
  24.1 0.0 collective-permute-done.4.low_one
  24.1 0.0 collective-permute-done.5.high_one
  24.1 0.0 copy-done.4
  24.2 0.0 copy-done.10
  24.2 0.0 copy-start.2
  24.2 0.4 shard_map.130
  24.6 0.1 collective-permute-start.8
  24.7 5.1 %collective-permute-start.9 = (f32[8,3584]{1,0:T(8,128)S(1)}, f32[8,3584]{1,0:T(8,128)S(1)}, u32[]{:S(2)}, u32[]{:S(2)}) collective-permute-start(f32[8,3584]{1,0:T(8,128)S(1)} %get-tuple-element.46), channel_id=1, source_target_pairs={{0,248},{8,0},{16,8},{24,16},{32,24},{40,32},{48,40},{56,48},{64,5... | collective-permute-start | bytes 344072 | tf_op jit(solution)/shard_map/ppermute | solution.py:573
  29.8 0.0 copy-done.2
  29.8 1.5 %shard_map.131.partial = f32[160,1024]{1,0:T(8,128)S(1)} custom-call(f32[72,1792]{1,0:T(8,128)S(1)} %get-tuple-element.44.ext, f32[160,288]{1,0:T(8,128)S(1)} %copy-done.2), custom_call_target="tpu_custom_call" | custom-call | tf_op jit(solution)/shard_map/pallas_call | solution.py:562
  31.4 0.5 collective-permute-done.8.left
  31.9 0.0 collective-permute-done.9.right
  31.9 0.0 copy-done.6
  31.9 0.8 %shard_map.132 = (f32[192,512]{1,0:T(8,128)S(1)}, f32[16,512]{1,0:T(8,128)S(1)}, f32[16,512]{1,0:T(8,128)S(1)}, f32[528,128]{1,0:T(8,128)S(1)}, f32[528,128]{1,0:T(8,128)S(1)}) custom-call(f32[160,1024]{1,0:T(8,128)S(1)} %shard_map.131.partial, f32[8,3584]{1,0:T(8,128)S(1)} %collective-permute-done.8.left, f32[8,3584]{1,0:T(8,128)S(1)} %collective-permute-done.9.right, ...), custom_call_target="tpu_custom_call" | custom-call | tf_op jit(solution)/shard_map/pallas_call | solution.py:562
  32.7 2.9 %collective-permute-start.10 = (f32[528,128]{1,0:T(8,128)S(1)}, f32[528,128]{1,0:T(8,128)S(1)}, u32[]{:S(2)}, u32[]{:S(2)}) collective-permute-start(f32[528,128]{1,0:T(8,128)S(1)} %get-tuple-element.50), channel_id=1, source_target_pairs={{0,1},{1,2},{2,3},{3,4},{4,5},{5,6},{6,7},{7,0},{8,9},{9,10},{10,1... | collective-permute-start | bytes 811016 | tf_op jit(solution)/shard_map/ppermute | solution.py:573
  35.5 0.0 collective-permute-start.11
  35.5 1.0 %shard_map.133.rough = f32[192,512]{1,0:T(8,128)S(1)} custom-call(f32[192,512]{1,0:T(8,128)S(1)} %get-tuple-element.32.refs_0_.flat, f32[192,512]{1,0:T(8,128)S(1)} %get-tuple-element.47.refs_1_.flat, f32[64,512]{1,0:T(8,128)S(1)} %get-tuple-element.33.refs_1_.thick.refs_2_, f32[128,64]{1,0:T(8,128)S(1)} %copy-done.1), custom_call_target="tpu_custom_call" | custom-call | tf_op jit(solution)/shard_map/pallas_call | solution.py:562
  36.5 2.4 %collective-permute-done.10.low = f32[528,128]{1,0:T(8,128)S(1)} collective-permute-done((f32[528,128]{1,0:T(8,128)S(1)}, f32[528,128]{1,0:T(8,128)S(1)}, u32[]{:S(2)}, u32[]{:S(2)}) %collective-permute-start.10) | collective-permute-done | bytes 270368 | tf_op jit(solution)/shard_map/ppermute | solution.py:573
  38.9 2.7 %collective-permute-done.11.high = f32[528,128]{1,0:T(8,128)S(1)} collective-permute-done((f32[528,128]{1,0:T(8,128)S(1)}, f32[528,128]{1,0:T(8,128)S(1)}, u32[]{:S(2)}, u32[]{:S(2)}) %collective-permute-start.11) | collective-permute-done | bytes 270368 | tf_op jit(solution)/shard_map/ppermute | solution.py:573
  41.6 0.0 copy-done.8
  41.6 0.7 %shard_map.134 = (f32[192,512]{1,0:T(8,128)S(1)}, f32[288,128]{1,0:T(8,128)S(1)}, f32[72,128]{1,0:T(8,128)S(1)}, f32[72,128]{1,0:T(8,128)S(1)}) custom-call(f32[192,512]{1,0:T(8,128)S(1)} %shard_map.133.rough, f32[192,512]{1,0:T(8,128)S(1)} %get-tuple-element.47.refs_1_.flat, f32[64,512]{1,0:T(8,128)S(1)} %get-tuple-element.33.refs_1_.thick.refs_2_, ...), custom_call_target="tpu_custom_call" | custom-call | tf_op jit(solution)/shard_map/pallas_call | solution.py:562
  42.4 0.4 collective-permute-start.13
  42.8 1.3 %collective-permute-start.12 = (f32[288,128]{1,0:T(8,128)S(1)}, f32[288,128]{1,0:T(8,128)S(1)}, u32[]{:S(2)}, u32[]{:S(2)}) collective-permute-start(f32[288,128]{1,0:T(8,128)S(1)} %get-tuple-element.52.near), channel_id=1, source_target_pairs={{0,1},{1,2},{2,3},{3,4},{4,5},{5,6},{6,7},{7,0},{8,9},{9,10},{10,1... | collective-permute-start | bytes 442376 | tf_op jit(solution)/shard_map/ppermute | solution.py:573
  44.1 0.8 %collective-permute-start.14 = (f32[72,128]{1,0:T(8,128)S(1)}, f32[72,128]{1,0:T(8,128)S(1)}, u32[]{:S(2)}, u32[]{:S(2)}) collective-permute-start(f32[72,128]{1,0:T(8,128)S(1)} %get-tuple-element.53), channel_id=1, source_target_pairs={{0,2},{1,3},{2,4},{3,5},{4,6},{5,7},{6,0},{7,1},{8,10},{9,11},{10,... | collective-permute-start | bytes 110600 | tf_op jit(solution)/shard_map/ppermute | solution.py:573
  44.9 3.4 %collective-permute-start.15 = (f32[72,128]{1,0:T(8,128)S(1)}, f32[72,128]{1,0:T(8,128)S(1)}, u32[]{:S(2)}, u32[]{:S(2)}) collective-permute-start(f32[72,128]{1,0:T(8,128)S(1)} %get-tuple-element.54), channel_id=1, source_target_pairs={{0,6},{1,7},{2,0},{3,1},{4,2},{5,3},{6,4},{7,5},{8,14},{9,15},{10,... | collective-permute-start | bytes 110600 | tf_op jit(solution)/shard_map/ppermute | solution.py:573
  48.3 3.3 %collective-permute-done.14.low_two = f32[72,128]{1,0:T(8,128)S(1)} collective-permute-done((f32[72,128]{1,0:T(8,128)S(1)}, f32[72,128]{1,0:T(8,128)S(1)}, u32[]{:S(2)}, u32[]{:S(2)}) %collective-permute-start.14) | collective-permute-done | bytes 36896 | tf_op jit(solution)/shard_map/ppermute | solution.py:573
  51.6 0.0 collective-permute-done.15.high_two
  51.6 0.0 collective-permute-done.13.high_one
  51.6 0.0 collective-permute-done.12.low_one
  51.6 0.0 copy-done.9
  51.6 0.3 shard_map.135
  51.9 0.1 collective-permute-start.16
  52.0 5.2 %collective-permute-start.17 = (f32[8,2688]{1,0:T(8,128)S(1)}, f32[8,2688]{1,0:T(8,128)S(1)}, u32[]{:S(2)}, u32[]{:S(2)}) collective-permute-start(f32[8,2688]{1,0:T(8,128)S(1)} %get-tuple-element.57), channel_id=1, source_target_pairs={{0,248},{8,0},{16,8},{24,16},{32,24},{40,32},{48,40},{56,48},{64,5... | collective-permute-start | bytes 258056 | tf_op jit(solution)/shard_map/ppermute | solution.py:573
  57.2 0.0 copy-done.3
  57.2 1.4 %shard_map.136.partial = f32[128,1024]{1,0:T(8,128)S(1)} custom-call(f32[72,1792]{1,0:T(8,128)S(1)} %get-tuple-element.55.ext, f32[128,288]{1,0:T(8,128)S(1)} %copy-done.3), custom_call_target="tpu_custom_call" | custom-call | tf_op jit(solution)/shard_map/pallas_call | solution.py:562
  58.6 1.2 %collective-permute-done.16.left = f32[8,2688]{1,0:T(8,128)S(1)} collective-permute-done((f32[8,2688]{1,0:T(8,128)S(1)}, f32[8,2688]{1,0:T(8,128)S(1)}, u32[]{:S(2)}, u32[]{:S(2)}) %collective-permute-start.16) | collective-permute-done | bytes 86048 | tf_op jit(solution)/shard_map/ppermute | solution.py:573
  59.9 0.0 collective-permute-done.17.right
  59.9 0.0 copy-done.7
  59.9 1.5 %shard_map.137 = f32[3,64,4,128]{3,2,1,0:T(4,128)} custom-call(f32[128,1024]{1,0:T(8,128)S(1)} %shard_map.136.partial, f32[8,2688]{1,0:T(8,128)S(1)} %collective-permute-done.16.left, f32[8,2688]{1,0:T(8,128)S(1)} %collective-permute-done.17.right, f32[192,512]{1,0:T(8,128)S(1)} %get-tuple-element.58.section, bf16[128,384]{1,0:T(8,128)(2,1)S(1)} %copy-done.7), custom_call_target="tpu_custom_call" | custom-call | tf_op jit(solution)/shard_map/pallas_call | solution.py:562
  (5 shorter events, 0.0 us)
Async XLA Ops:
  0.0 11.9 %copy-start.1 = (f32[128,64]{1,0:T(8,128)S(1)}, f32[128,64]{1,0:T(8,128)}, u32[]{:S(2)}) copy-start(f32[128,64]{1,0:T(8,128)} %constant.22.clone.refs_2_.refs_3_) | copy-start | bytes 98308
  1.5 11.8 %collective-permute-start.2 = (f32[256,256]{1,0:T(8,128)S(1)}, f32[256,256]{1,0:T(8,128)S(1)}, u32[]{:S(2)}, u32[]{:S(2)}) collective-permute-start(f32[256,256]{1,0:T(8,128)S(1)} %get-tuple-element.36), channel_id=1, source_target_pairs={{0,1},{1,2},{2,3},{3,4},{4,5},{5,6},{6,7},{7,0},{8,9},{9,10},{10,1... | collective-permute-start | bytes 786440 | tf_op jit(solution)/shard_map/ppermute | solution.py:573
  4.2 9.1 %collective-permute-start.3 = (f32[256,256]{1,0:T(8,128)S(1)}, f32[256,256]{1,0:T(8,128)S(1)}, u32[]{:S(2)}, u32[]{:S(2)}) collective-permute-start(f32[256,256]{1,0:T(8,128)S(1)} %get-tuple-element.37), channel_id=1, source_target_pairs={{0,7},{1,0},{2,1},{3,2},{4,3},{5,4},{6,5},{7,6},{8,15},{9,8},{10,9... | collective-permute-start | bytes 786440 | tf_op jit(solution)/shard_map/ppermute | solution.py:573
  4.7 8.5 %collective-permute-start = (f32[16,512]{1,0:T(8,128)S(1)}, f32[16,512]{1,0:T(8,128)S(1)}, u32[]{:S(2)}, u32[]{:S(2)}) collective-permute-start(f32[16,512]{1,0:T(8,128)S(1)} %get-tuple-element.34), channel_id=1, source_target_pairs={{0,8},{8,16},{16,24},{24,32},{32,40},{40,48},{48,56},{56,64},{64,7... | collective-permute-start | bytes 98312 | tf_op jit(solution)/shard_map/ppermute | solution.py:573
  5.4 7.9 %collective-permute-start.1 = (f32[16,512]{1,0:T(8,128)S(1)}, f32[16,512]{1,0:T(8,128)S(1)}, u32[]{:S(2)}, u32[]{:S(2)}) collective-permute-start(f32[16,512]{1,0:T(8,128)S(1)} %get-tuple-element.35), channel_id=1, source_target_pairs={{0,248},{8,0},{16,8},{24,16},{32,24},{40,32},{48,40},{56,48},{64,5... | collective-permute-start | bytes 98312 | tf_op jit(solution)/shard_map/ppermute | solution.py:573
  11.9 1.3 %copy-start = (bf16[3,128,96]{2,1,0:T(8,128)(2,1)S(1)}, bf16[3,128,96]{2,1,0:T(8,128)(2,1)}, u32[]{:S(2)}) copy-start(bf16[3,128,96]{2,1,0:T(8,128)(2,1)} %constant.24.clone.slopes) | copy-start | bytes 221188
  11.9 1.3 %copy-start.5 = (bf16[72,192]{1,0:T(8,128)(2,1)S(1)}, bf16[72,192]{1,0:T(8,128)(2,1)}, u32[]{:S(2)}) copy-start(bf16[72,192]{1,0:T(8,128)(2,1)} %constant.27.clone.lateral) | copy-start | bytes 82948
  12.9 11.3 %copy-start.4 = (bf16[32,576]{1,0:T(8,128)(2,1)S(1)}, bf16[32,576]{1,0:T(8,128)(2,1)}, u32[]{:S(2)}) copy-start(bf16[32,576]{1,0:T(8,128)(2,1)} %constant.26.clone.moments) | copy-start | bytes 110596
  13.3 10.9 %copy-start.10 = (bf16[64,240]{1,0:T(8,128)(2,1)S(1)}, bf16[64,240]{1,0:T(8,128)(2,1)}, u32[]{:S(2)}) copy-start(bf16[64,240]{1,0:T(8,128)(2,1)} %constant.28.clone.source) | copy-start | bytes 92164
  13.8 10.3 %collective-permute-start.4 = (f32[480,128]{1,0:T(8,128)S(1)}, f32[480,128]{1,0:T(8,128)S(1)}, u32[]{:S(2)}, u32[]{:S(2)}) collective-permute-start(f32[480,128]{1,0:T(8,128)S(1)} %get-tuple-element.40), channel_id=1, source_target_pairs={{0,1},{1,2},{2,3},{3,4},{4,5},{5,6},{6,7},{7,0},{8,9},{9,10},{10,1... | collective-permute-start | bytes 737288 | tf_op jit(solution)/shard_map/ppermute | solution.py:573
  16.4 7.7 %collective-permute-start.5 = (f32[480,128]{1,0:T(8,128)S(1)}, f32[480,128]{1,0:T(8,128)S(1)}, u32[]{:S(2)}, u32[]{:S(2)}) collective-permute-start(f32[480,128]{1,0:T(8,128)S(1)} %get-tuple-element.41), channel_id=1, source_target_pairs={{0,7},{1,0},{2,1},{3,2},{4,3},{5,4},{6,5},{7,6},{8,15},{9,8},{10,9... | collective-permute-start | bytes 737288 | tf_op jit(solution)/shard_map/ppermute | solution.py:573
  16.5 7.6 %collective-permute-start.6 = (f32[200,128]{1,0:T(8,128)S(1)}, f32[200,128]{1,0:T(8,128)S(1)}, u32[]{:S(2)}, u32[]{:S(2)}) collective-permute-start(f32[200,128]{1,0:T(8,128)S(1)} %get-tuple-element.42), channel_id=1, source_target_pairs={{0,2},{1,3},{2,4},{3,5},{4,6},{5,7},{6,0},{7,1},{8,10},{9,11},{10,... | collective-permute-start | bytes 307208 | tf_op jit(solution)/shard_map/ppermute | solution.py:573
  17.7 6.4 %collective-permute-start.7 = (f32[200,128]{1,0:T(8,128)S(1)}, f32[200,128]{1,0:T(8,128)S(1)}, u32[]{:S(2)}, u32[]{:S(2)}) collective-permute-start(f32[200,128]{1,0:T(8,128)S(1)} %get-tuple-element.43), channel_id=1, source_target_pairs={{0,6},{1,7},{2,0},{3,1},{4,2},{5,3},{6,4},{7,5},{8,14},{9,15},{10,... | collective-permute-start | bytes 307208 | tf_op jit(solution)/shard_map/ppermute | solution.py:573
  24.2 5.6 %copy-start.2 = (f32[160,288]{1,0:T(8,128)S(1)}, f32[160,288]{1,0:T(8,128)}, u32[]{:S(2)}) copy-start(f32[160,288]{1,0:T(8,128)} %constant.23.clone.solve) | copy-start | bytes 552964
  24.6 7.3 %collective-permute-start.8 = (f32[8,3584]{1,0:T(8,128)S(1)}, f32[8,3584]{1,0:T(8,128)S(1)}, u32[]{:S(2)}, u32[]{:S(2)}) collective-permute-start(f32[8,3584]{1,0:T(8,128)S(1)} %get-tuple-element.45), channel_id=1, source_target_pairs={{0,8},{8,16},{16,24},{24,32},{32,40},{40,48},{48,56},{56,64},{64,7... | collective-permute-start | bytes 344072 | tf_op jit(solution)/shard_map/ppermute | solution.py:573
  24.7 7.2 %collective-permute-start.9 = (f32[8,3584]{1,0:T(8,128)S(1)}, f32[8,3584]{1,0:T(8,128)S(1)}, u32[]{:S(2)}, u32[]{:S(2)}) collective-permute-start(f32[8,3584]{1,0:T(8,128)S(1)} %get-tuple-element.46), channel_id=1, source_target_pairs={{0,248},{8,0},{16,8},{24,16},{32,24},{40,32},{48,40},{56,48},{64,5... | collective-permute-start | bytes 344072 | tf_op jit(solution)/shard_map/ppermute | solution.py:573
  29.8 2.1 %copy-start.6 = (bf16[160,384]{1,0:T(8,128)(2,1)S(1)}, bf16[160,384]{1,0:T(8,128)(2,1)}, u32[]{:S(2)}) copy-start(bf16[160,384]{1,0:T(8,128)(2,1)} %constant.29.clone.solve) | copy-start | bytes 368644
  32.7 6.3 %collective-permute-start.10 = (f32[528,128]{1,0:T(8,128)S(1)}, f32[528,128]{1,0:T(8,128)S(1)}, u32[]{:S(2)}, u32[]{:S(2)}) collective-permute-start(f32[528,128]{1,0:T(8,128)S(1)} %get-tuple-element.50), channel_id=1, source_target_pairs={{0,1},{1,2},{2,3},{3,4},{4,5},{5,6},{6,7},{7,0},{8,9},{9,10},{10,1... | collective-permute-start | bytes 811016 | tf_op jit(solution)/shard_map/ppermute | solution.py:573
  35.5 6.1 %collective-permute-start.11 = (f32[528,128]{1,0:T(8,128)S(1)}, f32[528,128]{1,0:T(8,128)S(1)}, u32[]{:S(2)}, u32[]{:S(2)}) collective-permute-start(f32[528,128]{1,0:T(8,128)S(1)} %get-tuple-element.51), channel_id=1, source_target_pairs={{0,7},{1,0},{2,1},{3,2},{4,3},{5,4},{6,5},{7,6},{8,15},{9,8},{10,9... | collective-permute-start | bytes 811016 | tf_op jit(solution)/shard_map/ppermute | solution.py:573
  35.5 6.1 %copy-start.8 = (bf16[128,240]{1,0:T(8,128)(2,1)S(1)}, bf16[128,240]{1,0:T(8,128)(2,1)}, u32[]{:S(2)}) copy-start(bf16[128,240]{1,0:T(8,128)(2,1)} %constant.25.clone.rim) | copy-start | bytes 184324
  41.6 10.0 %copy-start.9 = (bf16[64,240]{1,0:T(8,128)(2,1)S(1)}, bf16[64,240]{1,0:T(8,128)(2,1)}, u32[]{:S(2)}) copy-start(bf16[64,240]{1,0:T(8,128)(2,1)} %constant.31.clone.source) | copy-start | bytes 92164
  42.4 9.2 %collective-permute-start.13 = (f32[288,128]{1,0:T(8,128)S(1)}, f32[288,128]{1,0:T(8,128)S(1)}, u32[]{:S(2)}, u32[]{:S(2)}) collective-permute-start(f32[288,128]{1,0:T(8,128)S(1)} %get-tuple-element.52.near), channel_id=1, source_target_pairs={{0,7},{1,0},{2,1},{3,2},{4,3},{5,4},{6,5},{7,6},{8,15},{9,8},{10,9... | collective-permute-start | bytes 442376 | tf_op jit(solution)/shard_map/ppermute | solution.py:573
  42.8 8.8 %collective-permute-start.12 = (f32[288,128]{1,0:T(8,128)S(1)}, f32[288,128]{1,0:T(8,128)S(1)}, u32[]{:S(2)}, u32[]{:S(2)}) collective-permute-start(f32[288,128]{1,0:T(8,128)S(1)} %get-tuple-element.52.near), channel_id=1, source_target_pairs={{0,1},{1,2},{2,3},{3,4},{4,5},{5,6},{6,7},{7,0},{8,9},{9,10},{10,1... | collective-permute-start | bytes 442376 | tf_op jit(solution)/shard_map/ppermute | solution.py:573
  44.1 7.5 %collective-permute-start.14 = (f32[72,128]{1,0:T(8,128)S(1)}, f32[72,128]{1,0:T(8,128)S(1)}, u32[]{:S(2)}, u32[]{:S(2)}) collective-permute-start(f32[72,128]{1,0:T(8,128)S(1)} %get-tuple-element.53), channel_id=1, source_target_pairs={{0,2},{1,3},{2,4},{3,5},{4,6},{5,7},{6,0},{7,1},{8,10},{9,11},{10,... | collective-permute-start | bytes 110600 | tf_op jit(solution)/shard_map/ppermute | solution.py:573
  44.9 12.3 %copy-start.3 = (f32[128,288]{1,0:T(8,128)S(1)}, f32[128,288]{1,0:T(8,128)}, u32[]{:S(2)}) copy-start(f32[128,288]{1,0:T(8,128)} %constant.30.clone.solve) | copy-start | bytes 442372
  44.9 6.7 %collective-permute-start.15 = (f32[72,128]{1,0:T(8,128)S(1)}, f32[72,128]{1,0:T(8,128)S(1)}, u32[]{:S(2)}, u32[]{:S(2)}) collective-permute-start(f32[72,128]{1,0:T(8,128)S(1)} %get-tuple-element.54), channel_id=1, source_target_pairs={{0,6},{1,7},{2,0},{3,1},{4,2},{5,3},{6,4},{7,5},{8,14},{9,15},{10,... | collective-permute-start | bytes 110600 | tf_op jit(solution)/shard_map/ppermute | solution.py:573
  51.9 7.9 %collective-permute-start.16 = (f32[8,2688]{1,0:T(8,128)S(1)}, f32[8,2688]{1,0:T(8,128)S(1)}, u32[]{:S(2)}, u32[]{:S(2)}) collective-permute-start(f32[8,2688]{1,0:T(8,128)S(1)} %get-tuple-element.56), channel_id=1, source_target_pairs={{0,8},{8,16},{16,24},{24,32},{32,40},{40,48},{48,56},{56,64},{64,7... | collective-permute-start | bytes 258056 | tf_op jit(solution)/shard_map/ppermute | solution.py:573
  52.0 7.8 %collective-permute-start.17 = (f32[8,2688]{1,0:T(8,128)S(1)}, f32[8,2688]{1,0:T(8,128)S(1)}, u32[]{:S(2)}, u32[]{:S(2)}) collective-permute-start(f32[8,2688]{1,0:T(8,128)S(1)} %get-tuple-element.57), channel_id=1, source_target_pairs={{0,248},{8,0},{16,8},{24,16},{32,24},{40,32},{48,40},{56,48},{64,5... | collective-permute-start | bytes 258056 | tf_op jit(solution)/shard_map/ppermute | solution.py:573
  57.2 2.6 %copy-start.7 = (bf16[128,384]{1,0:T(8,128)(2,1)S(1)}, bf16[128,384]{1,0:T(8,128)(2,1)}, u32[]{:S(2)}) copy-start(bf16[128,384]{1,0:T(8,128)(2,1)} %constant.32.clone.solve) | copy-start | bytes 294916

commit v6 on v4

v6 whole, which is shorter than its diff:
```python
import functools

import jax
import jax.numpy as jnp
import ml_dtypes
import numpy as np
from jax import lax
from jax.experimental import pallas as pl
from jax.experimental.pallas import tpu as pltpu
from jax.sharding import PartitionSpec as P

SWEEPS = 4
ROWS = 4
LANES = 128
time_step = 0.1
highest = lax.Precision.HIGHEST
PAD_V = 16
PAD_S = 16
PAD_M = 8
GROUP = 8
PACK = 16
RANK_V = 3
RANK_M = 2


def symbols(length):
    w = 2.0 * np.pi * np.arange(length) / length
    first = (14.0 / 9.0 * np.sin(w) + np.sin(2.0 * w) / 18.0) / (1.0 + 2.0 / 3.0 * np.cos(w))
    second = (24.0 / 11.0 * (1.0 - np.cos(w)) + 3.0 / 22.0 * (1.0 - np.cos(2.0 * w))) / (
        1.0 + 4.0 / 11.0 * np.cos(w)
    )
    return 1j * first, -second, 1.0 / (4.0 + second)


def block_of(symbol, cells, offset):
    kernel = np.fft.ifft(symbol).real
    at = np.arange(cells)
    return kernel[(at[:, None] - (at[None, :] + offset * cells)) % len(kernel)]


def low_rank(stack, rank):
    left, scale, right = np.linalg.svd(stack, full_matrices=False)
    return left[:, :rank] * scale[:rank], right[:rank]


@functools.lru_cache(None)
def tables(length, cells, last):
    first, second, inverse = symbols(length)
    at = lambda symbol, offset: block_of(symbol, cells, offset)
    from_left, take_left = low_rank(np.concatenate([at(first, -1), at(second, -1)]), RANK_V)
    from_right, take_right = low_rank(np.concatenate([at(first, 1), at(second, 1)]), RANK_V)
    own = np.concatenate([at(first, 0), at(second, 0)])
    slopes = np.zeros((3, 2 * cells, 2 * PAD_V))
    moments = np.zeros((2 * PAD_V, 3 * cells))
    for c in range(3):
        rows = slice(RANK_V * c, RANK_V * (c + 1))
        slopes[c, :, :PAD_V][:, rows] = from_left
        slopes[c, :, PAD_V:][:, rows] = from_right
        moments[rows, cells * c : cells * (c + 1)] = take_left
        moments[PAD_V:][rows, cells * c : cells * (c + 1)] = take_right
    m_left, t_left = low_rank(at(first, -1), RANK_M)
    m_right, t_right = low_rank(at(first, 1), RANK_M)
    lateral = np.zeros((cells + PAD_M, cells))
    lateral[:cells] = at(first, 0)
    lateral[cells : cells + RANK_M] = t_left
    lateral[cells + RANK_M : cells + 2 * RANK_M] = t_right
    powers = [inverse ** (j + 1) for j in range(SWEEPS)]
    stacked = [p for p in powers] + [first * p for p in powers]
    count = len(stacked)
    RANK_S = 2 * SWEEPS + (1 if last else 3)
    kept = [] if last else stacked
    s_left, q_left = low_rank(
        np.concatenate([at(p, -1) for p in stacked] + [take_left @ at(p, 0) for p in kept]), RANK_S
    )
    s_right, q_right = low_rank(
        np.concatenate([at(p, 1) for p in stacked] + [take_right @ at(p, 0) for p in kept]), RANK_S
    )
    e_left, e_right = s_left[count * cells :], s_right[count * cells :]
    source = np.zeros((8 * GROUP, cells + PAD_M))
    for side, q in enumerate((q_left, q_right)):
        rows = np.zeros((PAD_S, cells + PAD_M))
        rows[:RANK_S, :cells] = q
        at_m = cells + RANK_M * side
        rows[RANK_S : RANK_S + RANK_M, at_m : at_m + RANK_M] = np.eye(RANK_M)
        top = 4 * GROUP * side
        source[top : top + 8] = rows[:8]
        source[top + 8 : top + 12] = rows[8:12]
        source[top + 20 : top + 24] = rows[8:12]
        source[top + 24] = rows[12]
    near, wide = cells + PAD_M, 2 * PAD_S
    height = 2 * cells + (0 if last else 4 * GROUP)
    solve_own = np.zeros((height, SWEEPS * near))
    solve_sides = np.zeros((height, SWEEPS * wide))
    for j in range(SWEEPS):
        for half in range(2):
            index = half * SWEEPS + j
            rows = slice(cells * index, cells * (index + 1))
            edge = slice(RANK_V * index, RANK_V * (index + 1))
            center = at(stacked[index], 0)
            by_left, by_right = s_left[rows], s_right[rows]
            mine, sides = np.zeros((cells, near)), np.zeros((cells, wide))
            mine[:, :cells] = center
            mine[:, cells : cells + RANK_M] = by_right @ (q_right @ m_left)
            mine[:, cells + RANK_M : cells + 2 * RANK_M] = by_left @ (q_left @ m_right)
            sides[:, :RANK_S] = by_left
            sides[:, RANK_S : RANK_S + RANK_M] = center @ m_left
            sides[:, PAD_S : PAD_S + RANK_S] = by_right
            sides[:, PAD_S + RANK_S : PAD_S + RANK_S + RANK_M] = center @ m_right
            solve_own[cells * half : cells * (half + 1), near * j : near * (j + 1)] = -mine
            solve_sides[cells * half : cells * (half + 1), wide * j : wide * (j + 1)] = -sides
            for side in range(0 if last else 2):
                mine, sides = np.zeros((RANK_V, near)), np.zeros((RANK_V, wide))
                if side == 0:
                    back = take_left @ by_right @ q_right
                    mine[:, cells + RANK_M : cells + 2 * RANK_M] = take_left @ center @ m_right
                    sides[:, :RANK_S] = e_left[edge]
                else:
                    back = take_right @ by_left @ q_left
                    mine[:, cells : cells + RANK_M] = take_right @ center @ m_left
                    sides[:, PAD_S : PAD_S + RANK_S] = e_right[edge]
                mine[:, :cells] = back
                sides[:, RANK_S : RANK_S + RANK_M] = back @ m_left
                sides[:, PAD_S + RANK_S : PAD_S + RANK_S + RANK_M] = back @ m_right
                top = 2 * cells + GROUP * (2 * side + half)
                solve_own[top : top + RANK_V, near * j : near * (j + 1)] = -mine
                solve_sides[top : top + RANK_V, wide * j : wide * (j + 1)] = -sides
    full = np.concatenate([np.broadcast_to(own, (3,) + own.shape), slopes], axis=2)
    plain, split = (own, solve_own), (slopes, full, moments, lateral, source, solve_sides)
    return [x.astype(np.float32) for x in plain] + [split_table(x.astype(np.float32)) for x in split]


def dot(a, b):
    return jnp.dot(a, b, precision=highest, preferred_element_type=jnp.float32)


def halves(x):
    high = x.astype(jnp.bfloat16)
    return high, (x - high.astype(jnp.float32)).astype(jnp.bfloat16)


def split_table(table):
    gap = -table.shape[-1] % PACK
    table = np.pad(table, [(0, 0)] * (table.ndim - 1) + [(0, gap)])
    high = table.astype(ml_dtypes.bfloat16)
    low = (table - high.astype(np.float32)).astype(ml_dtypes.bfloat16)
    return np.concatenate([high, high, low], axis=-1)


def split_dot(table, x):
    gap = -x.shape[0] % PACK
    if gap:
        x = jnp.concatenate([x, jnp.zeros((gap, x.shape[1]), x.dtype)], axis=0)
    high, low = halves(x)
    return jnp.dot(table, jnp.concatenate([high, low, high], axis=0), preferred_element_type=jnp.float32)


class Extent:
    def __init__(self, margin):
        self.margin = margin
        self.reach = margin + SWEEPS - 1
        self.breadth = ROWS + 2 * self.reach
        self.packed = self.breadth + self.breadth // 2
        self.found = ROWS + 2 * margin


FIRST, LAST = Extent(3), Extent(2)


DIFFERENCE = ((1, 2.0 / 3.0), (-1, -2.0 / 3.0), (2, -1.0 / 12.0), (-2, 1.0 / 12.0))
CURVE = ((1, 4.0 / 3.0), (-1, 4.0 / 3.0), (2, -1.0 / 12.0), (-2, -1.0 / 12.0))


def lane(r, count=1):
    return slice(r * LANES, (r + count) * LANES)


def turned(tile, step):
    return pltpu.roll(tile, (-step) % LANES, 1)


def edge_masks():
    at = lax.axis_index("cross")
    last = lax.axis_size("cross") - 1
    flag = lambda test: jnp.where(test, 1.0, 0.0).astype(jnp.float32)
    return (flag(at >= 1), flag(at >= 2), flag(at <= last - 1), flag(at <= last - 2))


def masked(tile, e, masks):
    if e < -ROWS:
        return tile * masks[1]
    if e < 0:
        return tile * masks[0]
    if e >= 2 * ROWS:
        return tile * masks[3]
    if e >= ROWS:
        return tile * masks[2]
    return tile


def first_diff(up_one, down_one, up_two, down_two):
    return (8.0 * (up_one - down_one) - (up_two - down_two)) * (1.0 / 12.0)


def second_diff(middle, up_one, down_one, up_two, down_two):
    return (16.0 * (up_one + down_one) - (up_two + down_two) - 30.0 * middle) * (1.0 / 12.0)


def stream_slope(tile):
    return first_diff(turned(tile, 1), turned(tile, -1), turned(tile, 2), turned(tile, -2))


def open_kernel(
    cells, velocity, viscosity, moments, flat, thick, to_right, to_left, upward, downward, weights, sems
):
    copies = [pltpu.make_async_copy(moments, weights, sems.at[0])]
    for c in range(3):
        rows = slice(cells * c, cells * (c + 1))
        for r in range(ROWS):
            copies.append(
                pltpu.make_async_copy(velocity.at[c, :, r, :], flat.at[rows, lane(r)], sems.at[len(copies)])
            )
    apart = len(copies)
    for r in range(ROWS):
        copies.append(pltpu.make_async_copy(viscosity.at[:, r, :], thick.at[:, lane(r)], sems.at[len(copies)]))
    for copy in copies:
        copy.start()
    for copy in copies[:apart]:
        copy.wait()
    upward[...] = flat[:, lane(ROWS - 2, 2)]
    downward[...] = flat[:, lane(0, 2)]
    both = split_dot(weights[...], flat[...])
    to_right[...] = both[:PAD_V]
    to_left[...] = both[PAD_V:]
    for copy in copies[apart:]:
        copy.wait()


def weighed(weights, value_at, r, home):
    total = None
    for reach, factor in weights:
        if (0 <= r + reach < ROWS) == home:
            part = factor * value_at(r + reach)
            total = part if total is None else total + part
    return total


def rough_kernel(cells, flat, thick, own, rough):
    for c in range(3):
        rows = slice(cells * c, cells * (c + 1))
        at = lambda r: flat[rows, lane(r)]
        spanned = dot(own[...], flat[rows, :])
        for r in range(ROWS):
            here = at(r)
            up_one, down_one = turned(here, 1), turned(here, -1)
            up_two, down_two = turned(here, 2), turned(here, -2)
            carried = (
                flat[:cells, lane(r)] * first_diff(up_one, down_one, up_two, down_two)
                + flat[cells : 2 * cells, lane(r)] * weighed(DIFFERENCE, at, r, True)
                + flat[2 * cells :, lane(r)] * spanned[:cells, lane(r)]
            )
            spread = (
                (4.0 / 3.0) * (up_one + down_one)
                - (1.0 / 12.0) * (up_two + down_two)
                - 5.0 * here
                + weighed(CURVE, at, r, True)
                + spanned[cells:, lane(r)]
            )
            rough[rows, lane(r)] = here + time_step * (thick[:, lane(r)] * spread - carried)


def add_beyond(cells, rough, flat, thick, left, right, low, high, slopes, section):
    masks = edge_masks()
    sides = jnp.concatenate([left[...], right[...]], axis=0)
    for c in range(3):
        rows = slice(cells * c, cells * (c + 1))
        spanned = split_dot(slopes[c], sides)

        def beyond(r):
            if r < 0:
                return masked(low[rows, lane(r + 2)], r, masks)
            return masked(high[rows, lane(r - ROWS)], r, masks)

        for r in range(ROWS):
            spread = spanned[cells:, lane(r)] + weighed(CURVE, beyond, r, False)
            carried = flat[cells : 2 * cells, lane(r)] * weighed(DIFFERENCE, beyond, r, False)
            carried = carried + flat[2 * cells :, lane(r)] * spanned[:cells, lane(r)]
            section[rows, lane(r)] = rough[rows, lane(r)] + time_step * (thick[:, lane(r)] * spread - carried)


def slot(ref, cells, k):
    return ref.at[cells * k : cells * (k + 1), :]


def fill_slots(ref, cells, blocks, moments):
    for k, block in enumerate(blocks):
        slot(ref, cells, k)[...] = block
    for k, block in enumerate(moments):
        top = cells * len(blocks) + PAD_M * k
        ref[top : top + PAD_M, :] = block


def own_source(cells, section, lateral, parts):
    side = split_dot(lateral[...], section[2 * cells :, :])
    at = lambda r: section[cells : 2 * cells, lane(r)]
    blocks = []
    for r in range(ROWS):
        total = stream_slope(section[:cells, lane(r)]) + side[:cells, lane(r)] + weighed(DIFFERENCE, at, r, True)
        parts[:cells, lane(r)] = total
        blocks.append(total)
    parts[cells:, :] = side[cells:]
    moments = [side[cells:, lane(r)] for r in range(ROWS)]
    up = (2.0 / 3.0) * at(0) - (1.0 / 12.0) * at(1)
    down = (1.0 / 12.0) * at(ROWS - 2) - (2.0 / 3.0) * at(ROWS - 1)
    return blocks, moments, at, up, down


def tendency_kernel(
    cells, rough, flat, thick, left, right, low, high, slopes, lateral,
    section, parts, up_near, down_near, up_far, down_far,
):
    add_beyond(cells, rough, flat, thick, left, right, low, high, slopes, section)
    blocks, moments, at, up, down = own_source(cells, section, lateral, parts)
    row = lambda c, r: section[cells * c : cells * (c + 1), lane(r)]
    fill_slots(
        up_near, cells,
        blocks + [at(2), at(3), up, at(0), row(0, 2), row(0, 3), row(2, 2), row(2, 3)], moments,
    )
    fill_slots(
        down_near, cells,
        blocks + [at(0), at(1), down, at(3), row(0, 0), row(0, 1), row(2, 0), row(2, 1)], moments,
    )
    fill_slots(up_far, cells, blocks[2:] + [at(2), at(3)], moments[2:])
    fill_slots(down_far, cells, blocks[:2] + [at(0), at(1)], moments[:2])


def extend_source(cells, extent, near_slots, far_slots, parts, section, arrived, extra, ext):
    low_one, high_one, low_two, high_two = arrived
    masks = edge_masks()
    span, tail = slice(0, cells), slice(cells, cells + PAD_M)
    outer = extent.reach - ROWS
    pick = lambda ref, k: slot(ref, cells, k)[...]

    def joined(e):
        if 0 <= e < ROWS:
            return parts[span, lane(e)], parts[tail, lane(e)]
        if e < -ROWS or e >= 2 * ROWS:
            given, k, count = (low_two, e + extent.reach, far_slots) if e < 0 else (high_two, e - 2 * ROWS, far_slots)
        else:
            given, k, count = (low_one, e + ROWS, near_slots) if e < 0 else (high_one, e - ROWS, near_slots)
        top = count * cells + PAD_M * k
        return pick(given, k), given[top : top + PAD_M, :]

    def across(e, home):
        if e // ROWS == home // ROWS or home // ROWS in (-2, 2):
            return None
        if e < -ROWS:
            return masked(pick(low_two, outer + e + ROWS + 2), e, masks)
        if e < 0:
            return masked(pick(low_one, ROWS + e + 2), e, masks)
        if e < ROWS:
            return section[cells : 2 * cells, lane(e)]
        if e < 2 * ROWS:
            return masked(pick(high_one, e), e, masks)
        return masked(pick(high_two, outer + e - 2 * ROWS), e, masks)

    for e in range(-extent.reach, ROWS + extent.reach):
        total, side = joined(e)
        if e == -ROWS - 1:
            total = total + pick(low_one, 6)
        if e == -ROWS - 2:
            total = total - (1.0 / 12.0) * pick(low_one, 7)
        if e == 2 * ROWS:
            total = total + pick(high_one, 6)
        if e == 2 * ROWS + 1:
            total = total + (1.0 / 12.0) * pick(high_one, 7)
        for reach, factor in DIFFERENCE:
            other = across(e + reach, e)
            if other is not None:
                total = total + factor * other
            if e + reach in extra:
                total = total + factor * extra[e + reach]
        ext[span, lane(e + extent.reach)] = masked(total, e, masks)
        ext[tail, lane(e + extent.reach)] = masked(side, e, masks)


def pack_moments(extent, both, to_right, to_left):
    for side, out in enumerate((to_right, to_left)):
        top = 4 * GROUP * side
        out[:, lane(0, extent.breadth)] = both[top : top + 8]
        for k in range(extent.breadth // 2):
            out[:, lane(extent.breadth + k)] = (
                both[top + 8 : top + 16, lane(2 * k)] + both[top + 16 : top + 24, lane(2 * k + 1)]
            )


def source_kernel(
    cells, parts, section, low_one, high_one, low_two, high_two, source, moments, ext, to_right, to_left
):
    extend_source(cells, FIRST, 12, 4, parts, section, (low_one, high_one, low_two, high_two), {}, ext)
    both = split_dot(source[...], ext[...])
    pack_moments(FIRST, both, to_right, to_left)
    held = split_dot(moments[...], section[...])
    for side, out in enumerate((to_right, to_left)):
        top, base = 4 * GROUP * side, PAD_V * side
        out[:, lane(FIRST.packed, ROWS)] = held[base : base + 8]
        out[:, lane(FIRST.packed + ROWS, 3)] = jnp.zeros((GROUP, 3 * LANES), jnp.float32)
        for e in range(FIRST.breadth + ROWS):
            value = (
                both[top + 24 : top + 25, lane(e)]
                if e < FIRST.breadth
                else held[base + 8 : base + 9, lane(e - FIRST.breadth)]
            )
            row, tile = e % GROUP, FIRST.packed + ROWS + e // GROUP
            out[row : row + 1, lane(tile)] = value


def last_source_kernel(
    cells, parts, section, mine, low_one, high_one, low_two, high_two, source, ext, fixed, to_right, to_left
):
    masks = edge_masks()
    pick = lambda ref, k: slot(ref, cells, k)[...]
    phi_first, phi_last, factor_first, factor_last = 7, 8, 9, 10
    below, above = masks[0], masks[2]
    below_two, above_two = masks[1], masks[3]
    extra = {
        0: pick(mine, factor_first) * pick(low_one, phi_first) * below,
        ROWS - 1: pick(mine, factor_last) * pick(high_one, phi_last) * above,
        -1: pick(low_one, factor_last) * pick(mine, phi_last) * below,
        -ROWS: pick(low_one, factor_first) * pick(low_two, 4) * below_two,
        -ROWS - 1: pick(low_two, 3) * pick(low_one, phi_last) * below_two,
        ROWS: pick(high_one, factor_first) * pick(mine, phi_first) * above,
        2 * ROWS - 1: pick(high_one, factor_last) * pick(high_two, 4) * above_two,
        2 * ROWS: pick(high_two, 3) * pick(high_one, phi_first) * above_two,
    }
    fixed[:cells, :] = extra[0]
    fixed[cells:, :] = extra[ROWS - 1]
    extend_source(cells, LAST, 11, 5, parts, section, (low_one, high_one, low_two, high_two), extra, ext)
    pack_moments(LAST, split_dot(source[...], ext[...]), to_right, to_left)


def climb(extent, levels, depth):
    masks = edge_masks()
    for j in range(1, SWEEPS):
        before = slice(depth * (j - 1), depth * j)
        after = slice(depth * j, depth * (j + 1))
        for e in range(-extent.reach + j, ROWS + extent.reach - j):
            k = e + extent.reach
            here = levels[before, lane(k)]
            beside = (
                turned(here, 1) + turned(here, -1) + levels[before, lane(k + 1)] + levels[before, lane(k - 1)]
            )
            levels[after, lane(k)] = masked(beside, e, masks)
    return levels[:, lane(SWEEPS - 1, extent.found)]


def home_kernel(extent, ext, solve, partial, levels):
    depth = ext.shape[0]
    levels[:depth, :] = ext[...]
    partial[...] = dot(solve[...], climb(extent, levels, depth))


def spare(given, e):
    row, tile = e % GROUP, FIRST.packed + ROWS + e // GROUP
    return given[row : row + 1, lane(tile)]


def finish(extent, partial, left, right, solve, levels):
    for side, given in enumerate((left, right)):
        top = PAD_S * side
        levels[top : top + 8, :] = given[:, lane(0, extent.breadth)]
        for e in range(extent.breadth):
            tile = given[:, lane(extent.breadth + e // 2)]
            levels[top + 8 : top + 16, lane(e)] = pltpu.roll(tile, 4, 0) if e % 2 else tile
            if extent is FIRST:
                levels[top + 12 : top + 13, lane(e)] = spare(given, e)
    return partial[...] + split_dot(solve[...], climb(extent, levels, 2 * PAD_S))


def gradient(extent, found, c, rows, slope_rows, r):
    masks = edge_masks()
    phi = lambda r: masked(found[rows, lane(r + extent.margin)], r, masks)
    if c == 0:
        return stream_slope(phi(r))
    if c == 1:
        inside = lambda r: -extent.margin <= r < ROWS + extent.margin
        return sum(factor * phi(r + reach) for reach, factor in DIFFERENCE if inside(r + reach))
    return found[slope_rows, lane(r + extent.margin)]


def middle_kernel(
    cells, partial, left, right, section, solve, low_one, high_one, start, thick, full, lateral,
    following, parts, up_near, down_near, up_far, down_far, levels, flat, rim, sides,
):
    masks = edge_masks()
    found = finish(FIRST, partial, left, right, solve, levels)
    home, home_slope = slice(0, cells), slice(cells, 2 * cells)
    outer = (-2, -1, ROWS, ROWS + 1)
    for c in range(3):
        rows = slice(cells * c, cells * (c + 1))
        for r in range(ROWS):
            flat[rows, lane(r)] = section[rows, lane(r)] - gradient(FIRST, found, c, home, home_slope, r)
        first = (8, 4, 10)[c]
        for k, r in enumerate(outer):
            value = slot(low_one if r < 0 else high_one, cells, first + k % 2)[...]
            value = value - gradient(FIRST, found, c, home, home_slope, r)
            rim[rows, lane(k)] = masked(value, r, masks)
    for side, given in enumerate((left, right)):
        base, top = PAD_V * side, 2 * cells + 2 * GROUP * side
        phi_rows, slope_rows = slice(top, top + GROUP), slice(top + GROUP, top + 2 * GROUP)
        sides[base : base + GROUP, :] = given[:, lane(FIRST.packed, ROWS)]
        sides[base + GROUP : base + PAD_V, :] = jnp.zeros((PAD_V - GROUP, ROWS * LANES), jnp.float32)
        for r in range(ROWS):
            sides[base + GROUP : base + GROUP + 1, lane(r)] = spare(given, FIRST.breadth + r)
            for c in range(3):
                rows = slice(base + RANK_V * c, base + RANK_V * (c + 1))
                change = gradient(FIRST, found, c, phi_rows, slope_rows, r)[:RANK_V]
                sides[rows, lane(r)] = sides[rows, lane(r)] - change

    def tile(c, r):
        rows = slice(cells * c, cells * (c + 1))
        return flat[rows, lane(r)] if 0 <= r < ROWS else rim[rows, lane(r + 2 if r < 0 else r - 2)]

    for c in range(3):
        rows = slice(cells * c, cells * (c + 1))
        spanned = split_dot(full[c], jnp.concatenate([flat[rows, :], sides[...]], axis=0))
        for r in range(ROWS):
            here = tile(c, r)
            up_one, down_one = turned(here, 1), turned(here, -1)
            up_two, down_two = turned(here, 2), turned(here, -2)
            carried = (
                tile(0, r) * first_diff(up_one, down_one, up_two, down_two)
                + tile(1, r) * sum(factor * tile(c, r + reach) for reach, factor in DIFFERENCE)
                + tile(2, r) * spanned[:cells, lane(r)]
            )
            spread = (
                (4.0 / 3.0) * (up_one + down_one)
                - (1.0 / 12.0) * (up_two + down_two)
                - 5.0 * here
                + sum(factor * tile(c, r + reach) for reach, factor in CURVE)
                + spanned[cells:, lane(r)]
            )
            moved = here + time_step * (thick[:, lane(r)] * spread - carried)
            following[rows, lane(r)] = 0.5 * start[rows, lane(r)] + 0.5 * moved
    blocks, moments, at, up, down = own_source(cells, following, lateral, parts)
    phi = lambda r: found[:cells, lane(r + FIRST.margin)]
    scale = 0.5 * time_step / 144.0
    first = scale * (thick[:, lane(0)] + tile(1, 0))
    last = scale * (tile(1, ROWS - 1) - thick[:, lane(ROWS - 1)])
    owed = [phi(0), phi(ROWS - 1), first, last]
    fill_slots(up_near, cells, blocks + [at(2), at(3), up] + owed, moments)
    fill_slots(down_near, cells, blocks + [at(0), at(1), down] + owed, moments)
    fill_slots(up_far, cells, [blocks[3], at(2), at(3), last, phi(0)], moments[3:])
    fill_slots(down_far, cells, [blocks[0], at(0), at(1), first, phi(ROWS - 1)], moments[:1])


def last_kernel(cells, partial, left, right, section, fixed, solve, out, levels, staged, sems):
    found = finish(LAST, partial, left, right, solve, levels)
    copies = []
    for c in range(3):
        rows = slice(cells * c, cells * (c + 1))
        for r in range(ROWS):
            value = section[rows, lane(r)]
            if c == 1 and r in (0, ROWS - 1):
                value = value + fixed[cells * (r > 0) : cells * (1 + (r > 0)), :]
            value = value - gradient(LAST, found, c, slice(0, cells), slice(cells, 2 * cells), r)
            staged[rows, lane(r)] = value
            copies.append(
                pltpu.make_async_copy(staged.at[rows, lane(r)], out.at[c, :, r, :], sems.at[len(copies)])
            )
            copies[-1].start()
    for copy in copies:
        copy.wait()


def call(body, shapes, *args, scratch=(), **options):
    return pl.pallas_call(
        body,
        out_shape=[jax.ShapeDtypeStruct(s, jnp.float32) for s in shapes],
        scratch_shapes=scratch,
        compiler_params=pltpu.CompilerParams(vmem_limit_bytes=40 * 1024 * 1024),
        **options,
    )(*args)


def shifted(block, axis, step):
    count = lax.axis_size(axis)
    return lax.ppermute(block, axis, [(i, (i + step) % count) for i in range(count)])


def per_device(velocity, viscosity):
    components, cells, row_cells, columns = velocity.shape
    length = cells * lax.axis_size("span")
    own, first_own, slopes, full, moments, lateral, *first = (
        jnp.asarray(t) for t in tables(length, cells, False)
    )
    _, last_own, _, _, _, _, *last = (jnp.asarray(t) for t in tables(length, cells, True))
    width = row_cells * columns
    near = cells + PAD_M
    whole, edge, rim = (components * cells, width), (PAD_V, width), (components * cells, 2 * columns)

    def across(up_near, down_near, up_far, down_far):
        return (
            shifted(up_near, "cross", 1), shifted(down_near, "cross", -1),
            shifted(up_far, "cross", 2), shifted(down_far, "cross", -2),
        )

    def message(near_slots, far_slots, far_rows):
        near_shape = (near_slots * cells + row_cells * PAD_M, columns)
        far_shape = (far_slots * cells + far_rows * PAD_M, columns)
        return [near_shape] * 2 + [far_shape] * 2

    def levels(extent, depth):
        return pltpu.VMEM((SWEEPS * depth, extent.breadth * columns), jnp.float32)

    start, thick, to_right, to_left, upward, downward = call(
        functools.partial(open_kernel, cells),
        [whole, (cells, width), edge, edge, rim, rim],
        *(pltpu.with_memory_space_constraint(x, pltpu.HBM) for x in (velocity, viscosity, moments)),
        in_specs=[pl.BlockSpec(memory_space=pltpu.HBM)] * 3,
        scratch=[pltpu.VMEM(moments.shape, moments.dtype), pltpu.SemaphoreType.DMA((1 + 4 * ROWS,))],
    )
    left = shifted(to_right, "span", 1)
    right = shifted(to_left, "span", -1)
    low = shifted(upward, "cross", 1)
    high = shifted(downward, "cross", -1)
    (rough,) = call(functools.partial(rough_kernel, cells), [whole], start, thick, own)
    section, parts, *sent = call(
        functools.partial(tendency_kernel, cells),
        [whole, (near, width)] + message(12, 4, 2),
        rough, start, thick, left, right, low, high, slopes, lateral,
    )
    arrived = across(*sent)
    ext, to_right, to_left = call(
        functools.partial(source_kernel, cells),
        [(near, FIRST.breadth * columns)] + [(GROUP, (FIRST.packed + ROWS + 3) * columns)] * 2,
        parts, section, *arrived, first[0], moments,
    )
    left = shifted(to_right, "span", 1)
    right = shifted(to_left, "span", -1)
    (partial,) = call(
        functools.partial(home_kernel, FIRST),
        [(first_own.shape[0], FIRST.found * columns)],
        ext, first_own,
        scratch=[levels(FIRST, near)],
    )

    section, parts, *sent = call(
        functools.partial(middle_kernel, cells),
        [whole, (near, width)] + message(11, 5, 1),
        partial, left, right, section, first[1], *arrived[:2], start, thick, full, lateral,
        scratch=[
            levels(FIRST, 2 * PAD_S),
            pltpu.VMEM(whole, jnp.float32),
            pltpu.VMEM((components * cells, 4 * columns), jnp.float32),
            pltpu.VMEM((2 * PAD_V, width), jnp.float32),
        ],
    )
    arrived = across(*sent)
    ext, fixed, to_right, to_left = call(
        functools.partial(last_source_kernel, cells),
        [(near, LAST.breadth * columns), (2 * cells, columns)] + [(GROUP, LAST.packed * columns)] * 2,
        parts, section, sent[0], *arrived, last[0],
    )
    left = shifted(to_right, "span", 1)
    right = shifted(to_left, "span", -1)
    (partial,) = call(
        functools.partial(home_kernel, LAST),
        [(last_own.shape[0], LAST.found * columns)],
        ext, last_own,
        scratch=[levels(LAST, near)],
    )
    (out,) = call(
        functools.partial(last_kernel, cells),
        [velocity.shape],
        partial, left, right, section, fixed, last[1],
        scratch=[
            levels(LAST, 2 * PAD_S),
            pltpu.VMEM(whole, jnp.float32),
            pltpu.SemaphoreType.DMA((3 * ROWS,)),
        ],
        out_specs=[pl.BlockSpec(memory_space=pltpu.HBM)],
    )
    return out


def solution(mesh):
    in_specs = (P(None, "span", "cross", None), P("span", "cross", None))
    out_specs = P(None, "span", "cross", None)
    return jax.shard_map(
        per_device, mesh=mesh, in_specs=in_specs, out_specs=out_specs, check_vma=False
    )
```

time: 60.4 us -> 60.2 us (level)
  the two profiles are of different devices: /device:TPU:126 before, /device:TPU:1 now
where the time goes in v6:
time: 60.2 us; the launch traced here: 60.1 us
  starting transfers between devices  30.6 us (51%)
  waiting for transfers between devices  18.9 us (31%)
  Pallas kernels  10.1 us (17%)
    ppermute x16, starting transfers between devices, shifted(): lax.ppermute(block, axis, [(i, (i + step) % count) for i in range(count)])  30.6 us
    ppermute x16, waiting for transfers between devices, shifted(): lax.ppermute(block, axis, [(i, (i + step) % count) for i in range(count)])  18.9 us
    pallas_call x9, Pallas kernels, call(): pl.pallas_call(body, out_shape=[jax.ShapeDtypeStruct(s, jnp.float32) for...  10.1 us
  transfers between devices with their start and end apart: 16, of which 5 were waited for; matrix products, arithmetic and copies ran while one was open for 0% of the time, Pallas kernels for 7%

profile of v6, /device:TPU:1, one launch (start us, length us, event | category | flops | bytes accessed | tf_op | source)
XLA Modules:
  0.0 60.1 jit_solution(16482479558412745104)
XLA Ops:
  0.0 0.0 copy-start.8
  0.0 1.4 %shard_map.127 = (f32[192,512]{1,0:T(8,128)S(1)}, f32[64,512]{1,0:T(8,128)S(1)}, f32[16,512]{1,0:T(8,128)S(1)}, f32[16,512]{1,0:T(8,128)S(1)}, f32[192,256]{1,0:T(8,128)S(1)}, /*index=5*/f32[192,256]{1,0:T(8,128)S(1)}) custom-call(f32[3,64,4,128]{3,2,1,0:T(4,128)} %velocity.1, f32[64,4,128]{2,1,0:T(4,128)} %viscosity.1, bf16[32,576]{1,0:T(8,128)(2,1)} %constant.26.clone.moments), custom_call_target="tpu_custom_call" | custom-call | tf_op jit(solution)/shard_map/pallas_call | solution.py:576
  1.4 2.7 %collective-permute-start.2 = (f32[192,256]{1,0:T(8,128)S(1)}, f32[192,256]{1,0:T(8,128)S(1)}, u32[]{:S(2)}, u32[]{:S(2)}) collective-permute-start(f32[192,256]{1,0:T(8,128)S(1)} %get-tuple-element.34), channel_id=1, source_target_pairs={{0,1},{1,2},{2,3},{3,4},{4,5},{5,6},{6,7},{7,0},{8,9},{9,10},{10,1... | collective-permute-start | bytes 589832 | tf_op jit(solution)/shard_map/ppermute | solution.py:587
  4.1 0.6 collective-permute-start.3
  4.7 0.6 %collective-permute-start = (f32[16,512]{1,0:T(8,128)S(1)}, f32[16,512]{1,0:T(8,128)S(1)}, u32[]{:S(2)}, u32[]{:S(2)}) collective-permute-start(f32[16,512]{1,0:T(8,128)S(1)} %get-tuple-element.32), channel_id=1, source_target_pairs={{0,8},{8,16},{16,24},{24,32},{32,40},{40,48},{48,56},{56,64},{64,7... | collective-permute-start | bytes 98312 | tf_op jit(solution)/shard_map/ppermute | solution.py:587
  5.3 6.6 %collective-permute-start.1 = (f32[16,512]{1,0:T(8,128)S(1)}, f32[16,512]{1,0:T(8,128)S(1)}, u32[]{:S(2)}, u32[]{:S(2)}) collective-permute-start(f32[16,512]{1,0:T(8,128)S(1)} %get-tuple-element.33), channel_id=1, source_target_pairs={{0,248},{8,0},{16,8},{24,16},{32,24},{40,32},{48,40},{56,48},{64,5... | collective-permute-start | bytes 98312 | tf_op jit(solution)/shard_map/ppermute | solution.py:587
  11.9 0.0 copy-done.8
  11.9 0.0 copy-start.4
  11.9 0.0 copy-start.7
  11.9 0.9 %shard_map.128.rough = f32[192,512]{1,0:T(8,128)S(1)} custom-call(f32[192,512]{1,0:T(8,128)S(1)} %get-tuple-element.30.flat.start, f32[64,512]{1,0:T(8,128)S(1)} %get-tuple-element.31.thick, f32[128,64]{1,0:T(8,128)S(1)} %copy-done.8), custom_call_target="tpu_custom_call" | custom-call | tf_op jit(solution)/shard_map/pallas_call | solution.py:576
  12.8 0.0 copy-start.3
  12.8 0.3 collective-permute-done.left
  13.2 0.0 collective-permute-done.1.right
  13.2 0.0 collective-permute-done.2.low
  13.2 0.0 collective-permute-done.3.high
  13.2 0.0 copy-done.4
  13.2 0.0 copy-done.7
  13.2 0.0 copy-start.10
  13.2 0.5 shard_map.129
  13.8 2.6 %collective-permute-start.4 = (f32[800,128]{1,0:T(8,128)S(1)}, f32[800,128]{1,0:T(8,128)S(1)}, u32[]{:S(2)}, u32[]{:S(2)}) collective-permute-start(f32[800,128]{1,0:T(8,128)S(1)} %get-tuple-element.38), channel_id=1, source_target_pairs={{0,1},{1,2},{2,3},{3,4},{4,5},{5,6},{6,7},{7,0},{8,9},{9,10},{10,1... | collective-permute-start | bytes 1228808 | tf_op jit(solution)/shard_map/ppermute | solution.py:587
  16.4 0.1 collective-permute-start.5
  16.4 1.2 %collective-permute-start.6 = (f32[272,128]{1,0:T(8,128)S(1)}, f32[272,128]{1,0:T(8,128)S(1)}, u32[]{:S(2)}, u32[]{:S(2)}) collective-permute-start(f32[272,128]{1,0:T(8,128)S(1)} %get-tuple-element.40), channel_id=1, source_target_pairs={{0,2},{1,3},{2,4},{3,5},{4,6},{5,7},{6,0},{7,1},{8,10},{9,11},{10,... | collective-permute-start | bytes 417800 | tf_op jit(solution)/shard_map/ppermute | solution.py:587
  17.7 1.4 %collective-permute-start.7 = (f32[272,128]{1,0:T(8,128)S(1)}, f32[272,128]{1,0:T(8,128)S(1)}, u32[]{:S(2)}, u32[]{:S(2)}) collective-permute-start(f32[272,128]{1,0:T(8,128)S(1)} %get-tuple-element.41), channel_id=1, source_target_pairs={{0,6},{1,7},{2,0},{3,1},{4,2},{5,3},{6,4},{7,5},{8,14},{9,15},{10,... | collective-permute-start | bytes 417800 | tf_op jit(solution)/shard_map/ppermute | solution.py:587
  19.1 8.2 %collective-permute-done.6.low_two = f32[272,128]{1,0:T(8,128)S(1)} collective-permute-done((f32[272,128]{1,0:T(8,128)S(1)}, f32[272,128]{1,0:T(8,128)S(1)}, u32[]{:S(2)}, u32[]{:S(2)}) %collective-permute-start.6) | collective-permute-done | bytes 139296 | tf_op jit(solution)/shard_map/ppermute | solution.py:587
  27.3 0.0 collective-permute-done.7.high_two
  27.3 0.0 collective-permute-done.4.low_one
  27.3 0.0 collective-permute-done.5.high_one
  27.3 0.0 copy-done.3
  27.3 0.0 copy-done.10
  27.3 0.0 copy-start.1
  27.3 0.4 shard_map.130
  27.7 0.0 collective-permute-start.8
  27.8 5.1 %collective-permute-start.9 = (f32[8,3968]{1,0:T(8,128)S(1)}, f32[8,3968]{1,0:T(8,128)S(1)}, u32[]{:S(2)}, u32[]{:S(2)}) collective-permute-start(f32[8,3968]{1,0:T(8,128)S(1)} %get-tuple-element.44), channel_id=1, source_target_pairs={{0,248},{8,0},{16,8},{24,16},{32,24},{40,32},{48,40},{56,48},{64,5... | collective-permute-start | bytes 380936 | tf_op jit(solution)/shard_map/ppermute | solution.py:587
  32.9 0.0 copy-done.1
  32.9 0.0 copy-start
  32.9 0.0 copy-start.5
  32.9 1.8 %shard_map.131.partial = f32[160,1280]{1,0:T(8,128)S(1)} custom-call(f32[72,2048]{1,0:T(8,128)S(1)} %get-tuple-element.42.ext, f32[160,288]{1,0:T(8,128)S(1)} %copy-done.1), custom_call_target="tpu_custom_call" | custom-call | tf_op jit(solution)/shard_map/pallas_call | solution.py:576
  34.8 1.7 %collective-permute-done.8.left = f32[8,3968]{1,0:T(8,128)S(1)} collective-permute-done((f32[8,3968]{1,0:T(8,128)S(1)}, f32[8,3968]{1,0:T(8,128)S(1)}, u32[]{:S(2)}, u32[]{:S(2)}) %collective-permute-start.8) | collective-permute-done | bytes 127008 | tf_op jit(solution)/shard_map/ppermute | solution.py:587
  36.5 0.0 collective-permute-done.9.right
  36.5 0.0 copy-done
  36.5 0.0 copy-done.5
  36.5 0.0 copy-start.9
  36.5 1.8 %shard_map.132 = (f32[192,512]{1,0:T(8,128)S(1)}, f32[72,512]{1,0:T(8,128)S(1)}, f32[736,128]{1,0:T(8,128)S(1)}, f32[736,128]{1,0:T(8,128)S(1)}, f32[328,128]{1,0:T(8,128)S(1)}, /*index=5*/f32[328,128]{1,0:T(8,128)S(1)}) custom-call(f32[160,1280]{1,0:T(8,128)S(1)} %shard_map.131.partial, f32[8,3968]{1,0:T(8,128)S(1)} %collective-permute-done.8.left, ...), custom_call_target="tpu_custom_call" | custom-call | tf_op jit(solution)/shard_map/pallas_call | solution.py:576
  38.3 0.7 %collective-permute-start.11 = (f32[736,128]{1,0:T(8,128)S(1)}, f32[736,128]{1,0:T(8,128)S(1)}, u32[]{:S(2)}, u32[]{:S(2)}) collective-permute-start(f32[736,128]{1,0:T(8,128)S(1)} %get-tuple-element.48), channel_id=1, source_target_pairs={{0,7},{1,0},{2,1},{3,2},{4,3},{5,4},{6,5},{7,6},{8,15},{9,8},{10,9... | collective-permute-start | bytes 1130504 | tf_op jit(solution)/shard_map/ppermute | solution.py:587
  39.0 1.0 %collective-permute-start.10 = (f32[736,128]{1,0:T(8,128)S(1)}, f32[736,128]{1,0:T(8,128)S(1)}, u32[]{:S(2)}, u32[]{:S(2)}) collective-permute-start(f32[736,128]{1,0:T(8,128)S(1)} %get-tuple-element.47.mine), channel_id=1, source_target_pairs={{0,1},{1,2},{2,3},{3,4},{4,5},{5,6},{6,7},{7,0},{8,9},{9,10},{10,1... | collective-permute-start | bytes 1130504 | tf_op jit(solution)/shard_map/ppermute | solution.py:587
  40.1 0.1 collective-permute-start.12
  40.2 2.5 %collective-permute-start.13 = (f32[328,128]{1,0:T(8,128)S(1)}, f32[328,128]{1,0:T(8,128)S(1)}, u32[]{:S(2)}, u32[]{:S(2)}) collective-permute-start(f32[328,128]{1,0:T(8,128)S(1)} %get-tuple-element.50), channel_id=1, source_target_pairs={{0,6},{1,7},{2,0},{3,1},{4,2},{5,3},{6,4},{7,5},{8,14},{9,15},{10,... | collective-permute-start | bytes 503816 | tf_op jit(solution)/shard_map/ppermute | solution.py:587
  42.7 7.5 %collective-permute-done.12.low_two = f32[328,128]{1,0:T(8,128)S(1)} collective-permute-done((f32[328,128]{1,0:T(8,128)S(1)}, f32[328,128]{1,0:T(8,128)S(1)}, u32[]{:S(2)}, u32[]{:S(2)}) %collective-permute-start.12) | collective-permute-done | bytes 167968 | tf_op jit(solution)/shard_map/ppermute | solution.py:587
  50.2 0.0 collective-permute-done.13.high_two
  50.2 0.0 collective-permute-done.11.high_one
  50.2 0.0 collective-permute-done.10.low_one
  50.2 0.0 copy-done.9
  50.2 0.0 copy-start.2
  50.2 0.4 shard_map.133
  50.6 0.3 collective-permute-start.14
  50.9 4.9 %collective-permute-start.15 = (f32[8,2688]{1,0:T(8,128)S(1)}, f32[8,2688]{1,0:T(8,128)S(1)}, u32[]{:S(2)}, u32[]{:S(2)}) collective-permute-start(f32[8,2688]{1,0:T(8,128)S(1)} %get-tuple-element.53), channel_id=1, source_target_pairs={{0,248},{8,0},{16,8},{24,16},{32,24},{40,32},{48,40},{56,48},{64,5... | collective-permute-start | bytes 258056 | tf_op jit(solution)/shard_map/ppermute | solution.py:587
  55.8 0.0 copy-done.2
  55.8 0.0 copy-start.6
  55.8 1.4 %shard_map.134.partial = f32[128,1024]{1,0:T(8,128)S(1)} custom-call(f32[72,1792]{1,0:T(8,128)S(1)} %get-tuple-element.51.ext, f32[128,288]{1,0:T(8,128)S(1)} %copy-done.2), custom_call_target="tpu_custom_call" | custom-call | tf_op jit(solution)/shard_map/pallas_call | solution.py:576
  57.2 1.2 %collective-permute-done.14.left = f32[8,2688]{1,0:T(8,128)S(1)} collective-permute-done((f32[8,2688]{1,0:T(8,128)S(1)}, f32[8,2688]{1,0:T(8,128)S(1)}, u32[]{:S(2)}, u32[]{:S(2)}) %collective-permute-start.14) | collective-permute-done | bytes 86048 | tf_op jit(solution)/shard_map/ppermute | solution.py:587
  58.4 0.0 collective-permute-done.15.right
  58.4 0.0 copy-done.6
  58.4 1.5 %shard_map.135 = f32[3,64,4,128]{3,2,1,0:T(4,128)} custom-call(f32[128,1024]{1,0:T(8,128)S(1)} %shard_map.134.partial, f32[8,2688]{1,0:T(8,128)S(1)} %collective-permute-done.14.left, f32[8,2688]{1,0:T(8,128)S(1)} %collective-permute-done.15.right, f32[192,512]{1,0:T(8,128)S(1)} %get-tuple-element.46.section, f32[128,128]{1,0:T(8,128)S(1)} %get-tuple-element.54.fixed, ...), custom_call_target="tpu_custom_call" | custom-call | tf_op jit(solution)/shard_map/pallas_call | solution.py:576
Async XLA Ops:
  0.0 11.9 %copy-start.8 = (f32[128,64]{1,0:T(8,128)S(1)}, f32[128,64]{1,0:T(8,128)}, u32[]{:S(2)}) copy-start(f32[128,64]{1,0:T(8,128)} %constant.22.clone.own) | copy-start | bytes 98308
  1.4 11.8 %collective-permute-start.2 = (f32[192,256]{1,0:T(8,128)S(1)}, f32[192,256]{1,0:T(8,128)S(1)}, u32[]{:S(2)}, u32[]{:S(2)}) collective-permute-start(f32[192,256]{1,0:T(8,128)S(1)} %get-tuple-element.34), channel_id=1, source_target_pairs={{0,1},{1,2},{2,3},{3,4},{4,5},{5,6},{6,7},{7,0},{8,9},{9,10},{10,1... | collective-permute-start | bytes 589832 | tf_op jit(solution)/shard_map/ppermute | solution.py:587
  4.1 9.1 %collective-permute-start.3 = (f32[192,256]{1,0:T(8,128)S(1)}, f32[192,256]{1,0:T(8,128)S(1)}, u32[]{:S(2)}, u32[]{:S(2)}) collective-permute-start(f32[192,256]{1,0:T(8,128)S(1)} %get-tuple-element.35), channel_id=1, source_target_pairs={{0,7},{1,0},{2,1},{3,2},{4,3},{5,4},{6,5},{7,6},{8,15},{9,8},{10,9... | collective-permute-start | bytes 589832 | tf_op jit(solution)/shard_map/ppermute | solution.py:587
  4.7 8.5 %collective-permute-start = (f32[16,512]{1,0:T(8,128)S(1)}, f32[16,512]{1,0:T(8,128)S(1)}, u32[]{:S(2)}, u32[]{:S(2)}) collective-permute-start(f32[16,512]{1,0:T(8,128)S(1)} %get-tuple-element.32), channel_id=1, source_target_pairs={{0,8},{8,16},{16,24},{24,32},{32,40},{40,48},{48,56},{56,64},{64,7... | collective-permute-start | bytes 98312 | tf_op jit(solution)/shard_map/ppermute | solution.py:587
  5.3 7.9 %collective-permute-start.1 = (f32[16,512]{1,0:T(8,128)S(1)}, f32[16,512]{1,0:T(8,128)S(1)}, u32[]{:S(2)}, u32[]{:S(2)}) collective-permute-start(f32[16,512]{1,0:T(8,128)S(1)} %get-tuple-element.33), channel_id=1, source_target_pairs={{0,248},{8,0},{16,8},{24,16},{32,24},{40,32},{48,40},{56,48},{64,5... | collective-permute-start | bytes 98312 | tf_op jit(solution)/shard_map/ppermute | solution.py:587
  11.9 1.3 %copy-start.4 = (bf16[72,192]{1,0:T(8,128)(2,1)S(1)}, bf16[72,192]{1,0:T(8,128)(2,1)}, u32[]{:S(2)}) copy-start(bf16[72,192]{1,0:T(8,128)(2,1)} %constant.27.clone.lateral) | copy-start | bytes 82948
  11.9 1.3 %copy-start.7 = (bf16[3,128,96]{2,1,0:T(8,128)(2,1)S(1)}, bf16[3,128,96]{2,1,0:T(8,128)(2,1)}, u32[]{:S(2)}) copy-start(bf16[3,128,96]{2,1,0:T(8,128)(2,1)} %constant.24.clone.slopes) | copy-start | bytes 221188
  12.8 14.5 %copy-start.3 = (bf16[32,576]{1,0:T(8,128)(2,1)S(1)}, bf16[32,576]{1,0:T(8,128)(2,1)}, u32[]{:S(2)}) copy-start(bf16[32,576]{1,0:T(8,128)(2,1)} %constant.26.clone.moments) | copy-start | bytes 110596
  13.2 14.1 %copy-start.10 = (bf16[64,240]{1,0:T(8,128)(2,1)S(1)}, bf16[64,240]{1,0:T(8,128)(2,1)}, u32[]{:S(2)}) copy-start(bf16[64,240]{1,0:T(8,128)(2,1)} %constant.28.clone.source) | copy-start | bytes 92164
  13.8 13.5 %collective-permute-start.4 = (f32[800,128]{1,0:T(8,128)S(1)}, f32[800,128]{1,0:T(8,128)S(1)}, u32[]{:S(2)}, u32[]{:S(2)}) collective-permute-start(f32[800,128]{1,0:T(8,128)S(1)} %get-tuple-element.38), channel_id=1, source_target_pairs={{0,1},{1,2},{2,3},{3,4},{4,5},{5,6},{6,7},{7,0},{8,9},{9,10},{10,1... | collective-permute-start | bytes 1228808 | tf_op jit(solution)/shard_map/ppermute | solution.py:587
  16.4 10.9 %collective-permute-start.5 = (f32[800,128]{1,0:T(8,128)S(1)}, f32[800,128]{1,0:T(8,128)S(1)}, u32[]{:S(2)}, u32[]{:S(2)}) collective-permute-start(f32[800,128]{1,0:T(8,128)S(1)} %get-tuple-element.39), channel_id=1, source_target_pairs={{0,7},{1,0},{2,1},{3,2},{4,3},{5,4},{6,5},{7,6},{8,15},{9,8},{10,9... | collective-permute-start | bytes 1228808 | tf_op jit(solution)/shard_map/ppermute | solution.py:587
  16.4 10.9 %collective-permute-start.6 = (f32[272,128]{1,0:T(8,128)S(1)}, f32[272,128]{1,0:T(8,128)S(1)}, u32[]{:S(2)}, u32[]{:S(2)}) collective-permute-start(f32[272,128]{1,0:T(8,128)S(1)} %get-tuple-element.40), channel_id=1, source_target_pairs={{0,2},{1,3},{2,4},{3,5},{4,6},{5,7},{6,0},{7,1},{8,10},{9,11},{10,... | collective-permute-start | bytes 417800 | tf_op jit(solution)/shard_map/ppermute | solution.py:587
  17.7 9.6 %collective-permute-start.7 = (f32[272,128]{1,0:T(8,128)S(1)}, f32[272,128]{1,0:T(8,128)S(1)}, u32[]{:S(2)}, u32[]{:S(2)}) collective-permute-start(f32[272,128]{1,0:T(8,128)S(1)} %get-tuple-element.41), channel_id=1, source_target_pairs={{0,6},{1,7},{2,0},{3,1},{4,2},{5,3},{6,4},{7,5},{8,14},{9,15},{10,... | collective-permute-start | bytes 417800 | tf_op jit(solution)/shard_map/ppermute | solution.py:587
  27.3 5.6 %copy-start.1 = (f32[160,288]{1,0:T(8,128)S(1)}, f32[160,288]{1,0:T(8,128)}, u32[]{:S(2)}) copy-start(f32[160,288]{1,0:T(8,128)} %constant.23.clone.solve) | copy-start | bytes 552964
  27.7 8.7 %collective-permute-start.8 = (f32[8,3968]{1,0:T(8,128)S(1)}, f32[8,3968]{1,0:T(8,128)S(1)}, u32[]{:S(2)}, u32[]{:S(2)}) collective-permute-start(f32[8,3968]{1,0:T(8,128)S(1)} %get-tuple-element.43), channel_id=1, source_target_pairs={{0,8},{8,16},{16,24},{24,32},{32,40},{40,48},{48,56},{56,64},{64,7... | collective-permute-start | bytes 380936 | tf_op jit(solution)/shard_map/ppermute | solution.py:587
  27.8 8.7 %collective-permute-start.9 = (f32[8,3968]{1,0:T(8,128)S(1)}, f32[8,3968]{1,0:T(8,128)S(1)}, u32[]{:S(2)}, u32[]{:S(2)}) collective-permute-start(f32[8,3968]{1,0:T(8,128)S(1)} %get-tuple-element.44), channel_id=1, source_target_pairs={{0,248},{8,0},{16,8},{24,16},{32,24},{40,32},{48,40},{56,48},{64,5... | collective-permute-start | bytes 380936 | tf_op jit(solution)/shard_map/ppermute | solution.py:587
  32.9 3.5 %copy-start = (bf16[3,128,288]{2,1,0:T(8,128)(2,1)S(1)}, bf16[3,128,288]{2,1,0:T(8,128)(2,1)}, u32[]{:S(2)}) copy-start(bf16[3,128,288]{2,1,0:T(8,128)(2,1)} %constant.25.clone.full) | copy-start | bytes 663556
  32.9 3.5 %copy-start.5 = (bf16[160,384]{1,0:T(8,128)(2,1)S(1)}, bf16[160,384]{1,0:T(8,128)(2,1)}, u32[]{:S(2)}) copy-start(bf16[160,384]{1,0:T(8,128)(2,1)} %constant.29.clone.solve) | copy-start | bytes 368644
  36.5 13.7 %copy-start.9 = (bf16[64,240]{1,0:T(8,128)(2,1)S(1)}, bf16[64,240]{1,0:T(8,128)(2,1)}, u32[]{:S(2)}) copy-start(bf16[64,240]{1,0:T(8,128)(2,1)} %constant.31.clone.source) | copy-start | bytes 92164
  38.3 11.9 %collective-permute-start.11 = (f32[736,128]{1,0:T(8,128)S(1)}, f32[736,128]{1,0:T(8,128)S(1)}, u32[]{:S(2)}, u32[]{:S(2)}) collective-permute-start(f32[736,128]{1,0:T(8,128)S(1)} %get-tuple-element.48), channel_id=1, source_target_pairs={{0,7},{1,0},{2,1},{3,2},{4,3},{5,4},{6,5},{7,6},{8,15},{9,8},{10,9... | collective-permute-start | bytes 1130504 | tf_op jit(solution)/shard_map/ppermute | solution.py:587
  39.0 11.2 %collective-permute-start.10 = (f32[736,128]{1,0:T(8,128)S(1)}, f32[736,128]{1,0:T(8,128)S(1)}, u32[]{:S(2)}, u32[]{:S(2)}) collective-permute-start(f32[736,128]{1,0:T(8,128)S(1)} %get-tuple-element.47.mine), channel_id=1, source_target_pairs={{0,1},{1,2},{2,3},{3,4},{4,5},{5,6},{6,7},{7,0},{8,9},{9,10},{10,1... | collective-permute-start | bytes 1130504 | tf_op jit(solution)/shard_map/ppermute | solution.py:587
  40.1 10.1 %collective-permute-start.12 = (f32[328,128]{1,0:T(8,128)S(1)}, f32[328,128]{1,0:T(8,128)S(1)}, u32[]{:S(2)}, u32[]{:S(2)}) collective-permute-start(f32[328,128]{1,0:T(8,128)S(1)} %get-tuple-element.49), channel_id=1, source_target_pairs={{0,2},{1,3},{2,4},{3,5},{4,6},{5,7},{6,0},{7,1},{8,10},{9,11},{10,... | collective-permute-start | bytes 503816 | tf_op jit(solution)/shard_map/ppermute | solution.py:587
  40.2 10.0 %collective-permute-start.13 = (f32[328,128]{1,0:T(8,128)S(1)}, f32[328,128]{1,0:T(8,128)S(1)}, u32[]{:S(2)}, u32[]{:S(2)}) collective-permute-start(f32[328,128]{1,0:T(8,128)S(1)} %get-tuple-element.50), channel_id=1, source_target_pairs={{0,6},{1,7},{2,0},{3,1},{4,2},{5,3},{6,4},{7,5},{8,14},{9,15},{10,... | collective-permute-start | bytes 503816 | tf_op jit(solution)/shard_map/ppermute | solution.py:587
  50.2 5.6 %copy-start.2 = (f32[128,288]{1,0:T(8,128)S(1)}, f32[128,288]{1,0:T(8,128)}, u32[]{:S(2)}) copy-start(f32[128,288]{1,0:T(8,128)} %constant.30.clone.solve) | copy-start | bytes 442372
  50.6 7.8 %collective-permute-start.14 = (f32[8,2688]{1,0:T(8,128)S(1)}, f32[8,2688]{1,0:T(8,128)S(1)}, u32[]{:S(2)}, u32[]{:S(2)}) collective-permute-start(f32[8,2688]{1,0:T(8,128)S(1)} %get-tuple-element.52), channel_id=1, source_target_pairs={{0,8},{8,16},{16,24},{24,32},{32,40},{40,48},{48,56},{56,64},{64,7... | collective-permute-start | bytes 258056 | tf_op jit(solution)/shard_map/ppermute | solution.py:587
  50.9 7.5 %collective-permute-start.15 = (f32[8,2688]{1,0:T(8,128)S(1)}, f32[8,2688]{1,0:T(8,128)S(1)}, u32[]{:S(2)}, u32[]{:S(2)}) collective-permute-start(f32[8,2688]{1,0:T(8,128)S(1)} %get-tuple-element.53), channel_id=1, source_target_pairs={{0,248},{8,0},{16,8},{24,16},{32,24},{40,32},{48,40},{56,48},{64,5... | collective-permute-start | bytes 258056 | tf_op jit(solution)/shard_map/ppermute | solution.py:587
  55.8 2.6 %copy-start.6 = (bf16[128,384]{1,0:T(8,128)(2,1)S(1)}, bf16[128,384]{1,0:T(8,128)(2,1)}, u32[]{:S(2)}) copy-start(bf16[128,384]{1,0:T(8,128)(2,1)} %constant.32.clone.solve) | copy-start | bytes 294916

commit v7 on v6

--- a/solution.py
+++ b/solution.py
@@ -219,20 +219,18 @@
             copies.append(
                 pltpu.make_async_copy(velocity.at[c, :, r, :], flat.at[rows, lane(r)], sems.at[len(copies)])
             )
-    apart = len(copies)
     for r in range(ROWS):
         copies.append(pltpu.make_async_copy(viscosity.at[:, r, :], thick.at[:, lane(r)], sems.at[len(copies)]))
     for copy in copies:
         copy.start()
-    for copy in copies[:apart]:
+    for copy in copies:
         copy.wait()
-    upward[...] = flat[:, lane(ROWS - 2, 2)]
-    downward[...] = flat[:, lane(0, 2)]
+    row = lambda c, r: flat[cells * c : cells * (c + 1), lane(r)]
+    fill_slots(upward, cells, [row(c, r) for c in range(3) for r in (2, 3)] + [thick[:, lane(3)]], [])
+    fill_slots(downward, cells, [row(c, r) for c in range(3) for r in (0, 1)] + [thick[:, lane(0)]], [])
     both = split_dot(weights[...], flat[...])
     to_right[...] = both[:PAD_V]
     to_left[...] = both[PAD_V:]
-    for copy in copies[apart:]:
-        copy.wait()
 
 
 def weighed(weights, value_at, r, home):
@@ -277,8 +275,8 @@
 
         def beyond(r):
             if r < 0:
-                return masked(low[rows, lane(r + 2)], r, masks)
-            return masked(high[rows, lane(r - ROWS)], r, masks)
+                return masked(slot(low, cells, 2 * c + r + 2)[...], r, masks)
+            return masked(slot(high, cells, 2 * c + r - ROWS)[...], r, masks)
 
         for r in range(ROWS):
             spread = spanned[cells:, lane(r)] + weighed(CURVE, beyond, r, False)
@@ -299,12 +297,15 @@
         ref[top : top + PAD_M, :] = block
 
 
-def own_source(cells, section, lateral, parts):
+def own_source(cells, section, lateral, parts, owed={}):
     side = split_dot(lateral[...], section[2 * cells :, :])
     at = lambda r: section[cells : 2 * cells, lane(r)]
     blocks = []
     for r in range(ROWS):
         total = stream_slope(section[:cells, lane(r)]) + side[:cells, lane(r)] + weighed(DIFFERENCE, at, r, True)
+        for reach, factor in DIFFERENCE:
+            if r + reach in owed:
+                total = total + factor * owed[r + reach]
         parts[:cells, lane(r)] = total
         blocks.append(total)
     parts[cells:, :] = side[cells:]
@@ -319,68 +320,97 @@
     section, parts, up_near, down_near, up_far, down_far,
 ):
     add_beyond(cells, rough, flat, thick, left, right, low, high, slopes, section)
-    blocks, moments, at, up, down = own_source(cells, section, lateral, parts)
+    blocks, moments, at, _, _ = own_source(cells, section, lateral, parts)
     row = lambda c, r: section[cells * c : cells * (c + 1), lane(r)]
-    fill_slots(
-        up_near, cells,
-        blocks + [at(2), at(3), up, at(0), row(0, 2), row(0, 3), row(2, 2), row(2, 3)], moments,
-    )
-    fill_slots(
-        down_near, cells,
-        blocks + [at(0), at(1), down, at(3), row(0, 0), row(0, 1), row(2, 0), row(2, 1)], moments,
-    )
-    fill_slots(up_far, cells, blocks[2:] + [at(2), at(3)], moments[2:])
-    fill_slots(down_far, cells, blocks[:2] + [at(0), at(1)], moments[:2])
-
-
-def extend_source(cells, extent, near_slots, far_slots, parts, section, arrived, extra, ext):
+    every = [at(r) for r in range(ROWS)]
+    for near, far, outer, inner in ((up_near, up_far, 0, 2), (down_near, down_far, 2, 0)):
+        side = [row(c, inner + k) for c in (0, 2) for k in range(2)]
+        fill_slots(near, cells, blocks[outer : outer + 2] + every + side, moments[outer : outer + 2])
+        fill_slots(far, cells, blocks[inner : inner + 2] + [at(inner), at(inner + 1)], moments[inner : inner + 2])
+
+
+def first_source(cells, parts, section, arrived, lateral, ext):
     low_one, high_one, low_two, high_two = arrived
     masks = edge_masks()
     span, tail = slice(0, cells), slice(cells, cells + PAD_M)
-    outer = extent.reach - ROWS
+    pick = lambda ref, k: slot(ref, cells, k)[...]
+
+    def across(e):
+        if 0 <= e < ROWS:
+            return section[cells : 2 * cells, lane(e)]
+        if e < -ROWS or e >= 2 * ROWS:
+            tile = pick(low_two, e + 8) if e < 0 else pick(high_two, e - 6)
+        else:
+            tile = pick(low_one, e + 6) if e < 0 else pick(high_one, e - 2)
+        return masked(tile, e, masks)
+
+    whole = (-2, -1, ROWS, ROWS + 1)
+    given = [(low_one if e < 0 else high_one, e % 2) for e in whole]
+    beside = split_dot(lateral[...], jnp.concatenate([pick(ref, 8 + k) for ref, k in given], axis=1))
+
+    for e in range(-FIRST.reach, ROWS + FIRST.reach):
+        if e in whole:
+            at = whole.index(e)
+            ref, k = given[at]
+            total = stream_slope(pick(ref, 6 + k)) + beside[:cells, lane(at)]
+            side = beside[cells:, lane(at)]
+        elif 0 <= e < ROWS:
+            total, side = parts[span, lane(e)], parts[tail, lane(e)]
+        else:
+            far = e < -ROWS or e >= 2 * ROWS
+            ref = (low_two if e < 0 else high_two) if far else (low_one if e < 0 else high_one)
+            top = (4 if far else 10) * cells + PAD_M * (e % 2)
+            total, side = pick(ref, e % 2), ref[top : top + PAD_M, :]
+        for reach, factor in DIFFERENCE:
+            if e in whole or (e + reach) // ROWS != e // ROWS:
+                total = total + factor * across(e + reach)
+        ext[span, lane(e + FIRST.reach)] = masked(total, e, masks)
+        ext[tail, lane(e + FIRST.reach)] = masked(side, e, masks)
+
+
+def last_source(cells, parts, section, arrived, extra, ext):
+    low_one, high_one, low_two, high_two = arrived
+    masks = edge_masks()
+    span, tail = slice(0, cells), slice(cells, cells + PAD_M)
     pick = lambda ref, k: slot(ref, cells, k)[...]
 
     def joined(e):
         if 0 <= e < ROWS:
             return parts[span, lane(e)], parts[tail, lane(e)]
         if e < -ROWS or e >= 2 * ROWS:
-            given, k, count = (low_two, e + extent.reach, far_slots) if e < 0 else (high_two, e - 2 * ROWS, far_slots)
-        else:
-            given, k, count = (low_one, e + ROWS, near_slots) if e < 0 else (high_one, e - ROWS, near_slots)
-        top = count * cells + PAD_M * k
-        return pick(given, k), given[top : top + PAD_M, :]
+            ref = low_two if e < 0 else high_two
+            return pick(ref, 0), ref[4 * cells :, :]
+        ref, k = (low_one, e + ROWS) if e < 0 else (high_one, e - ROWS)
+        top = 9 * cells + PAD_M * k
+        return pick(ref, k), ref[top : top + PAD_M, :]
 
     def across(e, home):
         if e // ROWS == home // ROWS or home // ROWS in (-2, 2):
             return None
         if e < -ROWS:
-            return masked(pick(low_two, outer + e + ROWS + 2), e, masks)
+            return masked(pick(low_two, 1 + e + ROWS + 2), e, masks)
         if e < 0:
             return masked(pick(low_one, ROWS + e + 2), e, masks)
         if e < ROWS:
             return section[cells : 2 * cells, lane(e)]
         if e < 2 * ROWS:
             return masked(pick(high_one, e), e, masks)
-        return masked(pick(high_two, outer + e - 2 * ROWS), e, masks)
-
-    for e in range(-extent.reach, ROWS + extent.reach):
+        return masked(pick(high_two, 1 + e - 2 * ROWS), e, masks)
+
+    for e in range(-LAST.reach, ROWS + LAST.reach):
         total, side = joined(e)
         if e == -ROWS - 1:
             total = total + pick(low_one, 6)
-        if e == -ROWS - 2:
-            total = total - (1.0 / 12.0) * pick(low_one, 7)
         if e == 2 * ROWS:
             total = total + pick(high_one, 6)
-        if e == 2 * ROWS + 1:
-            total = total + (1.0 / 12.0) * pick(high_one, 7)
         for reach, factor in DIFFERENCE:
             other = across(e + reach, e)
             if other is not None:
                 total = total + factor * other
-            if e + reach in extra:
+            if e + reach in extra and (e + reach) // ROWS == e // ROWS:
                 total = total + factor * extra[e + reach]
-        ext[span, lane(e + extent.reach)] = masked(total, e, masks)
-        ext[tail, lane(e + extent.reach)] = masked(side, e, masks)
+        ext[span, lane(e + LAST.reach)] = masked(total, e, masks)
+        ext[tail, lane(e + LAST.reach)] = masked(side, e, masks)
 
 
 def pack_moments(extent, both, to_right, to_left):
@@ -394,9 +424,9 @@
 
 
 def source_kernel(
-    cells, parts, section, low_one, high_one, low_two, high_two, source, moments, ext, to_right, to_left
+    cells, parts, section, low_one, high_one, low_two, high_two, lateral, source, moments, ext, to_right, to_left
 ):
-    extend_source(cells, FIRST, 12, 4, parts, section, (low_one, high_one, low_two, high_two), {}, ext)
+    first_source(cells, parts, section, (low_one, high_one, low_two, high_two), lateral, ext)
     both = split_dot(source[...], ext[...])
     pack_moments(FIRST, both, to_right, to_left)
     held = split_dot(moments[...], section[...])
@@ -415,26 +445,23 @@
 
 
 def last_source_kernel(
-    cells, parts, section, mine, low_one, high_one, low_two, high_two, source, ext, fixed, to_right, to_left
+    cells, parts, section, up_near, down_near, debts, low_one, high_one, low_two, high_two, source,
+    ext, fixed, to_right, to_left,
 ):
     masks = edge_masks()
     pick = lambda ref, k: slot(ref, cells, k)[...]
-    phi_first, phi_last, factor_first, factor_last = 7, 8, 9, 10
-    below, above = masks[0], masks[2]
-    below_two, above_two = masks[1], masks[3]
+    phi, factor = 7, 8
     extra = {
-        0: pick(mine, factor_first) * pick(low_one, phi_first) * below,
-        ROWS - 1: pick(mine, factor_last) * pick(high_one, phi_last) * above,
-        -1: pick(low_one, factor_last) * pick(mine, phi_last) * below,
-        -ROWS: pick(low_one, factor_first) * pick(low_two, 4) * below_two,
-        -ROWS - 1: pick(low_two, 3) * pick(low_one, phi_last) * below_two,
-        ROWS: pick(high_one, factor_first) * pick(mine, phi_first) * above,
-        2 * ROWS - 1: pick(high_one, factor_last) * pick(high_two, 4) * above_two,
-        2 * ROWS: pick(high_two, 3) * pick(high_one, phi_first) * above_two,
+        0: pick(up_near, factor) * pick(low_one, phi) * masks[0],
+        ROWS - 1: pick(down_near, factor) * pick(high_one, phi) * masks[2],
+        -1: pick(debts, 0),
+        ROWS: pick(debts, 1),
+        -ROWS: pick(low_one, factor) * pick(low_two, 3) * masks[1],
+        2 * ROWS - 1: pick(high_one, factor) * pick(high_two, 3) * masks[3],
     }
     fixed[:cells, :] = extra[0]
     fixed[cells:, :] = extra[ROWS - 1]
-    extend_source(cells, LAST, 11, 5, parts, section, (low_one, high_one, low_two, high_two), extra, ext)
+    last_source(cells, parts, section, (low_one, high_one, low_two, high_two), extra, ext)
     pack_moments(LAST, split_dot(source[...], ext[...]), to_right, to_left)
 
 
@@ -488,8 +515,8 @@
 
 
 def middle_kernel(
-    cells, partial, left, right, section, solve, low_one, high_one, start, thick, full, lateral,
-    following, parts, up_near, down_near, up_far, down_far, levels, flat, rim, sides,
+    cells, partial, left, right, section, solve, low_one, high_one, low, high, start, thick, full, lateral,
+    following, parts, debts, up_near, down_near, up_far, down_far, levels, flat, rim, sides,
 ):
     masks = edge_masks()
     found = finish(FIRST, partial, left, right, solve, levels)
@@ -499,8 +526,8 @@
         rows = slice(cells * c, cells * (c + 1))
         for r in range(ROWS):
             flat[rows, lane(r)] = section[rows, lane(r)] - gradient(FIRST, found, c, home, home_slope, r)
-        first = (8, 4, 10)[c]
         for k, r in enumerate(outer):
+            first = (6, 4 if r < 0 else 2, 8)[c]
             value = slot(low_one if r < 0 else high_one, cells, first + k % 2)[...]
             value = value - gradient(FIRST, found, c, home, home_slope, r)
             rim[rows, lane(k)] = masked(value, r, masks)
@@ -541,16 +568,21 @@
             )
             moved = here + time_step * (thick[:, lane(r)] * spread - carried)
             following[rows, lane(r)] = 0.5 * start[rows, lane(r)] + 0.5 * moved
-    blocks, moments, at, up, down = own_source(cells, following, lateral, parts)
     phi = lambda r: found[:cells, lane(r + FIRST.margin)]
     scale = 0.5 * time_step / 144.0
+    owed = {
+        -1: scale * (tile(1, -1) - slot(low, cells, 6)[...]) * phi(ROWS - 1) * masks[0],
+        ROWS: scale * (tile(1, ROWS) + slot(high, cells, 6)[...]) * phi(0) * masks[2],
+    }
+    slot(debts, cells, 0)[...] = owed[-1]
+    slot(debts, cells, 1)[...] = owed[ROWS]
+    blocks, moments, at, up, down = own_source(cells, following, lateral, parts, owed)
     first = scale * (thick[:, lane(0)] + tile(1, 0))
     last = scale * (tile(1, ROWS - 1) - thick[:, lane(ROWS - 1)])
-    owed = [phi(0), phi(ROWS - 1), first, last]
-    fill_slots(up_near, cells, blocks + [at(2), at(3), up] + owed, moments)
-    fill_slots(down_near, cells, blocks + [at(0), at(1), down] + owed, moments)
-    fill_slots(up_far, cells, [blocks[3], at(2), at(3), last, phi(0)], moments[3:])
-    fill_slots(down_far, cells, [blocks[0], at(0), at(1), first, phi(ROWS - 1)], moments[:1])
+    fill_slots(up_near, cells, blocks + [at(2), at(3), up, phi(0), first], moments)
+    fill_slots(down_near, cells, blocks + [at(0), at(1), down, phi(ROWS - 1), last], moments)
+    fill_slots(up_far, cells, [blocks[3], at(2), at(3), phi(0)], moments[3:])
+    fill_slots(down_far, cells, [blocks[0], at(0), at(1), phi(ROWS - 1)], moments[:1])
 
 
 def last_kernel(cells, partial, left, right, section, fixed, solve, out, levels, staged, sems):
@@ -596,7 +628,7 @@
     _, last_own, _, _, _, _, *last = (jnp.asarray(t) for t in tables(length, cells, True))
     width = row_cells * columns
     near = cells + PAD_M
-    whole, edge, rim = (components * cells, width), (PAD_V, width), (components * cells, 2 * columns)
+    whole, edge, rim = (components * cells, width), (PAD_V, width), (7 * cells, columns)
 
     def across(up_near, down_near, up_far, down_far):
         return (
@@ -604,8 +636,8 @@
             shifted(up_far, "cross", 2), shifted(down_far, "cross", -2),
         )
 
-    def message(near_slots, far_slots, far_rows):
-        near_shape = (near_slots * cells + row_cells * PAD_M, columns)
+    def message(near_slots, near_rows, far_slots, far_rows):
+        near_shape = (near_slots * cells + near_rows * PAD_M, columns)
         far_shape = (far_slots * cells + far_rows * PAD_M, columns)
         return [near_shape] * 2 + [far_shape] * 2
 
@@ -626,14 +658,14 @@
     (rough,) = call(functools.partial(rough_kernel, cells), [whole], start, thick, own)
     section, parts, *sent = call(
         functools.partial(tendency_kernel, cells),
-        [whole, (near, width)] + message(12, 4, 2),
+        [whole, (near, width)] + message(10, 2, 4, 2),
         rough, start, thick, left, right, low, high, slopes, lateral,
     )
     arrived = across(*sent)
     ext, to_right, to_left = call(
         functools.partial(source_kernel, cells),
         [(near, FIRST.breadth * columns)] + [(GROUP, (FIRST.packed + ROWS + 3) * columns)] * 2,
-        parts, section, *arrived, first[0], moments,
+        parts, section, *arrived, lateral, first[0], moments,
     )
     left = shifted(to_right, "span", 1)
     right = shifted(to_left, "span", -1)
@@ -644,10 +676,10 @@
         scratch=[levels(FIRST, near)],
     )
 
-    section, parts, *sent = call(
+    section, parts, debts, *sent = call(
         functools.partial(middle_kernel, cells),
-        [whole, (near, width)] + message(11, 5, 1),
-        partial, left, right, section, first[1], *arrived[:2], start, thick, full, lateral,
+        [whole, (near, width), (2 * cells, columns)] + message(9, 4, 4, 1),
+        partial, left, right, section, first[1], *arrived[:2], low, high, start, thick, full, lateral,
         scratch=[
             levels(FIRST, 2 * PAD_S),
             pltpu.VMEM(whole, jnp.float32),
@@ -659,7 +691,7 @@
     ext, fixed, to_right, to_left = call(
         functools.partial(last_source_kernel, cells),
         [(near, LAST.breadth * columns), (2 * cells, columns)] + [(GROUP, LAST.packed * columns)] * 2,
-        parts, section, sent[0], *arrived, last[0],
+        parts, section, *sent[:2], debts, *arrived, last[0],
     )
     left = shifted(to_right, "span", 1)
     right = shifted(to_left, "span", -1)

time: 60.2 us -> 58.3 us (0.968)
  the two profiles are of different devices: /device:TPU:1 before, /device:TPU:126 now
where the time goes in v7:
time: 58.3 us; the launch traced here: 58.2 us
  waiting for transfers between devices  30.2 us (52%)
  starting transfers between devices  17.3 us (30%)
  Pallas kernels  10.2 us (17%)
    ppermute x16, waiting for transfers between devices, shifted(): lax.ppermute(block, axis, [(i, (i + step) % count) for i in range(count)])  30.2 us
    ppermute x16, starting transfers between devices, shifted(): lax.ppermute(block, axis, [(i, (i + step) % count) for i in range(count)])  17.3 us
    pallas_call x9, Pallas kernels, call(): pl.pallas_call(body, out_shape=[jax.ShapeDtypeStruct(s, jnp.float32) for...  10.2 us
  transfers between devices with their start and end apart: 16, of which 10 were waited for; matrix products, arithmetic and copies ran while one was open for 0% of the time, Pallas kernels for 7%

profile of v7, /device:TPU:126, one launch (start us, length us, event | category | flops | bytes accessed | tf_op | source)
XLA Modules:
  0.0 58.2 jit_solution(17118742180340708200)
XLA Ops:
  0.0 0.0 copy-start.8
  0.0 1.4 %shard_map.127 = (f32[192,512]{1,0:T(8,128)S(1)}, f32[64,512]{1,0:T(8,128)S(1)}, f32[16,512]{1,0:T(8,128)S(1)}, f32[16,512]{1,0:T(8,128)S(1)}, f32[448,128]{1,0:T(8,128)S(1)}, /*index=5*/f32[448,128]{1,0:T(8,128)S(1)}) custom-call(f32[3,64,4,128]{3,2,1,0:T(4,128)} %velocity.1, f32[64,4,128]{2,1,0:T(4,128)} %viscosity.1, bf16[32,576]{1,0:T(8,128)(2,1)} %constant.26.clone.moments), custom_call_target="tpu_custom_call" | custom-call | tf_op jit(solution)/shard_map/pallas_call | solution.py:608
  1.5 0.0 collective-permute-start.2
  1.5 1.7 %collective-permute-start.3 = (f32[448,128]{1,0:T(8,128)S(1)}, f32[448,128]{1,0:T(8,128)S(1)}, u32[]{:S(2)}, u32[]{:S(2)}) collective-permute-start(f32[448,128]{1,0:T(8,128)S(1)} %get-tuple-element.36), channel_id=1, source_target_pairs={{0,7},{1,0},{2,1},{3,2},{4,3},{5,4},{6,5},{7,6},{8,15},{9,8},{10,9... | collective-permute-start | bytes 688136 | tf_op jit(solution)/shard_map/ppermute | solution.py:619
  3.2 3.0 %collective-permute-start = (f32[16,512]{1,0:T(8,128)S(1)}, f32[16,512]{1,0:T(8,128)S(1)}, u32[]{:S(2)}, u32[]{:S(2)}) collective-permute-start(f32[16,512]{1,0:T(8,128)S(1)} %get-tuple-element.33), channel_id=1, source_target_pairs={{0,8},{8,16},{16,24},{24,32},{32,40},{40,48},{48,56},{56,64},{64,7... | collective-permute-start | bytes 98312 | tf_op jit(solution)/shard_map/ppermute | solution.py:619
  6.3 0.0 collective-permute-start.1
  6.3 0.0 copy-done.8
  6.3 0.0 copy-start
  6.3 0.0 copy-start.7
  6.3 0.9 %shard_map.128.rough = f32[192,512]{1,0:T(8,128)S(1)} custom-call(f32[192,512]{1,0:T(8,128)S(1)} %get-tuple-element.31.flat.start, f32[64,512]{1,0:T(8,128)S(1)} %get-tuple-element.32.thick, f32[128,64]{1,0:T(8,128)S(1)} %copy-done.8), custom_call_target="tpu_custom_call" | custom-call | tf_op jit(solution)/shard_map/pallas_call | solution.py:608
  7.2 0.0 copy-start.4
  7.2 0.6 %collective-permute-done.left = f32[16,512]{1,0:T(8,128)S(1)} collective-permute-done((f32[16,512]{1,0:T(8,128)S(1)}, f32[16,512]{1,0:T(8,128)S(1)}, u32[]{:S(2)}, u32[]{:S(2)}) %collective-permute-start) | collective-permute-done | bytes 32800 | tf_op jit(solution)/shard_map/ppermute | solution.py:619
  7.9 5.6 %collective-permute-done.1.right = f32[16,512]{1,0:T(8,128)S(1)} collective-permute-done((f32[16,512]{1,0:T(8,128)S(1)}, f32[16,512]{1,0:T(8,128)S(1)}, u32[]{:S(2)}, u32[]{:S(2)}) %collective-permute-start.1) | collective-permute-done | bytes 32800 | tf_op jit(solution)/shard_map/ppermute | solution.py:619
  13.5 0.0 collective-permute-done.2.low
  13.5 0.0 collective-permute-done.3.high
  13.5 0.0 copy-done
  13.5 0.0 copy-done.7
  13.5 0.0 copy-start.10
  13.5 0.5 shard_map.129
  14.0 0.0 collective-permute-start.4
  14.1 1.7 %collective-permute-start.5 = (f32[656,128]{1,0:T(8,128)S(1)}, f32[656,128]{1,0:T(8,128)S(1)}, u32[]{:S(2)}, u32[]{:S(2)}) collective-permute-start(f32[656,128]{1,0:T(8,128)S(1)} %get-tuple-element.40), channel_id=1, source_target_pairs={{0,7},{1,0},{2,1},{3,2},{4,3},{5,4},{6,5},{7,6},{8,15},{9,8},{10,9... | collective-permute-start | bytes 1007624 | tf_op jit(solution)/shard_map/ppermute | solution.py:619
  15.8 2.6 %collective-permute-start.6 = (f32[272,128]{1,0:T(8,128)S(1)}, f32[272,128]{1,0:T(8,128)S(1)}, u32[]{:S(2)}, u32[]{:S(2)}) collective-permute-start(f32[272,128]{1,0:T(8,128)S(1)} %get-tuple-element.41), channel_id=1, source_target_pairs={{0,2},{1,3},{2,4},{3,5},{4,6},{5,7},{6,0},{7,1},{8,10},{9,11},{10,... | collective-permute-start | bytes 417800 | tf_op jit(solution)/shard_map/ppermute | solution.py:619
  18.4 0.0 collective-permute-start.7
  18.5 4.1 %collective-permute-done.6.low_two = f32[272,128]{1,0:T(8,128)S(1)} collective-permute-done((f32[272,128]{1,0:T(8,128)S(1)}, f32[272,128]{1,0:T(8,128)S(1)}, u32[]{:S(2)}, u32[]{:S(2)}) %collective-permute-start.6) | collective-permute-done | bytes 139296 | tf_op jit(solution)/shard_map/ppermute | solution.py:619
  22.6 3.6 %collective-permute-done.7.high_two = f32[272,128]{1,0:T(8,128)S(1)} collective-permute-done((f32[272,128]{1,0:T(8,128)S(1)}, f32[272,128]{1,0:T(8,128)S(1)}, u32[]{:S(2)}, u32[]{:S(2)}) %collective-permute-start.7) | collective-permute-done | bytes 139296 | tf_op jit(solution)/shard_map/ppermute | solution.py:619
  26.1 0.0 collective-permute-done.4.low_one
  26.1 0.0 collective-permute-done.5.high_one
  26.1 0.0 copy-done.4
  26.1 0.0 copy-done.10
  26.2 0.0 copy-start.2
  26.2 0.5 shard_map.130
  26.7 0.1 collective-permute-start.8
  26.8 2.0 %collective-permute-start.9 = (f32[8,3968]{1,0:T(8,128)S(1)}, f32[8,3968]{1,0:T(8,128)S(1)}, u32[]{:S(2)}, u32[]{:S(2)}) collective-permute-start(f32[8,3968]{1,0:T(8,128)S(1)} %get-tuple-element.45), channel_id=1, source_target_pairs={{0,248},{8,0},{16,8},{24,16},{32,24},{40,32},{48,40},{56,48},{64,5... | collective-permute-start | bytes 380936 | tf_op jit(solution)/shard_map/ppermute | solution.py:619
  28.8 0.0 copy-done.2
  28.8 0.0 copy-start.1
  28.8 0.0 copy-start.5
  28.8 1.8 %shard_map.131.partial = f32[160,1280]{1,0:T(8,128)S(1)} custom-call(f32[72,2048]{1,0:T(8,128)S(1)} %get-tuple-element.43.ext, f32[160,288]{1,0:T(8,128)S(1)} %copy-done.2), custom_call_target="tpu_custom_call" | custom-call | tf_op jit(solution)/shard_map/pallas_call | solution.py:608
  30.6 1.1 %collective-permute-done.8.left = f32[8,3968]{1,0:T(8,128)S(1)} collective-permute-done((f32[8,3968]{1,0:T(8,128)S(1)}, f32[8,3968]{1,0:T(8,128)S(1)}, u32[]{:S(2)}, u32[]{:S(2)}) %collective-permute-start.8) | collective-permute-done | bytes 127008 | tf_op jit(solution)/shard_map/ppermute | solution.py:619
  31.7 3.4 %collective-permute-done.9.right = f32[8,3968]{1,0:T(8,128)S(1)} collective-permute-done((f32[8,3968]{1,0:T(8,128)S(1)}, f32[8,3968]{1,0:T(8,128)S(1)}, u32[]{:S(2)}, u32[]{:S(2)}) %collective-permute-start.9) | collective-permute-done | bytes 127008 | tf_op jit(solution)/shard_map/ppermute | solution.py:619
  35.1 0.0 copy-done.1
  35.1 0.0 copy-done.5
  35.1 0.0 copy-start.9
  35.1 1.8 %shard_map.132 = (f32[192,512]{1,0:T(8,128)S(1)}, f32[72,512]{1,0:T(8,128)S(1)}, f32[128,128]{1,0:T(8,128)S(1)}, f32[608,128]{1,0:T(8,128)S(1)}, f32[608,128]{1,...) custom-call(f32[160,1280]{1,0:T(8,128)S(1)} %shard_map.131.partial, ...), custom_call_target="tpu_custom_call" | custom-call | tf_op jit(solution)/shard_map/pallas_call | solution.py:608
  36.9 0.0 collective-permute-start.10
  36.9 1.7 %collective-permute-start.11 = (f32[608,128]{1,0:T(8,128)S(1)}, f32[608,128]{1,0:T(8,128)S(1)}, u32[]{:S(2)}, u32[]{:S(2)}) collective-permute-start(f32[608,128]{1,0:T(8,128)S(1)} %get-tuple-element.49.down_near), channel_id=1, source_target_pairs={{0,7},{1,0},{2,1},{3,2},{4,3},{5,4},{6,5},{7,6},{8,15},{9,8},{10,9... | collective-permute-start | bytes 933896 | tf_op jit(solution)/shard_map/ppermute | solution.py:619
  38.7 1.9 %collective-permute-start.12 = (f32[264,128]{1,0:T(8,128)S(1)}, f32[264,128]{1,0:T(8,128)S(1)}, u32[]{:S(2)}, u32[]{:S(2)}) collective-permute-start(f32[264,128]{1,0:T(8,128)S(1)} %get-tuple-element.51), channel_id=1, source_target_pairs={{0,2},{1,3},{2,4},{3,5},{4,6},{5,7},{6,0},{7,1},{8,10},{9,11},{10,... | collective-permute-start | bytes 405512 | tf_op jit(solution)/shard_map/ppermute | solution.py:619
  40.5 0.2 collective-permute-start.13
  40.7 4.5 %collective-permute-done.12.low_two = f32[264,128]{1,0:T(8,128)S(1)} collective-permute-done((f32[264,128]{1,0:T(8,128)S(1)}, f32[264,128]{1,0:T(8,128)S(1)}, u32[]{:S(2)}, u32[]{:S(2)}) %collective-permute-start.12) | collective-permute-done | bytes 135200 | tf_op jit(solution)/shard_map/ppermute | solution.py:619
  45.2 2.8 %collective-permute-done.13.high_two = f32[264,128]{1,0:T(8,128)S(1)} collective-permute-done((f32[264,128]{1,0:T(8,128)S(1)}, f32[264,128]{1,0:T(8,128)S(1)}, u32[]{:S(2)}, u32[]{:S(2)}) %collective-permute-start.13) | collective-permute-done | bytes 135200 | tf_op jit(solution)/shard_map/ppermute | solution.py:619
  48.0 0.0 collective-permute-done.10.low_one
  48.0 0.0 collective-permute-done.11.high_one
  48.0 0.0 copy-done.9
  48.0 0.0 copy-start.3
  48.0 0.3 shard_map.133
  48.3 0.4 collective-permute-start.14
  48.7 1.9 %collective-permute-start.15 = (f32[8,2688]{1,0:T(8,128)S(1)}, f32[8,2688]{1,0:T(8,128)S(1)}, u32[]{:S(2)}, u32[]{:S(2)}) collective-permute-start(f32[8,2688]{1,0:T(8,128)S(1)} %get-tuple-element.55), channel_id=1, source_target_pairs={{0,248},{8,0},{16,8},{24,16},{32,24},{40,32},{48,40},{56,48},{64,5... | collective-permute-start | bytes 258056 | tf_op jit(solution)/shard_map/ppermute | solution.py:619
  50.6 0.0 copy-done.3
  50.6 0.0 copy-start.6
  50.6 1.4 %shard_map.134.partial = f32[128,1024]{1,0:T(8,128)S(1)} custom-call(f32[72,1792]{1,0:T(8,128)S(1)} %get-tuple-element.53.ext, f32[128,288]{1,0:T(8,128)S(1)} %copy-done.3), custom_call_target="tpu_custom_call" | custom-call | tf_op jit(solution)/shard_map/pallas_call | solution.py:608
  52.0 1.1 %collective-permute-done.14.left = f32[8,2688]{1,0:T(8,128)S(1)} collective-permute-done((f32[8,2688]{1,0:T(8,128)S(1)}, f32[8,2688]{1,0:T(8,128)S(1)}, u32[]{:S(2)}, u32[]{:S(2)}) %collective-permute-start.14) | collective-permute-done | bytes 86048 | tf_op jit(solution)/shard_map/ppermute | solution.py:619
  53.1 3.4 %collective-permute-done.15.right = f32[8,2688]{1,0:T(8,128)S(1)} collective-permute-done((f32[8,2688]{1,0:T(8,128)S(1)}, f32[8,2688]{1,0:T(8,128)S(1)}, u32[]{:S(2)}, u32[]{:S(2)}) %collective-permute-start.15) | collective-permute-done | bytes 86048 | tf_op jit(solution)/shard_map/ppermute | solution.py:619
  56.5 0.0 copy-done.6
  56.5 1.5 %shard_map.135 = f32[3,64,4,128]{3,2,1,0:T(4,128)} custom-call(f32[128,1024]{1,0:T(8,128)S(1)} %shard_map.134.partial, f32[8,2688]{1,0:T(8,128)S(1)} %collective-permute-done.14.left, f32[8,2688]{1,0:T(8,128)S(1)} %collective-permute-done.15.right, f32[192,512]{1,0:T(8,128)S(1)} %get-tuple-element.47.section, f32[128,128]{1,0:T(8,128)S(1)} %get-tuple-element.56.fixed, ...), custom_call_target="tpu_custom_call" | custom-call | tf_op jit(solution)/shard_map/pallas_call | solution.py:608
Async XLA Ops:
  0.0 6.3 %copy-start.8 = (f32[128,64]{1,0:T(8,128)S(1)}, f32[128,64]{1,0:T(8,128)}, u32[]{:S(2)}) copy-start(f32[128,64]{1,0:T(8,128)} %constant.22.clone.own) | copy-start | bytes 98308
  1.5 12.0 %collective-permute-start.2 = (f32[448,128]{1,0:T(8,128)S(1)}, f32[448,128]{1,0:T(8,128)S(1)}, u32[]{:S(2)}, u32[]{:S(2)}) collective-permute-start(f32[448,128]{1,0:T(8,128)S(1)} %get-tuple-element.35), channel_id=1, source_target_pairs={{0,1},{1,2},{2,3},{3,4},{4,5},{5,6},{6,7},{7,0},{8,9},{9,10},{10,1... | collective-permute-start | bytes 688136 | tf_op jit(solution)/shard_map/ppermute | solution.py:619
  1.5 12.0 %collective-permute-start.3 = (f32[448,128]{1,0:T(8,128)S(1)}, f32[448,128]{1,0:T(8,128)S(1)}, u32[]{:S(2)}, u32[]{:S(2)}) collective-permute-start(f32[448,128]{1,0:T(8,128)S(1)} %get-tuple-element.36), channel_id=1, source_target_pairs={{0,7},{1,0},{2,1},{3,2},{4,3},{5,4},{6,5},{7,6},{8,15},{9,8},{10,9... | collective-permute-start | bytes 688136 | tf_op jit(solution)/shard_map/ppermute | solution.py:619
  3.2 4.6 %collective-permute-start = (f32[16,512]{1,0:T(8,128)S(1)}, f32[16,512]{1,0:T(8,128)S(1)}, u32[]{:S(2)}, u32[]{:S(2)}) collective-permute-start(f32[16,512]{1,0:T(8,128)S(1)} %get-tuple-element.33), channel_id=1, source_target_pairs={{0,8},{8,16},{16,24},{24,32},{32,40},{40,48},{48,56},{56,64},{64,7... | collective-permute-start | bytes 98312 | tf_op jit(solution)/shard_map/ppermute | solution.py:619
  6.3 7.2 %collective-permute-start.1 = (f32[16,512]{1,0:T(8,128)S(1)}, f32[16,512]{1,0:T(8,128)S(1)}, u32[]{:S(2)}, u32[]{:S(2)}) collective-permute-start(f32[16,512]{1,0:T(8,128)S(1)} %get-tuple-element.34), channel_id=1, source_target_pairs={{0,248},{8,0},{16,8},{24,16},{32,24},{40,32},{48,40},{56,48},{64,5... | collective-permute-start | bytes 98312 | tf_op jit(solution)/shard_map/ppermute | solution.py:619
  6.3 7.2 %copy-start = (bf16[72,192]{1,0:T(8,128)(2,1)S(1)}, bf16[72,192]{1,0:T(8,128)(2,1)}, u32[]{:S(2)}) copy-start(bf16[72,192]{1,0:T(8,128)(2,1)} %constant.27.clone.lateral) | copy-start | bytes 82948
  6.3 7.2 %copy-start.7 = (bf16[3,128,96]{2,1,0:T(8,128)(2,1)S(1)}, bf16[3,128,96]{2,1,0:T(8,128)(2,1)}, u32[]{:S(2)}) copy-start(bf16[3,128,96]{2,1,0:T(8,128)(2,1)} %constant.24.clone.slopes) | copy-start | bytes 221188
  7.2 18.9 %copy-start.4 = (bf16[32,576]{1,0:T(8,128)(2,1)S(1)}, bf16[32,576]{1,0:T(8,128)(2,1)}, u32[]{:S(2)}) copy-start(bf16[32,576]{1,0:T(8,128)(2,1)} %constant.26.clone.moments) | copy-start | bytes 110596
  13.5 12.6 %copy-start.10 = (bf16[64,240]{1,0:T(8,128)(2,1)S(1)}, bf16[64,240]{1,0:T(8,128)(2,1)}, u32[]{:S(2)}) copy-start(bf16[64,240]{1,0:T(8,128)(2,1)} %constant.28.clone.source) | copy-start | bytes 92164
  14.0 12.1 %collective-permute-start.4 = (f32[656,128]{1,0:T(8,128)S(1)}, f32[656,128]{1,0:T(8,128)S(1)}, u32[]{:S(2)}, u32[]{:S(2)}) collective-permute-start(f32[656,128]{1,0:T(8,128)S(1)} %get-tuple-element.39), channel_id=1, source_target_pairs={{0,1},{1,2},{2,3},{3,4},{4,5},{5,6},{6,7},{7,0},{8,9},{9,10},{10,1... | collective-permute-start | bytes 1007624 | tf_op jit(solution)/shard_map/ppermute | solution.py:619
  14.1 12.1 %collective-permute-start.5 = (f32[656,128]{1,0:T(8,128)S(1)}, f32[656,128]{1,0:T(8,128)S(1)}, u32[]{:S(2)}, u32[]{:S(2)}) collective-permute-start(f32[656,128]{1,0:T(8,128)S(1)} %get-tuple-element.40), channel_id=1, source_target_pairs={{0,7},{1,0},{2,1},{3,2},{4,3},{5,4},{6,5},{7,6},{8,15},{9,8},{10,9... | collective-permute-start | bytes 1007624 | tf_op jit(solution)/shard_map/ppermute | solution.py:619
  15.8 6.8 %collective-permute-start.6 = (f32[272,128]{1,0:T(8,128)S(1)}, f32[272,128]{1,0:T(8,128)S(1)}, u32[]{:S(2)}, u32[]{:S(2)}) collective-permute-start(f32[272,128]{1,0:T(8,128)S(1)} %get-tuple-element.41), channel_id=1, source_target_pairs={{0,2},{1,3},{2,4},{3,5},{4,6},{5,7},{6,0},{7,1},{8,10},{9,11},{10,... | collective-permute-start | bytes 417800 | tf_op jit(solution)/shard_map/ppermute | solution.py:619
  18.4 7.7 %collective-permute-start.7 = (f32[272,128]{1,0:T(8,128)S(1)}, f32[272,128]{1,0:T(8,128)S(1)}, u32[]{:S(2)}, u32[]{:S(2)}) collective-permute-start(f32[272,128]{1,0:T(8,128)S(1)} %get-tuple-element.42), channel_id=1, source_target_pairs={{0,6},{1,7},{2,0},{3,1},{4,2},{5,3},{6,4},{7,5},{8,14},{9,15},{10,... | collective-permute-start | bytes 417800 | tf_op jit(solution)/shard_map/ppermute | solution.py:619
  26.2 2.6 %copy-start.2 = (f32[160,288]{1,0:T(8,128)S(1)}, f32[160,288]{1,0:T(8,128)}, u32[]{:S(2)}) copy-start(f32[160,288]{1,0:T(8,128)} %constant.23.clone.solve) | copy-start | bytes 552964
  26.7 5.0 %collective-permute-start.8 = (f32[8,3968]{1,0:T(8,128)S(1)}, f32[8,3968]{1,0:T(8,128)S(1)}, u32[]{:S(2)}, u32[]{:S(2)}) collective-permute-start(f32[8,3968]{1,0:T(8,128)S(1)} %get-tuple-element.44), channel_id=1, source_target_pairs={{0,8},{8,16},{16,24},{24,32},{32,40},{40,48},{48,56},{56,64},{64,7... | collective-permute-start | bytes 380936 | tf_op jit(solution)/shard_map/ppermute | solution.py:619
  26.8 8.3 %collective-permute-start.9 = (f32[8,3968]{1,0:T(8,128)S(1)}, f32[8,3968]{1,0:T(8,128)S(1)}, u32[]{:S(2)}, u32[]{:S(2)}) collective-permute-start(f32[8,3968]{1,0:T(8,128)S(1)} %get-tuple-element.45), channel_id=1, source_target_pairs={{0,248},{8,0},{16,8},{24,16},{32,24},{40,32},{48,40},{56,48},{64,5... | collective-permute-start | bytes 380936 | tf_op jit(solution)/shard_map/ppermute | solution.py:619
  28.8 6.3 %copy-start.1 = (bf16[3,128,288]{2,1,0:T(8,128)(2,1)S(1)}, bf16[3,128,288]{2,1,0:T(8,128)(2,1)}, u32[]{:S(2)}) copy-start(bf16[3,128,288]{2,1,0:T(8,128)(2,1)} %constant.25.clone.full) | copy-start | bytes 663556
  28.8 6.3 %copy-start.5 = (bf16[160,384]{1,0:T(8,128)(2,1)S(1)}, bf16[160,384]{1,0:T(8,128)(2,1)}, u32[]{:S(2)}) copy-start(bf16[160,384]{1,0:T(8,128)(2,1)} %constant.29.clone.solve) | copy-start | bytes 368644
  35.1 12.9 %copy-start.9 = (bf16[64,240]{1,0:T(8,128)(2,1)S(1)}, bf16[64,240]{1,0:T(8,128)(2,1)}, u32[]{:S(2)}) copy-start(bf16[64,240]{1,0:T(8,128)(2,1)} %constant.31.clone.source) | copy-start | bytes 92164
  36.9 11.1 %collective-permute-start.10 = (f32[608,128]{1,0:T(8,128)S(1)}, f32[608,128]{1,0:T(8,128)S(1)}, u32[]{:S(2)}, u32[]{:S(2)}) collective-permute-start(f32[608,128]{1,0:T(8,128)S(1)} %get-tuple-element.48.up_near), channel_id=1, source_target_pairs={{0,1},{1,2},{2,3},{3,4},{4,5},{5,6},{6,7},{7,0},{8,9},{9,10},{10,1... | collective-permute-start | bytes 933896 | tf_op jit(solution)/shard_map/ppermute | solution.py:619
  36.9 11.0 %collective-permute-start.11 = (f32[608,128]{1,0:T(8,128)S(1)}, f32[608,128]{1,0:T(8,128)S(1)}, u32[]{:S(2)}, u32[]{:S(2)}) collective-permute-start(f32[608,128]{1,0:T(8,128)S(1)} %get-tuple-element.49.down_near), channel_id=1, source_target_pairs={{0,7},{1,0},{2,1},{3,2},{4,3},{5,4},{6,5},{7,6},{8,15},{9,8},{10,9... | collective-permute-start | bytes 933896 | tf_op jit(solution)/shard_map/ppermute | solution.py:619
  38.7 6.5 %collective-permute-start.12 = (f32[264,128]{1,0:T(8,128)S(1)}, f32[264,128]{1,0:T(8,128)S(1)}, u32[]{:S(2)}, u32[]{:S(2)}) collective-permute-start(f32[264,128]{1,0:T(8,128)S(1)} %get-tuple-element.51), channel_id=1, source_target_pairs={{0,2},{1,3},{2,4},{3,5},{4,6},{5,7},{6,0},{7,1},{8,10},{9,11},{10,... | collective-permute-start | bytes 405512 | tf_op jit(solution)/shard_map/ppermute | solution.py:619
  40.5 7.4 %collective-permute-start.13 = (f32[264,128]{1,0:T(8,128)S(1)}, f32[264,128]{1,0:T(8,128)S(1)}, u32[]{:S(2)}, u32[]{:S(2)}) collective-permute-start(f32[264,128]{1,0:T(8,128)S(1)} %get-tuple-element.52), channel_id=1, source_target_pairs={{0,6},{1,7},{2,0},{3,1},{4,2},{5,3},{6,4},{7,5},{8,14},{9,15},{10,... | collective-permute-start | bytes 405512 | tf_op jit(solution)/shard_map/ppermute | solution.py:619
  48.0 2.7 %copy-start.3 = (f32[128,288]{1,0:T(8,128)S(1)}, f32[128,288]{1,0:T(8,128)}, u32[]{:S(2)}) copy-start(f32[128,288]{1,0:T(8,128)} %constant.30.clone.solve) | copy-start | bytes 442372
  48.3 4.7 %collective-permute-start.14 = (f32[8,2688]{1,0:T(8,128)S(1)}, f32[8,2688]{1,0:T(8,128)S(1)}, u32[]{:S(2)}, u32[]{:S(2)}) collective-permute-start(f32[8,2688]{1,0:T(8,128)S(1)} %get-tuple-element.54), channel_id=1, source_target_pairs={{0,8},{8,16},{16,24},{24,32},{32,40},{40,48},{48,56},{56,64},{64,7... | collective-permute-start | bytes 258056 | tf_op jit(solution)/shard_map/ppermute | solution.py:619
  48.7 7.8 %collective-permute-start.15 = (f32[8,2688]{1,0:T(8,128)S(1)}, f32[8,2688]{1,0:T(8,128)S(1)}, u32[]{:S(2)}, u32[]{:S(2)}) collective-permute-start(f32[8,2688]{1,0:T(8,128)S(1)} %get-tuple-element.55), channel_id=1, source_target_pairs={{0,248},{8,0},{16,8},{24,16},{32,24},{40,32},{48,40},{56,48},{64,5... | collective-permute-start | bytes 258056 | tf_op jit(solution)/shard_map/ppermute | solution.py:619
  50.6 5.9 %copy-start.6 = (bf16[128,384]{1,0:T(8,128)(2,1)S(1)}, bf16[128,384]{1,0:T(8,128)(2,1)}, u32[]{:S(2)}) copy-start(bf16[128,384]{1,0:T(8,128)(2,1)} %constant.32.clone.solve) | copy-start | bytes 294916

commit v8 on v7

--- a/solution.py
+++ b/solution.py
@@ -381,7 +381,7 @@
             ref = low_two if e < 0 else high_two
             return pick(ref, 0), ref[4 * cells :, :]
         ref, k = (low_one, e + ROWS) if e < 0 else (high_one, e - ROWS)
-        top = 9 * cells + PAD_M * k
+        top = 8 * cells + PAD_M * k
         return pick(ref, k), ref[top : top + PAD_M, :]
 
     def across(e, home):
@@ -445,19 +445,18 @@
 
 
 def last_source_kernel(
-    cells, parts, section, up_near, down_near, debts, low_one, high_one, low_two, high_two, source,
+    cells, parts, section, debts, low_one, high_one, low_two, high_two, source,
     ext, fixed, to_right, to_left,
 ):
     masks = edge_masks()
     pick = lambda ref, k: slot(ref, cells, k)[...]
-    phi, factor = 7, 8
     extra = {
-        0: pick(up_near, factor) * pick(low_one, phi) * masks[0],
-        ROWS - 1: pick(down_near, factor) * pick(high_one, phi) * masks[2],
+        0: pick(low_one, 7) * masks[0],
+        ROWS - 1: pick(high_one, 7) * masks[2],
         -1: pick(debts, 0),
         ROWS: pick(debts, 1),
-        -ROWS: pick(low_one, factor) * pick(low_two, 3) * masks[1],
-        2 * ROWS - 1: pick(high_one, factor) * pick(high_two, 3) * masks[3],
+        -ROWS: pick(low_two, 3) * masks[1],
+        2 * ROWS - 1: pick(high_two, 3) * masks[3],
     }
     fixed[:cells, :] = extra[0]
     fixed[cells:, :] = extra[ROWS - 1]
@@ -577,12 +576,10 @@
     slot(debts, cells, 0)[...] = owed[-1]
     slot(debts, cells, 1)[...] = owed[ROWS]
     blocks, moments, at, up, down = own_source(cells, following, lateral, parts, owed)
-    first = scale * (thick[:, lane(0)] + tile(1, 0))
-    last = scale * (tile(1, ROWS - 1) - thick[:, lane(ROWS - 1)])
-    fill_slots(up_near, cells, blocks + [at(2), at(3), up, phi(0), first], moments)
-    fill_slots(down_near, cells, blocks + [at(0), at(1), down, phi(ROWS - 1), last], moments)
-    fill_slots(up_far, cells, [blocks[3], at(2), at(3), phi(0)], moments[3:])
-    fill_slots(down_far, cells, [blocks[0], at(0), at(1), phi(ROWS - 1)], moments[:1])
+    fill_slots(up_near, cells, blocks + [at(2), at(3), up, owed[ROWS]], moments)
+    fill_slots(down_near, cells, blocks + [at(0), at(1), down, owed[-1]], moments)
+    fill_slots(up_far, cells, [blocks[3], at(2), at(3), owed[ROWS]], moments[3:])
+    fill_slots(down_far, cells, [blocks[0], at(0), at(1), owed[-1]], moments[:1])
 
 
 def last_kernel(cells, partial, left, right, section, fixed, solve, out, levels, staged, sems):
@@ -678,7 +675,7 @@
 
     section, parts, debts, *sent = call(
         functools.partial(middle_kernel, cells),
-        [whole, (near, width), (2 * cells, columns)] + message(9, 4, 4, 1),
+        [whole, (near, width), (2 * cells, columns)] + message(8, 4, 4, 1),
         partial, left, right, section, first[1], *arrived[:2], low, high, start, thick, full, lateral,
         scratch=[
             levels(FIRST, 2 * PAD_S),
@@ -691,7 +688,7 @@
     ext, fixed, to_right, to_left = call(
         functools.partial(last_source_kernel, cells),
         [(near, LAST.breadth * columns), (2 * cells, columns)] + [(GROUP, LAST.packed * columns)] * 2,
-        parts, section, *sent[:2], debts, *arrived, last[0],
+        parts, section, debts, *arrived, last[0],
     )
     left = shifted(to_right, "span", 1)
     right = shifted(to_left, "span", -1)

time: 58.3 us -> 57.9 us (level)
  no operation moved by 1% of the time
where the time goes in v8:
time: 57.9 us; the launch traced here: 57.8 us
  waiting for transfers between devices  29.9 us (52%)
  starting transfers between devices  17.3 us (30%)
  Pallas kernels  10.2 us (18%)
    ppermute x16, waiting for transfers between devices, shifted(): lax.ppermute(block, axis, [(i, (i + step) % count) for i in range(count)])  29.9 us
    ppermute x16, starting transfers between devices, shifted(): lax.ppermute(block, axis, [(i, (i + step) % count) for i in range(count)])  17.3 us
    pallas_call x9, Pallas kernels, call(): pl.pallas_call(body, out_shape=[jax.ShapeDtypeStruct(s, jnp.float32) for...  10.2 us
  transfers between devices with their start and end apart: 16, of which 10 were waited for; matrix products, arithmetic and copies ran while one was open for 0% of the time, Pallas kernels for 7%

profile of v8, /device:TPU:126, one launch (start us, length us, event | category | flops | bytes accessed | tf_op | source)
XLA Modules:
  0.0 57.8 jit_solution(1114441912224699645)
XLA Ops:
  0.0 0.0 copy-start.8
  0.0 1.4 %shard_map.127 = (f32[192,512]{1,0:T(8,128)S(1)}, f32[64,512]{1,0:T(8,128)S(1)}, f32[16,512]{1,0:T(8,128)S(1)}, f32[16,512]{1,0:T(8,128)S(1)}, f32[448,128]{1,0:T(8,128)S(1)}, /*index=5*/f32[448,128]{1,0:T(8,128)S(1)}) custom-call(f32[3,64,4,128]{3,2,1,0:T(4,128)} %velocity.1, f32[64,4,128]{2,1,0:T(4,128)} %viscosity.1, bf16[32,576]{1,0:T(8,128)(2,1)} %constant.26.clone.moments), custom_call_target="tpu_custom_call" | custom-call | tf_op jit(solution)/shard_map/pallas_call | solution.py:605
  1.5 0.0 collective-permute-start.2
  1.5 1.7 %collective-permute-start.3 = (f32[448,128]{1,0:T(8,128)S(1)}, f32[448,128]{1,0:T(8,128)S(1)}, u32[]{:S(2)}, u32[]{:S(2)}) collective-permute-start(f32[448,128]{1,0:T(8,128)S(1)} %get-tuple-element.36), channel_id=1, source_target_pairs={{0,7},{1,0},{2,1},{3,2},{4,3},{5,4},{6,5},{7,6},{8,15},{9,8},{10,9... | collective-permute-start | bytes 688136 | tf_op jit(solution)/shard_map/ppermute | solution.py:616
  3.2 3.0 %collective-permute-start = (f32[16,512]{1,0:T(8,128)S(1)}, f32[16,512]{1,0:T(8,128)S(1)}, u32[]{:S(2)}, u32[]{:S(2)}) collective-permute-start(f32[16,512]{1,0:T(8,128)S(1)} %get-tuple-element.33), channel_id=1, source_target_pairs={{0,8},{8,16},{16,24},{24,32},{32,40},{40,48},{48,56},{56,64},{64,7... | collective-permute-start | bytes 98312 | tf_op jit(solution)/shard_map/ppermute | solution.py:616
  6.3 0.0 collective-permute-start.1
  6.3 0.0 copy-done.8
  6.3 0.0 copy-start
  6.3 0.0 copy-start.7
  6.3 0.9 %shard_map.128.rough = f32[192,512]{1,0:T(8,128)S(1)} custom-call(f32[192,512]{1,0:T(8,128)S(1)} %get-tuple-element.31.flat.start, f32[64,512]{1,0:T(8,128)S(1)} %get-tuple-element.32.thick, f32[128,64]{1,0:T(8,128)S(1)} %copy-done.8), custom_call_target="tpu_custom_call" | custom-call | tf_op jit(solution)/shard_map/pallas_call | solution.py:605
  7.2 0.0 copy-start.4
  7.2 0.6 %collective-permute-done.left = f32[16,512]{1,0:T(8,128)S(1)} collective-permute-done((f32[16,512]{1,0:T(8,128)S(1)}, f32[16,512]{1,0:T(8,128)S(1)}, u32[]{:S(2)}, u32[]{:S(2)}) %collective-permute-start) | collective-permute-done | bytes 32800 | tf_op jit(solution)/shard_map/ppermute | solution.py:616
  7.9 5.6 %collective-permute-done.1.right = f32[16,512]{1,0:T(8,128)S(1)} collective-permute-done((f32[16,512]{1,0:T(8,128)S(1)}, f32[16,512]{1,0:T(8,128)S(1)}, u32[]{:S(2)}, u32[]{:S(2)}) %collective-permute-start.1) | collective-permute-done | bytes 32800 | tf_op jit(solution)/shard_map/ppermute | solution.py:616
  13.5 0.0 collective-permute-done.2.low
  13.5 0.0 collective-permute-done.3.high
  13.5 0.0 copy-done
  13.5 0.0 copy-done.7
  13.5 0.0 copy-start.10
  13.5 0.5 shard_map.129
  14.1 0.0 collective-permute-start.4
  14.1 1.7 %collective-permute-start.5 = (f32[656,128]{1,0:T(8,128)S(1)}, f32[656,128]{1,0:T(8,128)S(1)}, u32[]{:S(2)}, u32[]{:S(2)}) collective-permute-start(f32[656,128]{1,0:T(8,128)S(1)} %get-tuple-element.40), channel_id=1, source_target_pairs={{0,7},{1,0},{2,1},{3,2},{4,3},{5,4},{6,5},{7,6},{8,15},{9,8},{10,9... | collective-permute-start | bytes 1007624 | tf_op jit(solution)/shard_map/ppermute | solution.py:616
  15.8 2.6 %collective-permute-start.6 = (f32[272,128]{1,0:T(8,128)S(1)}, f32[272,128]{1,0:T(8,128)S(1)}, u32[]{:S(2)}, u32[]{:S(2)}) collective-permute-start(f32[272,128]{1,0:T(8,128)S(1)} %get-tuple-element.41), channel_id=1, source_target_pairs={{0,2},{1,3},{2,4},{3,5},{4,6},{5,7},{6,0},{7,1},{8,10},{9,11},{10,... | collective-permute-start | bytes 417800 | tf_op jit(solution)/shard_map/ppermute | solution.py:616
  18.5 0.0 collective-permute-start.7
  18.5 4.1 %collective-permute-done.6.low_two = f32[272,128]{1,0:T(8,128)S(1)} collective-permute-done((f32[272,128]{1,0:T(8,128)S(1)}, f32[272,128]{1,0:T(8,128)S(1)}, u32[]{:S(2)}, u32[]{:S(2)}) %collective-permute-start.6) | collective-permute-done | bytes 139296 | tf_op jit(solution)/shard_map/ppermute | solution.py:616
  22.6 3.6 %collective-permute-done.7.high_two = f32[272,128]{1,0:T(8,128)S(1)} collective-permute-done((f32[272,128]{1,0:T(8,128)S(1)}, f32[272,128]{1,0:T(8,128)S(1)}, u32[]{:S(2)}, u32[]{:S(2)}) %collective-permute-start.7) | collective-permute-done | bytes 139296 | tf_op jit(solution)/shard_map/ppermute | solution.py:616
  26.1 0.0 collective-permute-done.4.low_one
  26.1 0.0 collective-permute-done.5.high_one
  26.1 0.0 copy-done.4
  26.2 0.0 copy-done.10
  26.2 0.0 copy-start.2
  26.2 0.5 shard_map.130
  26.7 0.1 collective-permute-start.8
  26.8 2.0 %collective-permute-start.9 = (f32[8,3968]{1,0:T(8,128)S(1)}, f32[8,3968]{1,0:T(8,128)S(1)}, u32[]{:S(2)}, u32[]{:S(2)}) collective-permute-start(f32[8,3968]{1,0:T(8,128)S(1)} %get-tuple-element.45), channel_id=1, source_target_pairs={{0,248},{8,0},{16,8},{24,16},{32,24},{40,32},{48,40},{56,48},{64,5... | collective-permute-start | bytes 380936 | tf_op jit(solution)/shard_map/ppermute | solution.py:616
  28.8 0.0 copy-done.2
  28.8 0.0 copy-start.1
  28.8 0.0 copy-start.5
  28.8 1.8 %shard_map.131.partial = f32[160,1280]{1,0:T(8,128)S(1)} custom-call(f32[72,2048]{1,0:T(8,128)S(1)} %get-tuple-element.43.ext, f32[160,288]{1,0:T(8,128)S(1)} %copy-done.2), custom_call_target="tpu_custom_call" | custom-call | tf_op jit(solution)/shard_map/pallas_call | solution.py:605
  30.6 1.1 %collective-permute-done.8.left = f32[8,3968]{1,0:T(8,128)S(1)} collective-permute-done((f32[8,3968]{1,0:T(8,128)S(1)}, f32[8,3968]{1,0:T(8,128)S(1)}, u32[]{:S(2)}, u32[]{:S(2)}) %collective-permute-start.8) | collective-permute-done | bytes 127008 | tf_op jit(solution)/shard_map/ppermute | solution.py:616
  31.7 3.4 %collective-permute-done.9.right = f32[8,3968]{1,0:T(8,128)S(1)} collective-permute-done((f32[8,3968]{1,0:T(8,128)S(1)}, f32[8,3968]{1,0:T(8,128)S(1)}, u32[]{:S(2)}, u32[]{:S(2)}) %collective-permute-start.9) | collective-permute-done | bytes 127008 | tf_op jit(solution)/shard_map/ppermute | solution.py:616
  35.1 0.0 copy-done.1
  35.1 0.0 copy-done.5
  35.1 0.0 copy-start.9
  35.1 1.8 %shard_map.132 = (f32[192,512]{1,0:T(8,128)S(1)}, f32[72,512]{1,0:T(8,128)S(1)}, f32[128,128]{1,0:T(8,128)S(1)}, f32[544,128]{1,0:T(8,128)S(1)}, f32[544,128]{1,...) custom-call(f32[160,1280]{1,0:T(8,128)S(1)} %shard_map.131.partial, ...), custom_call_target="tpu_custom_call" | custom-call | tf_op jit(solution)/shard_map/pallas_call | solution.py:605
  36.9 0.0 collective-permute-start.10
  36.9 1.7 %collective-permute-start.11 = (f32[544,128]{1,0:T(8,128)S(1)}, f32[544,128]{1,0:T(8,128)S(1)}, u32[]{:S(2)}, u32[]{:S(2)}) collective-permute-start(f32[544,128]{1,0:T(8,128)S(1)} %get-tuple-element.50), channel_id=1, source_target_pairs={{0,7},{1,0},{2,1},{3,2},{4,3},{5,4},{6,5},{7,6},{8,15},{9,8},{10,9... | collective-permute-start | bytes 835592 | tf_op jit(solution)/shard_map/ppermute | solution.py:616
  38.7 1.9 %collective-permute-start.12 = (f32[264,128]{1,0:T(8,128)S(1)}, f32[264,128]{1,0:T(8,128)S(1)}, u32[]{:S(2)}, u32[]{:S(2)}) collective-permute-start(f32[264,128]{1,0:T(8,128)S(1)} %get-tuple-element.51), channel_id=1, source_target_pairs={{0,2},{1,3},{2,4},{3,5},{4,6},{5,7},{6,0},{7,1},{8,10},{9,11},{10,... | collective-permute-start | bytes 405512 | tf_op jit(solution)/shard_map/ppermute | solution.py:616
  40.5 0.2 collective-permute-start.13
  40.7 4.5 %collective-permute-done.12.low_two = f32[264,128]{1,0:T(8,128)S(1)} collective-permute-done((f32[264,128]{1,0:T(8,128)S(1)}, f32[264,128]{1,0:T(8,128)S(1)}, u32[]{:S(2)}, u32[]{:S(2)}) %collective-permute-start.12) | collective-permute-done | bytes 135200 | tf_op jit(solution)/shard_map/ppermute | solution.py:616
  45.2 2.4 %collective-permute-done.13.high_two = f32[264,128]{1,0:T(8,128)S(1)} collective-permute-done((f32[264,128]{1,0:T(8,128)S(1)}, f32[264,128]{1,0:T(8,128)S(1)}, u32[]{:S(2)}, u32[]{:S(2)}) %collective-permute-start.13) | collective-permute-done | bytes 135200 | tf_op jit(solution)/shard_map/ppermute | solution.py:616
  47.6 0.0 collective-permute-done.10.low_one
  47.6 0.0 collective-permute-done.11.high_one
  47.6 0.0 copy-done.9
  47.6 0.0 copy-start.3
  47.6 0.3 shard_map.133
  48.0 0.4 collective-permute-start.14
  48.3 1.9 %collective-permute-start.15 = (f32[8,2688]{1,0:T(8,128)S(1)}, f32[8,2688]{1,0:T(8,128)S(1)}, u32[]{:S(2)}, u32[]{:S(2)}) collective-permute-start(f32[8,2688]{1,0:T(8,128)S(1)} %get-tuple-element.55), channel_id=1, source_target_pairs={{0,248},{8,0},{16,8},{24,16},{32,24},{40,32},{48,40},{56,48},{64,5... | collective-permute-start | bytes 258056 | tf_op jit(solution)/shard_map/ppermute | solution.py:616
  50.2 0.0 copy-done.3
  50.2 0.0 copy-start.6
  50.2 1.4 %shard_map.134.partial = f32[128,1024]{1,0:T(8,128)S(1)} custom-call(f32[72,1792]{1,0:T(8,128)S(1)} %get-tuple-element.53.ext, f32[128,288]{1,0:T(8,128)S(1)} %copy-done.3), custom_call_target="tpu_custom_call" | custom-call | tf_op jit(solution)/shard_map/pallas_call | solution.py:605
  51.6 1.1 %collective-permute-done.14.left = f32[8,2688]{1,0:T(8,128)S(1)} collective-permute-done((f32[8,2688]{1,0:T(8,128)S(1)}, f32[8,2688]{1,0:T(8,128)S(1)}, u32[]{:S(2)}, u32[]{:S(2)}) %collective-permute-start.14) | collective-permute-done | bytes 86048 | tf_op jit(solution)/shard_map/ppermute | solution.py:616
  52.7 3.4 %collective-permute-done.15.right = f32[8,2688]{1,0:T(8,128)S(1)} collective-permute-done((f32[8,2688]{1,0:T(8,128)S(1)}, f32[8,2688]{1,0:T(8,128)S(1)}, u32[]{:S(2)}, u32[]{:S(2)}) %collective-permute-start.15) | collective-permute-done | bytes 86048 | tf_op jit(solution)/shard_map/ppermute | solution.py:616
  56.1 0.0 copy-done.6
  56.1 1.5 %shard_map.135 = f32[3,64,4,128]{3,2,1,0:T(4,128)} custom-call(f32[128,1024]{1,0:T(8,128)S(1)} %shard_map.134.partial, f32[8,2688]{1,0:T(8,128)S(1)} %collective-permute-done.14.left, f32[8,2688]{1,0:T(8,128)S(1)} %collective-permute-done.15.right, f32[192,512]{1,0:T(8,128)S(1)} %get-tuple-element.47.section, f32[128,128]{1,0:T(8,128)S(1)} %get-tuple-element.56.fixed, ...), custom_call_target="tpu_custom_call" | custom-call | tf_op jit(solution)/shard_map/pallas_call | solution.py:605
Async XLA Ops:
  0.0 6.3 %copy-start.8 = (f32[128,64]{1,0:T(8,128)S(1)}, f32[128,64]{1,0:T(8,128)}, u32[]{:S(2)}) copy-start(f32[128,64]{1,0:T(8,128)} %constant.22.clone.own) | copy-start | bytes 98308
  1.5 12.0 %collective-permute-start.2 = (f32[448,128]{1,0:T(8,128)S(1)}, f32[448,128]{1,0:T(8,128)S(1)}, u32[]{:S(2)}, u32[]{:S(2)}) collective-permute-start(f32[448,128]{1,0:T(8,128)S(1)} %get-tuple-element.35), channel_id=1, source_target_pairs={{0,1},{1,2},{2,3},{3,4},{4,5},{5,6},{6,7},{7,0},{8,9},{9,10},{10,1... | collective-permute-start | bytes 688136 | tf_op jit(solution)/shard_map/ppermute | solution.py:616
  1.5 12.0 %collective-permute-start.3 = (f32[448,128]{1,0:T(8,128)S(1)}, f32[448,128]{1,0:T(8,128)S(1)}, u32[]{:S(2)}, u32[]{:S(2)}) collective-permute-start(f32[448,128]{1,0:T(8,128)S(1)} %get-tuple-element.36), channel_id=1, source_target_pairs={{0,7},{1,0},{2,1},{3,2},{4,3},{5,4},{6,5},{7,6},{8,15},{9,8},{10,9... | collective-permute-start | bytes 688136 | tf_op jit(solution)/shard_map/ppermute | solution.py:616
  3.2 4.6 %collective-permute-start = (f32[16,512]{1,0:T(8,128)S(1)}, f32[16,512]{1,0:T(8,128)S(1)}, u32[]{:S(2)}, u32[]{:S(2)}) collective-permute-start(f32[16,512]{1,0:T(8,128)S(1)} %get-tuple-element.33), channel_id=1, source_target_pairs={{0,8},{8,16},{16,24},{24,32},{32,40},{40,48},{48,56},{56,64},{64,7... | collective-permute-start | bytes 98312 | tf_op jit(solution)/shard_map/ppermute | solution.py:616
  6.3 7.2 %collective-permute-start.1 = (f32[16,512]{1,0:T(8,128)S(1)}, f32[16,512]{1,0:T(8,128)S(1)}, u32[]{:S(2)}, u32[]{:S(2)}) collective-permute-start(f32[16,512]{1,0:T(8,128)S(1)} %get-tuple-element.34), channel_id=1, source_target_pairs={{0,248},{8,0},{16,8},{24,16},{32,24},{40,32},{48,40},{56,48},{64,5... | collective-permute-start | bytes 98312 | tf_op jit(solution)/shard_map/ppermute | solution.py:616
  6.3 7.2 %copy-start = (bf16[72,192]{1,0:T(8,128)(2,1)S(1)}, bf16[72,192]{1,0:T(8,128)(2,1)}, u32[]{:S(2)}) copy-start(bf16[72,192]{1,0:T(8,128)(2,1)} %constant.27.clone.lateral) | copy-start | bytes 82948
  6.3 7.2 %copy-start.7 = (bf16[3,128,96]{2,1,0:T(8,128)(2,1)S(1)}, bf16[3,128,96]{2,1,0:T(8,128)(2,1)}, u32[]{:S(2)}) copy-start(bf16[3,128,96]{2,1,0:T(8,128)(2,1)} %constant.24.clone.slopes) | copy-start | bytes 221188
  7.2 18.9 %copy-start.4 = (bf16[32,576]{1,0:T(8,128)(2,1)S(1)}, bf16[32,576]{1,0:T(8,128)(2,1)}, u32[]{:S(2)}) copy-start(bf16[32,576]{1,0:T(8,128)(2,1)} %constant.26.clone.moments) | copy-start | bytes 110596
  13.5 12.6 %copy-start.10 = (bf16[64,240]{1,0:T(8,128)(2,1)S(1)}, bf16[64,240]{1,0:T(8,128)(2,1)}, u32[]{:S(2)}) copy-start(bf16[64,240]{1,0:T(8,128)(2,1)} %constant.28.clone.source) | copy-start | bytes 92164
  14.1 12.1 %collective-permute-start.4 = (f32[656,128]{1,0:T(8,128)S(1)}, f32[656,128]{1,0:T(8,128)S(1)}, u32[]{:S(2)}, u32[]{:S(2)}) collective-permute-start(f32[656,128]{1,0:T(8,128)S(1)} %get-tuple-element.39), channel_id=1, source_target_pairs={{0,1},{1,2},{2,3},{3,4},{4,5},{5,6},{6,7},{7,0},{8,9},{9,10},{10,1... | collective-permute-start | bytes 1007624 | tf_op jit(solution)/shard_map/ppermute | solution.py:616
  14.1 12.1 %collective-permute-start.5 = (f32[656,128]{1,0:T(8,128)S(1)}, f32[656,128]{1,0:T(8,128)S(1)}, u32[]{:S(2)}, u32[]{:S(2)}) collective-permute-start(f32[656,128]{1,0:T(8,128)S(1)} %get-tuple-element.40), channel_id=1, source_target_pairs={{0,7},{1,0},{2,1},{3,2},{4,3},{5,4},{6,5},{7,6},{8,15},{9,8},{10,9... | collective-permute-start | bytes 1007624 | tf_op jit(solution)/shard_map/ppermute | solution.py:616
  15.8 6.8 %collective-permute-start.6 = (f32[272,128]{1,0:T(8,128)S(1)}, f32[272,128]{1,0:T(8,128)S(1)}, u32[]{:S(2)}, u32[]{:S(2)}) collective-permute-start(f32[272,128]{1,0:T(8,128)S(1)} %get-tuple-element.41), channel_id=1, source_target_pairs={{0,2},{1,3},{2,4},{3,5},{4,6},{5,7},{6,0},{7,1},{8,10},{9,11},{10,... | collective-permute-start | bytes 417800 | tf_op jit(solution)/shard_map/ppermute | solution.py:616
  18.5 7.7 %collective-permute-start.7 = (f32[272,128]{1,0:T(8,128)S(1)}, f32[272,128]{1,0:T(8,128)S(1)}, u32[]{:S(2)}, u32[]{:S(2)}) collective-permute-start(f32[272,128]{1,0:T(8,128)S(1)} %get-tuple-element.42), channel_id=1, source_target_pairs={{0,6},{1,7},{2,0},{3,1},{4,2},{5,3},{6,4},{7,5},{8,14},{9,15},{10,... | collective-permute-start | bytes 417800 | tf_op jit(solution)/shard_map/ppermute | solution.py:616
  26.2 2.6 %copy-start.2 = (f32[160,288]{1,0:T(8,128)S(1)}, f32[160,288]{1,0:T(8,128)}, u32[]{:S(2)}) copy-start(f32[160,288]{1,0:T(8,128)} %constant.23.clone.solve) | copy-start | bytes 552964
  26.7 5.0 %collective-permute-start.8 = (f32[8,3968]{1,0:T(8,128)S(1)}, f32[8,3968]{1,0:T(8,128)S(1)}, u32[]{:S(2)}, u32[]{:S(2)}) collective-permute-start(f32[8,3968]{1,0:T(8,128)S(1)} %get-tuple-element.44), channel_id=1, source_target_pairs={{0,8},{8,16},{16,24},{24,32},{32,40},{40,48},{48,56},{56,64},{64,7... | collective-permute-start | bytes 380936 | tf_op jit(solution)/shard_map/ppermute | solution.py:616
  26.8 8.3 %collective-permute-start.9 = (f32[8,3968]{1,0:T(8,128)S(1)}, f32[8,3968]{1,0:T(8,128)S(1)}, u32[]{:S(2)}, u32[]{:S(2)}) collective-permute-start(f32[8,3968]{1,0:T(8,128)S(1)} %get-tuple-element.45), channel_id=1, source_target_pairs={{0,248},{8,0},{16,8},{24,16},{32,24},{40,32},{48,40},{56,48},{64,5... | collective-permute-start | bytes 380936 | tf_op jit(solution)/shard_map/ppermute | solution.py:616
  28.8 6.3 %copy-start.1 = (bf16[3,128,288]{2,1,0:T(8,128)(2,1)S(1)}, bf16[3,128,288]{2,1,0:T(8,128)(2,1)}, u32[]{:S(2)}) copy-start(bf16[3,128,288]{2,1,0:T(8,128)(2,1)} %constant.25.clone.full) | copy-start | bytes 663556
  28.8 6.3 %copy-start.5 = (bf16[160,384]{1,0:T(8,128)(2,1)S(1)}, bf16[160,384]{1,0:T(8,128)(2,1)}, u32[]{:S(2)}) copy-start(bf16[160,384]{1,0:T(8,128)(2,1)} %constant.29.clone.solve) | copy-start | bytes 368644
  35.1 12.5 %copy-start.9 = (bf16[64,240]{1,0:T(8,128)(2,1)S(1)}, bf16[64,240]{1,0:T(8,128)(2,1)}, u32[]{:S(2)}) copy-start(bf16[64,240]{1,0:T(8,128)(2,1)} %constant.31.clone.source) | copy-start | bytes 92164
  36.9 10.7 %collective-permute-start.10 = (f32[544,128]{1,0:T(8,128)S(1)}, f32[544,128]{1,0:T(8,128)S(1)}, u32[]{:S(2)}, u32[]{:S(2)}) collective-permute-start(f32[544,128]{1,0:T(8,128)S(1)} %get-tuple-element.49), channel_id=1, source_target_pairs={{0,1},{1,2},{2,3},{3,4},{4,5},{5,6},{6,7},{7,0},{8,9},{9,10},{10,1... | collective-permute-start | bytes 835592 | tf_op jit(solution)/shard_map/ppermute | solution.py:616
  36.9 10.7 %collective-permute-start.11 = (f32[544,128]{1,0:T(8,128)S(1)}, f32[544,128]{1,0:T(8,128)S(1)}, u32[]{:S(2)}, u32[]{:S(2)}) collective-permute-start(f32[544,128]{1,0:T(8,128)S(1)} %get-tuple-element.50), channel_id=1, source_target_pairs={{0,7},{1,0},{2,1},{3,2},{4,3},{5,4},{6,5},{7,6},{8,15},{9,8},{10,9... | collective-permute-start | bytes 835592 | tf_op jit(solution)/shard_map/ppermute | solution.py:616
  38.7 6.5 %collective-permute-start.12 = (f32[264,128]{1,0:T(8,128)S(1)}, f32[264,128]{1,0:T(8,128)S(1)}, u32[]{:S(2)}, u32[]{:S(2)}) collective-permute-start(f32[264,128]{1,0:T(8,128)S(1)} %get-tuple-element.51), channel_id=1, source_target_pairs={{0,2},{1,3},{2,4},{3,5},{4,6},{5,7},{6,0},{7,1},{8,10},{9,11},{10,... | collective-permute-start | bytes 405512 | tf_op jit(solution)/shard_map/ppermute | solution.py:616
  40.5 7.1 %collective-permute-start.13 = (f32[264,128]{1,0:T(8,128)S(1)}, f32[264,128]{1,0:T(8,128)S(1)}, u32[]{:S(2)}, u32[]{:S(2)}) collective-permute-start(f32[264,128]{1,0:T(8,128)S(1)} %get-tuple-element.52), channel_id=1, source_target_pairs={{0,6},{1,7},{2,0},{3,1},{4,2},{5,3},{6,4},{7,5},{8,14},{9,15},{10,... | collective-permute-start | bytes 405512 | tf_op jit(solution)/shard_map/ppermute | solution.py:616
  47.6 2.6 %copy-start.3 = (f32[128,288]{1,0:T(8,128)S(1)}, f32[128,288]{1,0:T(8,128)}, u32[]{:S(2)}) copy-start(f32[128,288]{1,0:T(8,128)} %constant.30.clone.solve) | copy-start | bytes 442372
  48.0 4.7 %collective-permute-start.14 = (f32[8,2688]{1,0:T(8,128)S(1)}, f32[8,2688]{1,0:T(8,128)S(1)}, u32[]{:S(2)}, u32[]{:S(2)}) collective-permute-start(f32[8,2688]{1,0:T(8,128)S(1)} %get-tuple-element.54), channel_id=1, source_target_pairs={{0,8},{8,16},{16,24},{24,32},{32,40},{40,48},{48,56},{56,64},{64,7... | collective-permute-start | bytes 258056 | tf_op jit(solution)/shard_map/ppermute | solution.py:616
  48.3 7.8 %collective-permute-start.15 = (f32[8,2688]{1,0:T(8,128)S(1)}, f32[8,2688]{1,0:T(8,128)S(1)}, u32[]{:S(2)}, u32[]{:S(2)}) collective-permute-start(f32[8,2688]{1,0:T(8,128)S(1)} %get-tuple-element.55), channel_id=1, source_target_pairs={{0,248},{8,0},{16,8},{24,16},{32,24},{40,32},{48,40},{56,48},{64,5... | collective-permute-start | bytes 258056 | tf_op jit(solution)/shard_map/ppermute | solution.py:616
  50.2 5.9 %copy-start.6 = (bf16[128,384]{1,0:T(8,128)(2,1)S(1)}, bf16[128,384]{1,0:T(8,128)(2,1)}, u32[]{:S(2)}) copy-start(bf16[128,384]{1,0:T(8,128)(2,1)} %constant.32.clone.solve) | copy-start | bytes 294916

commit v9 on v8

--- a/solution.py
+++ b/solution.py
@@ -51,13 +51,13 @@
     from_right, take_right = low_rank(np.concatenate([at(first, 1), at(second, 1)]), RANK_V)
     own = np.concatenate([at(first, 0), at(second, 0)])
     slopes = np.zeros((3, 2 * cells, 2 * PAD_V))
-    moments = np.zeros((2 * PAD_V, 3 * cells))
+    moments = np.zeros((3, 2 * PAD_V, cells))
     for c in range(3):
         rows = slice(RANK_V * c, RANK_V * (c + 1))
         slopes[c, :, :PAD_V][:, rows] = from_left
         slopes[c, :, PAD_V:][:, rows] = from_right
-        moments[rows, cells * c : cells * (c + 1)] = take_left
-        moments[PAD_V:][rows, cells * c : cells * (c + 1)] = take_right
+        moments[c, rows] = take_left
+        moments[c, PAD_V:][rows] = take_right
     m_left, t_left = low_rank(at(first, -1), RANK_M)
     m_right, t_right = low_rank(at(first, 1), RANK_M)
     lateral = np.zeros((cells + PAD_M, cells))
@@ -223,14 +223,23 @@
         copies.append(pltpu.make_async_copy(viscosity.at[:, r, :], thick.at[:, lane(r)], sems.at[len(copies)]))
     for copy in copies:
         copy.start()
-    for copy in copies:
-        copy.wait()
-    row = lambda c, r: flat[cells * c : cells * (c + 1), lane(r)]
-    fill_slots(upward, cells, [row(c, r) for c in range(3) for r in (2, 3)] + [thick[:, lane(3)]], [])
-    fill_slots(downward, cells, [row(c, r) for c in range(3) for r in (0, 1)] + [thick[:, lane(0)]], [])
-    both = split_dot(weights[...], flat[...])
+    copies[0].wait()
+    both = None
+    for c in range(3):
+        for copy in copies[1 + ROWS * c : 1 + ROWS * (c + 1)]:
+            copy.wait()
+        rows = slice(cells * c, cells * (c + 1))
+        for k in range(2):
+            slot(upward, cells, 2 * c + k)[...] = flat[rows, lane(2 + k)]
+            slot(downward, cells, 2 * c + k)[...] = flat[rows, lane(k)]
+        part = split_dot(weights[c], flat[rows, :])
+        both = part if both is None else both + part
     to_right[...] = both[:PAD_V]
     to_left[...] = both[PAD_V:]
+    for copy in copies[1 + 3 * ROWS :]:
+        copy.wait()
+    slot(upward, cells, 6)[...] = thick[:, lane(ROWS - 1)]
+    slot(downward, cells, 6)[...] = thick[:, lane(0)]
 
 
 def weighed(weights, value_at, r, home):
@@ -429,7 +438,7 @@
     first_source(cells, parts, section, (low_one, high_one, low_two, high_two), lateral, ext)
     both = split_dot(source[...], ext[...])
     pack_moments(FIRST, both, to_right, to_left)
-    held = split_dot(moments[...], section[...])
+    held = sum(split_dot(moments[c], section[cells * c : cells * (c + 1), :]) for c in range(3))
     for side, out in enumerate((to_right, to_left)):
         top, base = 4 * GROUP * side, PAD_V * side
         out[:, lane(FIRST.packed, ROWS)] = held[base : base + 8]
@@ -585,7 +594,7 @@
 def last_kernel(cells, partial, left, right, section, fixed, solve, out, levels, staged, sems):
     found = finish(LAST, partial, left, right, solve, levels)
     copies = []
-    for c in range(3):
+    for c in (2, 0, 1):
         rows = slice(cells * c, cells * (c + 1))
         for r in range(ROWS):
             value = section[rows, lane(r)]

time: 57.9 us -> 57.8 us (level)
  no operation moved by 1% of the time
where the time goes in v9:
time: 57.8 us; the launch traced here: 57.6 us
  waiting for transfers between devices  29.9 us (52%)
  starting transfers between devices  17.4 us (30%)
  Pallas kernels  10 us (17%)
    ppermute x16, waiting for transfers between devices, shifted(): lax.ppermute(block, axis, [(i, (i + step) % count) for i in range(count)])  29.9 us
    ppermute x16, starting transfers between devices, shifted(): lax.ppermute(block, axis, [(i, (i + step) % count) for i in range(count)])  17.4 us
    pallas_call x9, Pallas kernels, call(): pl.pallas_call(body, out_shape=[jax.ShapeDtypeStruct(s, jnp.float32) for...  10 us
  transfers between devices with their start and end apart: 16, of which 10 were waited for; matrix products, arithmetic and copies ran while one was open for 0% of the time, Pallas kernels for 7%

profile of v9, /device:TPU:126, one launch (start us, length us, event | category | flops | bytes accessed | tf_op | source)
XLA Modules:
  0.0 57.6 jit_solution(3389066553877282648)
XLA Ops:
  0.0 0.0 copy-start.8
  0.0 1.3 %shard_map.127 = (f32[192,512]{1,0:T(8,128)S(1)}, f32[64,512]{1,0:T(8,128)S(1)}, f32[16,512]{1,0:T(8,128)S(1)}, f32[16,512]{1,0:T(8,128)S(1)}, f32[448,128]{1,0:T(8,128)S(1)}, /*index=5*/f32[448,128]{1,0:T(8,128)S(1)}) custom-call(f32[3,64,4,128]{3,2,1,0:T(4,128)} %velocity.1, f32[64,4,128]{2,1,0:T(4,128)} %viscosity.1, ...), custom_call_target="tpu_custom_call" | custom-call | tf_op jit(solution)/shard_map/pallas_call | solution.py:614
  1.3 0.0 collective-permute-start.2
  1.4 1.7 %collective-permute-start.3 = (f32[448,128]{1,0:T(8,128)S(1)}, f32[448,128]{1,0:T(8,128)S(1)}, u32[]{:S(2)}, u32[]{:S(2)}) collective-permute-start(f32[448,128]{1,0:T(8,128)S(1)} %get-tuple-element.36), channel_id=1, source_target_pairs={{0,7},{1,0},{2,1},{3,2},{4,3},{5,4},{6,5},{7,6},{8,15},{9,8},{10,9... | collective-permute-start | bytes 688136 | tf_op jit(solution)/shard_map/ppermute | solution.py:625
  3.1 3.0 %collective-permute-start = (f32[16,512]{1,0:T(8,128)S(1)}, f32[16,512]{1,0:T(8,128)S(1)}, u32[]{:S(2)}, u32[]{:S(2)}) collective-permute-start(f32[16,512]{1,0:T(8,128)S(1)} %get-tuple-element.33), channel_id=1, source_target_pairs={{0,8},{8,16},{16,24},{24,32},{32,40},{40,48},{48,56},{56,64},{64,7... | collective-permute-start | bytes 98312 | tf_op jit(solution)/shard_map/ppermute | solution.py:625
  6.1 0.0 collective-permute-start.1
  6.1 0.0 copy-done.8
  6.1 0.0 copy-start
  6.1 0.0 copy-start.7
  6.2 0.9 %shard_map.128.rough = f32[192,512]{1,0:T(8,128)S(1)} custom-call(f32[192,512]{1,0:T(8,128)S(1)} %get-tuple-element.31.flat.start, f32[64,512]{1,0:T(8,128)S(1)} %get-tuple-element.32.thick, f32[128,64]{1,0:T(8,128)S(1)} %copy-done.8), custom_call_target="tpu_custom_call" | custom-call | tf_op jit(solution)/shard_map/pallas_call | solution.py:614
  7.1 0.0 copy-start.3
  7.1 0.6 %collective-permute-done.left = f32[16,512]{1,0:T(8,128)S(1)} collective-permute-done((f32[16,512]{1,0:T(8,128)S(1)}, f32[16,512]{1,0:T(8,128)S(1)}, u32[]{:S(2)}, u32[]{:S(2)}) %collective-permute-start) | collective-permute-done | bytes 32800 | tf_op jit(solution)/shard_map/ppermute | solution.py:625
  7.7 5.6 %collective-permute-done.1.right = f32[16,512]{1,0:T(8,128)S(1)} collective-permute-done((f32[16,512]{1,0:T(8,128)S(1)}, f32[16,512]{1,0:T(8,128)S(1)}, u32[]{:S(2)}, u32[]{:S(2)}) %collective-permute-start.1) | collective-permute-done | bytes 32800 | tf_op jit(solution)/shard_map/ppermute | solution.py:625
  13.4 0.0 collective-permute-done.2.low
  13.4 0.0 collective-permute-done.3.high
  13.4 0.0 copy-done
  13.4 0.0 copy-done.7
  13.4 0.0 copy-start.10
  13.4 0.5 shard_map.129
  13.9 0.0 collective-permute-start.4
  13.9 1.7 %collective-permute-start.5 = (f32[656,128]{1,0:T(8,128)S(1)}, f32[656,128]{1,0:T(8,128)S(1)}, u32[]{:S(2)}, u32[]{:S(2)}) collective-permute-start(f32[656,128]{1,0:T(8,128)S(1)} %get-tuple-element.40), channel_id=1, source_target_pairs={{0,7},{1,0},{2,1},{3,2},{4,3},{5,4},{6,5},{7,6},{8,15},{9,8},{10,9... | collective-permute-start | bytes 1007624 | tf_op jit(solution)/shard_map/ppermute | solution.py:625
  15.7 2.6 %collective-permute-start.6 = (f32[272,128]{1,0:T(8,128)S(1)}, f32[272,128]{1,0:T(8,128)S(1)}, u32[]{:S(2)}, u32[]{:S(2)}) collective-permute-start(f32[272,128]{1,0:T(8,128)S(1)} %get-tuple-element.41), channel_id=1, source_target_pairs={{0,2},{1,3},{2,4},{3,5},{4,6},{5,7},{6,0},{7,1},{8,10},{9,11},{10,... | collective-permute-start | bytes 417800 | tf_op jit(solution)/shard_map/ppermute | solution.py:625
  18.3 0.0 collective-permute-start.7
  18.3 4.1 %collective-permute-done.6.low_two = f32[272,128]{1,0:T(8,128)S(1)} collective-permute-done((f32[272,128]{1,0:T(8,128)S(1)}, f32[272,128]{1,0:T(8,128)S(1)}, u32[]{:S(2)}, u32[]{:S(2)}) %collective-permute-start.6) | collective-permute-done | bytes 139296 | tf_op jit(solution)/shard_map/ppermute | solution.py:625
  22.5 3.6 %collective-permute-done.7.high_two = f32[272,128]{1,0:T(8,128)S(1)} collective-permute-done((f32[272,128]{1,0:T(8,128)S(1)}, f32[272,128]{1,0:T(8,128)S(1)}, u32[]{:S(2)}, u32[]{:S(2)}) %collective-permute-start.7) | collective-permute-done | bytes 139296 | tf_op jit(solution)/shard_map/ppermute | solution.py:625
  26.0 0.0 collective-permute-done.4.low_one
  26.0 0.0 collective-permute-done.5.high_one
  26.0 0.0 copy-done.3
  26.0 0.0 copy-done.10
  26.0 0.0 copy-start.2
  26.0 0.5 shard_map.130
  26.6 0.1 collective-permute-start.8
  26.7 2.0 %collective-permute-start.9 = (f32[8,3968]{1,0:T(8,128)S(1)}, f32[8,3968]{1,0:T(8,128)S(1)}, u32[]{:S(2)}, u32[]{:S(2)}) collective-permute-start(f32[8,3968]{1,0:T(8,128)S(1)} %get-tuple-element.45), channel_id=1, source_target_pairs={{0,248},{8,0},{16,8},{24,16},{32,24},{40,32},{48,40},{56,48},{64,5... | collective-permute-start | bytes 380936 | tf_op jit(solution)/shard_map/ppermute | solution.py:625
  28.7 0.0 copy-done.2
  28.7 0.0 copy-start.1
  28.7 0.0 copy-start.5
  28.7 1.8 %shard_map.131.partial = f32[160,1280]{1,0:T(8,128)S(1)} custom-call(f32[72,2048]{1,0:T(8,128)S(1)} %get-tuple-element.43.ext, f32[160,288]{1,0:T(8,128)S(1)} %copy-done.2), custom_call_target="tpu_custom_call" | custom-call | tf_op jit(solution)/shard_map/pallas_call | solution.py:614
  30.5 1.1 %collective-permute-done.8.left = f32[8,3968]{1,0:T(8,128)S(1)} collective-permute-done((f32[8,3968]{1,0:T(8,128)S(1)}, f32[8,3968]{1,0:T(8,128)S(1)}, u32[]{:S(2)}, u32[]{:S(2)}) %collective-permute-start.8) | collective-permute-done | bytes 127008 | tf_op jit(solution)/shard_map/ppermute | solution.py:625
  31.6 3.4 %collective-permute-done.9.right = f32[8,3968]{1,0:T(8,128)S(1)} collective-permute-done((f32[8,3968]{1,0:T(8,128)S(1)}, f32[8,3968]{1,0:T(8,128)S(1)}, u32[]{:S(2)}, u32[]{:S(2)}) %collective-permute-start.9) | collective-permute-done | bytes 127008 | tf_op jit(solution)/shard_map/ppermute | solution.py:625
  35.0 0.0 copy-done.1
  35.0 0.0 copy-done.5
  35.0 0.0 copy-start.9
  35.0 1.8 %shard_map.132 = (f32[192,512]{1,0:T(8,128)S(1)}, f32[72,512]{1,0:T(8,128)S(1)}, f32[128,128]{1,0:T(8,128)S(1)}, f32[544,128]{1,0:T(8,128)S(1)}, f32[544,128]{1,...) custom-call(f32[160,1280]{1,0:T(8,128)S(1)} %shard_map.131.partial, ...), custom_call_target="tpu_custom_call" | custom-call | tf_op jit(solution)/shard_map/pallas_call | solution.py:614
  36.8 0.0 collective-permute-start.10
  36.8 1.7 %collective-permute-start.11 = (f32[544,128]{1,0:T(8,128)S(1)}, f32[544,128]{1,0:T(8,128)S(1)}, u32[]{:S(2)}, u32[]{:S(2)}) collective-permute-start(f32[544,128]{1,0:T(8,128)S(1)} %get-tuple-element.50), channel_id=1, source_target_pairs={{0,7},{1,0},{2,1},{3,2},{4,3},{5,4},{6,5},{7,6},{8,15},{9,8},{10,9... | collective-permute-start | bytes 835592 | tf_op jit(solution)/shard_map/ppermute | solution.py:625
  38.5 1.9 %collective-permute-start.12 = (f32[264,128]{1,0:T(8,128)S(1)}, f32[264,128]{1,0:T(8,128)S(1)}, u32[]{:S(2)}, u32[]{:S(2)}) collective-permute-start(f32[264,128]{1,0:T(8,128)S(1)} %get-tuple-element.51), channel_id=1, source_target_pairs={{0,2},{1,3},{2,4},{3,5},{4,6},{5,7},{6,0},{7,1},{8,10},{9,11},{10,... | collective-permute-start | bytes 405512 | tf_op jit(solution)/shard_map/ppermute | solution.py:625
  40.4 0.2 collective-permute-start.13
  40.6 4.5 %collective-permute-done.12.low_two = f32[264,128]{1,0:T(8,128)S(1)} collective-permute-done((f32[264,128]{1,0:T(8,128)S(1)}, f32[264,128]{1,0:T(8,128)S(1)}, u32[]{:S(2)}, u32[]{:S(2)}) %collective-permute-start.12) | collective-permute-done | bytes 135200 | tf_op jit(solution)/shard_map/ppermute | solution.py:625
  45.1 2.4 %collective-permute-done.13.high_two = f32[264,128]{1,0:T(8,128)S(1)} collective-permute-done((f32[264,128]{1,0:T(8,128)S(1)}, f32[264,128]{1,0:T(8,128)S(1)}, u32[]{:S(2)}, u32[]{:S(2)}) %collective-permute-start.13) | collective-permute-done | bytes 135200 | tf_op jit(solution)/shard_map/ppermute | solution.py:625
  47.5 0.0 collective-permute-done.10.low_one
  47.5 0.0 collective-permute-done.11.high_one
  47.5 0.0 copy-done.9
  47.5 0.0 copy-start.4
  47.5 0.3 shard_map.133
  47.8 0.4 collective-permute-start.14
  48.2 1.9 %collective-permute-start.15 = (f32[8,2688]{1,0:T(8,128)S(1)}, f32[8,2688]{1,0:T(8,128)S(1)}, u32[]{:S(2)}, u32[]{:S(2)}) collective-permute-start(f32[8,2688]{1,0:T(8,128)S(1)} %get-tuple-element.55), channel_id=1, source_target_pairs={{0,248},{8,0},{16,8},{24,16},{32,24},{40,32},{48,40},{56,48},{64,5... | collective-permute-start | bytes 258056 | tf_op jit(solution)/shard_map/ppermute | solution.py:625
  50.1 0.0 copy-done.4
  50.1 0.0 copy-start.6
  50.1 1.4 %shard_map.134.partial = f32[128,1024]{1,0:T(8,128)S(1)} custom-call(f32[72,1792]{1,0:T(8,128)S(1)} %get-tuple-element.53.ext, f32[128,288]{1,0:T(8,128)S(1)} %copy-done.4), custom_call_target="tpu_custom_call" | custom-call | tf_op jit(solution)/shard_map/pallas_call | solution.py:614
  51.5 1.1 %collective-permute-done.14.left = f32[8,2688]{1,0:T(8,128)S(1)} collective-permute-done((f32[8,2688]{1,0:T(8,128)S(1)}, f32[8,2688]{1,0:T(8,128)S(1)}, u32[]{:S(2)}, u32[]{:S(2)}) %collective-permute-start.14) | collective-permute-done | bytes 86048 | tf_op jit(solution)/shard_map/ppermute | solution.py:625
  52.6 3.4 %collective-permute-done.15.right = f32[8,2688]{1,0:T(8,128)S(1)} collective-permute-done((f32[8,2688]{1,0:T(8,128)S(1)}, f32[8,2688]{1,0:T(8,128)S(1)}, u32[]{:S(2)}, u32[]{:S(2)}) %collective-permute-start.15) | collective-permute-done | bytes 86048 | tf_op jit(solution)/shard_map/ppermute | solution.py:625
  56.0 0.0 copy-done.6
  56.0 1.4 %shard_map.135 = f32[3,64,4,128]{3,2,1,0:T(4,128)} custom-call(f32[128,1024]{1,0:T(8,128)S(1)} %shard_map.134.partial, f32[8,2688]{1,0:T(8,128)S(1)} %collective-permute-done.14.left, f32[8,2688]{1,0:T(8,128)S(1)} %collective-permute-done.15.right, f32[192,512]{1,0:T(8,128)S(1)} %get-tuple-element.47.section, f32[128,128]{1,0:T(8,128)S(1)} %get-tuple-element.56.fixed, ...), custom_call_target="tpu_custom_call" | custom-call | tf_op jit(solution)/shard_map/pallas_call | solution.py:614
Async XLA Ops:
  0.0 6.1 %copy-start.8 = (f32[128,64]{1,0:T(8,128)S(1)}, f32[128,64]{1,0:T(8,128)}, u32[]{:S(2)}) copy-start(f32[128,64]{1,0:T(8,128)} %constant.22.clone.own) | copy-start | bytes 98308
  1.3 12.0 %collective-permute-start.2 = (f32[448,128]{1,0:T(8,128)S(1)}, f32[448,128]{1,0:T(8,128)S(1)}, u32[]{:S(2)}, u32[]{:S(2)}) collective-permute-start(f32[448,128]{1,0:T(8,128)S(1)} %get-tuple-element.35), channel_id=1, source_target_pairs={{0,1},{1,2},{2,3},{3,4},{4,5},{5,6},{6,7},{7,0},{8,9},{9,10},{10,1... | collective-permute-start | bytes 688136 | tf_op jit(solution)/shard_map/ppermute | solution.py:625
  1.4 12.0 %collective-permute-start.3 = (f32[448,128]{1,0:T(8,128)S(1)}, f32[448,128]{1,0:T(8,128)S(1)}, u32[]{:S(2)}, u32[]{:S(2)}) collective-permute-start(f32[448,128]{1,0:T(8,128)S(1)} %get-tuple-element.36), channel_id=1, source_target_pairs={{0,7},{1,0},{2,1},{3,2},{4,3},{5,4},{6,5},{7,6},{8,15},{9,8},{10,9... | collective-permute-start | bytes 688136 | tf_op jit(solution)/shard_map/ppermute | solution.py:625
  3.1 4.6 %collective-permute-start = (f32[16,512]{1,0:T(8,128)S(1)}, f32[16,512]{1,0:T(8,128)S(1)}, u32[]{:S(2)}, u32[]{:S(2)}) collective-permute-start(f32[16,512]{1,0:T(8,128)S(1)} %get-tuple-element.33), channel_id=1, source_target_pairs={{0,8},{8,16},{16,24},{24,32},{32,40},{40,48},{48,56},{56,64},{64,7... | collective-permute-start | bytes 98312 | tf_op jit(solution)/shard_map/ppermute | solution.py:625
  6.1 7.2 %collective-permute-start.1 = (f32[16,512]{1,0:T(8,128)S(1)}, f32[16,512]{1,0:T(8,128)S(1)}, u32[]{:S(2)}, u32[]{:S(2)}) collective-permute-start(f32[16,512]{1,0:T(8,128)S(1)} %get-tuple-element.34), channel_id=1, source_target_pairs={{0,248},{8,0},{16,8},{24,16},{32,24},{40,32},{48,40},{56,48},{64,5... | collective-permute-start | bytes 98312 | tf_op jit(solution)/shard_map/ppermute | solution.py:625
  6.1 7.2 %copy-start = (bf16[72,192]{1,0:T(8,128)(2,1)S(1)}, bf16[72,192]{1,0:T(8,128)(2,1)}, u32[]{:S(2)}) copy-start(bf16[72,192]{1,0:T(8,128)(2,1)} %constant.27.clone.lateral) | copy-start | bytes 82948
  6.1 7.2 %copy-start.7 = (bf16[3,128,96]{2,1,0:T(8,128)(2,1)S(1)}, bf16[3,128,96]{2,1,0:T(8,128)(2,1)}, u32[]{:S(2)}) copy-start(bf16[3,128,96]{2,1,0:T(8,128)(2,1)} %constant.24.clone.slopes) | copy-start | bytes 221188
  7.1 18.9 %copy-start.3 = (bf16[3,32,192]{2,1,0:T(8,128)(2,1)S(1)}, bf16[3,32,192]{2,1,0:T(8,128)(2,1)}, u32[]{:S(2)}) copy-start(bf16[3,32,192]{2,1,0:T(8,128)(2,1)} %constant.26.clone.moments) | copy-start | bytes 110596
  13.4 12.6 %copy-start.10 = (bf16[64,240]{1,0:T(8,128)(2,1)S(1)}, bf16[64,240]{1,0:T(8,128)(2,1)}, u32[]{:S(2)}) copy-start(bf16[64,240]{1,0:T(8,128)(2,1)} %constant.28.clone.source) | copy-start | bytes 92164
  13.9 12.1 %collective-permute-start.4 = (f32[656,128]{1,0:T(8,128)S(1)}, f32[656,128]{1,0:T(8,128)S(1)}, u32[]{:S(2)}, u32[]{:S(2)}) collective-permute-start(f32[656,128]{1,0:T(8,128)S(1)} %get-tuple-element.39), channel_id=1, source_target_pairs={{0,1},{1,2},{2,3},{3,4},{4,5},{5,6},{6,7},{7,0},{8,9},{9,10},{10,1... | collective-permute-start | bytes 1007624 | tf_op jit(solution)/shard_map/ppermute | solution.py:625
  13.9 12.1 %collective-permute-start.5 = (f32[656,128]{1,0:T(8,128)S(1)}, f32[656,128]{1,0:T(8,128)S(1)}, u32[]{:S(2)}, u32[]{:S(2)}) collective-permute-start(f32[656,128]{1,0:T(8,128)S(1)} %get-tuple-element.40), channel_id=1, source_target_pairs={{0,7},{1,0},{2,1},{3,2},{4,3},{5,4},{6,5},{7,6},{8,15},{9,8},{10,9... | collective-permute-start | bytes 1007624 | tf_op jit(solution)/shard_map/ppermute | solution.py:625
  15.7 6.8 %collective-permute-start.6 = (f32[272,128]{1,0:T(8,128)S(1)}, f32[272,128]{1,0:T(8,128)S(1)}, u32[]{:S(2)}, u32[]{:S(2)}) collective-permute-start(f32[272,128]{1,0:T(8,128)S(1)} %get-tuple-element.41), channel_id=1, source_target_pairs={{0,2},{1,3},{2,4},{3,5},{4,6},{5,7},{6,0},{7,1},{8,10},{9,11},{10,... | collective-permute-start | bytes 417800 | tf_op jit(solution)/shard_map/ppermute | solution.py:625
  18.3 7.7 %collective-permute-start.7 = (f32[272,128]{1,0:T(8,128)S(1)}, f32[272,128]{1,0:T(8,128)S(1)}, u32[]{:S(2)}, u32[]{:S(2)}) collective-permute-start(f32[272,128]{1,0:T(8,128)S(1)} %get-tuple-element.42), channel_id=1, source_target_pairs={{0,6},{1,7},{2,0},{3,1},{4,2},{5,3},{6,4},{7,5},{8,14},{9,15},{10,... | collective-permute-start | bytes 417800 | tf_op jit(solution)/shard_map/ppermute | solution.py:625
  26.0 2.6 %copy-start.2 = (f32[160,288]{1,0:T(8,128)S(1)}, f32[160,288]{1,0:T(8,128)}, u32[]{:S(2)}) copy-start(f32[160,288]{1,0:T(8,128)} %constant.23.clone.solve) | copy-start | bytes 552964
  26.6 5.0 %collective-permute-start.8 = (f32[8,3968]{1,0:T(8,128)S(1)}, f32[8,3968]{1,0:T(8,128)S(1)}, u32[]{:S(2)}, u32[]{:S(2)}) collective-permute-start(f32[8,3968]{1,0:T(8,128)S(1)} %get-tuple-element.44), channel_id=1, source_target_pairs={{0,8},{8,16},{16,24},{24,32},{32,40},{40,48},{48,56},{56,64},{64,7... | collective-permute-start | bytes 380936 | tf_op jit(solution)/shard_map/ppermute | solution.py:625
  26.7 8.3 %collective-permute-start.9 = (f32[8,3968]{1,0:T(8,128)S(1)}, f32[8,3968]{1,0:T(8,128)S(1)}, u32[]{:S(2)}, u32[]{:S(2)}) collective-permute-start(f32[8,3968]{1,0:T(8,128)S(1)} %get-tuple-element.45), channel_id=1, source_target_pairs={{0,248},{8,0},{16,8},{24,16},{32,24},{40,32},{48,40},{56,48},{64,5... | collective-permute-start | bytes 380936 | tf_op jit(solution)/shard_map/ppermute | solution.py:625
  28.7 6.3 %copy-start.1 = (bf16[3,128,288]{2,1,0:T(8,128)(2,1)S(1)}, bf16[3,128,288]{2,1,0:T(8,128)(2,1)}, u32[]{:S(2)}) copy-start(bf16[3,128,288]{2,1,0:T(8,128)(2,1)} %constant.25.clone.full) | copy-start | bytes 663556
  28.7 6.3 %copy-start.5 = (bf16[160,384]{1,0:T(8,128)(2,1)S(1)}, bf16[160,384]{1,0:T(8,128)(2,1)}, u32[]{:S(2)}) copy-start(bf16[160,384]{1,0:T(8,128)(2,1)} %constant.29.clone.solve) | copy-start | bytes 368644
  35.0 12.5 %copy-start.9 = (bf16[64,240]{1,0:T(8,128)(2,1)S(1)}, bf16[64,240]{1,0:T(8,128)(2,1)}, u32[]{:S(2)}) copy-start(bf16[64,240]{1,0:T(8,128)(2,1)} %constant.31.clone.source) | copy-start | bytes 92164
  36.8 10.7 %collective-permute-start.10 = (f32[544,128]{1,0:T(8,128)S(1)}, f32[544,128]{1,0:T(8,128)S(1)}, u32[]{:S(2)}, u32[]{:S(2)}) collective-permute-start(f32[544,128]{1,0:T(8,128)S(1)} %get-tuple-element.49), channel_id=1, source_target_pairs={{0,1},{1,2},{2,3},{3,4},{4,5},{5,6},{6,7},{7,0},{8,9},{9,10},{10,1... | collective-permute-start | bytes 835592 | tf_op jit(solution)/shard_map/ppermute | solution.py:625
  36.8 10.7 %collective-permute-start.11 = (f32[544,128]{1,0:T(8,128)S(1)}, f32[544,128]{1,0:T(8,128)S(1)}, u32[]{:S(2)}, u32[]{:S(2)}) collective-permute-start(f32[544,128]{1,0:T(8,128)S(1)} %get-tuple-element.50), channel_id=1, source_target_pairs={{0,7},{1,0},{2,1},{3,2},{4,3},{5,4},{6,5},{7,6},{8,15},{9,8},{10,9... | collective-permute-start | bytes 835592 | tf_op jit(solution)/shard_map/ppermute | solution.py:625
  38.5 6.5 %collective-permute-start.12 = (f32[264,128]{1,0:T(8,128)S(1)}, f32[264,128]{1,0:T(8,128)S(1)}, u32[]{:S(2)}, u32[]{:S(2)}) collective-permute-start(f32[264,128]{1,0:T(8,128)S(1)} %get-tuple-element.51), channel_id=1, source_target_pairs={{0,2},{1,3},{2,4},{3,5},{4,6},{5,7},{6,0},{7,1},{8,10},{9,11},{10,... | collective-permute-start | bytes 405512 | tf_op jit(solution)/shard_map/ppermute | solution.py:625
  40.4 7.1 %collective-permute-start.13 = (f32[264,128]{1,0:T(8,128)S(1)}, f32[264,128]{1,0:T(8,128)S(1)}, u32[]{:S(2)}, u32[]{:S(2)}) collective-permute-start(f32[264,128]{1,0:T(8,128)S(1)} %get-tuple-element.52), channel_id=1, source_target_pairs={{0,6},{1,7},{2,0},{3,1},{4,2},{5,3},{6,4},{7,5},{8,14},{9,15},{10,... | collective-permute-start | bytes 405512 | tf_op jit(solution)/shard_map/ppermute | solution.py:625
  47.5 2.6 %copy-start.4 = (f32[128,288]{1,0:T(8,128)S(1)}, f32[128,288]{1,0:T(8,128)}, u32[]{:S(2)}) copy-start(f32[128,288]{1,0:T(8,128)} %constant.30.clone.solve) | copy-start | bytes 442372
  47.8 4.7 %collective-permute-start.14 = (f32[8,2688]{1,0:T(8,128)S(1)}, f32[8,2688]{1,0:T(8,128)S(1)}, u32[]{:S(2)}, u32[]{:S(2)}) collective-permute-start(f32[8,2688]{1,0:T(8,128)S(1)} %get-tuple-element.54), channel_id=1, source_target_pairs={{0,8},{8,16},{16,24},{24,32},{32,40},{40,48},{48,56},{56,64},{64,7... | collective-permute-start | bytes 258056 | tf_op jit(solution)/shard_map/ppermute | solution.py:625
  48.2 7.8 %collective-permute-start.15 = (f32[8,2688]{1,0:T(8,128)S(1)}, f32[8,2688]{1,0:T(8,128)S(1)}, u32[]{:S(2)}, u32[]{:S(2)}) collective-permute-start(f32[8,2688]{1,0:T(8,128)S(1)} %get-tuple-element.55), channel_id=1, source_target_pairs={{0,248},{8,0},{16,8},{24,16},{32,24},{40,32},{48,40},{56,48},{64,5... | collective-permute-start | bytes 258056 | tf_op jit(solution)/shard_map/ppermute | solution.py:625
  50.1 5.9 %copy-start.6 = (bf16[128,384]{1,0:T(8,128)(2,1)S(1)}, bf16[128,384]{1,0:T(8,128)(2,1)}, u32[]{:S(2)}) copy-start(bf16[128,384]{1,0:T(8,128)(2,1)} %constant.32.clone.solve) | copy-start | bytes 294916

commit v10 on v9

--- a/solution.py
+++ b/solution.py
@@ -124,7 +124,8 @@
                 top = 2 * cells + GROUP * (2 * side + half)
                 solve_own[top : top + RANK_V, near * j : near * (j + 1)] = -mine
                 solve_sides[top : top + RANK_V, wide * j : wide * (j + 1)] = -sides
-    full = np.concatenate([np.broadcast_to(own, (3,) + own.shape), slopes], axis=2)
+    full = np.concatenate([own, from_left, from_right], axis=1)
+    full = np.pad(full, [(0, 0), (0, GROUP - 2 * RANK_V)])
     plain, split = (own, solve_own), (slopes, full, moments, lateral, source, solve_sides)
     return [x.astype(np.float32) for x in plain] + [split_table(x.astype(np.float32)) for x in split]
 
@@ -338,43 +339,64 @@
         fill_slots(far, cells, blocks[inner : inner + 2] + [at(inner), at(inner + 1)], moments[inner : inner + 2])
 
 
-def first_source(cells, parts, section, arrived, lateral, ext):
+WHOLE = (-2, -1, ROWS, ROWS + 1)
+
+
+def row_across(cells, section, arrived):
     low_one, high_one, low_two, high_two = arrived
     masks = edge_masks()
-    span, tail = slice(0, cells), slice(cells, cells + PAD_M)
-    pick = lambda ref, k: slot(ref, cells, k)[...]
-
-    def across(e):
+
+    def value(e):
         if 0 <= e < ROWS:
             return section[cells : 2 * cells, lane(e)]
         if e < -ROWS or e >= 2 * ROWS:
-            tile = pick(low_two, e + 8) if e < 0 else pick(high_two, e - 6)
+            ref, k = (low_two, e + 8) if e < 0 else (high_two, e - 6)
         else:
-            tile = pick(low_one, e + 6) if e < 0 else pick(high_one, e - 2)
-        return masked(tile, e, masks)
-
-    whole = (-2, -1, ROWS, ROWS + 1)
-    given = [(low_one if e < 0 else high_one, e % 2) for e in whole]
+            ref, k = (low_one, e + 6) if e < 0 else (high_one, e - 2)
+        return masked(slot(ref, cells, k)[...], e, masks)
+
+    return value
+
+
+def near_source_kernel(cells, parts, section, low_one, high_one, lateral, moments, middle, held):
+    masks = edge_masks()
+    across = row_across(cells, section, (low_one, high_one, None, None))
+    pick = lambda ref, k: slot(ref, cells, k)[...]
+    given = [(low_one if e < 0 else high_one, e % 2) for e in WHOLE]
     beside = split_dot(lateral[...], jnp.concatenate([pick(ref, 8 + k) for ref, k in given], axis=1))
-
-    for e in range(-FIRST.reach, ROWS + FIRST.reach):
-        if e in whole:
-            at = whole.index(e)
+    for e in range(-2, ROWS + 2):
+        if e in WHOLE:
+            at = WHOLE.index(e)
             ref, k = given[at]
             total = stream_slope(pick(ref, 6 + k)) + beside[:cells, lane(at)]
             side = beside[cells:, lane(at)]
-        elif 0 <= e < ROWS:
-            total, side = parts[span, lane(e)], parts[tail, lane(e)]
         else:
-            far = e < -ROWS or e >= 2 * ROWS
-            ref = (low_two if e < 0 else high_two) if far else (low_one if e < 0 else high_one)
-            top = (4 if far else 10) * cells + PAD_M * (e % 2)
-            total, side = pick(ref, e % 2), ref[top : top + PAD_M, :]
+            total, side = parts[:cells, lane(e)], parts[cells:, lane(e)]
         for reach, factor in DIFFERENCE:
-            if e in whole or (e + reach) // ROWS != e // ROWS:
+            if e in WHOLE or not 0 <= e + reach < ROWS:
                 total = total + factor * across(e + reach)
-        ext[span, lane(e + FIRST.reach)] = masked(total, e, masks)
-        ext[tail, lane(e + FIRST.reach)] = masked(side, e, masks)
+        middle[:cells, lane(e + 2)] = masked(total, e, masks)
+        middle[cells:, lane(e + 2)] = masked(side, e, masks)
+    held[...] = sum(split_dot(moments[c], section[cells * c : cells * (c + 1), :]) for c in range(3))
+
+
+def first_source(cells, middle, arrived, ext):
+    low_one, high_one, low_two, high_two = arrived
+    masks = edge_masks()
+    across = row_across(cells, None, arrived)
+    ext[:, lane(FIRST.reach - 2, ROWS + 4)] = middle[...]
+    for e in range(-FIRST.reach, ROWS + FIRST.reach):
+        if -2 <= e < ROWS + 2:
+            continue
+        far = e < -ROWS or e >= 2 * ROWS
+        ref = (low_two if e < 0 else high_two) if far else (low_one if e < 0 else high_one)
+        top = (4 if far else 10) * cells + PAD_M * (e % 2)
+        total, side = slot(ref, cells, e % 2)[...], ref[top : top + PAD_M, :]
+        for reach, factor in DIFFERENCE:
+            if (e + reach) // ROWS != e // ROWS:
+                total = total + factor * across(e + reach)
+        ext[:cells, lane(e + FIRST.reach)] = masked(total, e, masks)
+        ext[cells:, lane(e + FIRST.reach)] = masked(side, e, masks)
 
 
 def last_source(cells, parts, section, arrived, extra, ext):
@@ -433,12 +455,11 @@
 
 
 def source_kernel(
-    cells, parts, section, low_one, high_one, low_two, high_two, lateral, source, moments, ext, to_right, to_left
+    cells, middle, held, low_one, high_one, low_two, high_two, source, ext, to_right, to_left
 ):
-    first_source(cells, parts, section, (low_one, high_one, low_two, high_two), lateral, ext)
+    first_source(cells, middle, (low_one, high_one, low_two, high_two), ext)
     both = split_dot(source[...], ext[...])
     pack_moments(FIRST, both, to_right, to_left)
-    held = sum(split_dot(moments[c], section[cells * c : cells * (c + 1), :]) for c in range(3))
     for side, out in enumerate((to_right, to_left)):
         top, base = 4 * GROUP * side, PAD_V * side
         out[:, lane(FIRST.packed, ROWS)] = held[base : base + 8]
@@ -539,17 +560,20 @@
             value = slot(low_one if r < 0 else high_one, cells, first + k % 2)[...]
             value = value - gradient(FIRST, found, c, home, home_slope, r)
             rim[rows, lane(k)] = masked(value, r, masks)
+    sides[...] = jnp.zeros(sides.shape, jnp.float32)
     for side, given in enumerate((left, right)):
-        base, top = PAD_V * side, 2 * cells + 2 * GROUP * side
+        top = 2 * cells + 2 * GROUP * side
         phi_rows, slope_rows = slice(top, top + GROUP), slice(top + GROUP, top + 2 * GROUP)
-        sides[base : base + GROUP, :] = given[:, lane(FIRST.packed, ROWS)]
-        sides[base + GROUP : base + PAD_V, :] = jnp.zeros((PAD_V - GROUP, ROWS * LANES), jnp.float32)
         for r in range(ROWS):
-            sides[base + GROUP : base + GROUP + 1, lane(r)] = spare(given, FIRST.breadth + r)
             for c in range(3):
-                rows = slice(base + RANK_V * c, base + RANK_V * (c + 1))
-                change = gradient(FIRST, found, c, phi_rows, slope_rows, r)[:RANK_V]
-                sides[rows, lane(r)] = sides[rows, lane(r)] - change
+                change = gradient(FIRST, found, c, phi_rows, slope_rows, r)
+                base = GROUP * c + RANK_V * side
+                count = min(RANK_V, GROUP - RANK_V * c)
+                held = given[RANK_V * c : RANK_V * c + count, lane(FIRST.packed + r)]
+                sides[base : base + count, lane(r)] = held - change[:count]
+                if count < RANK_V:
+                    held = spare(given, FIRST.breadth + r)
+                    sides[base + count : base + RANK_V, lane(r)] = held - change[count:RANK_V]
 
     def tile(c, r):
         rows = slice(cells * c, cells * (c + 1))
@@ -557,7 +581,9 @@
 
     for c in range(3):
         rows = slice(cells * c, cells * (c + 1))
-        spanned = split_dot(full[c], jnp.concatenate([flat[rows, :], sides[...]], axis=0))
+        spanned = split_dot(
+            full[...], jnp.concatenate([flat[rows, :], sides[GROUP * c : GROUP * (c + 1), :]], axis=0)
+        )
         for r in range(ROWS):
             here = tile(c, r)
             up_one, down_one = turned(here, 1), turned(here, -1)
@@ -668,10 +694,15 @@
         rough, start, thick, left, right, low, high, slopes, lateral,
     )
     arrived = across(*sent)
+    middle, held = call(
+        functools.partial(near_source_kernel, cells),
+        [(near, 2 * width), (2 * PAD_V, width)],
+        parts, section, *arrived[:2], lateral, moments,
+    )
     ext, to_right, to_left = call(
         functools.partial(source_kernel, cells),
         [(near, FIRST.breadth * columns)] + [(GROUP, (FIRST.packed + ROWS + 3) * columns)] * 2,
-        parts, section, *arrived, lateral, first[0], moments,
+        middle, held, *arrived, first[0],
     )
     left = shifted(to_right, "span", 1)
     right = shifted(to_left, "span", -1)
@@ -690,7 +721,7 @@
             levels(FIRST, 2 * PAD_S),
             pltpu.VMEM(whole, jnp.float32),
             pltpu.VMEM((components * cells, 4 * columns), jnp.float32),
-            pltpu.VMEM((2 * PAD_V, width), jnp.float32),
+            pltpu.VMEM((components * GROUP, width), jnp.float32),
         ],
     )
     arrived = across(*sent)

time: 57.8 us -> 57.5 us (level)
    pallas_call x9 -> x10, Pallas kernels: 10 us -> 10.1 us  [call(): pl.pallas_call(body, out_shape=[jax.ShapeDtypeStruct(s, jnp.float32) for...]
  transfers between devices with their start and end apart: 16 -> 16, of which waited for: 10 -> 12; matrix products, arithmetic and copies ran while one was open for 0% -> 0% of each run, Pallas kernels for 7% -> 8%
where the time goes in v10:
time: 57.5 us; the launch traced here: 57.4 us
  waiting for transfers between devices  29.6 us (51%)
  starting transfers between devices  17.4 us (30%)
  Pallas kernels  10.1 us (18%)
    ppermute x16, waiting for transfers between devices, shifted(): lax.ppermute(block, axis, [(i, (i + step) % count) for i in range(count)])  29.6 us
    ppermute x16, starting transfers between devices, shifted(): lax.ppermute(block, axis, [(i, (i + step) % count) for i in range(count)])  17.4 us
    pallas_call x10, Pallas kernels, call(): pl.pallas_call(body, out_shape=[jax.ShapeDtypeStruct(s, jnp.float32) for...  10.1 us
  transfers between devices with their start and end apart: 16, of which 12 were waited for; matrix products, arithmetic and copies ran while one was open for 0% of the time, Pallas kernels for 8%

profile of v10, /device:TPU:126, one launch (start us, length us, event | category | flops | bytes accessed | tf_op | source)
XLA Modules:
  0.0 57.4 jit_solution(14624394671397636032)
XLA Ops:
  0.0 0.0 copy-start.8
  0.0 1.3 %shard_map.127 = (f32[192,512]{1,0:T(8,128)S(1)}, f32[64,512]{1,0:T(8,128)S(1)}, f32[16,512]{1,0:T(8,128)S(1)}, f32[16,512]{1,0:T(8,128)S(1)}, f32[448,128]{1,0:T(8,128)S(1)}, /*index=5*/f32[448,128]{1,0:T(8,128)S(1)}) custom-call(f32[3,64,4,128]{3,2,1,0:T(4,128)} %velocity.1, f32[64,4,128]{2,1,0:T(4,128)} %viscosity.1, ...), custom_call_target="tpu_custom_call" | custom-call | tf_op jit(solution)/shard_map/pallas_call | solution.py:640
  1.3 0.0 collective-permute-start.2
  1.4 1.7 %collective-permute-start.3 = (f32[448,128]{1,0:T(8,128)S(1)}, f32[448,128]{1,0:T(8,128)S(1)}, u32[]{:S(2)}, u32[]{:S(2)}) collective-permute-start(f32[448,128]{1,0:T(8,128)S(1)} %get-tuple-element.38), channel_id=1, source_target_pairs={{0,7},{1,0},{2,1},{3,2},{4,3},{5,4},{6,5},{7,6},{8,15},{9,8},{10,9... | collective-permute-start | bytes 688136 | tf_op jit(solution)/shard_map/ppermute | solution.py:651
  3.1 3.0 %collective-permute-start = (f32[16,512]{1,0:T(8,128)S(1)}, f32[16,512]{1,0:T(8,128)S(1)}, u32[]{:S(2)}, u32[]{:S(2)}) collective-permute-start(f32[16,512]{1,0:T(8,128)S(1)} %get-tuple-element.35), channel_id=1, source_target_pairs={{0,8},{8,16},{16,24},{24,32},{32,40},{40,48},{48,56},{56,64},{64,7... | collective-permute-start | bytes 98312 | tf_op jit(solution)/shard_map/ppermute | solution.py:651
  6.1 0.0 collective-permute-start.1
  6.1 0.0 copy-done.8
  6.1 0.0 copy-start
  6.1 0.0 copy-start.6
  6.2 0.9 %shard_map.128.rough = f32[192,512]{1,0:T(8,128)S(1)} custom-call(f32[192,512]{1,0:T(8,128)S(1)} %get-tuple-element.33.flat.start, f32[64,512]{1,0:T(8,128)S(1)} %get-tuple-element.34.thick, f32[128,64]{1,0:T(8,128)S(1)} %copy-done.8), custom_call_target="tpu_custom_call" | custom-call | tf_op jit(solution)/shard_map/pallas_call | solution.py:640
  7.1 0.0 copy-start.2
  7.1 0.6 %collective-permute-done.left = f32[16,512]{1,0:T(8,128)S(1)} collective-permute-done((f32[16,512]{1,0:T(8,128)S(1)}, f32[16,512]{1,0:T(8,128)S(1)}, u32[]{:S(2)}, u32[]{:S(2)}) %collective-permute-start) | collective-permute-done | bytes 32800 | tf_op jit(solution)/shard_map/ppermute | solution.py:651
  7.7 5.6 %collective-permute-done.1.right = f32[16,512]{1,0:T(8,128)S(1)} collective-permute-done((f32[16,512]{1,0:T(8,128)S(1)}, f32[16,512]{1,0:T(8,128)S(1)}, u32[]{:S(2)}, u32[]{:S(2)}) %collective-permute-start.1) | collective-permute-done | bytes 32800 | tf_op jit(solution)/shard_map/ppermute | solution.py:651
  13.4 0.0 collective-permute-done.2.low
  13.4 0.0 collective-permute-done.3.high
  13.4 0.0 copy-done
  13.4 0.0 copy-done.6
  13.4 0.5 shard_map.129
  13.9 0.0 collective-permute-start.4
  13.9 1.7 %collective-permute-start.5 = (f32[656,128]{1,0:T(8,128)S(1)}, f32[656,128]{1,0:T(8,128)S(1)}, u32[]{:S(2)}, u32[]{:S(2)}) collective-permute-start(f32[656,128]{1,0:T(8,128)S(1)} %get-tuple-element.42), channel_id=1, source_target_pairs={{0,7},{1,0},{2,1},{3,2},{4,3},{5,4},{6,5},{7,6},{8,15},{9,8},{10,9... | collective-permute-start | bytes 1007624 | tf_op jit(solution)/shard_map/ppermute | solution.py:651
  15.7 2.6 %collective-permute-start.6 = (f32[272,128]{1,0:T(8,128)S(1)}, f32[272,128]{1,0:T(8,128)S(1)}, u32[]{:S(2)}, u32[]{:S(2)}) collective-permute-start(f32[272,128]{1,0:T(8,128)S(1)} %get-tuple-element.45), channel_id=1, source_target_pairs={{0,2},{1,3},{2,4},{3,5},{4,6},{5,7},{6,0},{7,1},{8,10},{9,11},{10,... | collective-permute-start | bytes 417800 | tf_op jit(solution)/shard_map/ppermute | solution.py:651
  18.3 0.0 collective-permute-start.7
  18.3 3.4 %collective-permute-done.4.low_one = f32[656,128]{1,0:T(8,128)S(1)} collective-permute-done((f32[656,128]{1,0:T(8,128)S(1)}, f32[656,128]{1,0:T(8,128)S(1)}, u32[]{:S(2)}, u32[]{:S(2)}) %collective-permute-start.4) | collective-permute-done | bytes 335904 | tf_op jit(solution)/shard_map/ppermute | solution.py:651
  21.7 0.1 collective-permute-done.5.high_one
  21.8 0.0 copy-done.2
  21.8 0.0 copy-start.10
  21.8 0.3 shard_map.130
  22.1 0.3 collective-permute-done.6.low_two
  22.4 3.6 %collective-permute-done.7.high_two = f32[272,128]{1,0:T(8,128)S(1)} collective-permute-done((f32[272,128]{1,0:T(8,128)S(1)}, f32[272,128]{1,0:T(8,128)S(1)}, u32[]{:S(2)}, u32[]{:S(2)}) %collective-permute-start.7) | collective-permute-done | bytes 139296 | tf_op jit(solution)/shard_map/ppermute | solution.py:651
  26.0 0.0 copy-done.10
  26.0 0.0 copy-start.1
  26.0 0.4 shard_map.131
  26.4 0.1 collective-permute-start.8
  26.5 2.0 %collective-permute-start.9 = (f32[8,3968]{1,0:T(8,128)S(1)}, f32[8,3968]{1,0:T(8,128)S(1)}, u32[]{:S(2)}, u32[]{:S(2)}) collective-permute-start(f32[8,3968]{1,0:T(8,128)S(1)} %get-tuple-element.49), channel_id=1, source_target_pairs={{0,248},{8,0},{16,8},{24,16},{32,24},{40,32},{48,40},{56,48},{64,5... | collective-permute-start | bytes 380936 | tf_op jit(solution)/shard_map/ppermute | solution.py:651
  28.5 0.0 copy-done.1
  28.5 0.0 copy-start.4
  28.5 0.0 copy-start.7
  28.5 1.8 %shard_map.132.partial = f32[160,1280]{1,0:T(8,128)S(1)} custom-call(f32[72,2048]{1,0:T(8,128)S(1)} %get-tuple-element.47.ext, f32[160,288]{1,0:T(8,128)S(1)} %copy-done.1), custom_call_target="tpu_custom_call" | custom-call | tf_op jit(solution)/shard_map/pallas_call | solution.py:640
  30.3 1.1 %collective-permute-done.8.left = f32[8,3968]{1,0:T(8,128)S(1)} collective-permute-done((f32[8,3968]{1,0:T(8,128)S(1)}, f32[8,3968]{1,0:T(8,128)S(1)}, u32[]{:S(2)}, u32[]{:S(2)}) %collective-permute-start.8) | collective-permute-done | bytes 127008 | tf_op jit(solution)/shard_map/ppermute | solution.py:651
  31.4 3.4 %collective-permute-done.9.right = f32[8,3968]{1,0:T(8,128)S(1)} collective-permute-done((f32[8,3968]{1,0:T(8,128)S(1)}, f32[8,3968]{1,0:T(8,128)S(1)}, u32[]{:S(2)}, u32[]{:S(2)}) %collective-permute-start.9) | collective-permute-done | bytes 127008 | tf_op jit(solution)/shard_map/ppermute | solution.py:651
  34.8 0.0 copy-done.4
  34.8 0.0 copy-done.7
  34.8 0.0 copy-start.9
  34.8 1.7 %shard_map.133 = (f32[192,512]{1,0:T(8,128)S(1)}, f32[72,512]{1,0:T(8,128)S(1)}, f32[128,128]{1,0:T(8,128)S(1)}, f32[544,128]{1,0:T(8,128)S(1)}, f32[544,128]{1,...) custom-call(f32[160,1280]{1,0:T(8,128)S(1)} %shard_map.132.partial, ...), custom_call_target="tpu_custom_call" | custom-call | tf_op jit(solution)/shard_map/pallas_call | solution.py:640
  36.5 0.0 collective-permute-start.10
  36.5 1.7 %collective-permute-start.11 = (f32[544,128]{1,0:T(8,128)S(1)}, f32[544,128]{1,0:T(8,128)S(1)}, u32[]{:S(2)}, u32[]{:S(2)}) collective-permute-start(f32[544,128]{1,0:T(8,128)S(1)} %get-tuple-element.54), channel_id=1, source_target_pairs={{0,7},{1,0},{2,1},{3,2},{4,3},{5,4},{6,5},{7,6},{8,15},{9,8},{10,9... | collective-permute-start | bytes 835592 | tf_op jit(solution)/shard_map/ppermute | solution.py:651
  38.3 1.9 %collective-permute-start.12 = (f32[264,128]{1,0:T(8,128)S(1)}, f32[264,128]{1,0:T(8,128)S(1)}, u32[]{:S(2)}, u32[]{:S(2)}) collective-permute-start(f32[264,128]{1,0:T(8,128)S(1)} %get-tuple-element.55), channel_id=1, source_target_pairs={{0,2},{1,3},{2,4},{3,5},{4,6},{5,7},{6,0},{7,1},{8,10},{9,11},{10,... | collective-permute-start | bytes 405512 | tf_op jit(solution)/shard_map/ppermute | solution.py:651
  40.1 0.2 collective-permute-start.13
  40.3 4.5 %collective-permute-done.12.low_two = f32[264,128]{1,0:T(8,128)S(1)} collective-permute-done((f32[264,128]{1,0:T(8,128)S(1)}, f32[264,128]{1,0:T(8,128)S(1)}, u32[]{:S(2)}, u32[]{:S(2)}) %collective-permute-start.12) | collective-permute-done | bytes 135200 | tf_op jit(solution)/shard_map/ppermute | solution.py:651
  44.8 2.4 %collective-permute-done.13.high_two = f32[264,128]{1,0:T(8,128)S(1)} collective-permute-done((f32[264,128]{1,0:T(8,128)S(1)}, f32[264,128]{1,0:T(8,128)S(1)}, u32[]{:S(2)}, u32[]{:S(2)}) %collective-permute-start.13) | collective-permute-done | bytes 135200 | tf_op jit(solution)/shard_map/ppermute | solution.py:651
  47.2 0.0 collective-permute-done.10.low_one
  47.2 0.0 collective-permute-done.11.high_one
  47.2 0.0 copy-done.9
  47.2 0.0 copy-start.3
  47.2 0.3 shard_map.134
  47.6 0.4 collective-permute-start.14
  47.9 1.9 %collective-permute-start.15 = (f32[8,2688]{1,0:T(8,128)S(1)}, f32[8,2688]{1,0:T(8,128)S(1)}, u32[]{:S(2)}, u32[]{:S(2)}) collective-permute-start(f32[8,2688]{1,0:T(8,128)S(1)} %get-tuple-element.59), channel_id=1, source_target_pairs={{0,248},{8,0},{16,8},{24,16},{32,24},{40,32},{48,40},{56,48},{64,5... | collective-permute-start | bytes 258056 | tf_op jit(solution)/shard_map/ppermute | solution.py:651
  49.8 0.0 copy-done.3
  49.8 0.0 copy-start.5
  49.9 1.4 %shard_map.135.partial = f32[128,1024]{1,0:T(8,128)S(1)} custom-call(f32[72,1792]{1,0:T(8,128)S(1)} %get-tuple-element.57.ext, f32[128,288]{1,0:T(8,128)S(1)} %copy-done.3), custom_call_target="tpu_custom_call" | custom-call | tf_op jit(solution)/shard_map/pallas_call | solution.py:640
  51.2 1.1 %collective-permute-done.14.left = f32[8,2688]{1,0:T(8,128)S(1)} collective-permute-done((f32[8,2688]{1,0:T(8,128)S(1)}, f32[8,2688]{1,0:T(8,128)S(1)}, u32[]{:S(2)}, u32[]{:S(2)}) %collective-permute-start.14) | collective-permute-done | bytes 86048 | tf_op jit(solution)/shard_map/ppermute | solution.py:651
  52.3 3.4 %collective-permute-done.15.right = f32[8,2688]{1,0:T(8,128)S(1)} collective-permute-done((f32[8,2688]{1,0:T(8,128)S(1)}, f32[8,2688]{1,0:T(8,128)S(1)}, u32[]{:S(2)}, u32[]{:S(2)}) %collective-permute-start.15) | collective-permute-done | bytes 86048 | tf_op jit(solution)/shard_map/ppermute | solution.py:651
  55.7 0.0 copy-done.5
  55.7 1.4 %shard_map.136 = f32[3,64,4,128]{3,2,1,0:T(4,128)} custom-call(f32[128,1024]{1,0:T(8,128)S(1)} %shard_map.135.partial, f32[8,2688]{1,0:T(8,128)S(1)} %collective-permute-done.14.left, f32[8,2688]{1,0:T(8,128)S(1)} %collective-permute-done.15.right, f32[192,512]{1,0:T(8,128)S(1)} %get-tuple-element.51.section, f32[128,128]{1,0:T(8,128)S(1)} %get-tuple-element.60.fixed, ...), custom_call_target="tpu_custom_call" | custom-call | tf_op jit(solution)/shard_map/pallas_call | solution.py:640
Async XLA Ops:
  0.0 6.1 %copy-start.8 = (f32[128,64]{1,0:T(8,128)S(1)}, f32[128,64]{1,0:T(8,128)}, u32[]{:S(2)}) copy-start(f32[128,64]{1,0:T(8,128)} %constant.22.clone.own) | copy-start | bytes 98308
  1.3 12.0 %collective-permute-start.2 = (f32[448,128]{1,0:T(8,128)S(1)}, f32[448,128]{1,0:T(8,128)S(1)}, u32[]{:S(2)}, u32[]{:S(2)}) collective-permute-start(f32[448,128]{1,0:T(8,128)S(1)} %get-tuple-element.37), channel_id=1, source_target_pairs={{0,1},{1,2},{2,3},{3,4},{4,5},{5,6},{6,7},{7,0},{8,9},{9,10},{10,1... | collective-permute-start | bytes 688136 | tf_op jit(solution)/shard_map/ppermute | solution.py:651
  1.4 12.0 %collective-permute-start.3 = (f32[448,128]{1,0:T(8,128)S(1)}, f32[448,128]{1,0:T(8,128)S(1)}, u32[]{:S(2)}, u32[]{:S(2)}) collective-permute-start(f32[448,128]{1,0:T(8,128)S(1)} %get-tuple-element.38), channel_id=1, source_target_pairs={{0,7},{1,0},{2,1},{3,2},{4,3},{5,4},{6,5},{7,6},{8,15},{9,8},{10,9... | collective-permute-start | bytes 688136 | tf_op jit(solution)/shard_map/ppermute | solution.py:651
  3.1 4.6 %collective-permute-start = (f32[16,512]{1,0:T(8,128)S(1)}, f32[16,512]{1,0:T(8,128)S(1)}, u32[]{:S(2)}, u32[]{:S(2)}) collective-permute-start(f32[16,512]{1,0:T(8,128)S(1)} %get-tuple-element.35), channel_id=1, source_target_pairs={{0,8},{8,16},{16,24},{24,32},{32,40},{40,48},{48,56},{56,64},{64,7... | collective-permute-start | bytes 98312 | tf_op jit(solution)/shard_map/ppermute | solution.py:651
  6.1 7.2 %collective-permute-start.1 = (f32[16,512]{1,0:T(8,128)S(1)}, f32[16,512]{1,0:T(8,128)S(1)}, u32[]{:S(2)}, u32[]{:S(2)}) collective-permute-start(f32[16,512]{1,0:T(8,128)S(1)} %get-tuple-element.36), channel_id=1, source_target_pairs={{0,248},{8,0},{16,8},{24,16},{32,24},{40,32},{48,40},{56,48},{64,5... | collective-permute-start | bytes 98312 | tf_op jit(solution)/shard_map/ppermute | solution.py:651
  6.1 7.2 %copy-start = (bf16[72,192]{1,0:T(8,128)(2,1)S(1)}, bf16[72,192]{1,0:T(8,128)(2,1)}, u32[]{:S(2)}) copy-start(bf16[72,192]{1,0:T(8,128)(2,1)} %constant.27.clone.lateral) | copy-start | bytes 82948
  6.1 7.2 %copy-start.6 = (bf16[3,128,96]{2,1,0:T(8,128)(2,1)S(1)}, bf16[3,128,96]{2,1,0:T(8,128)(2,1)}, u32[]{:S(2)}) copy-start(bf16[3,128,96]{2,1,0:T(8,128)(2,1)} %constant.24.clone.slopes) | copy-start | bytes 221188
  7.1 14.8 %copy-start.2 = (bf16[3,32,192]{2,1,0:T(8,128)(2,1)S(1)}, bf16[3,32,192]{2,1,0:T(8,128)(2,1)}, u32[]{:S(2)}) copy-start(bf16[3,32,192]{2,1,0:T(8,128)(2,1)} %constant.26.clone.moments) | copy-start | bytes 110596
  13.9 7.8 %collective-permute-start.4 = (f32[656,128]{1,0:T(8,128)S(1)}, f32[656,128]{1,0:T(8,128)S(1)}, u32[]{:S(2)}, u32[]{:S(2)}) collective-permute-start(f32[656,128]{1,0:T(8,128)S(1)} %get-tuple-element.41), channel_id=1, source_target_pairs={{0,1},{1,2},{2,3},{3,4},{4,5},{5,6},{6,7},{7,0},{8,9},{9,10},{10,1... | collective-permute-start | bytes 1007624 | tf_op jit(solution)/shard_map/ppermute | solution.py:651
  13.9 7.9 %collective-permute-start.5 = (f32[656,128]{1,0:T(8,128)S(1)}, f32[656,128]{1,0:T(8,128)S(1)}, u32[]{:S(2)}, u32[]{:S(2)}) collective-permute-start(f32[656,128]{1,0:T(8,128)S(1)} %get-tuple-element.42), channel_id=1, source_target_pairs={{0,7},{1,0},{2,1},{3,2},{4,3},{5,4},{6,5},{7,6},{8,15},{9,8},{10,9... | collective-permute-start | bytes 1007624 | tf_op jit(solution)/shard_map/ppermute | solution.py:651
  15.7 6.8 %collective-permute-start.6 = (f32[272,128]{1,0:T(8,128)S(1)}, f32[272,128]{1,0:T(8,128)S(1)}, u32[]{:S(2)}, u32[]{:S(2)}) collective-permute-start(f32[272,128]{1,0:T(8,128)S(1)} %get-tuple-element.45), channel_id=1, source_target_pairs={{0,2},{1,3},{2,4},{3,5},{4,6},{5,7},{6,0},{7,1},{8,10},{9,11},{10,... | collective-permute-start | bytes 417800 | tf_op jit(solution)/shard_map/ppermute | solution.py:651
  18.3 7.7 %collective-permute-start.7 = (f32[272,128]{1,0:T(8,128)S(1)}, f32[272,128]{1,0:T(8,128)S(1)}, u32[]{:S(2)}, u32[]{:S(2)}) collective-permute-start(f32[272,128]{1,0:T(8,128)S(1)} %get-tuple-element.46), channel_id=1, source_target_pairs={{0,6},{1,7},{2,0},{3,1},{4,2},{5,3},{6,4},{7,5},{8,14},{9,15},{10,... | collective-permute-start | bytes 417800 | tf_op jit(solution)/shard_map/ppermute | solution.py:651
  21.8 4.2 %copy-start.10 = (bf16[64,240]{1,0:T(8,128)(2,1)S(1)}, bf16[64,240]{1,0:T(8,128)(2,1)}, u32[]{:S(2)}) copy-start(bf16[64,240]{1,0:T(8,128)(2,1)} %constant.28.clone.source) | copy-start | bytes 92164
  26.0 2.5 %copy-start.1 = (f32[160,288]{1,0:T(8,128)S(1)}, f32[160,288]{1,0:T(8,128)}, u32[]{:S(2)}) copy-start(f32[160,288]{1,0:T(8,128)} %constant.23.clone.solve) | copy-start | bytes 552964
  26.4 5.0 %collective-permute-start.8 = (f32[8,3968]{1,0:T(8,128)S(1)}, f32[8,3968]{1,0:T(8,128)S(1)}, u32[]{:S(2)}, u32[]{:S(2)}) collective-permute-start(f32[8,3968]{1,0:T(8,128)S(1)} %get-tuple-element.48), channel_id=1, source_target_pairs={{0,8},{8,16},{16,24},{24,32},{32,40},{40,48},{48,56},{56,64},{64,7... | collective-permute-start | bytes 380936 | tf_op jit(solution)/shard_map/ppermute | solution.py:651
  26.5 8.3 %collective-permute-start.9 = (f32[8,3968]{1,0:T(8,128)S(1)}, f32[8,3968]{1,0:T(8,128)S(1)}, u32[]{:S(2)}, u32[]{:S(2)}) collective-permute-start(f32[8,3968]{1,0:T(8,128)S(1)} %get-tuple-element.49), channel_id=1, source_target_pairs={{0,248},{8,0},{16,8},{24,16},{32,24},{40,32},{48,40},{56,48},{64,5... | collective-permute-start | bytes 380936 | tf_op jit(solution)/shard_map/ppermute | solution.py:651
  28.5 6.3 %copy-start.4 = (bf16[160,384]{1,0:T(8,128)(2,1)S(1)}, bf16[160,384]{1,0:T(8,128)(2,1)}, u32[]{:S(2)}) copy-start(bf16[160,384]{1,0:T(8,128)(2,1)} %constant.29.clone.solve) | copy-start | bytes 368644
  28.5 6.3 %copy-start.7 = (bf16[128,240]{1,0:T(8,128)(2,1)S(1)}, bf16[128,240]{1,0:T(8,128)(2,1)}, u32[]{:S(2)}) copy-start(bf16[128,240]{1,0:T(8,128)(2,1)} %constant.25.clone.full) | copy-start | bytes 184324
  34.8 12.4 %copy-start.9 = (bf16[64,240]{1,0:T(8,128)(2,1)S(1)}, bf16[64,240]{1,0:T(8,128)(2,1)}, u32[]{:S(2)}) copy-start(bf16[64,240]{1,0:T(8,128)(2,1)} %constant.31.clone.source) | copy-start | bytes 92164
  36.5 10.7 %collective-permute-start.10 = (f32[544,128]{1,0:T(8,128)S(1)}, f32[544,128]{1,0:T(8,128)S(1)}, u32[]{:S(2)}, u32[]{:S(2)}) collective-permute-start(f32[544,128]{1,0:T(8,128)S(1)} %get-tuple-element.53), channel_id=1, source_target_pairs={{0,1},{1,2},{2,3},{3,4},{4,5},{5,6},{6,7},{7,0},{8,9},{9,10},{10,1... | collective-permute-start | bytes 835592 | tf_op jit(solution)/shard_map/ppermute | solution.py:651
  36.5 10.7 %collective-permute-start.11 = (f32[544,128]{1,0:T(8,128)S(1)}, f32[544,128]{1,0:T(8,128)S(1)}, u32[]{:S(2)}, u32[]{:S(2)}) collective-permute-start(f32[544,128]{1,0:T(8,128)S(1)} %get-tuple-element.54), channel_id=1, source_target_pairs={{0,7},{1,0},{2,1},{3,2},{4,3},{5,4},{6,5},{7,6},{8,15},{9,8},{10,9... | collective-permute-start | bytes 835592 | tf_op jit(solution)/shard_map/ppermute | solution.py:651
  38.3 6.5 %collective-permute-start.12 = (f32[264,128]{1,0:T(8,128)S(1)}, f32[264,128]{1,0:T(8,128)S(1)}, u32[]{:S(2)}, u32[]{:S(2)}) collective-permute-start(f32[264,128]{1,0:T(8,128)S(1)} %get-tuple-element.55), channel_id=1, source_target_pairs={{0,2},{1,3},{2,4},{3,5},{4,6},{5,7},{6,0},{7,1},{8,10},{9,11},{10,... | collective-permute-start | bytes 405512 | tf_op jit(solution)/shard_map/ppermute | solution.py:651
  40.1 7.1 %collective-permute-start.13 = (f32[264,128]{1,0:T(8,128)S(1)}, f32[264,128]{1,0:T(8,128)S(1)}, u32[]{:S(2)}, u32[]{:S(2)}) collective-permute-start(f32[264,128]{1,0:T(8,128)S(1)} %get-tuple-element.56), channel_id=1, source_target_pairs={{0,6},{1,7},{2,0},{3,1},{4,2},{5,3},{6,4},{7,5},{8,14},{9,15},{10,... | collective-permute-start | bytes 405512 | tf_op jit(solution)/shard_map/ppermute | solution.py:651
  47.2 2.6 %copy-start.3 = (f32[128,288]{1,0:T(8,128)S(1)}, f32[128,288]{1,0:T(8,128)}, u32[]{:S(2)}) copy-start(f32[128,288]{1,0:T(8,128)} %constant.30.clone.solve) | copy-start | bytes 442372
  47.6 4.7 %collective-permute-start.14 = (f32[8,2688]{1,0:T(8,128)S(1)}, f32[8,2688]{1,0:T(8,128)S(1)}, u32[]{:S(2)}, u32[]{:S(2)}) collective-permute-start(f32[8,2688]{1,0:T(8,128)S(1)} %get-tuple-element.58), channel_id=1, source_target_pairs={{0,8},{8,16},{16,24},{24,32},{32,40},{40,48},{48,56},{56,64},{64,7... | collective-permute-start | bytes 258056 | tf_op jit(solution)/shard_map/ppermute | solution.py:651
  47.9 7.8 %collective-permute-start.15 = (f32[8,2688]{1,0:T(8,128)S(1)}, f32[8,2688]{1,0:T(8,128)S(1)}, u32[]{:S(2)}, u32[]{:S(2)}) collective-permute-start(f32[8,2688]{1,0:T(8,128)S(1)} %get-tuple-element.59), channel_id=1, source_target_pairs={{0,248},{8,0},{16,8},{24,16},{32,24},{40,32},{48,40},{56,48},{64,5... | collective-permute-start | bytes 258056 | tf_op jit(solution)/shard_map/ppermute | solution.py:651
  49.8 5.9 %copy-start.5 = (bf16[128,384]{1,0:T(8,128)(2,1)S(1)}, bf16[128,384]{1,0:T(8,128)(2,1)}, u32[]{:S(2)}) copy-start(bf16[128,384]{1,0:T(8,128)(2,1)} %constant.32.clone.solve) | copy-start | bytes 294916

commit v11 on v10

--- a/solution.py
+++ b/solution.py
@@ -126,8 +126,8 @@
                 solve_sides[top : top + RANK_V, wide * j : wide * (j + 1)] = -sides
     full = np.concatenate([own, from_left, from_right], axis=1)
     full = np.pad(full, [(0, 0), (0, GROUP - 2 * RANK_V)])
-    plain, split = (own, solve_own), (slopes, full, moments, lateral, source, solve_sides)
-    return [x.astype(np.float32) for x in plain] + [split_table(x.astype(np.float32)) for x in split]
+    split = (solve_own, slopes, full, moments, lateral, source, solve_sides)
+    return [own.astype(np.float32)] + [split_table(x.astype(np.float32)) for x in split]
 
 
 def dot(a, b):
@@ -512,7 +512,7 @@
 def home_kernel(extent, ext, solve, partial, levels):
     depth = ext.shape[0]
     levels[:depth, :] = ext[...]
-    partial[...] = dot(solve[...], climb(extent, levels, depth))
+    partial[...] = split_dot(solve[...], climb(extent, levels, depth))
 
 
 def spare(given, e):

time: 57.5 us -> 57.2 us (level)
  Pallas kernels: 10.1 us -> 9.11 us
  waiting for transfers between devices: 29.6 us -> 30.5 us
    ppermute x16, waiting for transfers between devices: 29.6 us -> 30.5 us  [shifted(): lax.ppermute(block, axis, [(i, (i + step) % count) for i in range(count)])]
    pallas_call x10, Pallas kernels: 10.1 us -> 9.11 us  [call(): pl.pallas_call(body, out_shape=[jax.ShapeDtypeStruct(s, jnp.float32) for...]
  transfers between devices with their start and end apart: 16 -> 16, of which waited for: 12 -> 12; matrix products, arithmetic and copies ran while one was open for 0% -> 0% of each run, Pallas kernels for 8% -> 6%
where the time goes in v11:
time: 57.2 us; the launch traced here: 57 us
  waiting for transfers between devices  30.5 us (53%)
  starting transfers between devices  17.2 us (30%)
  Pallas kernels  9.11 us (16%)
    ppermute x16, waiting for transfers between devices, shifted(): lax.ppermute(block, axis, [(i, (i + step) % count) for i in range(count)])  30.5 us
    ppermute x16, starting transfers between devices, shifted(): lax.ppermute(block, axis, [(i, (i + step) % count) for i in range(count)])  17.2 us
    pallas_call x10, Pallas kernels, call(): pl.pallas_call(body, out_shape=[jax.ShapeDtypeStruct(s, jnp.float32) for...  9.11 us
  transfers between devices with their start and end apart: 16, of which 12 were waited for; matrix products, arithmetic and copies ran while one was open for 0% of the time, Pallas kernels for 6%

profile of v11, /device:TPU:126, one launch (start us, length us, event | category | flops | bytes accessed | tf_op | source)
XLA Modules:
  0.0 57.0 jit_solution(2056698211001947197)
XLA Ops:
  0.0 0.0 copy-start.8
  0.0 1.3 %shard_map.127 = (f32[192,512]{1,0:T(8,128)S(1)}, f32[64,512]{1,0:T(8,128)S(1)}, f32[16,512]{1,0:T(8,128)S(1)}, f32[16,512]{1,0:T(8,128)S(1)}, f32[448,128]{1,0:T(8,128)S(1)}, /*index=5*/f32[448,128]{1,0:T(8,128)S(1)}) custom-call(f32[3,64,4,128]{3,2,1,0:T(4,128)} %velocity.1, f32[64,4,128]{2,1,0:T(4,128)} %viscosity.1, ...), custom_call_target="tpu_custom_call" | custom-call | tf_op jit(solution)/shard_map/pallas_call | solution.py:640
  1.3 0.0 collective-permute-start.2
  1.4 1.7 %collective-permute-start.3 = (f32[448,128]{1,0:T(8,128)S(1)}, f32[448,128]{1,0:T(8,128)S(1)}, u32[]{:S(2)}, u32[]{:S(2)}) collective-permute-start(f32[448,128]{1,0:T(8,128)S(1)} %get-tuple-element.38), channel_id=1, source_target_pairs={{0,7},{1,0},{2,1},{3,2},{4,3},{5,4},{6,5},{7,6},{8,15},{9,8},{10,9... | collective-permute-start | bytes 688136 | tf_op jit(solution)/shard_map/ppermute | solution.py:651
  3.1 3.0 %collective-permute-start = (f32[16,512]{1,0:T(8,128)S(1)}, f32[16,512]{1,0:T(8,128)S(1)}, u32[]{:S(2)}, u32[]{:S(2)}) collective-permute-start(f32[16,512]{1,0:T(8,128)S(1)} %get-tuple-element.35), channel_id=1, source_target_pairs={{0,8},{8,16},{16,24},{24,32},{32,40},{40,48},{48,56},{56,64},{64,7... | collective-permute-start | bytes 98312 | tf_op jit(solution)/shard_map/ppermute | solution.py:651
  6.1 0.0 collective-permute-start.1
  6.1 0.0 copy-done.8
  6.1 0.0 copy-start
  6.1 0.0 copy-start.6
  6.2 0.9 %shard_map.128.rough = f32[192,512]{1,0:T(8,128)S(1)} custom-call(f32[192,512]{1,0:T(8,128)S(1)} %get-tuple-element.33.flat.start, f32[64,512]{1,0:T(8,128)S(1)} %get-tuple-element.34.thick, f32[128,64]{1,0:T(8,128)S(1)} %copy-done.8), custom_call_target="tpu_custom_call" | custom-call | tf_op jit(solution)/shard_map/pallas_call | solution.py:640
  7.1 0.0 copy-start.3
  7.1 0.6 %collective-permute-done.left = f32[16,512]{1,0:T(8,128)S(1)} collective-permute-done((f32[16,512]{1,0:T(8,128)S(1)}, f32[16,512]{1,0:T(8,128)S(1)}, u32[]{:S(2)}, u32[]{:S(2)}) %collective-permute-start) | collective-permute-done | bytes 32800 | tf_op jit(solution)/shard_map/ppermute | solution.py:651
  7.7 5.6 %collective-permute-done.1.right = f32[16,512]{1,0:T(8,128)S(1)} collective-permute-done((f32[16,512]{1,0:T(8,128)S(1)}, f32[16,512]{1,0:T(8,128)S(1)}, u32[]{:S(2)}, u32[]{:S(2)}) %collective-permute-start.1) | collective-permute-done | bytes 32800 | tf_op jit(solution)/shard_map/ppermute | solution.py:651
  13.4 0.0 collective-permute-done.2.low
  13.4 0.0 collective-permute-done.3.high
  13.4 0.0 copy-done
  13.4 0.0 copy-done.6
  13.4 0.5 shard_map.129
  13.9 0.0 collective-permute-start.4
  13.9 1.7 %collective-permute-start.5 = (f32[656,128]{1,0:T(8,128)S(1)}, f32[656,128]{1,0:T(8,128)S(1)}, u32[]{:S(2)}, u32[]{:S(2)}) collective-permute-start(f32[656,128]{1,0:T(8,128)S(1)} %get-tuple-element.42), channel_id=1, source_target_pairs={{0,7},{1,0},{2,1},{3,2},{4,3},{5,4},{6,5},{7,6},{8,15},{9,8},{10,9... | collective-permute-start | bytes 1007624 | tf_op jit(solution)/shard_map/ppermute | solution.py:651
  15.7 2.6 %collective-permute-start.6 = (f32[272,128]{1,0:T(8,128)S(1)}, f32[272,128]{1,0:T(8,128)S(1)}, u32[]{:S(2)}, u32[]{:S(2)}) collective-permute-start(f32[272,128]{1,0:T(8,128)S(1)} %get-tuple-element.45), channel_id=1, source_target_pairs={{0,2},{1,3},{2,4},{3,5},{4,6},{5,7},{6,0},{7,1},{8,10},{9,11},{10,... | collective-permute-start | bytes 417800 | tf_op jit(solution)/shard_map/ppermute | solution.py:651
  18.3 0.0 collective-permute-start.7
  18.3 3.4 %collective-permute-done.4.low_one = f32[656,128]{1,0:T(8,128)S(1)} collective-permute-done((f32[656,128]{1,0:T(8,128)S(1)}, f32[656,128]{1,0:T(8,128)S(1)}, u32[]{:S(2)}, u32[]{:S(2)}) %collective-permute-start.4) | collective-permute-done | bytes 335904 | tf_op jit(solution)/shard_map/ppermute | solution.py:651
  21.7 0.1 collective-permute-done.5.high_one
  21.8 0.0 copy-done.3
  21.8 0.0 copy-start.10
  21.8 0.3 shard_map.130
  22.1 0.3 collective-permute-done.6.low_two
  22.4 3.6 %collective-permute-done.7.high_two = f32[272,128]{1,0:T(8,128)S(1)} collective-permute-done((f32[272,128]{1,0:T(8,128)S(1)}, f32[272,128]{1,0:T(8,128)S(1)}, u32[]{:S(2)}, u32[]{:S(2)}) %collective-permute-start.7) | collective-permute-done | bytes 139296 | tf_op jit(solution)/shard_map/ppermute | solution.py:651
  26.0 0.0 copy-done.10
  26.0 0.0 copy-start.1
  26.0 0.4 shard_map.131
  26.4 0.1 collective-permute-start.8
  26.5 2.0 %collective-permute-start.9 = (f32[8,3968]{1,0:T(8,128)S(1)}, f32[8,3968]{1,0:T(8,128)S(1)}, u32[]{:S(2)}, u32[]{:S(2)}) collective-permute-start(f32[8,3968]{1,0:T(8,128)S(1)} %get-tuple-element.49), channel_id=1, source_target_pairs={{0,248},{8,0},{16,8},{24,16},{32,24},{40,32},{48,40},{56,48},{64,5... | collective-permute-start | bytes 380936 | tf_op jit(solution)/shard_map/ppermute | solution.py:651
  28.5 0.0 copy-done.1
  28.5 0.0 copy-start.4
  28.5 0.0 copy-start.7
  28.5 1.2 %shard_map.132.partial = f32[160,1280]{1,0:T(8,128)S(1)} custom-call(f32[72,2048]{1,0:T(8,128)S(1)} %get-tuple-element.47.ext, bf16[160,864]{1,0:T(8,128)(2,1)S(1)} %copy-done.1), custom_call_target="tpu_custom_call" | custom-call | tf_op jit(solution)/shard_map/pallas_call | solution.py:640
  29.7 1.7 %collective-permute-done.8.left = f32[8,3968]{1,0:T(8,128)S(1)} collective-permute-done((f32[8,3968]{1,0:T(8,128)S(1)}, f32[8,3968]{1,0:T(8,128)S(1)}, u32[]{:S(2)}, u32[]{:S(2)}) %collective-permute-start.8) | collective-permute-done | bytes 127008 | tf_op jit(solution)/shard_map/ppermute | solution.py:651
  31.4 3.4 %collective-permute-done.9.right = f32[8,3968]{1,0:T(8,128)S(1)} collective-permute-done((f32[8,3968]{1,0:T(8,128)S(1)}, f32[8,3968]{1,0:T(8,128)S(1)}, u32[]{:S(2)}, u32[]{:S(2)}) %collective-permute-start.9) | collective-permute-done | bytes 127008 | tf_op jit(solution)/shard_map/ppermute | solution.py:651
  34.8 0.0 copy-done.4
  34.8 0.0 copy-done.7
  34.8 0.0 copy-start.9
  34.8 1.7 %shard_map.133 = (f32[192,512]{1,0:T(8,128)S(1)}, f32[72,512]{1,0:T(8,128)S(1)}, f32[128,128]{1,0:T(8,128)S(1)}, f32[544,128]{1,0:T(8,128)S(1)}, f32[544,128]{1,...) custom-call(f32[160,1280]{1,0:T(8,128)S(1)} %shard_map.132.partial, ...), custom_call_target="tpu_custom_call" | custom-call | tf_op jit(solution)/shard_map/pallas_call | solution.py:640
  36.5 0.0 collective-permute-start.10
  36.5 1.7 %collective-permute-start.11 = (f32[544,128]{1,0:T(8,128)S(1)}, f32[544,128]{1,0:T(8,128)S(1)}, u32[]{:S(2)}, u32[]{:S(2)}) collective-permute-start(f32[544,128]{1,0:T(8,128)S(1)} %get-tuple-element.54), channel_id=1, source_target_pairs={{0,7},{1,0},{2,1},{3,2},{4,3},{5,4},{6,5},{7,6},{8,15},{9,8},{10,9... | collective-permute-start | bytes 835592 | tf_op jit(solution)/shard_map/ppermute | solution.py:651
  38.3 1.9 %collective-permute-start.12 = (f32[264,128]{1,0:T(8,128)S(1)}, f32[264,128]{1,0:T(8,128)S(1)}, u32[]{:S(2)}, u32[]{:S(2)}) collective-permute-start(f32[264,128]{1,0:T(8,128)S(1)} %get-tuple-element.55), channel_id=1, source_target_pairs={{0,2},{1,3},{2,4},{3,5},{4,6},{5,7},{6,0},{7,1},{8,10},{9,11},{10,... | collective-permute-start | bytes 405512 | tf_op jit(solution)/shard_map/ppermute | solution.py:651
  40.1 0.2 collective-permute-start.13
  40.3 4.5 %collective-permute-done.12.low_two = f32[264,128]{1,0:T(8,128)S(1)} collective-permute-done((f32[264,128]{1,0:T(8,128)S(1)}, f32[264,128]{1,0:T(8,128)S(1)}, u32[]{:S(2)}, u32[]{:S(2)}) %collective-permute-start.12) | collective-permute-done | bytes 135200 | tf_op jit(solution)/shard_map/ppermute | solution.py:651
  44.8 2.4 %collective-permute-done.13.high_two = f32[264,128]{1,0:T(8,128)S(1)} collective-permute-done((f32[264,128]{1,0:T(8,128)S(1)}, f32[264,128]{1,0:T(8,128)S(1)}, u32[]{:S(2)}, u32[]{:S(2)}) %collective-permute-start.13) | collective-permute-done | bytes 135200 | tf_op jit(solution)/shard_map/ppermute | solution.py:651
  47.2 0.0 collective-permute-done.10.low_one
  47.2 0.0 collective-permute-done.11.high_one
  47.2 0.0 copy-done.9
  47.2 0.0 copy-start.2
  47.2 0.3 shard_map.134
  47.6 0.2 collective-permute-start.14
  47.8 1.9 %collective-permute-start.15 = (f32[8,2688]{1,0:T(8,128)S(1)}, f32[8,2688]{1,0:T(8,128)S(1)}, u32[]{:S(2)}, u32[]{:S(2)}) collective-permute-start(f32[8,2688]{1,0:T(8,128)S(1)} %get-tuple-element.59), channel_id=1, source_target_pairs={{0,248},{8,0},{16,8},{24,16},{32,24},{40,32},{48,40},{56,48},{64,5... | collective-permute-start | bytes 258056 | tf_op jit(solution)/shard_map/ppermute | solution.py:651
  49.7 0.0 copy-done.2
  49.7 0.0 copy-start.5
  49.7 1.0 %shard_map.135.partial = f32[128,1024]{1,0:T(8,128)S(1)} custom-call(f32[72,1792]{1,0:T(8,128)S(1)} %get-tuple-element.57.ext, bf16[128,864]{1,0:T(8,128)(2,1)S(1)} %copy-done.2), custom_call_target="tpu_custom_call" | custom-call | tf_op jit(solution)/shard_map/pallas_call | solution.py:640
  50.7 1.4 %collective-permute-done.14.left = f32[8,2688]{1,0:T(8,128)S(1)} collective-permute-done((f32[8,2688]{1,0:T(8,128)S(1)}, f32[8,2688]{1,0:T(8,128)S(1)}, u32[]{:S(2)}, u32[]{:S(2)}) %collective-permute-start.14) | collective-permute-done | bytes 86048 | tf_op jit(solution)/shard_map/ppermute | solution.py:651
  52.1 3.4 %collective-permute-done.15.right = f32[8,2688]{1,0:T(8,128)S(1)} collective-permute-done((f32[8,2688]{1,0:T(8,128)S(1)}, f32[8,2688]{1,0:T(8,128)S(1)}, u32[]{:S(2)}, u32[]{:S(2)}) %collective-permute-start.15) | collective-permute-done | bytes 86048 | tf_op jit(solution)/shard_map/ppermute | solution.py:651
  55.6 0.0 copy-done.5
  55.6 1.4 %shard_map.136 = f32[3,64,4,128]{3,2,1,0:T(4,128)} custom-call(f32[128,1024]{1,0:T(8,128)S(1)} %shard_map.135.partial, f32[8,2688]{1,0:T(8,128)S(1)} %collective-permute-done.14.left, f32[8,2688]{1,0:T(8,128)S(1)} %collective-permute-done.15.right, f32[192,512]{1,0:T(8,128)S(1)} %get-tuple-element.51.section, f32[128,128]{1,0:T(8,128)S(1)} %get-tuple-element.60.fixed, ...), custom_call_target="tpu_custom_call" | custom-call | tf_op jit(solution)/shard_map/pallas_call | solution.py:640
Async XLA Ops:
  0.0 6.1 %copy-start.8 = (f32[128,64]{1,0:T(8,128)S(1)}, f32[128,64]{1,0:T(8,128)}, u32[]{:S(2)}) copy-start(f32[128,64]{1,0:T(8,128)} %constant.22.clone.own) | copy-start | bytes 98308
  1.3 12.0 %collective-permute-start.2 = (f32[448,128]{1,0:T(8,128)S(1)}, f32[448,128]{1,0:T(8,128)S(1)}, u32[]{:S(2)}, u32[]{:S(2)}) collective-permute-start(f32[448,128]{1,0:T(8,128)S(1)} %get-tuple-element.37), channel_id=1, source_target_pairs={{0,1},{1,2},{2,3},{3,4},{4,5},{5,6},{6,7},{7,0},{8,9},{9,10},{10,1... | collective-permute-start | bytes 688136 | tf_op jit(solution)/shard_map/ppermute | solution.py:651
  1.4 12.0 %collective-permute-start.3 = (f32[448,128]{1,0:T(8,128)S(1)}, f32[448,128]{1,0:T(8,128)S(1)}, u32[]{:S(2)}, u32[]{:S(2)}) collective-permute-start(f32[448,128]{1,0:T(8,128)S(1)} %get-tuple-element.38), channel_id=1, source_target_pairs={{0,7},{1,0},{2,1},{3,2},{4,3},{5,4},{6,5},{7,6},{8,15},{9,8},{10,9... | collective-permute-start | bytes 688136 | tf_op jit(solution)/shard_map/ppermute | solution.py:651
  3.1 4.6 %collective-permute-start = (f32[16,512]{1,0:T(8,128)S(1)}, f32[16,512]{1,0:T(8,128)S(1)}, u32[]{:S(2)}, u32[]{:S(2)}) collective-permute-start(f32[16,512]{1,0:T(8,128)S(1)} %get-tuple-element.35), channel_id=1, source_target_pairs={{0,8},{8,16},{16,24},{24,32},{32,40},{40,48},{48,56},{56,64},{64,7... | collective-permute-start | bytes 98312 | tf_op jit(solution)/shard_map/ppermute | solution.py:651
  6.1 7.2 %collective-permute-start.1 = (f32[16,512]{1,0:T(8,128)S(1)}, f32[16,512]{1,0:T(8,128)S(1)}, u32[]{:S(2)}, u32[]{:S(2)}) collective-permute-start(f32[16,512]{1,0:T(8,128)S(1)} %get-tuple-element.36), channel_id=1, source_target_pairs={{0,248},{8,0},{16,8},{24,16},{32,24},{40,32},{48,40},{56,48},{64,5... | collective-permute-start | bytes 98312 | tf_op jit(solution)/shard_map/ppermute | solution.py:651
  6.1 7.2 %copy-start = (bf16[72,192]{1,0:T(8,128)(2,1)S(1)}, bf16[72,192]{1,0:T(8,128)(2,1)}, u32[]{:S(2)}) copy-start(bf16[72,192]{1,0:T(8,128)(2,1)} %constant.27.clone.lateral) | copy-start | bytes 82948
  6.1 7.2 %copy-start.6 = (bf16[3,128,96]{2,1,0:T(8,128)(2,1)S(1)}, bf16[3,128,96]{2,1,0:T(8,128)(2,1)}, u32[]{:S(2)}) copy-start(bf16[3,128,96]{2,1,0:T(8,128)(2,1)} %constant.24.clone.slopes) | copy-start | bytes 221188
  7.1 14.8 %copy-start.3 = (bf16[3,32,192]{2,1,0:T(8,128)(2,1)S(1)}, bf16[3,32,192]{2,1,0:T(8,128)(2,1)}, u32[]{:S(2)}) copy-start(bf16[3,32,192]{2,1,0:T(8,128)(2,1)} %constant.26.clone.moments) | copy-start | bytes 110596
  13.9 7.8 %collective-permute-start.4 = (f32[656,128]{1,0:T(8,128)S(1)}, f32[656,128]{1,0:T(8,128)S(1)}, u32[]{:S(2)}, u32[]{:S(2)}) collective-permute-start(f32[656,128]{1,0:T(8,128)S(1)} %get-tuple-element.41), channel_id=1, source_target_pairs={{0,1},{1,2},{2,3},{3,4},{4,5},{5,6},{6,7},{7,0},{8,9},{9,10},{10,1... | collective-permute-start | bytes 1007624 | tf_op jit(solution)/shard_map/ppermute | solution.py:651
  13.9 7.9 %collective-permute-start.5 = (f32[656,128]{1,0:T(8,128)S(1)}, f32[656,128]{1,0:T(8,128)S(1)}, u32[]{:S(2)}, u32[]{:S(2)}) collective-permute-start(f32[656,128]{1,0:T(8,128)S(1)} %get-tuple-element.42), channel_id=1, source_target_pairs={{0,7},{1,0},{2,1},{3,2},{4,3},{5,4},{6,5},{7,6},{8,15},{9,8},{10,9... | collective-permute-start | bytes 1007624 | tf_op jit(solution)/shard_map/ppermute | solution.py:651
  15.7 6.8 %collective-permute-start.6 = (f32[272,128]{1,0:T(8,128)S(1)}, f32[272,128]{1,0:T(8,128)S(1)}, u32[]{:S(2)}, u32[]{:S(2)}) collective-permute-start(f32[272,128]{1,0:T(8,128)S(1)} %get-tuple-element.45), channel_id=1, source_target_pairs={{0,2},{1,3},{2,4},{3,5},{4,6},{5,7},{6,0},{7,1},{8,10},{9,11},{10,... | collective-permute-start | bytes 417800 | tf_op jit(solution)/shard_map/ppermute | solution.py:651
  18.3 7.7 %collective-permute-start.7 = (f32[272,128]{1,0:T(8,128)S(1)}, f32[272,128]{1,0:T(8,128)S(1)}, u32[]{:S(2)}, u32[]{:S(2)}) collective-permute-start(f32[272,128]{1,0:T(8,128)S(1)} %get-tuple-element.46), channel_id=1, source_target_pairs={{0,6},{1,7},{2,0},{3,1},{4,2},{5,3},{6,4},{7,5},{8,14},{9,15},{10,... | collective-permute-start | bytes 417800 | tf_op jit(solution)/shard_map/ppermute | solution.py:651
  21.8 4.2 %copy-start.10 = (bf16[64,240]{1,0:T(8,128)(2,1)S(1)}, bf16[64,240]{1,0:T(8,128)(2,1)}, u32[]{:S(2)}) copy-start(bf16[64,240]{1,0:T(8,128)(2,1)} %constant.28.clone.source) | copy-start | bytes 92164
  26.0 2.5 %copy-start.1 = (bf16[160,864]{1,0:T(8,128)(2,1)S(1)}, bf16[160,864]{1,0:T(8,128)(2,1)}, u32[]{:S(2)}) copy-start(bf16[160,864]{1,0:T(8,128)(2,1)} %constant.23.clone.solve) | copy-start | bytes 829444
  26.4 5.0 %collective-permute-start.8 = (f32[8,3968]{1,0:T(8,128)S(1)}, f32[8,3968]{1,0:T(8,128)S(1)}, u32[]{:S(2)}, u32[]{:S(2)}) collective-permute-start(f32[8,3968]{1,0:T(8,128)S(1)} %get-tuple-element.48), channel_id=1, source_target_pairs={{0,8},{8,16},{16,24},{24,32},{32,40},{40,48},{48,56},{56,64},{64,7... | collective-permute-start | bytes 380936 | tf_op jit(solution)/shard_map/ppermute | solution.py:651
  26.5 8.3 %collective-permute-start.9 = (f32[8,3968]{1,0:T(8,128)S(1)}, f32[8,3968]{1,0:T(8,128)S(1)}, u32[]{:S(2)}, u32[]{:S(2)}) collective-permute-start(f32[8,3968]{1,0:T(8,128)S(1)} %get-tuple-element.49), channel_id=1, source_target_pairs={{0,248},{8,0},{16,8},{24,16},{32,24},{40,32},{48,40},{56,48},{64,5... | collective-permute-start | bytes 380936 | tf_op jit(solution)/shard_map/ppermute | solution.py:651
  28.5 6.3 %copy-start.4 = (bf16[160,384]{1,0:T(8,128)(2,1)S(1)}, bf16[160,384]{1,0:T(8,128)(2,1)}, u32[]{:S(2)}) copy-start(bf16[160,384]{1,0:T(8,128)(2,1)} %constant.29.clone.solve) | copy-start | bytes 368644
  28.5 6.3 %copy-start.7 = (bf16[128,240]{1,0:T(8,128)(2,1)S(1)}, bf16[128,240]{1,0:T(8,128)(2,1)}, u32[]{:S(2)}) copy-start(bf16[128,240]{1,0:T(8,128)(2,1)} %constant.25.clone.full) | copy-start | bytes 184324
  34.8 12.4 %copy-start.9 = (bf16[64,240]{1,0:T(8,128)(2,1)S(1)}, bf16[64,240]{1,0:T(8,128)(2,1)}, u32[]{:S(2)}) copy-start(bf16[64,240]{1,0:T(8,128)(2,1)} %constant.31.clone.source) | copy-start | bytes 92164
  36.5 10.7 %collective-permute-start.10 = (f32[544,128]{1,0:T(8,128)S(1)}, f32[544,128]{1,0:T(8,128)S(1)}, u32[]{:S(2)}, u32[]{:S(2)}) collective-permute-start(f32[544,128]{1,0:T(8,128)S(1)} %get-tuple-element.53), channel_id=1, source_target_pairs={{0,1},{1,2},{2,3},{3,4},{4,5},{5,6},{6,7},{7,0},{8,9},{9,10},{10,1... | collective-permute-start | bytes 835592 | tf_op jit(solution)/shard_map/ppermute | solution.py:651
  36.5 10.7 %collective-permute-start.11 = (f32[544,128]{1,0:T(8,128)S(1)}, f32[544,128]{1,0:T(8,128)S(1)}, u32[]{:S(2)}, u32[]{:S(2)}) collective-permute-start(f32[544,128]{1,0:T(8,128)S(1)} %get-tuple-element.54), channel_id=1, source_target_pairs={{0,7},{1,0},{2,1},{3,2},{4,3},{5,4},{6,5},{7,6},{8,15},{9,8},{10,9... | collective-permute-start | bytes 835592 | tf_op jit(solution)/shard_map/ppermute | solution.py:651
  38.3 6.5 %collective-permute-start.12 = (f32[264,128]{1,0:T(8,128)S(1)}, f32[264,128]{1,0:T(8,128)S(1)}, u32[]{:S(2)}, u32[]{:S(2)}) collective-permute-start(f32[264,128]{1,0:T(8,128)S(1)} %get-tuple-element.55), channel_id=1, source_target_pairs={{0,2},{1,3},{2,4},{3,5},{4,6},{5,7},{6,0},{7,1},{8,10},{9,11},{10,... | collective-permute-start | bytes 405512 | tf_op jit(solution)/shard_map/ppermute | solution.py:651
  40.1 7.1 %collective-permute-start.13 = (f32[264,128]{1,0:T(8,128)S(1)}, f32[264,128]{1,0:T(8,128)S(1)}, u32[]{:S(2)}, u32[]{:S(2)}) collective-permute-start(f32[264,128]{1,0:T(8,128)S(1)} %get-tuple-element.56), channel_id=1, source_target_pairs={{0,6},{1,7},{2,0},{3,1},{4,2},{5,3},{6,4},{7,5},{8,14},{9,15},{10,... | collective-permute-start | bytes 405512 | tf_op jit(solution)/shard_map/ppermute | solution.py:651
  47.2 2.5 %copy-start.2 = (bf16[128,864]{1,0:T(8,128)(2,1)S(1)}, bf16[128,864]{1,0:T(8,128)(2,1)}, u32[]{:S(2)}) copy-start(bf16[128,864]{1,0:T(8,128)(2,1)} %constant.30.clone.solve) | copy-start | bytes 663556
  47.6 4.6 %collective-permute-start.14 = (f32[8,2688]{1,0:T(8,128)S(1)}, f32[8,2688]{1,0:T(8,128)S(1)}, u32[]{:S(2)}, u32[]{:S(2)}) collective-permute-start(f32[8,2688]{1,0:T(8,128)S(1)} %get-tuple-element.58), channel_id=1, source_target_pairs={{0,8},{8,16},{16,24},{24,32},{32,40},{40,48},{48,56},{56,64},{64,7... | collective-permute-start | bytes 258056 | tf_op jit(solution)/shard_map/ppermute | solution.py:651
  47.8 7.8 %collective-permute-start.15 = (f32[8,2688]{1,0:T(8,128)S(1)}, f32[8,2688]{1,0:T(8,128)S(1)}, u32[]{:S(2)}, u32[]{:S(2)}) collective-permute-start(f32[8,2688]{1,0:T(8,128)S(1)} %get-tuple-element.59), channel_id=1, source_target_pairs={{0,248},{8,0},{16,8},{24,16},{32,24},{40,32},{48,40},{56,48},{64,5... | collective-permute-start | bytes 258056 | tf_op jit(solution)/shard_map/ppermute | solution.py:651
  49.7 5.9 %copy-start.5 = (bf16[128,384]{1,0:T(8,128)(2,1)S(1)}, bf16[128,384]{1,0:T(8,128)(2,1)}, u32[]{:S(2)}) copy-start(bf16[128,384]{1,0:T(8,128)(2,1)} %constant.32.clone.solve) | copy-start | bytes 294916

commit v12 on v10

--- a/solution.py
+++ b/solution.py
@@ -358,7 +358,7 @@
     return value
 
 
-def near_source_kernel(cells, parts, section, low_one, high_one, lateral, moments, middle, held):
+def near_source_kernel(cells, parts, section, low_one, high_one, lateral, middle):
     masks = edge_masks()
     across = row_across(cells, section, (low_one, high_one, None, None))
     pick = lambda ref, k: slot(ref, cells, k)[...]
@@ -377,7 +377,11 @@
                 total = total + factor * across(e + reach)
         middle[:cells, lane(e + 2)] = masked(total, e, masks)
         middle[cells:, lane(e + 2)] = masked(side, e, masks)
-    held[...] = sum(split_dot(moments[c], section[cells * c : cells * (c + 1), :]) for c in range(3))
+
+def held_kernel(cells, section, moments, to_right, to_left):
+    held = sum(split_dot(moments[c], section[cells * c : cells * (c + 1), :]) for c in range(3))
+    to_right[...] = held[:PAD_V]
+    to_left[...] = held[PAD_V:]
 
 
 def first_source(cells, middle, arrived, ext):
@@ -455,23 +459,16 @@
 
 
 def source_kernel(
-    cells, middle, held, low_one, high_one, low_two, high_two, source, ext, to_right, to_left
+    cells, middle, low_one, high_one, low_two, high_two, source, ext, to_right, to_left
 ):
     first_source(cells, middle, (low_one, high_one, low_two, high_two), ext)
     both = split_dot(source[...], ext[...])
     pack_moments(FIRST, both, to_right, to_left)
     for side, out in enumerate((to_right, to_left)):
-        top, base = 4 * GROUP * side, PAD_V * side
-        out[:, lane(FIRST.packed, ROWS)] = held[base : base + 8]
-        out[:, lane(FIRST.packed + ROWS, 3)] = jnp.zeros((GROUP, 3 * LANES), jnp.float32)
-        for e in range(FIRST.breadth + ROWS):
-            value = (
-                both[top + 24 : top + 25, lane(e)]
-                if e < FIRST.breadth
-                else held[base + 8 : base + 9, lane(e - FIRST.breadth)]
-            )
-            row, tile = e % GROUP, FIRST.packed + ROWS + e // GROUP
-            out[row : row + 1, lane(tile)] = value
+        top = 4 * GROUP * side
+        for e in range(FIRST.breadth):
+            row, tile = e % GROUP, FIRST.packed + e // GROUP
+            out[row : row + 1, lane(tile)] = both[top + 24 : top + 25, lane(e)]
 
 
 def last_source_kernel(
@@ -516,7 +513,7 @@
 
 
 def spare(given, e):
-    row, tile = e % GROUP, FIRST.packed + ROWS + e // GROUP
+    row, tile = e % GROUP, FIRST.packed + e // GROUP
     return given[row : row + 1, lane(tile)]
 
 
@@ -544,7 +541,8 @@
 
 
 def middle_kernel(
-    cells, partial, left, right, section, solve, low_one, high_one, low, high, start, thick, full, lateral,
+    cells, partial, left, right, held_left, held_right, section, solve, low_one, high_one, low, high, start,
+    thick, full, lateral,
     following, parts, debts, up_near, down_near, up_far, down_far, levels, flat, rim, sides,
 ):
     masks = edge_masks()
@@ -561,19 +559,15 @@
             value = value - gradient(FIRST, found, c, home, home_slope, r)
             rim[rows, lane(k)] = masked(value, r, masks)
     sides[...] = jnp.zeros(sides.shape, jnp.float32)
-    for side, given in enumerate((left, right)):
+    for side, given in enumerate((held_left, held_right)):
         top = 2 * cells + 2 * GROUP * side
         phi_rows, slope_rows = slice(top, top + GROUP), slice(top + GROUP, top + 2 * GROUP)
         for r in range(ROWS):
             for c in range(3):
                 change = gradient(FIRST, found, c, phi_rows, slope_rows, r)
                 base = GROUP * c + RANK_V * side
-                count = min(RANK_V, GROUP - RANK_V * c)
-                held = given[RANK_V * c : RANK_V * c + count, lane(FIRST.packed + r)]
-                sides[base : base + count, lane(r)] = held - change[:count]
-                if count < RANK_V:
-                    held = spare(given, FIRST.breadth + r)
-                    sides[base + count : base + RANK_V, lane(r)] = held - change[count:RANK_V]
+                held = given[RANK_V * c : RANK_V * (c + 1), lane(r)]
+                sides[base : base + RANK_V, lane(r)] = held - change[:RANK_V]
 
     def tile(c, r):
         rows = slice(cells * c, cells * (c + 1))
@@ -694,15 +688,19 @@
         rough, start, thick, left, right, low, high, slopes, lateral,
     )
     arrived = across(*sent)
-    middle, held = call(
+    to_right, to_left = call(functools.partial(held_kernel, cells), [edge, edge], section, moments)
+    held_left = shifted(to_right, "span", 1)
+    held_right = shifted(to_left, "span", -1)
+    (middle,) = call(
         functools.partial(near_source_kernel, cells),
-        [(near, 2 * width), (2 * PAD_V, width)],
-        parts, section, *arrived[:2], lateral, moments,
-    )
+        [(near, 2 * width)],
+        parts, section, *arrived[:2], lateral,
+    )
+    middle, held_left, held_right = lax.optimization_barrier((middle, held_left, held_right))
     ext, to_right, to_left = call(
         functools.partial(source_kernel, cells),
-        [(near, FIRST.breadth * columns)] + [(GROUP, (FIRST.packed + ROWS + 3) * columns)] * 2,
-        middle, held, *arrived, first[0],
+        [(near, FIRST.breadth * columns)] + [(GROUP, (FIRST.packed + 2) * columns)] * 2,
+        middle, *arrived, first[0],
     )
     left = shifted(to_right, "span", 1)
     right = shifted(to_left, "span", -1)
@@ -716,7 +714,7 @@
     section, parts, debts, *sent = call(
         functools.partial(middle_kernel, cells),
         [whole, (near, width), (2 * cells, columns)] + message(8, 4, 4, 1),
-        partial, left, right, section, first[1], *arrived[:2], low, high, start, thick, full, lateral,
+        partial, left, right, held_left, held_right, section, first[1], *arrived[:2], low, high, start, thick, full, lateral,
         scratch=[
             levels(FIRST, 2 * PAD_S),
             pltpu.VMEM(whole, jnp.float32),

time: 57.5 us -> 60.7 us (1.056)
  waiting for transfers between devices: 29.6 us -> 32.2 us
    ppermute x16 -> x18, waiting for transfers between devices: 29.6 us -> 32.2 us  [shifted(): lax.ppermute(block, axis, [(i, (i + step) % count) for i in range(count)])]
    ppermute x16 -> x18, starting transfers between devices: 17.4 us -> 17.8 us  [shifted(): lax.ppermute(block, axis, [(i, (i + step) % count) for i in range(count)])]
    pallas_call x10 -> x11, Pallas kernels: 10.1 us -> 10.2 us  [call(): pl.pallas_call(body, out_shape=[jax.ShapeDtypeStruct(s, jnp.float32) for...]
  transfers between devices with their start and end apart: 16 -> 18, of which waited for: 12 -> 12; matrix products, arithmetic and copies ran while one was open for 0% -> 0% of each run, Pallas kernels for 8% -> 8%
where the time goes in v12:
time: 60.7 us; the launch traced here: 60.6 us
  waiting for transfers between devices  32.2 us (53%)
  starting transfers between devices  17.8 us (29%)
  Pallas kernels  10.2 us (17%)
    ppermute x18, waiting for transfers between devices, shifted(): lax.ppermute(block, axis, [(i, (i + step) % count) for i in range(count)])  32.2 us
    ppermute x18, starting transfers between devices, shifted(): lax.ppermute(block, axis, [(i, (i + step) % count) for i in range(count)])  17.8 us
    pallas_call x11, Pallas kernels, call(): pl.pallas_call(body, out_shape=[jax.ShapeDtypeStruct(s, jnp.float32) for...  10.2 us
  transfers between devices with their start and end apart: 18, of which 12 were waited for; matrix products, arithmetic and copies ran while one was open for 0% of the time, Pallas kernels for 8%

profile of v12, /device:TPU:126, one launch (start us, length us, event | category | flops | bytes accessed | tf_op | source)
XLA Modules:
  0.0 60.6 jit_solution(17481532099389390522)
XLA Ops:
  0.0 0.0 copy-start.8
  0.0 1.3 %shard_map.127 = (f32[192,512]{1,0:T(8,128)S(1)}, f32[64,512]{1,0:T(8,128)S(1)}, f32[16,512]{1,0:T(8,128)S(1)}, f32[16,512]{1,0:T(8,128)S(1)}, f32[448,128]{1,0:T(8,128)S(1)}, /*index=5*/f32[448,128]{1,0:T(8,128)S(1)}) custom-call(f32[3,64,4,128]{3,2,1,0:T(4,128)} %velocity.1, f32[64,4,128]{2,1,0:T(4,128)} %viscosity.1, ...), custom_call_target="tpu_custom_call" | custom-call | tf_op jit(solution)/shard_map/pallas_call | solution.py:634
  1.3 0.0 collective-permute-start.2
  1.4 1.7 %collective-permute-start.3 = (f32[448,128]{1,0:T(8,128)S(1)}, f32[448,128]{1,0:T(8,128)S(1)}, u32[]{:S(2)}, u32[]{:S(2)}) collective-permute-start(f32[448,128]{1,0:T(8,128)S(1)} %get-tuple-element.41), channel_id=1, source_target_pairs={{0,7},{1,0},{2,1},{3,2},{4,3},{5,4},{6,5},{7,6},{8,15},{9,8},{10,9... | collective-permute-start | bytes 688136 | tf_op jit(solution)/shard_map/ppermute | solution.py:645
  3.1 3.0 %collective-permute-start = (f32[16,512]{1,0:T(8,128)S(1)}, f32[16,512]{1,0:T(8,128)S(1)}, u32[]{:S(2)}, u32[]{:S(2)}) collective-permute-start(f32[16,512]{1,0:T(8,128)S(1)} %get-tuple-element.38), channel_id=1, source_target_pairs={{0,8},{8,16},{16,24},{24,32},{32,40},{40,48},{48,56},{56,64},{64,7... | collective-permute-start | bytes 98312 | tf_op jit(solution)/shard_map/ppermute | solution.py:645
  6.1 0.0 collective-permute-start.1
  6.1 0.0 copy-done.8
  6.1 0.0 copy-start
  6.1 0.0 copy-start.6
  6.2 0.9 %shard_map.128.rough = f32[192,512]{1,0:T(8,128)S(1)} custom-call(f32[192,512]{1,0:T(8,128)S(1)} %get-tuple-element.36.flat.start, f32[64,512]{1,0:T(8,128)S(1)} %get-tuple-element.37.thick, f32[128,64]{1,0:T(8,128)S(1)} %copy-done.8), custom_call_target="tpu_custom_call" | custom-call | tf_op jit(solution)/shard_map/pallas_call | solution.py:634
  7.1 0.0 copy-start.3
  7.1 0.6 %collective-permute-done.left = f32[16,512]{1,0:T(8,128)S(1)} collective-permute-done((f32[16,512]{1,0:T(8,128)S(1)}, f32[16,512]{1,0:T(8,128)S(1)}, u32[]{:S(2)}, u32[]{:S(2)}) %collective-permute-start) | collective-permute-done | bytes 32800 | tf_op jit(solution)/shard_map/ppermute | solution.py:645
  7.7 5.6 %collective-permute-done.1.right = f32[16,512]{1,0:T(8,128)S(1)} collective-permute-done((f32[16,512]{1,0:T(8,128)S(1)}, f32[16,512]{1,0:T(8,128)S(1)}, u32[]{:S(2)}, u32[]{:S(2)}) %collective-permute-start.1) | collective-permute-done | bytes 32800 | tf_op jit(solution)/shard_map/ppermute | solution.py:645
  13.4 0.0 collective-permute-done.2.low
  13.4 0.0 collective-permute-done.3.high
  13.4 0.0 copy-done
  13.4 0.0 copy-done.6
  13.4 0.5 shard_map.129
  13.9 0.0 collective-permute-start.4
  13.9 1.7 %collective-permute-start.5 = (f32[656,128]{1,0:T(8,128)S(1)}, f32[656,128]{1,0:T(8,128)S(1)}, u32[]{:S(2)}, u32[]{:S(2)}) collective-permute-start(f32[656,128]{1,0:T(8,128)S(1)} %get-tuple-element.45), channel_id=1, source_target_pairs={{0,7},{1,0},{2,1},{3,2},{4,3},{5,4},{6,5},{7,6},{8,15},{9,8},{10,9... | collective-permute-start | bytes 1007624 | tf_op jit(solution)/shard_map/ppermute | solution.py:645
  15.7 2.6 %collective-permute-start.8 = (f32[272,128]{1,0:T(8,128)S(1)}, f32[272,128]{1,0:T(8,128)S(1)}, u32[]{:S(2)}, u32[]{:S(2)}) collective-permute-start(f32[272,128]{1,0:T(8,128)S(1)} %get-tuple-element.49), channel_id=1, source_target_pairs={{0,2},{1,3},{2,4},{3,5},{4,6},{5,7},{6,0},{7,1},{8,10},{9,11},{10,... | collective-permute-start | bytes 417800 | tf_op jit(solution)/shard_map/ppermute | solution.py:645
  18.3 0.0 collective-permute-start.9
  18.3 0.0 copy-done.3
  18.3 0.2 shard_map.131
  18.5 0.0 collective-permute-start.6
  18.6 3.2 %collective-permute-done.4.low_one = f32[656,128]{1,0:T(8,128)S(1)} collective-permute-done((f32[656,128]{1,0:T(8,128)S(1)}, f32[656,128]{1,0:T(8,128)S(1)}, u32[]{:S(2)}, u32[]{:S(2)}) %collective-permute-start.4) | collective-permute-done | bytes 335904 | tf_op jit(solution)/shard_map/ppermute | solution.py:645
  21.7 0.0 collective-permute-start.7
  21.7 0.1 collective-permute-done.5.high_one
  21.8 0.2 shard_map.130.middle
  22.1 0.0 copy-start.1
  22.1 0.3 collective-permute-done.6.held_left
  22.5 6.5 %collective-permute-done.7.held_right = f32[16,512]{1,0:T(8,128)S(1)} collective-permute-done((f32[16,512]{1,0:T(8,128)S(1)}, f32[16,512]{1,0:T(8,128)S(1)}, u32[]{:S(2)}, u32[]{:S(2)}) %collective-permute-start.7) | collective-permute-done | bytes 32800 | tf_op jit(solution)/shard_map/ppermute | solution.py:645
  29.0 0.0 collective-permute-done.8.low_two
  29.0 0.0 collective-permute-done.9.high_two
  29.0 0.0 copy-done.10
  29.0 0.4 shard_map.132
  29.3 0.1 collective-permute-start.10
  29.4 2.0 %collective-permute-start.11 = (f32[8,3328]{1,0:T(8,128)S(1)}, f32[8,3328]{1,0:T(8,128)S(1)}, u32[]{:S(2)}, u32[]{:S(2)}) collective-permute-start(f32[8,3328]{1,0:T(8,128)S(1)} %get-tuple-element.53), channel_id=1, source_target_pairs={{0,248},{8,0},{16,8},{24,16},{32,24},{40,32},{48,40},{56,48},{64,5... | collective-permute-start | bytes 319496 | tf_op jit(solution)/shard_map/ppermute | solution.py:645
  31.4 0.0 copy-done.1
  31.4 1.8 %shard_map.133.partial = f32[160,1280]{1,0:T(8,128)S(1)} custom-call(f32[72,2048]{1,0:T(8,128)S(1)} %get-tuple-element.51.ext, f32[160,288]{1,0:T(8,128)S(1)} %copy-done.1), custom_call_target="tpu_custom_call" | custom-call | tf_op jit(solution)/shard_map/pallas_call | solution.py:634
  33.2 0.9 %collective-permute-done.10.left = f32[8,3328]{1,0:T(8,128)S(1)} collective-permute-done((f32[8,3328]{1,0:T(8,128)S(1)}, f32[8,3328]{1,0:T(8,128)S(1)}, u32[]{:S(2)}, u32[]{:S(2)}) %collective-permute-start.10) | collective-permute-done | bytes 106528 | tf_op jit(solution)/shard_map/ppermute | solution.py:645
  34.1 3.4 %collective-permute-done.11.right = f32[8,3328]{1,0:T(8,128)S(1)} collective-permute-done((f32[8,3328]{1,0:T(8,128)S(1)}, f32[8,3328]{1,0:T(8,128)S(1)}, u32[]{:S(2)}, u32[]{:S(2)}) %collective-permute-start.11) | collective-permute-done | bytes 106528 | tf_op jit(solution)/shard_map/ppermute | solution.py:645
  37.5 0.0 copy-done.4
  37.5 0.0 copy-done.7
  37.5 1.7 %shard_map.134 = (f32[192,512]{1,0:T(8,128)S(1)}, f32[72,512]{1,0:T(8,128)S(1)}, f32[128,128]{1,0:T(8,128)S(1)}, f32[544,128]{1,0:T(8,128)S(1)}, f32[544,128]{1,...) custom-call(f32[160,1280]{1,0:T(8,128)S(1)} %shard_map.133.partial, ...), custom_call_target="tpu_custom_call" | custom-call | tf_op jit(solution)/shard_map/pallas_call | solution.py:634
  39.2 0.0 collective-permute-start.12
  39.3 1.7 %collective-permute-start.13 = (f32[544,128]{1,0:T(8,128)S(1)}, f32[544,128]{1,0:T(8,128)S(1)}, u32[]{:S(2)}, u32[]{:S(2)}) collective-permute-start(f32[544,128]{1,0:T(8,128)S(1)} %get-tuple-element.60), channel_id=1, source_target_pairs={{0,7},{1,0},{2,1},{3,2},{4,3},{5,4},{6,5},{7,6},{8,15},{9,8},{10,9... | collective-permute-start | bytes 835592 | tf_op jit(solution)/shard_map/ppermute | solution.py:645
  41.0 2.6 %collective-permute-start.14 = (f32[264,128]{1,0:T(8,128)S(1)}, f32[264,128]{1,0:T(8,128)S(1)}, u32[]{:S(2)}, u32[]{:S(2)}) collective-permute-start(f32[264,128]{1,0:T(8,128)S(1)} %get-tuple-element.61), channel_id=1, source_target_pairs={{0,2},{1,3},{2,4},{3,5},{4,6},{5,7},{6,0},{7,1},{8,10},{9,11},{10,... | collective-permute-start | bytes 405512 | tf_op jit(solution)/shard_map/ppermute | solution.py:645
  43.6 0.0 collective-permute-start.15
  43.7 3.9 %collective-permute-done.14.low_two = f32[264,128]{1,0:T(8,128)S(1)} collective-permute-done((f32[264,128]{1,0:T(8,128)S(1)}, f32[264,128]{1,0:T(8,128)S(1)}, u32[]{:S(2)}, u32[]{:S(2)}) %collective-permute-start.14) | collective-permute-done | bytes 135200 | tf_op jit(solution)/shard_map/ppermute | solution.py:645
  47.5 3.1 %collective-permute-done.15.high_two = f32[264,128]{1,0:T(8,128)S(1)} collective-permute-done((f32[264,128]{1,0:T(8,128)S(1)}, f32[264,128]{1,0:T(8,128)S(1)}, u32[]{:S(2)}, u32[]{:S(2)}) %collective-permute-start.15) | collective-permute-done | bytes 135200 | tf_op jit(solution)/shard_map/ppermute | solution.py:645
  50.6 0.0 collective-permute-done.12.low_one
  50.6 0.0 collective-permute-done.13.high_one
  50.6 0.0 copy-done.9
  50.6 0.0 copy-start.2
  50.7 0.3 shard_map.135
  51.0 0.1 collective-permute-start.16
  51.1 2.0 %collective-permute-start.17 = (f32[8,2688]{1,0:T(8,128)S(1)}, f32[8,2688]{1,0:T(8,128)S(1)}, u32[]{:S(2)}, u32[]{:S(2)}) collective-permute-start(f32[8,2688]{1,0:T(8,128)S(1)} %get-tuple-element.65), channel_id=1, source_target_pairs={{0,248},{8,0},{16,8},{24,16},{32,24},{40,32},{48,40},{56,48},{64,5... | collective-permute-start | bytes 258056 | tf_op jit(solution)/shard_map/ppermute | solution.py:645
  53.1 0.0 copy-done.2
  53.1 1.4 %shard_map.136.partial = f32[128,1024]{1,0:T(8,128)S(1)} custom-call(f32[72,1792]{1,0:T(8,128)S(1)} %get-tuple-element.63.ext, f32[128,288]{1,0:T(8,128)S(1)} %copy-done.2), custom_call_target="tpu_custom_call" | custom-call | tf_op jit(solution)/shard_map/pallas_call | solution.py:634
  54.5 1.1 %collective-permute-done.16.left = f32[8,2688]{1,0:T(8,128)S(1)} collective-permute-done((f32[8,2688]{1,0:T(8,128)S(1)}, f32[8,2688]{1,0:T(8,128)S(1)}, u32[]{:S(2)}, u32[]{:S(2)}) %collective-permute-start.16) | collective-permute-done | bytes 86048 | tf_op jit(solution)/shard_map/ppermute | solution.py:645
  55.6 3.4 %collective-permute-done.17.right = f32[8,2688]{1,0:T(8,128)S(1)} collective-permute-done((f32[8,2688]{1,0:T(8,128)S(1)}, f32[8,2688]{1,0:T(8,128)S(1)}, u32[]{:S(2)}, u32[]{:S(2)}) %collective-permute-start.17) | collective-permute-done | bytes 86048 | tf_op jit(solution)/shard_map/ppermute | solution.py:645
  59.0 0.0 copy-done.5
  59.0 1.4 %shard_map.137 = f32[3,64,4,128]{3,2,1,0:T(4,128)} custom-call(f32[128,1024]{1,0:T(8,128)S(1)} %shard_map.136.partial, f32[8,2688]{1,0:T(8,128)S(1)} %collective-permute-done.16.left, f32[8,2688]{1,0:T(8,128)S(1)} %collective-permute-done.17.right, f32[192,512]{1,0:T(8,128)S(1)} %get-tuple-element.57.section, f32[128,128]{1,0:T(8,128)S(1)} %get-tuple-element.66.fixed, ...), custom_call_target="tpu_custom_call" | custom-call | tf_op jit(solution)/shard_map/pallas_call | solution.py:634
  (5 shorter events, 0.0 us)
Async XLA Ops:
  0.0 6.1 %copy-start.8 = (f32[128,64]{1,0:T(8,128)S(1)}, f32[128,64]{1,0:T(8,128)}, u32[]{:S(2)}) copy-start(f32[128,64]{1,0:T(8,128)} %constant.22.clone.own) | copy-start | bytes 98308
  1.3 12.0 %collective-permute-start.2 = (f32[448,128]{1,0:T(8,128)S(1)}, f32[448,128]{1,0:T(8,128)S(1)}, u32[]{:S(2)}, u32[]{:S(2)}) collective-permute-start(f32[448,128]{1,0:T(8,128)S(1)} %get-tuple-element.40), channel_id=1, source_target_pairs={{0,1},{1,2},{2,3},{3,4},{4,5},{5,6},{6,7},{7,0},{8,9},{9,10},{10,1... | collective-permute-start | bytes 688136 | tf_op jit(solution)/shard_map/ppermute | solution.py:645
  1.4 12.0 %collective-permute-start.3 = (f32[448,128]{1,0:T(8,128)S(1)}, f32[448,128]{1,0:T(8,128)S(1)}, u32[]{:S(2)}, u32[]{:S(2)}) collective-permute-start(f32[448,128]{1,0:T(8,128)S(1)} %get-tuple-element.41), channel_id=1, source_target_pairs={{0,7},{1,0},{2,1},{3,2},{4,3},{5,4},{6,5},{7,6},{8,15},{9,8},{10,9... | collective-permute-start | bytes 688136 | tf_op jit(solution)/shard_map/ppermute | solution.py:645
  3.1 4.6 %collective-permute-start = (f32[16,512]{1,0:T(8,128)S(1)}, f32[16,512]{1,0:T(8,128)S(1)}, u32[]{:S(2)}, u32[]{:S(2)}) collective-permute-start(f32[16,512]{1,0:T(8,128)S(1)} %get-tuple-element.38), channel_id=1, source_target_pairs={{0,8},{8,16},{16,24},{24,32},{32,40},{40,48},{48,56},{56,64},{64,7... | collective-permute-start | bytes 98312 | tf_op jit(solution)/shard_map/ppermute | solution.py:645
  6.1 7.2 %collective-permute-start.1 = (f32[16,512]{1,0:T(8,128)S(1)}, f32[16,512]{1,0:T(8,128)S(1)}, u32[]{:S(2)}, u32[]{:S(2)}) collective-permute-start(f32[16,512]{1,0:T(8,128)S(1)} %get-tuple-element.39), channel_id=1, source_target_pairs={{0,248},{8,0},{16,8},{24,16},{32,24},{40,32},{48,40},{56,48},{64,5... | collective-permute-start | bytes 98312 | tf_op jit(solution)/shard_map/ppermute | solution.py:645
  6.1 7.2 %copy-start = (bf16[72,192]{1,0:T(8,128)(2,1)S(1)}, bf16[72,192]{1,0:T(8,128)(2,1)}, u32[]{:S(2)}) copy-start(bf16[72,192]{1,0:T(8,128)(2,1)} %constant.27.clone.lateral) | copy-start | bytes 82948
  6.1 7.2 %copy-start.6 = (bf16[3,128,96]{2,1,0:T(8,128)(2,1)S(1)}, bf16[3,128,96]{2,1,0:T(8,128)(2,1)}, u32[]{:S(2)}) copy-start(bf16[3,128,96]{2,1,0:T(8,128)(2,1)} %constant.24.clone.slopes) | copy-start | bytes 221188
  7.1 11.2 %copy-start.3 = (bf16[3,32,192]{2,1,0:T(8,128)(2,1)S(1)}, bf16[3,32,192]{2,1,0:T(8,128)(2,1)}, u32[]{:S(2)}) copy-start(bf16[3,32,192]{2,1,0:T(8,128)(2,1)} %constant.26.clone.moments) | copy-start | bytes 110596
  13.9 7.8 %collective-permute-start.4 = (f32[656,128]{1,0:T(8,128)S(1)}, f32[656,128]{1,0:T(8,128)S(1)}, u32[]{:S(2)}, u32[]{:S(2)}) collective-permute-start(f32[656,128]{1,0:T(8,128)S(1)} %get-tuple-element.44), channel_id=1, source_target_pairs={{0,1},{1,2},{2,3},{3,4},{4,5},{5,6},{6,7},{7,0},{8,9},{9,10},{10,1... | collective-permute-start | bytes 1007624 | tf_op jit(solution)/shard_map/ppermute | solution.py:645
  13.9 7.9 %collective-permute-start.5 = (f32[656,128]{1,0:T(8,128)S(1)}, f32[656,128]{1,0:T(8,128)S(1)}, u32[]{:S(2)}, u32[]{:S(2)}) collective-permute-start(f32[656,128]{1,0:T(8,128)S(1)} %get-tuple-element.45), channel_id=1, source_target_pairs={{0,7},{1,0},{2,1},{3,2},{4,3},{5,4},{6,5},{7,6},{8,15},{9,8},{10,9... | collective-permute-start | bytes 1007624 | tf_op jit(solution)/shard_map/ppermute | solution.py:645
  15.7 13.3 %collective-permute-start.8 = (f32[272,128]{1,0:T(8,128)S(1)}, f32[272,128]{1,0:T(8,128)S(1)}, u32[]{:S(2)}, u32[]{:S(2)}) collective-permute-start(f32[272,128]{1,0:T(8,128)S(1)} %get-tuple-element.49), channel_id=1, source_target_pairs={{0,2},{1,3},{2,4},{3,5},{4,6},{5,7},{6,0},{7,1},{8,10},{9,11},{10,... | collective-permute-start | bytes 417800 | tf_op jit(solution)/shard_map/ppermute | solution.py:645
  18.3 10.6 %collective-permute-start.9 = (f32[272,128]{1,0:T(8,128)S(1)}, f32[272,128]{1,0:T(8,128)S(1)}, u32[]{:S(2)}, u32[]{:S(2)}) collective-permute-start(f32[272,128]{1,0:T(8,128)S(1)} %get-tuple-element.50), channel_id=1, source_target_pairs={{0,6},{1,7},{2,0},{3,1},{4,2},{5,3},{6,4},{7,5},{8,14},{9,15},{10,... | collective-permute-start | bytes 417800 | tf_op jit(solution)/shard_map/ppermute | solution.py:645
  18.5 3.9 %collective-permute-start.6 = (f32[16,512]{1,0:T(8,128)S(1)}, f32[16,512]{1,0:T(8,128)S(1)}, u32[]{:S(2)}, u32[]{:S(2)}) collective-permute-start(f32[16,512]{1,0:T(8,128)S(1)} %get-tuple-element.46), channel_id=1, source_target_pairs={{0,8},{8,16},{16,24},{24,32},{32,40},{40,48},{48,56},{56,64},{64,7... | collective-permute-start | bytes 98312 | tf_op jit(solution)/shard_map/ppermute | solution.py:645
  21.7 7.2 %collective-permute-start.7 = (f32[16,512]{1,0:T(8,128)S(1)}, f32[16,512]{1,0:T(8,128)S(1)}, u32[]{:S(2)}, u32[]{:S(2)}) collective-permute-start(f32[16,512]{1,0:T(8,128)S(1)} %get-tuple-element.47), channel_id=1, source_target_pairs={{0,248},{8,0},{16,8},{24,16},{32,24},{40,32},{48,40},{56,48},{64,5... | collective-permute-start | bytes 98312 | tf_op jit(solution)/shard_map/ppermute | solution.py:645
  21.8 7.1 %copy-start.10 = (bf16[64,240]{1,0:T(8,128)(2,1)S(1)}, bf16[64,240]{1,0:T(8,128)(2,1)}, u32[]{:S(2)}) copy-start(bf16[64,240]{1,0:T(8,128)(2,1)} %constant.28.clone.source) | copy-start | bytes 92164
  22.1 9.3 %copy-start.1 = (f32[160,288]{1,0:T(8,128)S(1)}, f32[160,288]{1,0:T(8,128)}, u32[]{:S(2)}) copy-start(f32[160,288]{1,0:T(8,128)} %constant.23.clone.solve) | copy-start | bytes 552964
  29.3 4.8 %collective-permute-start.10 = (f32[8,3328]{1,0:T(8,128)S(1)}, f32[8,3328]{1,0:T(8,128)S(1)}, u32[]{:S(2)}, u32[]{:S(2)}) collective-permute-start(f32[8,3328]{1,0:T(8,128)S(1)} %get-tuple-element.52), channel_id=1, source_target_pairs={{0,8},{8,16},{16,24},{24,32},{32,40},{40,48},{48,56},{56,64},{64,7... | collective-permute-start | bytes 319496 | tf_op jit(solution)/shard_map/ppermute | solution.py:645
  29.4 8.1 %collective-permute-start.11 = (f32[8,3328]{1,0:T(8,128)S(1)}, f32[8,3328]{1,0:T(8,128)S(1)}, u32[]{:S(2)}, u32[]{:S(2)}) collective-permute-start(f32[8,3328]{1,0:T(8,128)S(1)} %get-tuple-element.53), channel_id=1, source_target_pairs={{0,248},{8,0},{16,8},{24,16},{32,24},{40,32},{48,40},{56,48},{64,5... | collective-permute-start | bytes 319496 | tf_op jit(solution)/shard_map/ppermute | solution.py:645
  31.4 6.1 %copy-start.4 = (bf16[160,384]{1,0:T(8,128)(2,1)S(1)}, bf16[160,384]{1,0:T(8,128)(2,1)}, u32[]{:S(2)}) copy-start(bf16[160,384]{1,0:T(8,128)(2,1)} %constant.29.clone.solve) | copy-start | bytes 368644
  31.4 6.1 %copy-start.7 = (bf16[128,240]{1,0:T(8,128)(2,1)S(1)}, bf16[128,240]{1,0:T(8,128)(2,1)}, u32[]{:S(2)}) copy-start(bf16[128,240]{1,0:T(8,128)(2,1)} %constant.25.clone.full) | copy-start | bytes 184324
  37.5 13.1 %copy-start.9 = (bf16[64,240]{1,0:T(8,128)(2,1)S(1)}, bf16[64,240]{1,0:T(8,128)(2,1)}, u32[]{:S(2)}) copy-start(bf16[64,240]{1,0:T(8,128)(2,1)} %constant.31.clone.source) | copy-start | bytes 92164
  39.2 11.4 %collective-permute-start.12 = (f32[544,128]{1,0:T(8,128)S(1)}, f32[544,128]{1,0:T(8,128)S(1)}, u32[]{:S(2)}, u32[]{:S(2)}) collective-permute-start(f32[544,128]{1,0:T(8,128)S(1)} %get-tuple-element.59), channel_id=1, source_target_pairs={{0,1},{1,2},{2,3},{3,4},{4,5},{5,6},{6,7},{7,0},{8,9},{9,10},{10,1... | collective-permute-start | bytes 835592 | tf_op jit(solution)/shard_map/ppermute | solution.py:645
  39.3 11.4 %collective-permute-start.13 = (f32[544,128]{1,0:T(8,128)S(1)}, f32[544,128]{1,0:T(8,128)S(1)}, u32[]{:S(2)}, u32[]{:S(2)}) collective-permute-start(f32[544,128]{1,0:T(8,128)S(1)} %get-tuple-element.60), channel_id=1, source_target_pairs={{0,7},{1,0},{2,1},{3,2},{4,3},{5,4},{6,5},{7,6},{8,15},{9,8},{10,9... | collective-permute-start | bytes 835592 | tf_op jit(solution)/shard_map/ppermute | solution.py:645
  41.0 6.5 %collective-permute-start.14 = (f32[264,128]{1,0:T(8,128)S(1)}, f32[264,128]{1,0:T(8,128)S(1)}, u32[]{:S(2)}, u32[]{:S(2)}) collective-permute-start(f32[264,128]{1,0:T(8,128)S(1)} %get-tuple-element.61), channel_id=1, source_target_pairs={{0,2},{1,3},{2,4},{3,5},{4,6},{5,7},{6,0},{7,1},{8,10},{9,11},{10,... | collective-permute-start | bytes 405512 | tf_op jit(solution)/shard_map/ppermute | solution.py:645
  43.6 7.0 %collective-permute-start.15 = (f32[264,128]{1,0:T(8,128)S(1)}, f32[264,128]{1,0:T(8,128)S(1)}, u32[]{:S(2)}, u32[]{:S(2)}) collective-permute-start(f32[264,128]{1,0:T(8,128)S(1)} %get-tuple-element.62), channel_id=1, source_target_pairs={{0,6},{1,7},{2,0},{3,1},{4,2},{5,3},{6,4},{7,5},{8,14},{9,15},{10,... | collective-permute-start | bytes 405512 | tf_op jit(solution)/shard_map/ppermute | solution.py:645
  50.6 2.5 %copy-start.2 = (f32[128,288]{1,0:T(8,128)S(1)}, f32[128,288]{1,0:T(8,128)}, u32[]{:S(2)}) copy-start(f32[128,288]{1,0:T(8,128)} %constant.30.clone.solve) | copy-start | bytes 442372
  51.0 4.6 %collective-permute-start.16 = (f32[8,2688]{1,0:T(8,128)S(1)}, f32[8,2688]{1,0:T(8,128)S(1)}, u32[]{:S(2)}, u32[]{:S(2)}) collective-permute-start(f32[8,2688]{1,0:T(8,128)S(1)} %get-tuple-element.64), channel_id=1, source_target_pairs={{0,8},{8,16},{16,24},{24,32},{32,40},{40,48},{48,56},{56,64},{64,7... | collective-permute-start | bytes 258056 | tf_op jit(solution)/shard_map/ppermute | solution.py:645
  51.1 7.9 %collective-permute-start.17 = (f32[8,2688]{1,0:T(8,128)S(1)}, f32[8,2688]{1,0:T(8,128)S(1)}, u32[]{:S(2)}, u32[]{:S(2)}) collective-permute-start(f32[8,2688]{1,0:T(8,128)S(1)} %get-tuple-element.65), channel_id=1, source_target_pairs={{0,248},{8,0},{16,8},{24,16},{32,24},{40,32},{48,40},{56,48},{64,5... | collective-permute-start | bytes 258056 | tf_op jit(solution)/shard_map/ppermute | solution.py:645
  53.1 5.9 %copy-start.5 = (bf16[128,384]{1,0:T(8,128)(2,1)S(1)}, bf16[128,384]{1,0:T(8,128)(2,1)}, u32[]{:S(2)}) copy-start(bf16[128,384]{1,0:T(8,128)(2,1)} %constant.32.clone.solve) | copy-start | bytes 294916

commit v13 on v10

--- a/solution.py
+++ b/solution.py
@@ -243,6 +243,10 @@
     slot(downward, cells, 6)[...] = thick[:, lane(0)]
 
 
+def added(parts):
+    return functools.reduce(lambda a, b: a + b, parts)
+
+
 def weighed(weights, value_at, r, home):
     total = None
     for reach, factor in weights:
@@ -377,7 +381,7 @@
                 total = total + factor * across(e + reach)
         middle[:cells, lane(e + 2)] = masked(total, e, masks)
         middle[cells:, lane(e + 2)] = masked(side, e, masks)
-    held[...] = sum(split_dot(moments[c], section[cells * c : cells * (c + 1), :]) for c in range(3))
+    held[...] = added(split_dot(moments[c], section[cells * c : cells * (c + 1), :]) for c in range(3))
 
 
 def first_source(cells, middle, arrived, ext):
@@ -539,7 +543,7 @@
         return stream_slope(phi(r))
     if c == 1:
         inside = lambda r: -extent.margin <= r < ROWS + extent.margin
-        return sum(factor * phi(r + reach) for reach, factor in DIFFERENCE if inside(r + reach))
+        return added(factor * phi(r + reach) for reach, factor in DIFFERENCE if inside(r + reach))
     return found[slope_rows, lane(r + extent.margin)]
 
 
@@ -590,18 +594,18 @@
             up_two, down_two = turned(here, 2), turned(here, -2)
             carried = (
                 tile(0, r) * first_diff(up_one, down_one, up_two, down_two)
-                + tile(1, r) * sum(factor * tile(c, r + reach) for reach, factor in DIFFERENCE)
+                + tile(1, r) * added(factor * tile(c, r + reach) for reach, factor in DIFFERENCE)
                 + tile(2, r) * spanned[:cells, lane(r)]
             )
             spread = (
                 (4.0 / 3.0) * (up_one + down_one)
                 - (1.0 / 12.0) * (up_two + down_two)
                 - 5.0 * here
-                + sum(factor * tile(c, r + reach) for reach, factor in CURVE)
+                + added(factor * tile(c, r + reach) for reach, factor in CURVE)
                 + spanned[cells:, lane(r)]
             )
-            moved = here + time_step * (thick[:, lane(r)] * spread - carried)
-            following[rows, lane(r)] = 0.5 * start[rows, lane(r)] + 0.5 * moved
+            change = (0.5 * time_step) * (thick[:, lane(r)] * spread - carried)
+            following[rows, lane(r)] = 0.5 * (start[rows, lane(r)] + here) + change
     phi = lambda r: found[:cells, lane(r + FIRST.margin)]
     scale = 0.5 * time_step / 144.0
     owed = {

time: 57.5 us -> 57.6 us (level)
  no operation moved by 1% of the time
where the time goes in v13:
time: 57.6 us; the launch traced here: 57.4 us
  waiting for transfers between devices  29.6 us (51%)
  starting transfers between devices  17.4 us (30%)
  Pallas kernels  10.1 us (18%)
    ppermute x16, waiting for transfers between devices, shifted(): lax.ppermute(block, axis, [(i, (i + step) % count) for i in range(count)])  29.6 us
    ppermute x16, starting transfers between devices, shifted(): lax.ppermute(block, axis, [(i, (i + step) % count) for i in range(count)])  17.4 us
    pallas_call x10, Pallas kernels, call(): pl.pallas_call(body, out_shape=[jax.ShapeDtypeStruct(s, jnp.float32) for...  10.1 us
  transfers between devices with their start and end apart: 16, of which 12 were waited for; matrix products, arithmetic and copies ran while one was open for 0% of the time, Pallas kernels for 8%

profile of v13, /device:TPU:126, one launch (start us, length us, event | category | flops | bytes accessed | tf_op | source)
XLA Modules:
  0.0 57.4 jit_solution(3833134884906814487)
XLA Ops:
  0.0 0.0 copy-start.8
  0.0 1.3 %shard_map.127 = (f32[192,512]{1,0:T(8,128)S(1)}, f32[64,512]{1,0:T(8,128)S(1)}, f32[16,512]{1,0:T(8,128)S(1)}, f32[16,512]{1,0:T(8,128)S(1)}, f32[448,128]{1,0:T(8,128)S(1)}, /*index=5*/f32[448,128]{1,0:T(8,128)S(1)}) custom-call(f32[3,64,4,128]{3,2,1,0:T(4,128)} %velocity.1, f32[64,4,128]{2,1,0:T(4,128)} %viscosity.1, ...), custom_call_target="tpu_custom_call" | custom-call | tf_op jit(solution)/shard_map/pallas_call | solution.py:644
  1.3 0.0 collective-permute-start.2
  1.4 1.7 %collective-permute-start.3 = (f32[448,128]{1,0:T(8,128)S(1)}, f32[448,128]{1,0:T(8,128)S(1)}, u32[]{:S(2)}, u32[]{:S(2)}) collective-permute-start(f32[448,128]{1,0:T(8,128)S(1)} %get-tuple-element.38), channel_id=1, source_target_pairs={{0,7},{1,0},{2,1},{3,2},{4,3},{5,4},{6,5},{7,6},{8,15},{9,8},{10,9... | collective-permute-start | bytes 688136 | tf_op jit(solution)/shard_map/ppermute | solution.py:655
  3.1 3.0 %collective-permute-start = (f32[16,512]{1,0:T(8,128)S(1)}, f32[16,512]{1,0:T(8,128)S(1)}, u32[]{:S(2)}, u32[]{:S(2)}) collective-permute-start(f32[16,512]{1,0:T(8,128)S(1)} %get-tuple-element.35), channel_id=1, source_target_pairs={{0,8},{8,16},{16,24},{24,32},{32,40},{40,48},{48,56},{56,64},{64,7... | collective-permute-start | bytes 98312 | tf_op jit(solution)/shard_map/ppermute | solution.py:655
  6.1 0.0 collective-permute-start.1
  6.1 0.0 copy-done.8
  6.1 0.0 copy-start
  6.1 0.0 copy-start.6
  6.2 0.9 %shard_map.128.rough = f32[192,512]{1,0:T(8,128)S(1)} custom-call(f32[192,512]{1,0:T(8,128)S(1)} %get-tuple-element.33.flat.start, f32[64,512]{1,0:T(8,128)S(1)} %get-tuple-element.34.thick, f32[128,64]{1,0:T(8,128)S(1)} %copy-done.8), custom_call_target="tpu_custom_call" | custom-call | tf_op jit(solution)/shard_map/pallas_call | solution.py:644
  7.1 0.0 copy-start.2
  7.1 0.6 %collective-permute-done.left = f32[16,512]{1,0:T(8,128)S(1)} collective-permute-done((f32[16,512]{1,0:T(8,128)S(1)}, f32[16,512]{1,0:T(8,128)S(1)}, u32[]{:S(2)}, u32[]{:S(2)}) %collective-permute-start) | collective-permute-done | bytes 32800 | tf_op jit(solution)/shard_map/ppermute | solution.py:655
  7.7 5.6 %collective-permute-done.1.right = f32[16,512]{1,0:T(8,128)S(1)} collective-permute-done((f32[16,512]{1,0:T(8,128)S(1)}, f32[16,512]{1,0:T(8,128)S(1)}, u32[]{:S(2)}, u32[]{:S(2)}) %collective-permute-start.1) | collective-permute-done | bytes 32800 | tf_op jit(solution)/shard_map/ppermute | solution.py:655
  13.4 0.0 collective-permute-done.2.low
  13.4 0.0 collective-permute-done.3.high
  13.4 0.0 copy-done
  13.4 0.0 copy-done.6
  13.4 0.5 shard_map.129
  13.9 0.0 collective-permute-start.4
  13.9 1.7 %collective-permute-start.5 = (f32[656,128]{1,0:T(8,128)S(1)}, f32[656,128]{1,0:T(8,128)S(1)}, u32[]{:S(2)}, u32[]{:S(2)}) collective-permute-start(f32[656,128]{1,0:T(8,128)S(1)} %get-tuple-element.42), channel_id=1, source_target_pairs={{0,7},{1,0},{2,1},{3,2},{4,3},{5,4},{6,5},{7,6},{8,15},{9,8},{10,9... | collective-permute-start | bytes 1007624 | tf_op jit(solution)/shard_map/ppermute | solution.py:655
  15.7 2.6 %collective-permute-start.6 = (f32[272,128]{1,0:T(8,128)S(1)}, f32[272,128]{1,0:T(8,128)S(1)}, u32[]{:S(2)}, u32[]{:S(2)}) collective-permute-start(f32[272,128]{1,0:T(8,128)S(1)} %get-tuple-element.45), channel_id=1, source_target_pairs={{0,2},{1,3},{2,4},{3,5},{4,6},{5,7},{6,0},{7,1},{8,10},{9,11},{10,... | collective-permute-start | bytes 417800 | tf_op jit(solution)/shard_map/ppermute | solution.py:655
  18.3 0.0 collective-permute-start.7
  18.3 3.4 %collective-permute-done.4.low_one = f32[656,128]{1,0:T(8,128)S(1)} collective-permute-done((f32[656,128]{1,0:T(8,128)S(1)}, f32[656,128]{1,0:T(8,128)S(1)}, u32[]{:S(2)}, u32[]{:S(2)}) %collective-permute-start.4) | collective-permute-done | bytes 335904 | tf_op jit(solution)/shard_map/ppermute | solution.py:655
  21.7 0.1 collective-permute-done.5.high_one
  21.8 0.0 copy-done.2
  21.8 0.0 copy-start.10
  21.8 0.3 shard_map.130
  22.1 0.3 collective-permute-done.6.low_two
  22.4 3.6 %collective-permute-done.7.high_two = f32[272,128]{1,0:T(8,128)S(1)} collective-permute-done((f32[272,128]{1,0:T(8,128)S(1)}, f32[272,128]{1,0:T(8,128)S(1)}, u32[]{:S(2)}, u32[]{:S(2)}) %collective-permute-start.7) | collective-permute-done | bytes 139296 | tf_op jit(solution)/shard_map/ppermute | solution.py:655
  26.0 0.0 copy-done.10
  26.0 0.0 copy-start.1
  26.0 0.4 shard_map.131
  26.4 0.1 collective-permute-start.8
  26.5 2.0 %collective-permute-start.9 = (f32[8,3968]{1,0:T(8,128)S(1)}, f32[8,3968]{1,0:T(8,128)S(1)}, u32[]{:S(2)}, u32[]{:S(2)}) collective-permute-start(f32[8,3968]{1,0:T(8,128)S(1)} %get-tuple-element.49), channel_id=1, source_target_pairs={{0,248},{8,0},{16,8},{24,16},{32,24},{40,32},{48,40},{56,48},{64,5... | collective-permute-start | bytes 380936 | tf_op jit(solution)/shard_map/ppermute | solution.py:655
  28.5 0.0 copy-done.1
  28.5 0.0 copy-start.4
  28.5 0.0 copy-start.7
  28.5 1.8 %shard_map.132.partial = f32[160,1280]{1,0:T(8,128)S(1)} custom-call(f32[72,2048]{1,0:T(8,128)S(1)} %get-tuple-element.47.ext, f32[160,288]{1,0:T(8,128)S(1)} %copy-done.1), custom_call_target="tpu_custom_call" | custom-call | tf_op jit(solution)/shard_map/pallas_call | solution.py:644
  30.3 1.1 %collective-permute-done.8.left = f32[8,3968]{1,0:T(8,128)S(1)} collective-permute-done((f32[8,3968]{1,0:T(8,128)S(1)}, f32[8,3968]{1,0:T(8,128)S(1)}, u32[]{:S(2)}, u32[]{:S(2)}) %collective-permute-start.8) | collective-permute-done | bytes 127008 | tf_op jit(solution)/shard_map/ppermute | solution.py:655
  31.4 3.4 %collective-permute-done.9.right = f32[8,3968]{1,0:T(8,128)S(1)} collective-permute-done((f32[8,3968]{1,0:T(8,128)S(1)}, f32[8,3968]{1,0:T(8,128)S(1)}, u32[]{:S(2)}, u32[]{:S(2)}) %collective-permute-start.9) | collective-permute-done | bytes 127008 | tf_op jit(solution)/shard_map/ppermute | solution.py:655
  34.8 0.0 copy-done.4
  34.8 0.0 copy-done.7
  34.8 0.0 copy-start.9
  34.8 1.7 %shard_map.133 = (f32[192,512]{1,0:T(8,128)S(1)}, f32[72,512]{1,0:T(8,128)S(1)}, f32[128,128]{1,0:T(8,128)S(1)}, f32[544,128]{1,0:T(8,128)S(1)}, f32[544,128]{1,...) custom-call(f32[160,1280]{1,0:T(8,128)S(1)} %shard_map.132.partial, ...), custom_call_target="tpu_custom_call" | custom-call | tf_op jit(solution)/shard_map/pallas_call | solution.py:644
  36.5 0.0 collective-permute-start.10
  36.5 1.7 %collective-permute-start.11 = (f32[544,128]{1,0:T(8,128)S(1)}, f32[544,128]{1,0:T(8,128)S(1)}, u32[]{:S(2)}, u32[]{:S(2)}) collective-permute-start(f32[544,128]{1,0:T(8,128)S(1)} %get-tuple-element.54), channel_id=1, source_target_pairs={{0,7},{1,0},{2,1},{3,2},{4,3},{5,4},{6,5},{7,6},{8,15},{9,8},{10,9... | collective-permute-start | bytes 835592 | tf_op jit(solution)/shard_map/ppermute | solution.py:655
  38.3 1.9 %collective-permute-start.12 = (f32[264,128]{1,0:T(8,128)S(1)}, f32[264,128]{1,0:T(8,128)S(1)}, u32[]{:S(2)}, u32[]{:S(2)}) collective-permute-start(f32[264,128]{1,0:T(8,128)S(1)} %get-tuple-element.55), channel_id=1, source_target_pairs={{0,2},{1,3},{2,4},{3,5},{4,6},{5,7},{6,0},{7,1},{8,10},{9,11},{10,... | collective-permute-start | bytes 405512 | tf_op jit(solution)/shard_map/ppermute | solution.py:655
  40.1 0.2 collective-permute-start.13
  40.3 4.5 %collective-permute-done.12.low_two = f32[264,128]{1,0:T(8,128)S(1)} collective-permute-done((f32[264,128]{1,0:T(8,128)S(1)}, f32[264,128]{1,0:T(8,128)S(1)}, u32[]{:S(2)}, u32[]{:S(2)}) %collective-permute-start.12) | collective-permute-done | bytes 135200 | tf_op jit(solution)/shard_map/ppermute | solution.py:655
  44.8 2.4 %collective-permute-done.13.high_two = f32[264,128]{1,0:T(8,128)S(1)} collective-permute-done((f32[264,128]{1,0:T(8,128)S(1)}, f32[264,128]{1,0:T(8,128)S(1)}, u32[]{:S(2)}, u32[]{:S(2)}) %collective-permute-start.13) | collective-permute-done | bytes 135200 | tf_op jit(solution)/shard_map/ppermute | solution.py:655
  47.2 0.0 collective-permute-done.10.low_one
  47.2 0.0 collective-permute-done.11.high_one
  47.2 0.0 copy-done.9
  47.2 0.0 copy-start.3
  47.2 0.3 shard_map.134
  47.6 0.4 collective-permute-start.14
  48.0 1.9 %collective-permute-start.15 = (f32[8,2688]{1,0:T(8,128)S(1)}, f32[8,2688]{1,0:T(8,128)S(1)}, u32[]{:S(2)}, u32[]{:S(2)}) collective-permute-start(f32[8,2688]{1,0:T(8,128)S(1)} %get-tuple-element.59), channel_id=1, source_target_pairs={{0,248},{8,0},{16,8},{24,16},{32,24},{40,32},{48,40},{56,48},{64,5... | collective-permute-start | bytes 258056 | tf_op jit(solution)/shard_map/ppermute | solution.py:655
  49.9 0.0 copy-done.3
  49.9 0.0 copy-start.5
  49.9 1.4 %shard_map.135.partial = f32[128,1024]{1,0:T(8,128)S(1)} custom-call(f32[72,1792]{1,0:T(8,128)S(1)} %get-tuple-element.57.ext, f32[128,288]{1,0:T(8,128)S(1)} %copy-done.3), custom_call_target="tpu_custom_call" | custom-call | tf_op jit(solution)/shard_map/pallas_call | solution.py:644
  51.3 1.1 %collective-permute-done.14.left = f32[8,2688]{1,0:T(8,128)S(1)} collective-permute-done((f32[8,2688]{1,0:T(8,128)S(1)}, f32[8,2688]{1,0:T(8,128)S(1)}, u32[]{:S(2)}, u32[]{:S(2)}) %collective-permute-start.14) | collective-permute-done | bytes 86048 | tf_op jit(solution)/shard_map/ppermute | solution.py:655
  52.3 3.4 %collective-permute-done.15.right = f32[8,2688]{1,0:T(8,128)S(1)} collective-permute-done((f32[8,2688]{1,0:T(8,128)S(1)}, f32[8,2688]{1,0:T(8,128)S(1)}, u32[]{:S(2)}, u32[]{:S(2)}) %collective-permute-start.15) | collective-permute-done | bytes 86048 | tf_op jit(solution)/shard_map/ppermute | solution.py:655
  55.8 0.0 copy-done.5
  55.8 1.4 %shard_map.136 = f32[3,64,4,128]{3,2,1,0:T(4,128)} custom-call(f32[128,1024]{1,0:T(8,128)S(1)} %shard_map.135.partial, f32[8,2688]{1,0:T(8,128)S(1)} %collective-permute-done.14.left, f32[8,2688]{1,0:T(8,128)S(1)} %collective-permute-done.15.right, f32[192,512]{1,0:T(8,128)S(1)} %get-tuple-element.51.section, f32[128,128]{1,0:T(8,128)S(1)} %get-tuple-element.60.fixed, ...), custom_call_target="tpu_custom_call" | custom-call | tf_op jit(solution)/shard_map/pallas_call | solution.py:644
Async XLA Ops:
  0.0 6.1 %copy-start.8 = (f32[128,64]{1,0:T(8,128)S(1)}, f32[128,64]{1,0:T(8,128)}, u32[]{:S(2)}) copy-start(f32[128,64]{1,0:T(8,128)} %constant.22.clone.own) | copy-start | bytes 98308
  1.3 12.0 %collective-permute-start.2 = (f32[448,128]{1,0:T(8,128)S(1)}, f32[448,128]{1,0:T(8,128)S(1)}, u32[]{:S(2)}, u32[]{:S(2)}) collective-permute-start(f32[448,128]{1,0:T(8,128)S(1)} %get-tuple-element.37), channel_id=1, source_target_pairs={{0,1},{1,2},{2,3},{3,4},{4,5},{5,6},{6,7},{7,0},{8,9},{9,10},{10,1... | collective-permute-start | bytes 688136 | tf_op jit(solution)/shard_map/ppermute | solution.py:655
  1.4 12.0 %collective-permute-start.3 = (f32[448,128]{1,0:T(8,128)S(1)}, f32[448,128]{1,0:T(8,128)S(1)}, u32[]{:S(2)}, u32[]{:S(2)}) collective-permute-start(f32[448,128]{1,0:T(8,128)S(1)} %get-tuple-element.38), channel_id=1, source_target_pairs={{0,7},{1,0},{2,1},{3,2},{4,3},{5,4},{6,5},{7,6},{8,15},{9,8},{10,9... | collective-permute-start | bytes 688136 | tf_op jit(solution)/shard_map/ppermute | solution.py:655
  3.1 4.6 %collective-permute-start = (f32[16,512]{1,0:T(8,128)S(1)}, f32[16,512]{1,0:T(8,128)S(1)}, u32[]{:S(2)}, u32[]{:S(2)}) collective-permute-start(f32[16,512]{1,0:T(8,128)S(1)} %get-tuple-element.35), channel_id=1, source_target_pairs={{0,8},{8,16},{16,24},{24,32},{32,40},{40,48},{48,56},{56,64},{64,7... | collective-permute-start | bytes 98312 | tf_op jit(solution)/shard_map/ppermute | solution.py:655
  6.1 7.2 %collective-permute-start.1 = (f32[16,512]{1,0:T(8,128)S(1)}, f32[16,512]{1,0:T(8,128)S(1)}, u32[]{:S(2)}, u32[]{:S(2)}) collective-permute-start(f32[16,512]{1,0:T(8,128)S(1)} %get-tuple-element.36), channel_id=1, source_target_pairs={{0,248},{8,0},{16,8},{24,16},{32,24},{40,32},{48,40},{56,48},{64,5... | collective-permute-start | bytes 98312 | tf_op jit(solution)/shard_map/ppermute | solution.py:655
  6.1 7.2 %copy-start = (bf16[72,192]{1,0:T(8,128)(2,1)S(1)}, bf16[72,192]{1,0:T(8,128)(2,1)}, u32[]{:S(2)}) copy-start(bf16[72,192]{1,0:T(8,128)(2,1)} %constant.27.clone.lateral) | copy-start | bytes 82948
  6.1 7.2 %copy-start.6 = (bf16[3,128,96]{2,1,0:T(8,128)(2,1)S(1)}, bf16[3,128,96]{2,1,0:T(8,128)(2,1)}, u32[]{:S(2)}) copy-start(bf16[3,128,96]{2,1,0:T(8,128)(2,1)} %constant.24.clone.slopes) | copy-start | bytes 221188
  7.1 14.8 %copy-start.2 = (bf16[3,32,192]{2,1,0:T(8,128)(2,1)S(1)}, bf16[3,32,192]{2,1,0:T(8,128)(2,1)}, u32[]{:S(2)}) copy-start(bf16[3,32,192]{2,1,0:T(8,128)(2,1)} %constant.26.clone.moments) | copy-start | bytes 110596
  13.9 7.8 %collective-permute-start.4 = (f32[656,128]{1,0:T(8,128)S(1)}, f32[656,128]{1,0:T(8,128)S(1)}, u32[]{:S(2)}, u32[]{:S(2)}) collective-permute-start(f32[656,128]{1,0:T(8,128)S(1)} %get-tuple-element.41), channel_id=1, source_target_pairs={{0,1},{1,2},{2,3},{3,4},{4,5},{5,6},{6,7},{7,0},{8,9},{9,10},{10,1... | collective-permute-start | bytes 1007624 | tf_op jit(solution)/shard_map/ppermute | solution.py:655
  13.9 7.9 %collective-permute-start.5 = (f32[656,128]{1,0:T(8,128)S(1)}, f32[656,128]{1,0:T(8,128)S(1)}, u32[]{:S(2)}, u32[]{:S(2)}) collective-permute-start(f32[656,128]{1,0:T(8,128)S(1)} %get-tuple-element.42), channel_id=1, source_target_pairs={{0,7},{1,0},{2,1},{3,2},{4,3},{5,4},{6,5},{7,6},{8,15},{9,8},{10,9... | collective-permute-start | bytes 1007624 | tf_op jit(solution)/shard_map/ppermute | solution.py:655
  15.7 6.8 %collective-permute-start.6 = (f32[272,128]{1,0:T(8,128)S(1)}, f32[272,128]{1,0:T(8,128)S(1)}, u32[]{:S(2)}, u32[]{:S(2)}) collective-permute-start(f32[272,128]{1,0:T(8,128)S(1)} %get-tuple-element.45), channel_id=1, source_target_pairs={{0,2},{1,3},{2,4},{3,5},{4,6},{5,7},{6,0},{7,1},{8,10},{9,11},{10,... | collective-permute-start | bytes 417800 | tf_op jit(solution)/shard_map/ppermute | solution.py:655
  18.3 7.7 %collective-permute-start.7 = (f32[272,128]{1,0:T(8,128)S(1)}, f32[272,128]{1,0:T(8,128)S(1)}, u32[]{:S(2)}, u32[]{:S(2)}) collective-permute-start(f32[272,128]{1,0:T(8,128)S(1)} %get-tuple-element.46), channel_id=1, source_target_pairs={{0,6},{1,7},{2,0},{3,1},{4,2},{5,3},{6,4},{7,5},{8,14},{9,15},{10,... | collective-permute-start | bytes 417800 | tf_op jit(solution)/shard_map/ppermute | solution.py:655
  21.8 4.2 %copy-start.10 = (bf16[64,240]{1,0:T(8,128)(2,1)S(1)}, bf16[64,240]{1,0:T(8,128)(2,1)}, u32[]{:S(2)}) copy-start(bf16[64,240]{1,0:T(8,128)(2,1)} %constant.28.clone.source) | copy-start | bytes 92164
  26.0 2.5 %copy-start.1 = (f32[160,288]{1,0:T(8,128)S(1)}, f32[160,288]{1,0:T(8,128)}, u32[]{:S(2)}) copy-start(f32[160,288]{1,0:T(8,128)} %constant.23.clone.solve) | copy-start | bytes 552964
  26.4 5.0 %collective-permute-start.8 = (f32[8,3968]{1,0:T(8,128)S(1)}, f32[8,3968]{1,0:T(8,128)S(1)}, u32[]{:S(2)}, u32[]{:S(2)}) collective-permute-start(f32[8,3968]{1,0:T(8,128)S(1)} %get-tuple-element.48), channel_id=1, source_target_pairs={{0,8},{8,16},{16,24},{24,32},{32,40},{40,48},{48,56},{56,64},{64,7... | collective-permute-start | bytes 380936 | tf_op jit(solution)/shard_map/ppermute | solution.py:655
  26.5 8.3 %collective-permute-start.9 = (f32[8,3968]{1,0:T(8,128)S(1)}, f32[8,3968]{1,0:T(8,128)S(1)}, u32[]{:S(2)}, u32[]{:S(2)}) collective-permute-start(f32[8,3968]{1,0:T(8,128)S(1)} %get-tuple-element.49), channel_id=1, source_target_pairs={{0,248},{8,0},{16,8},{24,16},{32,24},{40,32},{48,40},{56,48},{64,5... | collective-permute-start | bytes 380936 | tf_op jit(solution)/shard_map/ppermute | solution.py:655
  28.5 6.3 %copy-start.4 = (bf16[160,384]{1,0:T(8,128)(2,1)S(1)}, bf16[160,384]{1,0:T(8,128)(2,1)}, u32[]{:S(2)}) copy-start(bf16[160,384]{1,0:T(8,128)(2,1)} %constant.29.clone.solve) | copy-start | bytes 368644
  28.5 6.3 %copy-start.7 = (bf16[128,240]{1,0:T(8,128)(2,1)S(1)}, bf16[128,240]{1,0:T(8,128)(2,1)}, u32[]{:S(2)}) copy-start(bf16[128,240]{1,0:T(8,128)(2,1)} %constant.25.clone.full) | copy-start | bytes 184324
  34.8 12.4 %copy-start.9 = (bf16[64,240]{1,0:T(8,128)(2,1)S(1)}, bf16[64,240]{1,0:T(8,128)(2,1)}, u32[]{:S(2)}) copy-start(bf16[64,240]{1,0:T(8,128)(2,1)} %constant.31.clone.source) | copy-start | bytes 92164
  36.5 10.7 %collective-permute-start.10 = (f32[544,128]{1,0:T(8,128)S(1)}, f32[544,128]{1,0:T(8,128)S(1)}, u32[]{:S(2)}, u32[]{:S(2)}) collective-permute-start(f32[544,128]{1,0:T(8,128)S(1)} %get-tuple-element.53), channel_id=1, source_target_pairs={{0,1},{1,2},{2,3},{3,4},{4,5},{5,6},{6,7},{7,0},{8,9},{9,10},{10,1... | collective-permute-start | bytes 835592 | tf_op jit(solution)/shard_map/ppermute | solution.py:655
  36.5 10.7 %collective-permute-start.11 = (f32[544,128]{1,0:T(8,128)S(1)}, f32[544,128]{1,0:T(8,128)S(1)}, u32[]{:S(2)}, u32[]{:S(2)}) collective-permute-start(f32[544,128]{1,0:T(8,128)S(1)} %get-tuple-element.54), channel_id=1, source_target_pairs={{0,7},{1,0},{2,1},{3,2},{4,3},{5,4},{6,5},{7,6},{8,15},{9,8},{10,9... | collective-permute-start | bytes 835592 | tf_op jit(solution)/shard_map/ppermute | solution.py:655
  38.3 6.5 %collective-permute-start.12 = (f32[264,128]{1,0:T(8,128)S(1)}, f32[264,128]{1,0:T(8,128)S(1)}, u32[]{:S(2)}, u32[]{:S(2)}) collective-permute-start(f32[264,128]{1,0:T(8,128)S(1)} %get-tuple-element.55), channel_id=1, source_target_pairs={{0,2},{1,3},{2,4},{3,5},{4,6},{5,7},{6,0},{7,1},{8,10},{9,11},{10,... | collective-permute-start | bytes 405512 | tf_op jit(solution)/shard_map/ppermute | solution.py:655
  40.1 7.1 %collective-permute-start.13 = (f32[264,128]{1,0:T(8,128)S(1)}, f32[264,128]{1,0:T(8,128)S(1)}, u32[]{:S(2)}, u32[]{:S(2)}) collective-permute-start(f32[264,128]{1,0:T(8,128)S(1)} %get-tuple-element.56), channel_id=1, source_target_pairs={{0,6},{1,7},{2,0},{3,1},{4,2},{5,3},{6,4},{7,5},{8,14},{9,15},{10,... | collective-permute-start | bytes 405512 | tf_op jit(solution)/shard_map/ppermute | solution.py:655
  47.2 2.6 %copy-start.3 = (f32[128,288]{1,0:T(8,128)S(1)}, f32[128,288]{1,0:T(8,128)}, u32[]{:S(2)}) copy-start(f32[128,288]{1,0:T(8,128)} %constant.30.clone.solve) | copy-start | bytes 442372
  47.6 4.7 %collective-permute-start.14 = (f32[8,2688]{1,0:T(8,128)S(1)}, f32[8,2688]{1,0:T(8,128)S(1)}, u32[]{:S(2)}, u32[]{:S(2)}) collective-permute-start(f32[8,2688]{1,0:T(8,128)S(1)} %get-tuple-element.58), channel_id=1, source_target_pairs={{0,8},{8,16},{16,24},{24,32},{32,40},{40,48},{48,56},{56,64},{64,7... | collective-permute-start | bytes 258056 | tf_op jit(solution)/shard_map/ppermute | solution.py:655
  48.0 7.8 %collective-permute-start.15 = (f32[8,2688]{1,0:T(8,128)S(1)}, f32[8,2688]{1,0:T(8,128)S(1)}, u32[]{:S(2)}, u32[]{:S(2)}) collective-permute-start(f32[8,2688]{1,0:T(8,128)S(1)} %get-tuple-element.59), channel_id=1, source_target_pairs={{0,248},{8,0},{16,8},{24,16},{32,24},{40,32},{48,40},{56,48},{64,5... | collective-permute-start | bytes 258056 | tf_op jit(solution)/shard_map/ppermute | solution.py:655
  49.9 5.9 %copy-start.5 = (bf16[128,384]{1,0:T(8,128)(2,1)S(1)}, bf16[128,384]{1,0:T(8,128)(2,1)}, u32[]{:S(2)}) copy-start(bf16[128,384]{1,0:T(8,128)(2,1)} %constant.32.clone.solve) | copy-start | bytes 294916

commit v14 on v10

--- a/solution.py
+++ b/solution.py
@@ -222,7 +222,7 @@
             )
     for r in range(ROWS):
         copies.append(pltpu.make_async_copy(viscosity.at[:, r, :], thick.at[:, lane(r)], sems.at[len(copies)]))
-    for copy in copies:
+    for copy in copies[1:] + copies[:1]:
         copy.start()
     copies[0].wait()
     both = None

time: 57.5 us -> 57.7 us (level)
  no operation moved by 1% of the time
where the time goes in v14:
time: 57.7 us; the launch traced here: 57.6 us
  waiting for transfers between devices  29.6 us (51%)
  starting transfers between devices  17.3 us (30%)
  Pallas kernels  10.3 us (18%)
    ppermute x16, waiting for transfers between devices, shifted(): lax.ppermute(block, axis, [(i, (i + step) % count) for i in range(count)])  29.6 us
    ppermute x16, starting transfers between devices, shifted(): lax.ppermute(block, axis, [(i, (i + step) % count) for i in range(count)])  17.3 us
    pallas_call x10, Pallas kernels, call(): pl.pallas_call(body, out_shape=[jax.ShapeDtypeStruct(s, jnp.float32) for...  10.3 us
  transfers between devices with their start and end apart: 16, of which 12 were waited for; matrix products, arithmetic and copies ran while one was open for 0% of the time, Pallas kernels for 8%

profile of v14, /device:TPU:126, one launch (start us, length us, event | category | flops | bytes accessed | tf_op | source)
XLA Modules:
  0.0 57.6 jit_solution(17094171808723418381)
XLA Ops:
  0.0 0.0 copy-start.8
  0.0 1.5 %shard_map.127 = (f32[192,512]{1,0:T(8,128)S(1)}, f32[64,512]{1,0:T(8,128)S(1)}, f32[16,512]{1,0:T(8,128)S(1)}, f32[16,512]{1,0:T(8,128)S(1)}, f32[448,128]{1,0:T(8,128)S(1)}, /*index=5*/f32[448,128]{1,0:T(8,128)S(1)}) custom-call(f32[3,64,4,128]{3,2,1,0:T(4,128)} %velocity.1, f32[64,4,128]{2,1,0:T(4,128)} %viscosity.1, ...), custom_call_target="tpu_custom_call" | custom-call | tf_op jit(solution)/shard_map/pallas_call | solution.py:640
  1.5 0.0 collective-permute-start.2
  1.6 1.7 %collective-permute-start.3 = (f32[448,128]{1,0:T(8,128)S(1)}, f32[448,128]{1,0:T(8,128)S(1)}, u32[]{:S(2)}, u32[]{:S(2)}) collective-permute-start(f32[448,128]{1,0:T(8,128)S(1)} %get-tuple-element.38), channel_id=1, source_target_pairs={{0,7},{1,0},{2,1},{3,2},{4,3},{5,4},{6,5},{7,6},{8,15},{9,8},{10,9... | collective-permute-start | bytes 688136 | tf_op jit(solution)/shard_map/ppermute | solution.py:651
  3.3 3.0 %collective-permute-start = (f32[16,512]{1,0:T(8,128)S(1)}, f32[16,512]{1,0:T(8,128)S(1)}, u32[]{:S(2)}, u32[]{:S(2)}) collective-permute-start(f32[16,512]{1,0:T(8,128)S(1)} %get-tuple-element.35), channel_id=1, source_target_pairs={{0,8},{8,16},{16,24},{24,32},{32,40},{40,48},{48,56},{56,64},{64,7... | collective-permute-start | bytes 98312 | tf_op jit(solution)/shard_map/ppermute | solution.py:651
  6.3 0.0 collective-permute-start.1
  6.3 0.0 copy-done.8
  6.3 0.0 copy-start
  6.3 0.0 copy-start.6
  6.4 0.9 %shard_map.128.rough = f32[192,512]{1,0:T(8,128)S(1)} custom-call(f32[192,512]{1,0:T(8,128)S(1)} %get-tuple-element.33.flat.start, f32[64,512]{1,0:T(8,128)S(1)} %get-tuple-element.34.thick, f32[128,64]{1,0:T(8,128)S(1)} %copy-done.8), custom_call_target="tpu_custom_call" | custom-call | tf_op jit(solution)/shard_map/pallas_call | solution.py:640
  7.3 0.0 copy-start.2
  7.3 0.6 %collective-permute-done.left = f32[16,512]{1,0:T(8,128)S(1)} collective-permute-done((f32[16,512]{1,0:T(8,128)S(1)}, f32[16,512]{1,0:T(8,128)S(1)}, u32[]{:S(2)}, u32[]{:S(2)}) %collective-permute-start) | collective-permute-done | bytes 32800 | tf_op jit(solution)/shard_map/ppermute | solution.py:651
  7.9 5.6 %collective-permute-done.1.right = f32[16,512]{1,0:T(8,128)S(1)} collective-permute-done((f32[16,512]{1,0:T(8,128)S(1)}, f32[16,512]{1,0:T(8,128)S(1)}, u32[]{:S(2)}, u32[]{:S(2)}) %collective-permute-start.1) | collective-permute-done | bytes 32800 | tf_op jit(solution)/shard_map/ppermute | solution.py:651
  13.6 0.0 collective-permute-done.2.low
  13.6 0.0 collective-permute-done.3.high
  13.6 0.0 copy-done
  13.6 0.0 copy-done.6
  13.6 0.5 shard_map.129
  14.1 0.0 collective-permute-start.4
  14.1 1.7 %collective-permute-start.5 = (f32[656,128]{1,0:T(8,128)S(1)}, f32[656,128]{1,0:T(8,128)S(1)}, u32[]{:S(2)}, u32[]{:S(2)}) collective-permute-start(f32[656,128]{1,0:T(8,128)S(1)} %get-tuple-element.42), channel_id=1, source_target_pairs={{0,7},{1,0},{2,1},{3,2},{4,3},{5,4},{6,5},{7,6},{8,15},{9,8},{10,9... | collective-permute-start | bytes 1007624 | tf_op jit(solution)/shard_map/ppermute | solution.py:651
  15.9 2.6 %collective-permute-start.6 = (f32[272,128]{1,0:T(8,128)S(1)}, f32[272,128]{1,0:T(8,128)S(1)}, u32[]{:S(2)}, u32[]{:S(2)}) collective-permute-start(f32[272,128]{1,0:T(8,128)S(1)} %get-tuple-element.45), channel_id=1, source_target_pairs={{0,2},{1,3},{2,4},{3,5},{4,6},{5,7},{6,0},{7,1},{8,10},{9,11},{10,... | collective-permute-start | bytes 417800 | tf_op jit(solution)/shard_map/ppermute | solution.py:651
  18.5 0.0 collective-permute-start.7
  18.5 3.4 %collective-permute-done.4.low_one = f32[656,128]{1,0:T(8,128)S(1)} collective-permute-done((f32[656,128]{1,0:T(8,128)S(1)}, f32[656,128]{1,0:T(8,128)S(1)}, u32[]{:S(2)}, u32[]{:S(2)}) %collective-permute-start.4) | collective-permute-done | bytes 335904 | tf_op jit(solution)/shard_map/ppermute | solution.py:651
  21.9 0.1 collective-permute-done.5.high_one
  22.0 0.0 copy-done.2
  22.0 0.0 copy-start.10
  22.1 0.3 shard_map.130
  22.3 0.3 collective-permute-done.6.low_two
  22.6 3.6 %collective-permute-done.7.high_two = f32[272,128]{1,0:T(8,128)S(1)} collective-permute-done((f32[272,128]{1,0:T(8,128)S(1)}, f32[272,128]{1,0:T(8,128)S(1)}, u32[]{:S(2)}, u32[]{:S(2)}) %collective-permute-start.7) | collective-permute-done | bytes 139296 | tf_op jit(solution)/shard_map/ppermute | solution.py:651
  26.2 0.0 copy-done.10
  26.2 0.0 copy-start.1
  26.2 0.4 shard_map.131
  26.6 0.1 collective-permute-start.8
  26.7 2.0 %collective-permute-start.9 = (f32[8,3968]{1,0:T(8,128)S(1)}, f32[8,3968]{1,0:T(8,128)S(1)}, u32[]{:S(2)}, u32[]{:S(2)}) collective-permute-start(f32[8,3968]{1,0:T(8,128)S(1)} %get-tuple-element.49), channel_id=1, source_target_pairs={{0,248},{8,0},{16,8},{24,16},{32,24},{40,32},{48,40},{56,48},{64,5... | collective-permute-start | bytes 380936 | tf_op jit(solution)/shard_map/ppermute | solution.py:651
  28.7 0.0 copy-done.1
  28.7 0.0 copy-start.4
  28.7 0.0 copy-start.7
  28.7 1.8 %shard_map.132.partial = f32[160,1280]{1,0:T(8,128)S(1)} custom-call(f32[72,2048]{1,0:T(8,128)S(1)} %get-tuple-element.47.ext, f32[160,288]{1,0:T(8,128)S(1)} %copy-done.1), custom_call_target="tpu_custom_call" | custom-call | tf_op jit(solution)/shard_map/pallas_call | solution.py:640
  30.5 1.1 %collective-permute-done.8.left = f32[8,3968]{1,0:T(8,128)S(1)} collective-permute-done((f32[8,3968]{1,0:T(8,128)S(1)}, f32[8,3968]{1,0:T(8,128)S(1)}, u32[]{:S(2)}, u32[]{:S(2)}) %collective-permute-start.8) | collective-permute-done | bytes 127008 | tf_op jit(solution)/shard_map/ppermute | solution.py:651
  31.6 3.4 %collective-permute-done.9.right = f32[8,3968]{1,0:T(8,128)S(1)} collective-permute-done((f32[8,3968]{1,0:T(8,128)S(1)}, f32[8,3968]{1,0:T(8,128)S(1)}, u32[]{:S(2)}, u32[]{:S(2)}) %collective-permute-start.9) | collective-permute-done | bytes 127008 | tf_op jit(solution)/shard_map/ppermute | solution.py:651
  35.0 0.0 copy-done.4
  35.0 0.0 copy-done.7
  35.0 0.0 copy-start.9
  35.0 1.7 %shard_map.133 = (f32[192,512]{1,0:T(8,128)S(1)}, f32[72,512]{1,0:T(8,128)S(1)}, f32[128,128]{1,0:T(8,128)S(1)}, f32[544,128]{1,0:T(8,128)S(1)}, f32[544,128]{1,...) custom-call(f32[160,1280]{1,0:T(8,128)S(1)} %shard_map.132.partial, ...), custom_call_target="tpu_custom_call" | custom-call | tf_op jit(solution)/shard_map/pallas_call | solution.py:640
  36.7 0.0 collective-permute-start.10
  36.7 1.7 %collective-permute-start.11 = (f32[544,128]{1,0:T(8,128)S(1)}, f32[544,128]{1,0:T(8,128)S(1)}, u32[]{:S(2)}, u32[]{:S(2)}) collective-permute-start(f32[544,128]{1,0:T(8,128)S(1)} %get-tuple-element.54), channel_id=1, source_target_pairs={{0,7},{1,0},{2,1},{3,2},{4,3},{5,4},{6,5},{7,6},{8,15},{9,8},{10,9... | collective-permute-start | bytes 835592 | tf_op jit(solution)/shard_map/ppermute | solution.py:651
  38.5 1.9 %collective-permute-start.12 = (f32[264,128]{1,0:T(8,128)S(1)}, f32[264,128]{1,0:T(8,128)S(1)}, u32[]{:S(2)}, u32[]{:S(2)}) collective-permute-start(f32[264,128]{1,0:T(8,128)S(1)} %get-tuple-element.55), channel_id=1, source_target_pairs={{0,2},{1,3},{2,4},{3,5},{4,6},{5,7},{6,0},{7,1},{8,10},{9,11},{10,... | collective-permute-start | bytes 405512 | tf_op jit(solution)/shard_map/ppermute | solution.py:651
  40.3 0.2 collective-permute-start.13
  40.5 4.5 %collective-permute-done.12.low_two = f32[264,128]{1,0:T(8,128)S(1)} collective-permute-done((f32[264,128]{1,0:T(8,128)S(1)}, f32[264,128]{1,0:T(8,128)S(1)}, u32[]{:S(2)}, u32[]{:S(2)}) %collective-permute-start.12) | collective-permute-done | bytes 135200 | tf_op jit(solution)/shard_map/ppermute | solution.py:651
  45.0 2.4 %collective-permute-done.13.high_two = f32[264,128]{1,0:T(8,128)S(1)} collective-permute-done((f32[264,128]{1,0:T(8,128)S(1)}, f32[264,128]{1,0:T(8,128)S(1)}, u32[]{:S(2)}, u32[]{:S(2)}) %collective-permute-start.13) | collective-permute-done | bytes 135200 | tf_op jit(solution)/shard_map/ppermute | solution.py:651
  47.4 0.0 collective-permute-done.10.low_one
  47.4 0.0 collective-permute-done.11.high_one
  47.4 0.0 copy-done.9
  47.4 0.0 copy-start.3
  47.4 0.3 shard_map.134
  47.8 0.4 collective-permute-start.14
  48.1 1.9 %collective-permute-start.15 = (f32[8,2688]{1,0:T(8,128)S(1)}, f32[8,2688]{1,0:T(8,128)S(1)}, u32[]{:S(2)}, u32[]{:S(2)}) collective-permute-start(f32[8,2688]{1,0:T(8,128)S(1)} %get-tuple-element.59), channel_id=1, source_target_pairs={{0,248},{8,0},{16,8},{24,16},{32,24},{40,32},{48,40},{56,48},{64,5... | collective-permute-start | bytes 258056 | tf_op jit(solution)/shard_map/ppermute | solution.py:651
  50.0 0.0 copy-done.3
  50.1 0.0 copy-start.5
  50.1 1.4 %shard_map.135.partial = f32[128,1024]{1,0:T(8,128)S(1)} custom-call(f32[72,1792]{1,0:T(8,128)S(1)} %get-tuple-element.57.ext, f32[128,288]{1,0:T(8,128)S(1)} %copy-done.3), custom_call_target="tpu_custom_call" | custom-call | tf_op jit(solution)/shard_map/pallas_call | solution.py:640
  51.4 1.1 %collective-permute-done.14.left = f32[8,2688]{1,0:T(8,128)S(1)} collective-permute-done((f32[8,2688]{1,0:T(8,128)S(1)}, f32[8,2688]{1,0:T(8,128)S(1)}, u32[]{:S(2)}, u32[]{:S(2)}) %collective-permute-start.14) | collective-permute-done | bytes 86048 | tf_op jit(solution)/shard_map/ppermute | solution.py:651
  52.5 3.4 %collective-permute-done.15.right = f32[8,2688]{1,0:T(8,128)S(1)} collective-permute-done((f32[8,2688]{1,0:T(8,128)S(1)}, f32[8,2688]{1,0:T(8,128)S(1)}, u32[]{:S(2)}, u32[]{:S(2)}) %collective-permute-start.15) | collective-permute-done | bytes 86048 | tf_op jit(solution)/shard_map/ppermute | solution.py:651
  55.9 0.0 copy-done.5
  55.9 1.4 %shard_map.136 = f32[3,64,4,128]{3,2,1,0:T(4,128)} custom-call(f32[128,1024]{1,0:T(8,128)S(1)} %shard_map.135.partial, f32[8,2688]{1,0:T(8,128)S(1)} %collective-permute-done.14.left, f32[8,2688]{1,0:T(8,128)S(1)} %collective-permute-done.15.right, f32[192,512]{1,0:T(8,128)S(1)} %get-tuple-element.51.section, f32[128,128]{1,0:T(8,128)S(1)} %get-tuple-element.60.fixed, ...), custom_call_target="tpu_custom_call" | custom-call | tf_op jit(solution)/shard_map/pallas_call | solution.py:640
Async XLA Ops:
  0.0 6.3 %copy-start.8 = (f32[128,64]{1,0:T(8,128)S(1)}, f32[128,64]{1,0:T(8,128)}, u32[]{:S(2)}) copy-start(f32[128,64]{1,0:T(8,128)} %constant.22.clone.own) | copy-start | bytes 98308
  1.5 12.0 %collective-permute-start.2 = (f32[448,128]{1,0:T(8,128)S(1)}, f32[448,128]{1,0:T(8,128)S(1)}, u32[]{:S(2)}, u32[]{:S(2)}) collective-permute-start(f32[448,128]{1,0:T(8,128)S(1)} %get-tuple-element.37), channel_id=1, source_target_pairs={{0,1},{1,2},{2,3},{3,4},{4,5},{5,6},{6,7},{7,0},{8,9},{9,10},{10,1... | collective-permute-start | bytes 688136 | tf_op jit(solution)/shard_map/ppermute | solution.py:651
  1.6 12.0 %collective-permute-start.3 = (f32[448,128]{1,0:T(8,128)S(1)}, f32[448,128]{1,0:T(8,128)S(1)}, u32[]{:S(2)}, u32[]{:S(2)}) collective-permute-start(f32[448,128]{1,0:T(8,128)S(1)} %get-tuple-element.38), channel_id=1, source_target_pairs={{0,7},{1,0},{2,1},{3,2},{4,3},{5,4},{6,5},{7,6},{8,15},{9,8},{10,9... | collective-permute-start | bytes 688136 | tf_op jit(solution)/shard_map/ppermute | solution.py:651
  3.3 4.6 %collective-permute-start = (f32[16,512]{1,0:T(8,128)S(1)}, f32[16,512]{1,0:T(8,128)S(1)}, u32[]{:S(2)}, u32[]{:S(2)}) collective-permute-start(f32[16,512]{1,0:T(8,128)S(1)} %get-tuple-element.35), channel_id=1, source_target_pairs={{0,8},{8,16},{16,24},{24,32},{32,40},{40,48},{48,56},{56,64},{64,7... | collective-permute-start | bytes 98312 | tf_op jit(solution)/shard_map/ppermute | solution.py:651
  6.3 7.2 %collective-permute-start.1 = (f32[16,512]{1,0:T(8,128)S(1)}, f32[16,512]{1,0:T(8,128)S(1)}, u32[]{:S(2)}, u32[]{:S(2)}) collective-permute-start(f32[16,512]{1,0:T(8,128)S(1)} %get-tuple-element.36), channel_id=1, source_target_pairs={{0,248},{8,0},{16,8},{24,16},{32,24},{40,32},{48,40},{56,48},{64,5... | collective-permute-start | bytes 98312 | tf_op jit(solution)/shard_map/ppermute | solution.py:651
  6.3 7.2 %copy-start = (bf16[72,192]{1,0:T(8,128)(2,1)S(1)}, bf16[72,192]{1,0:T(8,128)(2,1)}, u32[]{:S(2)}) copy-start(bf16[72,192]{1,0:T(8,128)(2,1)} %constant.27.clone.lateral) | copy-start | bytes 82948
  6.3 7.2 %copy-start.6 = (bf16[3,128,96]{2,1,0:T(8,128)(2,1)S(1)}, bf16[3,128,96]{2,1,0:T(8,128)(2,1)}, u32[]{:S(2)}) copy-start(bf16[3,128,96]{2,1,0:T(8,128)(2,1)} %constant.24.clone.slopes) | copy-start | bytes 221188
  7.3 14.7 %copy-start.2 = (bf16[3,32,192]{2,1,0:T(8,128)(2,1)S(1)}, bf16[3,32,192]{2,1,0:T(8,128)(2,1)}, u32[]{:S(2)}) copy-start(bf16[3,32,192]{2,1,0:T(8,128)(2,1)} %constant.26.clone.moments) | copy-start | bytes 110596
  14.1 7.8 %collective-permute-start.4 = (f32[656,128]{1,0:T(8,128)S(1)}, f32[656,128]{1,0:T(8,128)S(1)}, u32[]{:S(2)}, u32[]{:S(2)}) collective-permute-start(f32[656,128]{1,0:T(8,128)S(1)} %get-tuple-element.41), channel_id=1, source_target_pairs={{0,1},{1,2},{2,3},{3,4},{4,5},{5,6},{6,7},{7,0},{8,9},{9,10},{10,1... | collective-permute-start | bytes 1007624 | tf_op jit(solution)/shard_map/ppermute | solution.py:651
  14.1 7.9 %collective-permute-start.5 = (f32[656,128]{1,0:T(8,128)S(1)}, f32[656,128]{1,0:T(8,128)S(1)}, u32[]{:S(2)}, u32[]{:S(2)}) collective-permute-start(f32[656,128]{1,0:T(8,128)S(1)} %get-tuple-element.42), channel_id=1, source_target_pairs={{0,7},{1,0},{2,1},{3,2},{4,3},{5,4},{6,5},{7,6},{8,15},{9,8},{10,9... | collective-permute-start | bytes 1007624 | tf_op jit(solution)/shard_map/ppermute | solution.py:651
  15.9 6.8 %collective-permute-start.6 = (f32[272,128]{1,0:T(8,128)S(1)}, f32[272,128]{1,0:T(8,128)S(1)}, u32[]{:S(2)}, u32[]{:S(2)}) collective-permute-start(f32[272,128]{1,0:T(8,128)S(1)} %get-tuple-element.45), channel_id=1, source_target_pairs={{0,2},{1,3},{2,4},{3,5},{4,6},{5,7},{6,0},{7,1},{8,10},{9,11},{10,... | collective-permute-start | bytes 417800 | tf_op jit(solution)/shard_map/ppermute | solution.py:651
  18.5 7.7 %collective-permute-start.7 = (f32[272,128]{1,0:T(8,128)S(1)}, f32[272,128]{1,0:T(8,128)S(1)}, u32[]{:S(2)}, u32[]{:S(2)}) collective-permute-start(f32[272,128]{1,0:T(8,128)S(1)} %get-tuple-element.46), channel_id=1, source_target_pairs={{0,6},{1,7},{2,0},{3,1},{4,2},{5,3},{6,4},{7,5},{8,14},{9,15},{10,... | collective-permute-start | bytes 417800 | tf_op jit(solution)/shard_map/ppermute | solution.py:651
  22.0 4.2 %copy-start.10 = (bf16[64,240]{1,0:T(8,128)(2,1)S(1)}, bf16[64,240]{1,0:T(8,128)(2,1)}, u32[]{:S(2)}) copy-start(bf16[64,240]{1,0:T(8,128)(2,1)} %constant.28.clone.source) | copy-start | bytes 92164
  26.2 2.5 %copy-start.1 = (f32[160,288]{1,0:T(8,128)S(1)}, f32[160,288]{1,0:T(8,128)}, u32[]{:S(2)}) copy-start(f32[160,288]{1,0:T(8,128)} %constant.23.clone.solve) | copy-start | bytes 552964
  26.6 5.0 %collective-permute-start.8 = (f32[8,3968]{1,0:T(8,128)S(1)}, f32[8,3968]{1,0:T(8,128)S(1)}, u32[]{:S(2)}, u32[]{:S(2)}) collective-permute-start(f32[8,3968]{1,0:T(8,128)S(1)} %get-tuple-element.48), channel_id=1, source_target_pairs={{0,8},{8,16},{16,24},{24,32},{32,40},{40,48},{48,56},{56,64},{64,7... | collective-permute-start | bytes 380936 | tf_op jit(solution)/shard_map/ppermute | solution.py:651
  26.7 8.3 %collective-permute-start.9 = (f32[8,3968]{1,0:T(8,128)S(1)}, f32[8,3968]{1,0:T(8,128)S(1)}, u32[]{:S(2)}, u32[]{:S(2)}) collective-permute-start(f32[8,3968]{1,0:T(8,128)S(1)} %get-tuple-element.49), channel_id=1, source_target_pairs={{0,248},{8,0},{16,8},{24,16},{32,24},{40,32},{48,40},{56,48},{64,5... | collective-permute-start | bytes 380936 | tf_op jit(solution)/shard_map/ppermute | solution.py:651
  28.7 6.3 %copy-start.4 = (bf16[160,384]{1,0:T(8,128)(2,1)S(1)}, bf16[160,384]{1,0:T(8,128)(2,1)}, u32[]{:S(2)}) copy-start(bf16[160,384]{1,0:T(8,128)(2,1)} %constant.29.clone.solve) | copy-start | bytes 368644
  28.7 6.3 %copy-start.7 = (bf16[128,240]{1,0:T(8,128)(2,1)S(1)}, bf16[128,240]{1,0:T(8,128)(2,1)}, u32[]{:S(2)}) copy-start(bf16[128,240]{1,0:T(8,128)(2,1)} %constant.25.clone.full) | copy-start | bytes 184324
  35.0 12.4 %copy-start.9 = (bf16[64,240]{1,0:T(8,128)(2,1)S(1)}, bf16[64,240]{1,0:T(8,128)(2,1)}, u32[]{:S(2)}) copy-start(bf16[64,240]{1,0:T(8,128)(2,1)} %constant.31.clone.source) | copy-start | bytes 92164
  36.7 10.7 %collective-permute-start.10 = (f32[544,128]{1,0:T(8,128)S(1)}, f32[544,128]{1,0:T(8,128)S(1)}, u32[]{:S(2)}, u32[]{:S(2)}) collective-permute-start(f32[544,128]{1,0:T(8,128)S(1)} %get-tuple-element.53), channel_id=1, source_target_pairs={{0,1},{1,2},{2,3},{3,4},{4,5},{5,6},{6,7},{7,0},{8,9},{9,10},{10,1... | collective-permute-start | bytes 835592 | tf_op jit(solution)/shard_map/ppermute | solution.py:651
  36.7 10.7 %collective-permute-start.11 = (f32[544,128]{1,0:T(8,128)S(1)}, f32[544,128]{1,0:T(8,128)S(1)}, u32[]{:S(2)}, u32[]{:S(2)}) collective-permute-start(f32[544,128]{1,0:T(8,128)S(1)} %get-tuple-element.54), channel_id=1, source_target_pairs={{0,7},{1,0},{2,1},{3,2},{4,3},{5,4},{6,5},{7,6},{8,15},{9,8},{10,9... | collective-permute-start | bytes 835592 | tf_op jit(solution)/shard_map/ppermute | solution.py:651
  38.5 6.5 %collective-permute-start.12 = (f32[264,128]{1,0:T(8,128)S(1)}, f32[264,128]{1,0:T(8,128)S(1)}, u32[]{:S(2)}, u32[]{:S(2)}) collective-permute-start(f32[264,128]{1,0:T(8,128)S(1)} %get-tuple-element.55), channel_id=1, source_target_pairs={{0,2},{1,3},{2,4},{3,5},{4,6},{5,7},{6,0},{7,1},{8,10},{9,11},{10,... | collective-permute-start | bytes 405512 | tf_op jit(solution)/shard_map/ppermute | solution.py:651
  40.3 7.1 %collective-permute-start.13 = (f32[264,128]{1,0:T(8,128)S(1)}, f32[264,128]{1,0:T(8,128)S(1)}, u32[]{:S(2)}, u32[]{:S(2)}) collective-permute-start(f32[264,128]{1,0:T(8,128)S(1)} %get-tuple-element.56), channel_id=1, source_target_pairs={{0,6},{1,7},{2,0},{3,1},{4,2},{5,3},{6,4},{7,5},{8,14},{9,15},{10,... | collective-permute-start | bytes 405512 | tf_op jit(solution)/shard_map/ppermute | solution.py:651
  47.4 2.6 %copy-start.3 = (f32[128,288]{1,0:T(8,128)S(1)}, f32[128,288]{1,0:T(8,128)}, u32[]{:S(2)}) copy-start(f32[128,288]{1,0:T(8,128)} %constant.30.clone.solve) | copy-start | bytes 442372
  47.8 4.7 %collective-permute-start.14 = (f32[8,2688]{1,0:T(8,128)S(1)}, f32[8,2688]{1,0:T(8,128)S(1)}, u32[]{:S(2)}, u32[]{:S(2)}) collective-permute-start(f32[8,2688]{1,0:T(8,128)S(1)} %get-tuple-element.58), channel_id=1, source_target_pairs={{0,8},{8,16},{16,24},{24,32},{32,40},{40,48},{48,56},{56,64},{64,7... | collective-permute-start | bytes 258056 | tf_op jit(solution)/shard_map/ppermute | solution.py:651
  48.1 7.8 %collective-permute-start.15 = (f32[8,2688]{1,0:T(8,128)S(1)}, f32[8,2688]{1,0:T(8,128)S(1)}, u32[]{:S(2)}, u32[]{:S(2)}) collective-permute-start(f32[8,2688]{1,0:T(8,128)S(1)} %get-tuple-element.59), channel_id=1, source_target_pairs={{0,248},{8,0},{16,8},{24,16},{32,24},{40,32},{48,40},{56,48},{64,5... | collective-permute-start | bytes 258056 | tf_op jit(solution)/shard_map/ppermute | solution.py:651
  50.1 5.9 %copy-start.5 = (bf16[128,384]{1,0:T(8,128)(2,1)S(1)}, bf16[128,384]{1,0:T(8,128)(2,1)}, u32[]{:S(2)}) copy-start(bf16[128,384]{1,0:T(8,128)(2,1)} %constant.32.clone.solve) | copy-start | bytes 294916
